TPU v7x, 512 devices: a whole 4x4x16 slice. The times are simulated.
512 devices in a mesh: seq: 64 (over z, y), tp: 8 (over x, core).
Axes of the slice: x: 4, y: 4, z: 16, core: 2. Of those that a mesh axis runs over, the one named last changes fastest.
Arguments:
- hidden: bfloat16 [384, 2048], P(None, 'seq'), may hold values from -12 to 12
- ln1_gain: float32 [2048], P('seq'), may hold values from 0.1 to 1.9
- wq: bfloat16 [2048, 2048], P('seq', 'tp'), may hold values from -0.125 to 0.125
- wk: bfloat16 [2048, 1024], P('seq', 'tp'), may hold values from -0.125 to 0.125
- wv: bfloat16 [2048, 1024], P('seq', 'tp'), may hold values from -0.125 to 0.125
- wg: bfloat16 [2048, 2048], P('seq', 'tp'), may hold values from -0.125 to 0.125
- q_gain: float32 [128], replicated, may hold values from 1 to 30
- key_gain: float32 [128], replicated, may hold values from 0.5 to 1.5
- wo: bfloat16 [2048, 2048], P('tp', 'seq'), may hold values from -0.5 to 0.5
- ln2_gain: float32 [2048], P('seq'), may hold values from 0.1 to 1.9
- w_gate: bfloat16 [2048, 6144], P('seq', 'tp'), may hold values from -0.125 to 0.125
- w_up: bfloat16 [2048, 6144], P('seq', 'tp'), may hold values from -0.125 to 0.125
- w_down: bfloat16 [6144, 2048], P('tp', 'seq'), may hold values from -0.078125 to 0.078125
- last_gain: float32 [2048], P('seq'), may hold values from 0.1 to 1.9
- head_weight: bfloat16 [2048, 131072], P(None, ('seq', 'tp')), may hold values from -0.125 to 0.125
- inv_temp: float32 [8], replicated, may hold values from 0.5 to 64
- key_cache: bfloat16 [8, 16384, 1024], P(None, 'seq', 'tp'), may hold values from -40 to 40
- value_cache: bfloat16 [8, 16384, 1024], P(None, 'seq', 'tp'), may hold values from -6 to 6
- lengths: int32 [8], replicated, may hold values from 1 to 16336
- parents: int32 [8, 48], replicated, may hold values from 0 to 46, as said below
- accepted: int32 [8], replicated, may hold values from 0 to 47
Outputs:
- logprobs: float32 [384, 131072], P(None, ('seq', 'tp'))
- next_hidden: bfloat16 [384, 2048], P(None, 'seq')
- updated_key_cache: bfloat16 [8, 16384, 1024], P(None, 'seq', 'tp')
- updated_value_cache: bfloat16 [8, 16384, 1024], P(None, 'seq', 'tp')
Inputs may be any that keep to these rules, and one draw needn't show every extreme that they name: parents[r, 0] = 0; for i >= 1, i - 4 <= parents[r, i] < i.
All inputs are finite; a program needn't handle non-finite values.
Results may differ from a plain program's by a relative error of at most 0.012.
Values may be sent and summed in bfloat16 or wider, within the bound.
No kernel may reach another device: no remote copies, remote signals or barrier semaphores. Data moves between devices by JAX's collectives and lax.ppermute only.
A program may use at most 128 MiB of HBM per device.

v0:
```python
import jax
import jax.numpy as jnp
from jax import lax
from jax.sharding import PartitionSpec as P

EPSILON = 1e-06
ROPE_BASE = 1000000.0
NEGATIVE = -1e30


def ancestry(parents):
    node_count = parents.shape[-1]
    node_ids = jnp.arange(node_count, dtype=jnp.int32)
    reachable = (parents[..., :, None] == node_ids[None, :]).astype(jnp.float32)
    reachable = jnp.maximum(reachable, jnp.eye(node_count, dtype=jnp.float32))
    for turn in range((node_count - 1).bit_length()):
        reachable = jnp.minimum(
            jnp.einsum("rij,rjk->rik", reachable, reachable, precision=lax.Precision.HIGHEST), 1.0
        )
    return reachable


def head_norm(values, gain):
    meansq = jnp.mean(values * values, axis=-1, keepdims=True)
    return values * lax.rsqrt(meansq + EPSILON) * gain


def apply_rotary(values, places):
    half_dim = values.shape[-1] // 2
    spread = ROPE_BASE ** (-jnp.arange(half_dim, dtype=jnp.float32) / half_dim)
    angles = places.astype(jnp.float32)[:, None] * spread[None, :]
    cosine = jnp.cos(angles)[:, None, :]
    sine = jnp.sin(angles)[:, None, :]
    lower_part = values[..., :half_dim]
    upper_part = values[..., half_dim:]
    return jnp.concatenate(
        [lower_part * cosine - upper_part * sine, upper_part * cosine + lower_part * sine], axis=-1
    )


def cache_part(query_blocks, key_block, value_block, valid_slot):
    scores = jnp.einsum(
        "rikgd,rckd->rkgic", query_blocks, key_block, preferred_element_type=jnp.float32
    )
    valid_slot = valid_slot[:, None, None, None, :]
    row_peak = jnp.max(jnp.where(valid_slot, scores, NEGATIVE), axis=-1)
    weights = jnp.where(valid_slot, jnp.exp(scores - row_peak[..., None]), 0.0)
    row_mass = jnp.sum(weights, axis=-1)
    weighted = jnp.einsum(
        "rkgic,rckd->rkgid",
        weights.astype(jnp.bfloat16),
        value_block,
        preferred_element_type=jnp.float32,
    )
    return (row_peak, row_mass, weighted)


def on_device(
    hidden,
    ln1_gain,
    wq,
    wk,
    wv,
    wg,
    q_gain,
    key_gain,
    wo,
    ln2_gain,
    w_gate,
    w_up,
    w_down,
    last_gain,
    head_weight,
    inv_temp,
    key_cache,
    value_cache,
    lengths,
    parents,
    accepted,
):
    seq_count = lax.axis_size("seq")
    model_width = hidden.shape[1] * seq_count
    head_dim = q_gain.shape[0]
    query_heads = wq.shape[1] // head_dim
    kv_heads = wk.shape[1] // head_dim
    query_group_size = query_heads // kv_heads
    requests, tree_size = parents.shape
    token_count = hidden.shape[0]
    slot_count = key_cache.shape[1]
    slot_start = lax.axis_index("seq") * slot_count
    parent_links = ancestry(parents)
    tree_node_depth = jnp.sum((parent_links > 0.5).astype(jnp.int32), axis=-1) - 1
    token_position = (lengths[:, None] + tree_node_depth).reshape(-1)
    hidden_wide = hidden.astype(jnp.float32)
    squares = lax.psum(jnp.sum(hidden_wide * hidden_wide, axis=1), "seq")
    normed1 = (hidden_wide * lax.rsqrt(squares / model_width + EPSILON)[:, None] * ln1_gain).astype(
        jnp.bfloat16
    )
    q_sum, key_sum, v_sum, gate = lax.psum(
        (
            jnp.dot(normed1, wq, preferred_element_type=jnp.float32),
            jnp.dot(normed1, wk, preferred_element_type=jnp.float32),
            jnp.dot(normed1, wv, preferred_element_type=jnp.float32),
            jnp.dot(normed1, wg, preferred_element_type=jnp.float32),
        ),
        "seq",
    )
    query_rows_all = apply_rotary(
        head_norm(q_sum.reshape(token_count, query_heads, head_dim), q_gain), token_position
    ) * head_dim ** (-0.5)
    query_rows_all = query_rows_all.astype(jnp.bfloat16).reshape(
        requests, tree_size, kv_heads, query_group_size, head_dim
    )
    draft_keys = apply_rotary(
        head_norm(key_sum.reshape(token_count, kv_heads, head_dim), key_gain), token_position
    ).astype(jnp.bfloat16)
    draft_values = v_sum.astype(jnp.bfloat16)
    tree_keys = draft_keys.reshape(requests, tree_size, kv_heads, head_dim)
    tree_values = draft_values.reshape(requests, tree_size, kv_heads, head_dim)
    cache_keys = key_cache.reshape(requests, slot_count, kv_heads, head_dim)
    cache_values = value_cache.reshape(requests, slot_count, kv_heads, head_dim)
    slot_ids = slot_start + jnp.arange(slot_count, dtype=jnp.int32)
    local_state = cache_part(
        query_rows_all, cache_keys, cache_values, slot_ids[None, :] < lengths[:, None]
    )
    local_peak, local_mass, local_sum = local_state
    cache_peak = lax.pmax(local_peak, "seq")
    factor = jnp.exp(local_peak - cache_peak)
    cache_mass, cache_sum = lax.psum((local_mass * factor, local_sum * factor[..., None]), "seq")
    tree_scores = jnp.einsum(
        "rikgd,rjkd->rkgij", query_rows_all, tree_keys, preferred_element_type=jnp.float32
    )
    valid_node = (parent_links > 0.5)[:, None, None, :, :]
    row_top = jnp.maximum(
        cache_peak, jnp.max(jnp.where(valid_node, tree_scores, NEGATIVE), axis=-1)
    )
    tree_weights = jnp.where(valid_node, jnp.exp(tree_scores - row_top[..., None]), 0.0)
    cache_factor = jnp.exp(cache_peak - row_top)
    row_mass = cache_mass * cache_factor + jnp.sum(tree_weights, axis=-1)
    weighted = cache_sum * cache_factor[..., None] + jnp.einsum(
        "rkgij,rjkd->rkgid",
        tree_weights.astype(jnp.bfloat16),
        tree_values,
        preferred_element_type=jnp.float32,
    )
    attention_result = jnp.transpose(weighted / row_mass[..., None], (0, 3, 1, 2, 4)).reshape(
        token_count, query_heads * head_dim
    )
    gated = (attention_result * jax.nn.sigmoid(gate)).astype(jnp.bfloat16)
    attn_sum = lax.psum(jnp.dot(gated, wo, preferred_element_type=jnp.float32), "tp")
    middle = (hidden_wide + attn_sum).astype(jnp.bfloat16)
    middle_wide = middle.astype(jnp.float32)
    squares_mid = lax.psum(jnp.sum(middle_wide * middle_wide, axis=1), "seq")
    normed2 = (
        middle_wide * lax.rsqrt(squares_mid / model_width + EPSILON)[:, None] * ln2_gain
    ).astype(jnp.bfloat16)
    gate_part, up_part = lax.psum(
        (
            jnp.dot(normed2, w_gate, preferred_element_type=jnp.float32),
            jnp.dot(normed2, w_up, preferred_element_type=jnp.float32),
        ),
        "seq",
    )
    activated = (jax.nn.silu(gate_part) * up_part).astype(jnp.bfloat16)
    down_part = jnp.dot(activated, w_down, preferred_element_type=jnp.float32)
    down_sum = lax.psum(down_part, "tp")
    next_hidden = (middle_wide + down_sum).astype(jnp.bfloat16)
    next_wide = next_hidden.astype(jnp.float32)
    squares_last = lax.psum(jnp.sum(next_wide * next_wide, axis=1), "seq")
    normed3 = (
        next_wide * lax.rsqrt(squares_last / model_width + EPSILON)[:, None] * last_gain
    ).astype(jnp.bfloat16)
    logits = jnp.dot(
        lax.all_gather(normed3, "seq", axis=1, tiled=True),
        head_weight,
        preferred_element_type=jnp.float32,
    )
    logits = logits * jnp.repeat(inv_temp, tree_size)[:, None]
    vocab_top = lax.pmax(jnp.max(logits, axis=1), ("seq", "tp"))
    vocab_total = lax.psum(jnp.sum(jnp.exp(logits - vocab_top[:, None]), axis=1), ("seq", "tp"))
    logprobs = logits - (vocab_top + jnp.log(vocab_total))[:, None]
    accepted_rows = parent_links[jnp.arange(requests), accepted]
    target = token_position.reshape(requests, tree_size)
    slot_all = slot_start + jnp.arange(slot_count, dtype=jnp.int32)
    placed = (slot_all[None, :, None] == target[:, None, :]).astype(jnp.float32) * accepted_rows[
        :, None, :
    ]
    hits = (jnp.sum(placed, axis=2) > 0.5)[:, :, None]
    placed_low = placed.astype(jnp.bfloat16)
    moved_keys = jnp.einsum(
        "rca,rae->rce",
        placed_low,
        draft_keys.reshape(requests, tree_size, kv_heads * head_dim),
        preferred_element_type=jnp.float32,
    ).astype(jnp.bfloat16)
    moved_values = jnp.einsum(
        "rca,rae->rce",
        placed_low,
        draft_values.reshape(requests, tree_size, kv_heads * head_dim),
        preferred_element_type=jnp.float32,
    ).astype(jnp.bfloat16)
    updated_key_cache = jnp.where(hits, moved_keys, key_cache)
    updated_value_cache = jnp.where(hits, moved_values, value_cache)
    return (logprobs, next_hidden, updated_key_cache, updated_value_cache)


def solution(mesh):
    in_specs = (
        P(None, "seq"),
        P("seq"),
        P("seq", "tp"),
        P("seq", "tp"),
        P("seq", "tp"),
        P("seq", "tp"),
        P(),
        P(),
        P("tp", "seq"),
        P("seq"),
        P("seq", "tp"),
        P("seq", "tp"),
        P("tp", "seq"),
        P("seq"),
        P(None, ("seq", "tp")),
        P(),
        P(None, "seq", "tp"),
        P(None, "seq", "tp"),
        P(),
        P(),
        P(),
    )
    out_specs = (P(None, ("seq", "tp")), P(None, "seq"), P(None, "seq", "tp"), P(None, "seq", "tp"))
    return jax.shard_map(
        on_device, mesh=mesh, in_specs=in_specs, out_specs=out_specs, check_vma=False
    )
```

profile of v0, /device:TPU:1, one launch (start us, length us, event | category | flops | bytes accessed | tf_op | source)
XLA Modules:
  0.0 1792.0 jit_solution(4256023891018787633)
XLA Ops:
  7.2 0.8 fusion.51
  8.1 122.9 %psum.98 = f32[384]{0:T(512)S(1)} all-reduce(f32[384]{0:T(512)S(1)} %fusion.51), channel_id=1, replica_groups=mesh['seq'=64,'tp'=8] {'seq'}, use_global_device_ids=true, to_apply=%region_1.0 | all-reduce | flops 384 | bytes 3072 | tf_op jit(solution)/shard_map/psum | solution.py:95
  130.9 1.8 fusion.88
  132.8 1.4 convolution_minimum_fusion.5
  136.2 1.0 fusion.86
  137.7 1.1 fusion.82
  138.7 269.0 %all-reduce.8.cloned.1.call-done = f32[384,2,128]{0,2,1:T(8,128)} async-done(((f32[384,2,128]{0,2,1:T(8,128)}), f32[384,2,128]{0,2,1:T(8,128)}) %all-reduce.8.cloned.1.call-update) | async-done | bytes 393232 | tf_op jit(solution)/shard_map/psum | solution.py:99
  407.7 1.0 multiply_reduce_fusion
  408.8 1.1 multiply_multiply_fusion
  411.8 114.2 %pmax.14 = f32[8,1,2,48]{3,2,0,1:T(2,128)S(1)} all-reduce(f32[8,1,2,48]{3,2,0,1:T(2,128)S(1)} %bitcast.134), channel_id=1, replica_groups=mesh['seq'=64,'tp'=8] {'seq'}, use_global_device_ids=true, to_apply=%region_6.0 | all-reduce | flops 768 | bytes 6144 | tf_op jit(solution)/shard_map/pmax | solution.py:127
  526.5 1.1 fusion.2
  528.0 219.4 %all-reduce.13 = (bf16[384,128]{1,0:T(8,128)(2,1)S(1)}, f32[8,1,2,48]{3,2,0,1:T(2,128)S(1)}) all-reduce(f32[384,128]{1,0:T(8,128)S(1)} %fusion.84, f32[8,1,2,48]{3,2,0,1:T(2,128)S(1)} %get-tuple-element.32), channel_id=1, replica_groups=mesh['seq'=64,'tp'=8] {'seq'}, use_global_device_ids=true, to_apply=%region_11.12 | all-reduce | flops 49920 | bytes 301056 | tf_op jit(solution)/shard_map/psum | solution.py:99
  747.3 74.5 %all-reduce.12.cloned.1.call-done = (f32[8,1,2,48,128]{4,3,2,0,1:T(8,128)}, f32[384,128]{1,0:T(8,128)}, f32[384,256]{1,0:T(8,128)}) async-done(((f32[8,1,2,48,128]{4,3,2,0,1:T(8,128)}, f32[384,128]{1,0:T(8,128)}, f32[384,256]{1,0:T(8,128)}), (f32[8,1,2,48,128]{4,3,2,0,1:T(8,128)}, f32[384,128]{1,0:T(8,128)}, f32[384,256]{1,0:T(8,128)})) %all-reduce.12.cloned.1.call-update) | async-done | bytes 983056 | tf_op jit(solution)/shard_map/psum | solution.py:129
  821.8 1.1 multiply_reduce_fusion.1
  822.9 1.1 multiply_bitcast_fusion
  824.0 0.8 fusion.25
  826.7 39.8 %psum.105 = f32[384,32]{0,1:T(8,128)S(1)} all-reduce(f32[384,32]{0,1:T(8,128)S(1)} %fusion.43), channel_id=1, replica_groups=mesh['seq'=64,'tp'=8] {'tp'}, use_global_device_ids=true, to_apply=%region_16.17 | all-reduce | flops 12288 | bytes 98304 | tf_op jit(solution)/shard_map/psum | solution.py:150
  866.5 110.1 %psum.106 = f32[384]{0:T(512)S(1)} all-reduce(f32[384]{0:T(512)S(1)} %get-tuple-element.21), channel_id=1, replica_groups=mesh['seq'=64,'tp'=8] {'seq'}, use_global_device_ids=true, to_apply=%region_18.19 | all-reduce | flops 384 | bytes 3072 | tf_op jit(solution)/shard_map/psum | solution.py:153
  976.7 1.4 fusion.63
  978.1 1.4 fusion.65
  979.6 295.4 %all-reduce.10.cloned.1.call-done = (f32[384,768]{1,0:T(8,128)}, f32[384,768]{1,0:T(8,128)}) async-done(((f32[384,768]{1,0:T(8,128)}, f32[384,768]{1,0:T(8,128)}), (f32[384,768]{1,0:T(8,128)}, f32[384,768]{1,0:T(8,128)})) %all-reduce.10.cloned.1.call-update) | async-done | bytes 2359312 | tf_op jit(solution)/shard_map/psum | solution.py:157
  1275.1 2.1 fusion.8
  1277.2 30.1 %psum.109 = f32[384,32]{0,1:T(8,128)S(1)} all-reduce(f32[384,32]{0,1:T(8,128)S(1)} %fusion.8), channel_id=1, replica_groups=mesh['seq'=64,'tp'=8] {'tp'}, use_global_device_ids=true, to_apply=%region_21.22 | all-reduce | flops 12288 | bytes 98304 | tf_op jit(solution)/shard_map/psum | solution.py:166
  1307.3 112.8 %psum.110 = f32[384]{0:T(512)S(1)} all-reduce(f32[384]{0:T(512)S(1)} %get-tuple-element.19), channel_id=1, replica_groups=mesh['seq'=64,'tp'=8] {'seq'}, use_global_device_ids=true, to_apply=%region_23.24 | all-reduce | flops 384 | bytes 3072 | tf_op jit(solution)/shard_map/psum | solution.py:169
  1420.1 0.7 fusion.50
  1421.9 1.7 fusion.1
  1423.5 1.6 fusion
  1425.1 148.8 %all-gather.2.cloned.1.call-done = bf16[384,2048]{0,1:T(8,128)(2,1)} async-done(((bf16[384,32]{0,1:T(8,128)(2,1)}), bf16[384,2048]{0,1:T(8,128)(2,1)}) %all-gather.2.cloned.1.call-update) | async-done | bytes 1572880 | tf_op jit(solution)/shard_map/all_gather | solution.py:174
  1573.9 2.2 fusion.93
  1576.1 109.6 %pmax.15 = f32[384]{0:T(512)S(1)} all-reduce(f32[384]{0:T(512)S(1)} %get-tuple-element.41), channel_id=1, replica_groups=mesh['seq'=64,'tp'=8] {'seq','tp'}, use_global_device_ids=true, to_apply=%region_25.26 | all-reduce | flops 384 | bytes 3072 | tf_op jit(solution)/shard_map/pmax | solution.py:179
  1685.8 98.8 %psum.111 = f32[384]{0:T(512)S(1)} all-reduce(f32[384]{0:T(512)S(1)} %exponential_reduce_fusion), channel_id=1, replica_groups=mesh['seq'=64,'tp'=8] {'seq','tp'}, use_global_device_ids=true, to_apply=%region_27.28 | all-reduce | flops 384 | bytes 3072 | tf_op jit(solution)/shard_map/psum | solution.py:180
  1784.6 0.9 copy.35
  (100 shorter events, 8.2 us)
Async XLA Ops:
  7.2 1566.7 %copy-start = (bf16[2048,256]{1,0:T(8,128)(2,1)S(1)}, bf16[2048,256]{1,0:T(8,128)(2,1)}, u32[]{:S(2)}) copy-start(bf16[2048,256]{1,0:T(8,128)(2,1)} %param.35) | copy-start | bytes 3145732
  7.2 400.6 %all-reduce.8.cloned.1.call-start = ((), (), s32[]{:S(2)}) async-start(), calls=%async_computation | async-start | bytes 786432 | tf_op jit(solution)/shard_map/psum | solution.py:99
  132.7 689.1 %all-reduce.12.cloned.1.call-start = ((), (), s32[]{:S(2)}) async-start(), calls=%async_computation.3 | async-start | bytes 1966080 | tf_op jit(solution)/shard_map/psum | solution.py:129
  134.6 1.4 copy-start.12
  134.6 1.6 copy-start.1
  134.6 1.6 copy-start.8
  134.6 1.6 copy-start.9
  135.0 2.7 copy-start.7
  135.3 273.5 %copy-start.16 = (f32[128]{0:T(128)S(1)}, f32[128]{0:T(128)}, u32[]{:S(2)}) copy-start(f32[128]{0:T(128)} %param.27) | copy-start | bytes 1540
  410.4 1.0 copy-start.2
  411.4 115.0 %copy-start.3 = (bf16[8,256,128]{2,1,0:T(8,128)(2,1)S(1)}, bf16[8,256,128]{2,1,0:T(8,128)(2,1)}, u32[]{:S(2)}) copy-start(bf16[8,256,128]{2,1,0:T(8,128)(2,1)} %param.38) | copy-start | bytes 1572868
  526.5 1.2 copy-start.10
  527.6 295.3 %copy-start.13 = (f32[128]{0:T(128)S(1)}, f32[128]{0:T(128)}, u32[]{:S(2)}) copy-start(f32[128]{0:T(128)} %param.28) | copy-start | bytes 1540
  527.6 747.5 %all-reduce.10.cloned.1.call-start = ((), (), s32[]{:S(2)}) async-start(), calls=%async_computation.2 | async-start | bytes 4718592 | tf_op jit(solution)/shard_map/psum | solution.py:157
  822.9 2.5 copy-start.18
  825.4 1.0 copy-start.17
  825.4 1.0 copy-start.20
  826.0 150.7 %copy-start.5 = (bf16[32,768]{1,0:T(8,128)(2,1)S(1)}, bf16[32,768]{1,0:T(8,128)(2,1)}, u32[]{:S(2)}) copy-start(bf16[32,768]{1,0:T(8,128)(2,1)} %param.32) | copy-start | bytes 147460
  826.0 150.7 %copy-start.11 = (f32[32]{0:T(128)S(1)}, f32[32]{0:T(128)}, u32[]{:S(2)}) copy-start(f32[32]{0:T(128)} %param.30) | copy-start | bytes 388
  826.7 151.5 %copy-start.6 = (bf16[32,768]{1,0:T(8,128)(2,1)S(1)}, bf16[32,768]{1,0:T(8,128)(2,1)}, u32[]{:S(2)}) copy-start(bf16[32,768]{1,0:T(8,128)(2,1)} %param.31) | copy-start | bytes 147460
  979.5 295.5 %copy-start.19 = (bf16[768,32]{0,1:T(8,128)(2,1)S(1)}, bf16[768,32]{0,1:T(8,128)(2,1)}, u32[]{:S(2)}) copy-start(bf16[768,32]{0,1:T(8,128)(2,1)} %param.33) | copy-start | bytes 147460
  979.6 594.3 %all-gather.2.cloned.1.call-start = ((), (), s32[]{:S(2)}) async-start(), calls=%async_computation.1 | async-start | bytes 1597440 | tf_op jit(solution)/shard_map/all_gather | solution.py:174
  1275.0 145.0 %copy-start.14 = (f32[32]{0:T(128)S(1)}, f32[32]{0:T(128)}, u32[]{:S(2)}) copy-start(f32[32]{0:T(128)} %param.34) | copy-start | bytes 388
  1275.0 145.7 %copy-start.15 = (f32[8]{0:T(128)S(1)}, f32[8]{0:T(128)}, u32[]{:S(2)}) copy-start(f32[8]{0:T(128)} %param.36) | copy-start | bytes 100
  1275.0 146.0 %copy-start.21 = (s32[8]{0:T(128)S(1)}, s32[8]{0:T(128)}, u32[]{:S(2)}) copy-start(s32[8]{0:T(128)} %param.41) | copy-start | bytes 100
  1307.3 117.8 %copy-start.4 = (bf16[384,32]{0,1:T(8,128)(2,1)}, bf16[384,32]{0,1:T(8,128)(2,1)S(1)}, u32[]{:S(2)}) copy-start(bf16[384,32]{0,1:T(8,128)(2,1)S(1)} %get-tuple-element.20) | copy-start | bytes 73732
Sparse Core Ops, SparseCore 0:
  132.9 274.8 all-reduce.7
  527.7 294.0 all-reduce.11
  979.7 295.2 all-reduce.9
  1420.9 152.9 all-gather.1
where the time goes:
time: 1790 us
  blocking collectives  958 us (54%)
  waiting for transfers between devices  788 us (44%)
  matrix products  19.9 us (1%)
    psum x1, waiting for transfers between devices, on_device(): lax.psum((jnp.dot(normed2, w_gate, preferred_element_type=jnp.float32), j...  295 us
    psum x1, waiting for transfers between devices, on_device(): lax.psum((jnp.dot(normed1, wq, preferred_element_type=jnp.float32), jnp.d...  269 us
    psum x1, blocking collectives, on_device(): lax.psum((jnp.dot(normed1, wq, preferred_element_type=jnp.float32), jnp.d...  219 us
    all_gather x1, waiting for transfers between devices, on_device(): lax.all_gather(normed3, 'seq', axis=1, tiled=True)  149 us
    psum x1, blocking collectives, on_device(): squares = lax.psum(jnp.sum(hidden_wide * hidden_wide, axis=1), 'seq')  123 us
    pmax x1, blocking collectives, on_device(): cache_peak = lax.pmax(local_peak, 'seq')  114 us
    psum x1, blocking collectives, on_device(): squares_last = lax.psum(jnp.sum(next_wide * next_wide, axis=1), 'seq')  113 us
    psum x1, blocking collectives, on_device(): squares_mid = lax.psum(jnp.sum(middle_wide * middle_wide, axis=1), 'seq')  110 us
  transfers between devices with their start and end apart: 4, of which 4 were waited for; matrix products, arithmetic and copies ran while one was open for 1% of the time, Pallas kernels for 0%

commit v1 on v0

v1 whole, which is shorter than its diff:
```python
import jax
import jax.numpy as jnp
from jax import lax
from jax.sharding import Mesh, PartitionSpec as P

EPSILON = 1e-06
ROPE_BASE = 1000000.0
NEGATIVE = -1e30
BF = jnp.bfloat16
F32 = jnp.float32


def ancestry(parents):
    node_count = parents.shape[-1]
    node_ids = jnp.arange(node_count, dtype=jnp.int32)
    reachable = (parents[..., :, None] == node_ids[None, :]).astype(BF)
    reachable = jnp.maximum(reachable, jnp.eye(node_count, dtype=BF))
    for turn in range((node_count - 1).bit_length()):
        reachable = jnp.minimum(
            jnp.einsum("rij,rjk->rik", reachable, reachable, preferred_element_type=F32), 1.0
        ).astype(BF)
    return reachable.astype(F32)


def head_norm(values, gain):
    meansq = jnp.mean(values * values, axis=-1, keepdims=True)
    return values * lax.rsqrt(meansq + EPSILON) * gain


def rotate(values, cosine, sine):
    half = values.shape[-1] // 2
    low, high = values[..., :half], values[..., half:]
    return jnp.concatenate([low * cosine - high * sine, high * cosine + low * sine], axis=-1)


def swap(values, axis):
    return lax.all_to_all(values, axis, 0, 0, tiled=True)


def spread(values, axis, count):
    return swap(jnp.broadcast_to(values[None], (count,) + values.shape), axis)


def split2(values):
    high = values.astype(BF)
    low = (values - high.astype(F32)).astype(BF)
    return high, low


def split3(values):
    high = values.astype(BF)
    rest = values - high.astype(F32)
    mid = rest.astype(BF)
    low = (rest - mid.astype(F32)).astype(BF)
    return high, mid, low


def pack_state(peak, mass, weighted):
    count = peak.shape[0]
    mass_high, mass_low = split2(mass)
    stats = jnp.stack([peak.astype(BF), mass_high, mass_low], axis=1).reshape(count, 6, 24)
    stats = jnp.pad(stats, ((0, 0), (0, 2), (0, 104)))
    return jnp.concatenate([weighted.astype(BF).reshape(count, 48, 128), stats], axis=1)


def merge_state(packed):
    count = packed.shape[0]
    weighted = packed[:, :48].reshape(count, 2, 24, 128).astype(F32)
    stats = packed[:, 48:54, :24].astype(F32).reshape(count, 3, 2, 24)
    peaks, masses = stats[:, 0], stats[:, 1] + stats[:, 2]
    peak = jnp.max(peaks, axis=0)
    factor = jnp.exp(peaks - peak)
    return peak, jnp.sum(masses * factor, axis=0), jnp.sum(weighted * factor[..., None], axis=0)


def on_device(
    hidden, ln1_gain, wq, wk, wv, wg, q_gain, key_gain, wo, ln2_gain, w_gate, w_up, w_down,
    last_gain, head_weight, inv_temp, key_cache, value_cache, lengths, parents, accepted,
):
    z, y, x, c = (lax.axis_index(name) for name in ("z", "y", "x", "c"))
    seq = z * 4 + y
    requests, tree = parents.shape
    slot_count = key_cache.shape[1]
    width = 2048

    token = jnp.arange(384, dtype=jnp.int32)
    token_y = (token // 6) % 4
    place = token_y * 128 + (token // 24) * 6 + token % 6
    scatter = (place[:, None] == jnp.arange(512, dtype=jnp.int32)[None, :]).astype(BF)
    hidden_t = jnp.dot(hidden.T, scatter, preferred_element_type=F32).astype(BF)
    gains = jnp.stack(split3(ln1_gain) + split3(ln2_gain) + split3(last_gain), axis=1)
    gains = jnp.pad(gains, ((0, 0), (96, 128 - 96 - 9)))
    down_t, wo_t = w_down.T, wo.T
    pieces = []
    for part in range(4):
        pieces.append(
            jnp.concatenate(
                [
                    w_gate[:, part * 192 : part * 192 + 192],
                    w_up[:, part * 192 : part * 192 + 192],
                    down_t[:, part * 192 : part * 192 + 192],
                    wo_t[:, part * 64 : part * 64 + 64],
                    wq,
                    wk,
                    wv,
                    wg,
                    hidden_t[:, part * 128 : part * 128 + 128] + gains,
                ],
                axis=1,
            )
        )
    mine = swap(jnp.stack(pieces), "y").reshape(128, 1536)
    ffn = lax.all_gather(mine[:, :640], "z", axis=0, tiled=True)
    proj = mine[:, 640:1408]
    side = mine[:, 1408:]
    side_wide = side.astype(F32)
    ln1_row = side_wide[:, 96:97] + side_wide[:, 97:98] + side_wide[:, 98:99]
    scaled = (side_wide * ln1_row).astype(BF)
    partial = lax.dot_general(scaled, proj, (((0,), (0,)), ((), ())), preferred_element_type=F32)
    sent = jnp.concatenate([partial[:96].astype(BF), side.T[:96]], axis=1).reshape(16, 6, 896)
    got = swap(sent, "z")
    sums = jnp.sum(got[:, :, :768].astype(F32), axis=0)
    rows = got[:, :, 768:]
    rows_wide = rows.astype(F32)
    squares = jnp.sum(rows_wide * rows_wide, axis=(0, 2))
    sums = sums * lax.rsqrt(squares / width + EPSILON)[:, None]

    links = ancestry(parents)
    depth = jnp.sum((links > 0.5).astype(jnp.int32), axis=-1) - 1
    target = lengths[:, None] + depth
    my_places = lax.dynamic_slice(target.reshape(-1), (z * 24 + y * 6,), (6,))
    inverse = ROPE_BASE ** (-jnp.arange(64, dtype=F32) / 64)
    angles = my_places.astype(F32)[:, None] * inverse[None, :]
    cosine, sine = jnp.cos(angles)[:, None, :], jnp.sin(angles)[:, None, :]
    query = rotate(head_norm(sums[:, :256].reshape(6, 2, 128), q_gain), cosine, sine) * 128 ** (-0.5)
    new_key = rotate(head_norm(sums[:, 256:384].reshape(6, 1, 128), key_gain), cosine, sine)
    outgate = jax.nn.sigmoid(sums[:, 512:])
    mine6 = jnp.concatenate(
        [query.reshape(6, 256), new_key.reshape(6, 128), sums[:, 384:512], outgate], axis=1
    ).astype(BF)
    gain_row = side[:, 99:105].T.reshape(1, 768)
    block = jnp.concatenate([mine6, gain_row, jnp.zeros((1, 768), BF)], axis=0)
    gathered = spread(block, "z", 16)
    gain_all = gathered[:, 6].reshape(16, 6, 128).astype(F32)
    ln2_all = gain_all[:, 0] + gain_all[:, 1] + gain_all[:, 2]
    last_all = gain_all[:, 3] + gain_all[:, 4] + gain_all[:, 5]
    tokens = spread(gathered[:, :6].reshape(96, 768), "y", 4).reshape(384, 768)
    order = token_y * 96 + (token // 24) * 6 + token % 6
    gather = (order[:, None] == token[None, :]).astype(BF)
    tokens = jnp.dot(gather, tokens, preferred_element_type=F32).astype(BF)
    queries = tokens[:, :256].reshape(requests, tree, 2, 128)
    tree_keys = tokens[:, 256:384].reshape(requests, tree, 128)
    tree_values = tokens[:, 384:512].reshape(requests, tree, 128)
    gates = tokens[:, 512:]

    slot_ids = seq * slot_count + jnp.arange(slot_count, dtype=jnp.int32)
    valid_slot = (slot_ids[None, :] < lengths[:, None])[:, None, None, :]
    valid_node = ((links > 0.5) & (seq == 0))[:, None, :, :]
    scores = jnp.einsum("rigd,rcd->rgic", queries, key_cache, preferred_element_type=F32)
    tree_scores = jnp.einsum("rigd,rjd->rgij", queries, tree_keys, preferred_element_type=F32)
    peak = jnp.maximum(
        jnp.max(jnp.where(valid_slot, scores, NEGATIVE), axis=-1),
        jnp.max(jnp.where(valid_node, tree_scores, NEGATIVE), axis=-1),
    )
    peak = lax.reduce_precision(peak, 8, 7)
    weights = jnp.where(valid_slot, jnp.exp(scores - peak[..., None]), 0.0)
    tree_weights = jnp.where(valid_node, jnp.exp(tree_scores - peak[..., None]), 0.0)
    mass = jnp.sum(weights, axis=-1) + jnp.sum(tree_weights, axis=-1)
    weighted = jnp.einsum(
        "rgic,rcd->rgid", weights.astype(BF), value_cache, preferred_element_type=F32
    ) + jnp.einsum("rgij,rjd->rgid", tree_weights.astype(BF), tree_values, preferred_element_type=F32)

    def by_z(values):
        split = values.reshape((requests, 2, 2, 24) + values.shape[3:])
        return jnp.swapaxes(split, 1, 2).reshape((16, 2, 24) + values.shape[3:])

    state = merge_state(swap(pack_state(by_z(peak), by_z(mass), by_z(weighted)), "z"))
    packed = pack_state(*(part[None] for part in state))[0]
    both = spread(jnp.concatenate([packed, rows.reshape(96, 128)], axis=0), "y", 4)
    peak, mass, weighted = merge_state(both[:, :56])
    my_gate = lax.dynamic_slice(gates, (z * 24, 0), (24, 256)).reshape(24, 2, 128)
    my_gate = jnp.swapaxes(my_gate, 0, 1).astype(F32)
    gated = (weighted / mass[..., None] * my_gate).astype(BF)
    gated = lax.dynamic_index_in_dim(gated, y // 2, 0, keepdims=False)
    gated = jnp.where(y % 2 == 0, gated[:, :64], gated[:, 64:])
    column = y * 4 + x
    hidden_mine = lax.dynamic_index_in_dim(
        both[:, 56:].reshape(4, 16, 6, 128), column, 1, keepdims=False
    ).reshape(24, 128)

    def reduce_columns(part):
        part = jnp.swapaxes(part.astype(BF).reshape(24, 16, 128), 0, 1)
        part = jnp.sum(swap(part, ("y", "x")).astype(F32), axis=0)
        return part + lax.ppermute(part, "c", [(0, 1), (1, 0)])

    attn = lax.dot_general(gated, ffn[:, 576:], (((1,), (1,)), ((), ())), preferred_element_type=F32)
    middle = (hidden_mine.astype(F32) + reduce_columns(attn)).astype(BF)
    middle_all = spread(middle, ("y", "x"), 16).astype(F32)
    squares_mid = jnp.sum(middle_all * middle_all, axis=(0, 2))
    scale_mid = lax.rsqrt(squares_mid / width + EPSILON)
    normed2 = (middle_all * scale_mid[None, :, None] * ln2_all[:, None, :]).astype(BF)
    normed2 = jnp.swapaxes(normed2, 0, 1).reshape(24, width)
    hidden_units = jnp.dot(normed2, ffn[:, :384], preferred_element_type=F32)
    activated = (jax.nn.silu(hidden_units[:, :192]) * hidden_units[:, 192:]).astype(BF)
    down = lax.dot_general(
        activated, ffn[:, 384:576], (((1,), (1,)), ((), ())), preferred_element_type=F32
    )
    following = (middle.astype(F32) + reduce_columns(down)).astype(BF)

    half = spread(following, "z", 16).reshape(384, 128)
    half = lax.dynamic_slice(half, (c * 192, 0), (192, 128))
    half = spread(spread(half, "y", 4), "x", 4)
    other = lax.ppermute(half, "c", [(0, 1), (1, 0)])
    full = jnp.stack([jnp.where(c == 0, half, other), jnp.where(c == 0, other, half)])
    own = lax.dynamic_slice(full, (0, z % 4, z // 4, 0, 0), (2, 1, 1, 192, 128)).reshape(384, 128)
    next_hidden = lax.dynamic_slice(own, (0, y * 32), (384, 32))
    full = jnp.transpose(full, (0, 3, 2, 1, 4)).reshape(384, width)
    wide = full.astype(F32)
    squares_last = jnp.sum(wide * wide, axis=1)
    normed3 = (
        wide * lax.rsqrt(squares_last / width + EPSILON)[:, None] * last_all.reshape(1, width)
    ).astype(BF)
    logits = jnp.dot(normed3, head_weight, preferred_element_type=F32)
    logits = logits * jnp.repeat(inv_temp, tree)[:, None]
    top = jnp.max(logits, axis=1)
    spot = top + jnp.log(jnp.sum(jnp.exp(logits - top[:, None]), axis=1))
    for axis, count in ((("y", "x", "c"), 32), ("z", 16)):
        spots = spread(spot.reshape(3, 128), axis, count)
        top = jnp.max(spots, axis=0)
        spot = top + jnp.log(jnp.sum(jnp.exp(spots - top), axis=0))
    logprobs = logits - spot.reshape(384, 1)

    accepted_rows = links[jnp.arange(requests), accepted]
    placed = (slot_ids[None, :, None] == target[:, None, :]).astype(F32) * accepted_rows[:, None, :]
    hits = (jnp.sum(placed, axis=2) > 0.5)[:, :, None]
    placed = placed.astype(BF)
    moved_keys = jnp.einsum("rca,rae->rce", placed, tree_keys, preferred_element_type=F32).astype(BF)
    moved_values = jnp.einsum("rca,rae->rce", placed, tree_values, preferred_element_type=F32).astype(BF)
    return (
        logprobs,
        next_hidden,
        jnp.where(hits, moved_keys, key_cache),
        jnp.where(hits, moved_values, value_cache),
    )


def solution(mesh):
    grid = Mesh(mesh.devices.reshape(16, 4, 4, 2), ("z", "y", "x", "c"))
    seq, tp = ("z", "y"), ("x", "c")
    in_specs = (
        P(None, seq), P(seq), P(seq, tp), P(seq, tp), P(seq, tp), P(seq, tp), P(), P(),
        P(tp, seq), P(seq), P(seq, tp), P(seq, tp), P(tp, seq), P(seq),
        P(None, seq + tp), P(), P(None, seq, tp), P(None, seq, tp), P(), P(), P(),
    )
    out_specs = (P(None, seq + tp), P(None, seq), P(None, seq, tp), P(None, seq, tp))
    return jax.shard_map(on_device, mesh=grid, in_specs=in_specs, out_specs=out_specs, check_vma=False)
```

time: 1790 us -> 325 us (0.18)
  blocking collectives: 958 us -> 17.3 us
  waiting for transfers between devices: 788 us -> 138 us
  starting transfers between devices: 0.16 us -> 94.6 us
  local copies, waits for them, and re-layouts: 3.79 us -> 30.7 us
    psum x7 -> x0, blocking collectives: 734 us -> none  [the longest x1 219 us: on_device(): lax.psum((jnp.dot(normed1, wq, preferred_element_type=jnp.float32), jnp.d...]
    psum x3 -> x0, waiting for transfers between devices: 639 us -> none  [the longest x1 295 us: on_device(): lax.psum((jnp.dot(normed2, w_gate, preferred_element_type=jnp.float32), j...]
    pmax x2 -> x0, blocking collectives: 224 us -> none  [the longest x1 114 us: on_device(): cache_peak = lax.pmax(local_peak, 'seq')]
    all_gather x1, waiting for transfers between devices: 149 us -> 34.2 us  [on_device(): ffn = lax.all_gather(mine[:, :640], 'z', axis=0, tiled=True)]
    all_to_all x0 -> x12, waiting for transfers between devices: none -> 102 us  [swap(): return lax.all_to_all(values, axis, 0, 0, tiled=True)]
    all_to_all x0 -> x12, starting transfers between devices: none -> 71 us  [swap(): return lax.all_to_all(values, axis, 0, 0, tiled=True)]
    ppermute x0 -> x3, starting transfers between devices: none -> 23.6 us  [the longest x2 16.6 us: reduce_columns(): return part + lax.ppermute(part, 'c', [(0, 1), (1, 0)])]
  transfers between devices with their start and end apart: 4 -> 16, of which waited for: 4 -> 15; matrix products, arithmetic and copies ran while one was open for 1% -> 5% of each run, Pallas kernels for 0% -> 0%
where the time goes in v1:
time: 325 us; the launch traced here: 323 us
  waiting for transfers between devices  138 us (42%)
  starting transfers between devices  94.6 us (29%)
  local copies, waits for them, and re-layouts  30.7 us (9%)
  blocking collectives  17.3 us (5%)
  matrix products  15.9 us (5%)
  between operations  14.9 us (5%)
  other arithmetic  11.1 us (3%)
    all_to_all x12, waiting for transfers between devices, swap(): return lax.all_to_all(values, axis, 0, 0, tiled=True)  102 us
    all_to_all x12, starting transfers between devices, swap(): return lax.all_to_all(values, axis, 0, 0, tiled=True)  71 us
    all_gather x1, waiting for transfers between devices, on_device(): ffn = lax.all_gather(mine[:, :640], 'z', axis=0, tiled=True)  34.2 us
    all_to_all x2, blocking collectives, swap(): return lax.all_to_all(values, axis, 0, 0, tiled=True)  17.3 us
    ppermute x2, starting transfers between devices, reduce_columns(): return part + lax.ppermute(part, 'c', [(0, 1), (1, 0)])  16.6 us
    convert_element_type x2, local copies, waits for them, and re-layouts, on_device(): wide = full.astype(F32)  10.6 us
    ppermute x1, starting transfers between devices, on_device(): other = lax.ppermute(half, 'c', [(0, 1), (1, 0)])  7.02 us
  transfers between devices with their start and end apart: 16, of which 15 were waited for; matrix products, arithmetic and copies ran while one was open for 5% of the time, Pallas kernels for 0%

profile of v1, /device:TPU:1, one launch (start us, length us, event | category | flops | bytes accessed | tf_op | source)
XLA Modules:
  0.0 322.7 jit_solution(3381878387999184094)
XLA Ops:
  18.5 5.0 %all-to-all-start = ((bf16[4,32,1536]{2,1,0:T(8,128)(2,1)}), bf16[4,32,1536]{2,1,0:T(8,128)(2,1)S(1)}, u32[]{:S(2)}, u32[]{:S(2)}) async-start(bf16[4,32,1536]{2,1,0:T(8,128)(2,1)} %pad_maximum_fusion.1), calls=%async_computation | async-start | bytes 786432 | tf_op jit(solution)/shard_map/all_to_all | solution.py:37
  26.1 3.7 %all-to-all-done = bf16[4,32,1536]{2,1,0:T(8,128)(2,1)S(1)} async-done(((bf16[4,32,1536]{2,1,0:T(8,128)(2,1)}), bf16[4,32,1536]{2,1,0:T(8,128)(2,1)S(1)}, u32[]{:S(2)}, u32[]{:S(2)}) %all-to-all-start) | async-done | bytes 393248 | tf_op jit(solution)/shard_map/all_to_all | solution.py:37
  30.9 15.6 %all-to-all-start.1 = ((bf16[16,6,896]{2,1,0:T(8,128)(2,1)}), bf16[16,6,896]{2,1,0:T(8,128)(2,1)S(1)}, u32[]{:S(2)}, u32[]{:S(2)}) async-start(bf16[16,6,896]{2,1,0:T(8,128)(2,1)} %reshape.543), calls=%async_computation.1 | async-start | bytes 458752 | tf_op jit(solution)/shard_map/all_to_all | solution.py:37
  46.9 12.2 %all-to-all-done.1 = bf16[16,6,896]{2,1,0:T(8,128)(2,1)S(1)} async-done(((bf16[16,6,896]{2,1,0:T(8,128)(2,1)}), bf16[16,6,896]{2,1,0:T(8,128)(2,1)S(1)}, u32[]{:S(2)}, u32[]{:S(2)}) %all-to-all-start.1) | async-done | bytes 172064 | tf_op jit(solution)/shard_map/all_to_all | solution.py:37
  60.9 8.4 %all-to-all-start.2 = ((bf16[16,8,768]{2,1,0:T(8,128)(2,1)}), bf16[16,8,768]{2,1,0:T(8,128)(2,1)S(1)}, u32[]{:S(2)}, u32[]{:S(2)}) async-start(bf16[16,8,768]{2,1,0:T(8,128)(2,1)} %broadcast_in_dim.72), calls=%async_computation.2 | async-start | bytes 393216 | tf_op jit(solution)/shard_map/all_to_all | solution.py:37
  69.6 12.1 %all-to-all-done.2 = bf16[16,8,768]{2,1,0:T(8,128)(2,1)S(1)} async-done(((bf16[16,8,768]{2,1,0:T(8,128)(2,1)}), bf16[16,8,768]{2,1,0:T(8,128)(2,1)S(1)}, u32[]{:S(2)}, u32[]{:S(2)}) %all-to-all-start.2) | async-done | bytes 196640 | tf_op jit(solution)/shard_map/all_to_all | solution.py:37
  82.6 3.6 %all-to-all-start.3 = ((bf16[4,96,768]{2,1,0:T(8,128)(2,1)}), bf16[4,96,768]{2,1,0:T(8,128)(2,1)S(1)}, u32[]{:S(2)}, u32[]{:S(2)}) async-start(bf16[4,96,768]{2,1,0:T(8,128)(2,1)} %broadcast_in_dim.74), calls=%async_computation.3 | async-start | bytes 1179648 | tf_op jit(solution)/shard_map/all_to_all | solution.py:37
  87.1 6.4 %all-to-all-done.3 = bf16[4,96,768]{2,1,0:T(8,128)(2,1)S(1)} async-done(((bf16[4,96,768]{2,1,0:T(8,128)(2,1)}), bf16[4,96,768]{2,1,0:T(8,128)(2,1)S(1)}, u32[]{:S(2)}, u32[]{:S(2)}) %all-to-all-start.3) | async-done | bytes 589856 | tf_op jit(solution)/shard_map/all_to_all | solution.py:37
  97.1 7.2 %all-to-all-start.4 = ((bf16[16,56,128]{2,1,0:T(8,128)(2,1)}), bf16[16,56,128]{2,1,0:T(8,128)(2,1)S(1)}, u32[]{:S(2)}, u32[]{:S(2)}) async-start(bf16[16,56,128]{2,1,0:T(8,128)(2,1)} %fusion.36), calls=%async_computation.4 | async-start | bytes 458752 | tf_op jit(solution)/shard_map/all_to_all | solution.py:37
  104.4 13.2 %all-to-all-done.4 = bf16[16,56,128]{2,1,0:T(8,128)(2,1)S(1)} async-done(((bf16[16,56,128]{2,1,0:T(8,128)(2,1)}), bf16[16,56,128]{2,1,0:T(8,128)(2,1)S(1)}, u32[]{:S(2)}, u32[]{:S(2)}) %all-to-all-start.4) | async-done | bytes 229408 | tf_op jit(solution)/shard_map/all_to_all | solution.py:37
  118.9 3.3 %all-to-all-start.5 = ((bf16[4,152,128]{2,1,0:T(8,128)(2,1)}), bf16[4,152,128]{2,1,0:T(8,128)(2,1)S(1)}, u32[]{:S(2)}, u32[]{:S(2)}) async-start(bf16[4,152,128]{2,1,0:T(8,128)(2,1)} %broadcast_in_dim.80), calls=%async_computation.5 | async-start | bytes 311296 | tf_op jit(solution)/shard_map/all_to_all | solution.py:37
  122.3 4.9 %all-to-all-done.5 = bf16[4,152,128]{2,1,0:T(8,128)(2,1)S(1)} async-done(((bf16[4,152,128]{2,1,0:T(8,128)(2,1)}), bf16[4,152,128]{2,1,0:T(8,128)(2,1)S(1)}, u32[]{:S(2)}, u32[]{:S(2)}) %all-to-all-start.5) | async-done | bytes 155680 | tf_op jit(solution)/shard_map/all_to_all | solution.py:37
  127.6 34.2 %all-gather.2.cloned.1.call-done = bf16[2048,640]{1,0:T(8,128)(2,1)} async-done(((bf16[128,640]{1,0:T(8,128)(2,1)}), bf16[2048,640]{1,0:T(8,128)(2,1)}) %all-gather.2.cloned.1.call-update) | async-done | bytes 2621456 | tf_op jit(solution)/shard_map/all_gather | solution.py:113
  163.8 5.8 %all-to-all-start.6 = ((bf16[16,24,128]{2,1,0:T(8,128)(2,1)}), bf16[16,24,128]{2,1,0:T(8,128)(2,1)S(1)}, u32[]{:S(2)}, u32[]{:S(2)}) async-start(bf16[16,24,128]{2,1,0:T(8,128)(2,1)} %bitcast.189), calls=%async_computation.6 | async-start | bytes 196608 | tf_op jit(solution)/shard_map/all_to_all | solution.py:37
  169.9 6.4 %all-to-all-done.6 = bf16[16,24,128]{2,1,0:T(8,128)(2,1)S(1)} async-done(((bf16[16,24,128]{2,1,0:T(8,128)(2,1)}), bf16[16,24,128]{2,1,0:T(8,128)(2,1)S(1)}, u32[]{:S(2)}, u32[]{:S(2)}) %all-to-all-start.6) | async-done | bytes 98336 | tf_op jit(solution)/shard_map/all_to_all | solution.py:37
  176.3 12.0 %collective-permute-start = (f32[24,128]{1,0:T(8,128)S(1)}, f32[24,128]{1,0:T(8,128)S(1)}, u32[]{:S(2)}, u32[]{:S(2)}) collective-permute-start(f32[24,128]{1,0:T(8,128)S(1)} %convert_reduce_fusion.2), channel_id=1, source_target_pairs={{0,1},{1,0},{2,3},{3,2},{4,5},{5,4},{6,7},{7,6},{8,9},{9,8},{10,11... | collective-permute-start | bytes 36872 | tf_op jit(solution)/shard_map/ppermute | solution.py:194
  189.8 3.5 %all-to-all-start.7 = ((bf16[16,24,128]{2,1,0:T(8,128)(2,1)}), bf16[16,24,128]{2,1,0:T(8,128)(2,1)S(1)}, u32[]{:S(2)}, u32[]{:S(2)}) async-start(bf16[16,24,128]{2,1,0:T(8,128)(2,1)} %broadcast_in_dim.81), calls=%async_computation.7 | async-start | bytes 196608 | tf_op jit(solution)/shard_map/all_to_all | solution.py:37
  193.4 6.6 %all-to-all-done.7 = bf16[16,24,128]{2,1,0:T(8,128)(2,1)S(1)} async-done(((bf16[16,24,128]{2,1,0:T(8,128)(2,1)}), bf16[16,24,128]{2,1,0:T(8,128)(2,1)S(1)}, u32[]{:S(2)}, u32[]{:S(2)}) %all-to-all-start.7) | async-done | bytes 98336 | tf_op jit(solution)/shard_map/all_to_all | solution.py:37
  203.5 9.8 %all_to_all.70 = bf16[16,24,128]{2,1,0:T(8,128)(2,1)S(1)} all-to-all(bf16[16,24,128]{2,1,0:T(8,128)(2,1)S(1)} %bitcast.208), channel_id=1, replica_groups=mesh['z'=16,'y'=4,'x'=4,'c'=2] {'y','x'}, dimensions={0} | all-to-all | bytes 196608 | tf_op jit(solution)/shard_map/all_to_all | solution.py:37
  213.4 4.5 %collective-permute-start.1 = (f32[24,128]{1,0:T(8,128)S(1)}, f32[24,128]{1,0:T(8,128)S(1)}, u32[]{:S(2)}, u32[]{:S(2)}) collective-permute-start(f32[24,128]{1,0:T(8,128)S(1)} %convert_reduce_fusion.1), channel_id=1, source_target_pairs={{0,1},{1,0},{2,3},{3,2},{4,5},{5,4},{6,7},{7,6},{8,9},{9,8},{10,11... | collective-permute-start | bytes 36872 | tf_op jit(solution)/shard_map/ppermute | solution.py:194
  219.4 6.5 %all-to-all-start.9 = ((bf16[16,24,128]{2,1,0:T(8,128)(2,1)}), bf16[16,24,128]{2,1,0:T(8,128)(2,1)S(1)}, u32[]{:S(2)}, u32[]{:S(2)}) async-start(bf16[16,24,128]{2,1,0:T(8,128)(2,1)} %broadcast_in_dim.82), calls=%async_computation.9 | async-start | bytes 196608 | tf_op jit(solution)/shard_map/all_to_all | solution.py:37
  225.9 11.9 %all-to-all-done.9 = bf16[16,24,128]{2,1,0:T(8,128)(2,1)S(1)} async-done(((bf16[16,24,128]{2,1,0:T(8,128)(2,1)}), bf16[16,24,128]{2,1,0:T(8,128)(2,1)S(1)}, u32[]{:S(2)}, u32[]{:S(2)}) %all-to-all-start.9) | async-done | bytes 98336 | tf_op jit(solution)/shard_map/all_to_all | solution.py:37
  237.8 7.5 %all_to_all.71 = bf16[4,192,128]{2,1,0:T(8,128)(2,1)S(1)} all-to-all(bf16[4,192,128]{2,1,0:T(8,128)(2,1)S(1)} %broadcast_in_dim.83), channel_id=1, replica_groups=mesh['z'=16,'y'=4,'x'=4,'c'=2] {'y'}, dimensions={0} | all-to-all | bytes 393216 | tf_op jit(solution)/shard_map/all_to_all | solution.py:37
  246.4 3.5 %all-to-all-start.11 = ((bf16[4,4,192,128]{3,2,1,0:T(8,128)(2,1)}), bf16[4,4,192,128]{3,2,1,0:T(8,128)(2,1)S(1)}, u32[]{:S(2)}, u32[]{:S(2)}) async-start(bf16[4,4,192,128]{3,2,1,0:T(8,128)(2,1)} %broadcast_in_dim.84), calls=%async_computation.11 | async-start | bytes 1572864 | tf_op jit(solution)/shard_map/all_to_all | solution.py:37
  251.4 6.8 %all-to-all-done.11 = bf16[4,4,192,128]{3,2,1,0:T(8,128)(2,1)S(1)} async-done(((bf16[4,4,192,128]{3,2,1,0:T(8,128)(2,1)}), bf16[4,4,192,128]{3,2,1,0:T(8,128)(2,1)S(1)}, u32[]{:S(2)}, u32[]{:S(2)}) %all-to-all-start.11) | async-done | bytes 786464 | tf_op jit(solution)/shard_map/all_to_all | solution.py:37
  258.2 7.0 %collective-permute-start.2 = (bf16[4,4,192,128]{3,2,1,0:T(8,128)(2,1)S(1)}, bf16[4,4,192,128]{3,2,1,0:T(8,128)(2,1)}, u32[]{:S(2)}, u32[]{:S(2)}) collective-permute-start(bf16[4,4,192,128]{3,2,1,0:T(8,128)(2,1)S(1)} %all-to-all-done.11), channel_id=1, source_target_pairs={{0,1},{1,0},{2,3},{3,2},{4,5},{5,4},{6,7},{7,6},{8,9},{9,8},{10,11... | collective-permute-start | bytes 2359304 | tf_op jit(solution)/shard_map/ppermute | solution.py:213
  272.5 5.6 %copy.190 = f32[2,192,4,4,128]{4,3,2,1,0:T(4,128)} copy(f32[2,192,4,4,128]{4,1,2,3,0:T(8,128)} %convert_bitcast_fusion) | data formatting | bytes 6291456 | tf_op jit(solution)/shard_map/convert_element_type | solution.py:218
  278.1 5.1 %reshape.571 = f32[384,2048]{1,0:T(8,128)} reshape(f32[2,192,4,4,128]{4,3,2,1,0:T(4,128)} %copy.190) | data formatting | bytes 6291456 | tf_op jit(solution)/shard_map/convert_element_type | solution.py:218
  286.7 3.6 %all-to-all-start.12 = ((f32[32,3,128]{2,1,0:T(4,128)}), f32[32,3,128]{2,1,0:T(4,128)S(1)}, u32[]{:S(2)}, u32[]{:S(2)}) async-start(f32[32,3,128]{2,1,0:T(4,128)} %broadcast_in_dim.86), calls=%async_computation.12 | async-start | bytes 131072 | tf_op jit(solution)/shard_map/all_to_all | solution.py:37
  290.4 7.3 %all-to-all-done.12 = f32[32,3,128]{2,1,0:T(4,128)S(1)} async-done(((f32[32,3,128]{2,1,0:T(4,128)}), f32[32,3,128]{2,1,0:T(4,128)S(1)}, u32[]{:S(2)}, u32[]{:S(2)}) %all-to-all-start.12) | async-done | bytes 49184 | tf_op jit(solution)/shard_map/all_to_all | solution.py:37
  298.4 4.9 %all-to-all-start.13 = ((f32[16,3,128]{2,1,0:T(4,128)}), f32[16,3,128]{2,1,0:T(4,128)S(1)}, u32[]{:S(2)}, u32[]{:S(2)}) async-start(f32[16,3,128]{2,1,0:T(4,128)} %broadcast_in_dim.87), calls=%async_computation.13 | async-start | bytes 65536 | tf_op jit(solution)/shard_map/all_to_all | solution.py:37
  304.1 10.7 %all-to-all-done.13 = f32[16,3,128]{2,1,0:T(4,128)S(1)} async-done(((f32[16,3,128]{2,1,0:T(4,128)}), f32[16,3,128]{2,1,0:T(4,128)S(1)}, u32[]{:S(2)}, u32[]{:S(2)}) %all-to-all-start.13) | async-done | bytes 24608 | tf_op jit(solution)/shard_map/all_to_all | solution.py:37
  (206 shorter events, 48.7 us)
Async XLA Ops:
  7.2 276.0 %copy-start = (bf16[2048,256]{1,0:T(8,128)(2,1)S(1)}, bf16[2048,256]{1,0:T(8,128)(2,1)}, u32[]{:S(2)}) copy-start(bf16[2048,256]{1,0:T(8,128)(2,1)} %param.35) | copy-start | bytes 3145732
  7.2 16.4 %copy-start.7 = (s32[8,48]{1,0:T(8,128)S(1)}, s32[8,48]{1,0:T(8,128)}, u32[]{:S(2)}) copy-start(s32[8,48]{1,0:T(8,128)} %param.40) | copy-start | bytes 4612
  7.2 18.6 %copy-start.3 = (s32[8]{0:T(128)S(1)}, s32[8]{0:T(128)}, u32[]{:S(2)}) copy-start(s32[8]{0:T(128)} %param.39) | copy-start | bytes 100
  17.7 41.9 %copy-start.4 = (f32[128]{0:T(128)S(1)}, f32[128]{0:T(128)}, u32[]{:S(2)}) copy-start(f32[128]{0:T(128)} %param.27) | copy-start | bytes 1540
  17.7 42.2 %copy-start.5 = (f32[128]{0:T(128)S(1)}, f32[128]{0:T(128)}, u32[]{:S(2)}) copy-start(f32[128]{0:T(128)} %param.28) | copy-start | bytes 1540
  18.5 11.2 %all-to-all-start = ((bf16[4,32,1536]{2,1,0:T(8,128)(2,1)}), bf16[4,32,1536]{2,1,0:T(8,128)(2,1)S(1)}, u32[]{:S(2)}, u32[]{:S(2)}) async-start(bf16[4,32,1536]{2,1,0:T(8,128)(2,1)} %pad_maximum_fusion.1), calls=%async_computation | async-start | bytes 786432 | tf_op jit(solution)/shard_map/all_to_all | solution.py:37
  30.9 28.2 %all-to-all-start.1 = ((bf16[16,6,896]{2,1,0:T(8,128)(2,1)}), bf16[16,6,896]{2,1,0:T(8,128)(2,1)S(1)}, u32[]{:S(2)}, u32[]{:S(2)}) async-start(bf16[16,6,896]{2,1,0:T(8,128)(2,1)} %reshape.543), calls=%async_computation.1 | async-start | bytes 458752 | tf_op jit(solution)/shard_map/all_to_all | solution.py:37
  60.9 20.8 %all-to-all-start.2 = ((bf16[16,8,768]{2,1,0:T(8,128)(2,1)}), bf16[16,8,768]{2,1,0:T(8,128)(2,1)S(1)}, u32[]{:S(2)}, u32[]{:S(2)}) async-start(bf16[16,8,768]{2,1,0:T(8,128)(2,1)} %broadcast_in_dim.72), calls=%async_computation.2 | async-start | bytes 393216 | tf_op jit(solution)/shard_map/all_to_all | solution.py:37
  82.6 11.9 %copy-start.1 = (bf16[8,256,128]{2,1,0:T(8,128)(2,1)S(1)}, bf16[8,256,128]{2,1,0:T(8,128)(2,1)}, u32[]{:S(2)}) copy-start(bf16[8,256,128]{2,1,0:T(8,128)(2,1)} %param.37) | copy-start | bytes 1572868
  82.6 10.9 %all-to-all-start.3 = ((bf16[4,96,768]{2,1,0:T(8,128)(2,1)}), bf16[4,96,768]{2,1,0:T(8,128)(2,1)S(1)}, u32[]{:S(2)}, u32[]{:S(2)}) async-start(bf16[4,96,768]{2,1,0:T(8,128)(2,1)} %broadcast_in_dim.74), calls=%async_computation.3 | async-start | bytes 1179648 | tf_op jit(solution)/shard_map/all_to_all | solution.py:37
  86.2 75.6 %all-gather.2.cloned.1.call-start = ((), (), s32[]{:S(2)}) async-start(), calls=%async_computation.14 | async-start | bytes 2785280 | tf_op jit(solution)/shard_map/all_gather | solution.py:113
  94.0 1.7 copy-start.2
  97.1 20.5 %all-to-all-start.4 = ((bf16[16,56,128]{2,1,0:T(8,128)(2,1)}), bf16[16,56,128]{2,1,0:T(8,128)(2,1)S(1)}, u32[]{:S(2)}, u32[]{:S(2)}) async-start(bf16[16,56,128]{2,1,0:T(8,128)(2,1)} %fusion.36), calls=%async_computation.4 | async-start | bytes 458752 | tf_op jit(solution)/shard_map/all_to_all | solution.py:37
  118.9 8.3 %all-to-all-start.5 = ((bf16[4,152,128]{2,1,0:T(8,128)(2,1)}), bf16[4,152,128]{2,1,0:T(8,128)(2,1)S(1)}, u32[]{:S(2)}, u32[]{:S(2)}) async-start(bf16[4,152,128]{2,1,0:T(8,128)(2,1)} %broadcast_in_dim.80), calls=%async_computation.5 | async-start | bytes 311296 | tf_op jit(solution)/shard_map/all_to_all | solution.py:37
  163.8 12.4 %all-to-all-start.6 = ((bf16[16,24,128]{2,1,0:T(8,128)(2,1)}), bf16[16,24,128]{2,1,0:T(8,128)(2,1)S(1)}, u32[]{:S(2)}, u32[]{:S(2)}) async-start(bf16[16,24,128]{2,1,0:T(8,128)(2,1)} %bitcast.189), calls=%async_computation.6 | async-start | bytes 196608 | tf_op jit(solution)/shard_map/all_to_all | solution.py:37
  176.3 12.8 %collective-permute-start = (f32[24,128]{1,0:T(8,128)S(1)}, f32[24,128]{1,0:T(8,128)S(1)}, u32[]{:S(2)}, u32[]{:S(2)}) collective-permute-start(f32[24,128]{1,0:T(8,128)S(1)} %convert_reduce_fusion.2), channel_id=1, source_target_pairs={{0,1},{1,0},{2,3},{3,2},{4,5},{5,4},{6,7},{7,6},{8,9},{9,8},{10,11... | collective-permute-start | bytes 36872 | tf_op jit(solution)/shard_map/ppermute | solution.py:194
  189.8 10.1 %all-to-all-start.7 = ((bf16[16,24,128]{2,1,0:T(8,128)(2,1)}), bf16[16,24,128]{2,1,0:T(8,128)(2,1)S(1)}, u32[]{:S(2)}, u32[]{:S(2)}) async-start(bf16[16,24,128]{2,1,0:T(8,128)(2,1)} %broadcast_in_dim.81), calls=%async_computation.7 | async-start | bytes 196608 | tf_op jit(solution)/shard_map/all_to_all | solution.py:37
  201.9 48.0 %copy-start.8 = (s32[8]{0:T(128)S(1)}, s32[8]{0:T(128)}, u32[]{:S(2)}) copy-start(s32[8]{0:T(128)} %param.41) | copy-start | bytes 100
  201.9 63.6 %copy-start.6 = (f32[8]{0:T(128)S(1)}, f32[8]{0:T(128)}, u32[]{:S(2)}) copy-start(f32[8]{0:T(128)} %param.36) | copy-start | bytes 100
  213.4 5.4 %collective-permute-start.1 = (f32[24,128]{1,0:T(8,128)S(1)}, f32[24,128]{1,0:T(8,128)S(1)}, u32[]{:S(2)}, u32[]{:S(2)}) collective-permute-start(f32[24,128]{1,0:T(8,128)S(1)} %convert_reduce_fusion.1), channel_id=1, source_target_pairs={{0,1},{1,0},{2,3},{3,2},{4,5},{5,4},{6,7},{7,6},{8,9},{9,8},{10,11... | collective-permute-start | bytes 36872 | tf_op jit(solution)/shard_map/ppermute | solution.py:194
  219.4 18.4 %all-to-all-start.9 = ((bf16[16,24,128]{2,1,0:T(8,128)(2,1)}), bf16[16,24,128]{2,1,0:T(8,128)(2,1)S(1)}, u32[]{:S(2)}, u32[]{:S(2)}) async-start(bf16[16,24,128]{2,1,0:T(8,128)(2,1)} %broadcast_in_dim.82), calls=%async_computation.9 | async-start | bytes 196608 | tf_op jit(solution)/shard_map/all_to_all | solution.py:37
  246.4 11.8 %all-to-all-start.11 = ((bf16[4,4,192,128]{3,2,1,0:T(8,128)(2,1)}), bf16[4,4,192,128]{3,2,1,0:T(8,128)(2,1)S(1)}, u32[]{:S(2)}, u32[]{:S(2)}) async-start(bf16[4,4,192,128]{3,2,1,0:T(8,128)(2,1)} %broadcast_in_dim.84), calls=%async_computation.11 | async-start | bytes 1572864 | tf_op jit(solution)/shard_map/all_to_all | solution.py:37
  258.2 10.7 %collective-permute-start.2 = (bf16[4,4,192,128]{3,2,1,0:T(8,128)(2,1)S(1)}, bf16[4,4,192,128]{3,2,1,0:T(8,128)(2,1)}, u32[]{:S(2)}, u32[]{:S(2)}) collective-permute-start(bf16[4,4,192,128]{3,2,1,0:T(8,128)(2,1)S(1)} %all-to-all-done.11), channel_id=1, source_target_pairs={{0,1},{1,0},{2,3},{3,2},{4,5},{5,4},{6,7},{7,6},{8,9},{9,8},{10,11... | collective-permute-start | bytes 2359304 | tf_op jit(solution)/shard_map/ppermute | solution.py:213
  286.7 11.0 %all-to-all-start.12 = ((f32[32,3,128]{2,1,0:T(4,128)}), f32[32,3,128]{2,1,0:T(4,128)S(1)}, u32[]{:S(2)}, u32[]{:S(2)}) async-start(f32[32,3,128]{2,1,0:T(4,128)} %broadcast_in_dim.86), calls=%async_computation.12 | async-start | bytes 131072 | tf_op jit(solution)/shard_map/all_to_all | solution.py:37
  298.4 16.4 %all-to-all-start.13 = ((f32[16,3,128]{2,1,0:T(4,128)}), f32[16,3,128]{2,1,0:T(4,128)S(1)}, u32[]{:S(2)}, u32[]{:S(2)}) async-start(f32[16,3,128]{2,1,0:T(4,128)} %broadcast_in_dim.87), calls=%async_computation.13 | async-start | bytes 65536 | tf_op jit(solution)/shard_map/all_to_all | solution.py:37
Sparse Core Ops, SparseCore 0:
  89.7 72.0 all-gather.1

commit v2 on v1

v2 whole, which is shorter than its diff:
```python
import jax
import jax.numpy as jnp
from jax import lax
from jax.experimental import pallas as pl
from jax.experimental.pallas import tpu as pltpu
from jax.sharding import Mesh, PartitionSpec as P

EPSILON = 1e-06
ROPE_BASE = 1000000.0
NEGATIVE = -1e30
BF = jnp.bfloat16
F32 = jnp.float32


def ancestry(parents):
    node_count = parents.shape[-1]
    node_ids = jnp.arange(node_count, dtype=jnp.int32)
    reachable = (parents[..., :, None] == node_ids[None, :]).astype(BF)
    reachable = jnp.maximum(reachable, jnp.eye(node_count, dtype=BF))
    for turn in range((node_count - 1).bit_length()):
        reachable = jnp.minimum(
            jnp.einsum("rij,rjk->rik", reachable, reachable, preferred_element_type=F32), 1.0
        ).astype(BF)
    return reachable.astype(F32)


def head_norm(values, gain):
    meansq = jnp.mean(values * values, axis=-1, keepdims=True)
    return values * lax.rsqrt(meansq + EPSILON) * gain


def rotate(values, cosine, sine):
    half = values.shape[-1] // 2
    low, high = values[..., :half], values[..., half:]
    return jnp.concatenate([low * cosine - high * sine, high * cosine + low * sine], axis=-1)


def swap(values, axis):
    return lax.all_to_all(values, axis, 0, 0, tiled=True)


def spread(values, axis, count):
    return swap(jnp.broadcast_to(values[None], (count,) + values.shape), axis)


def split2(values):
    high = lax.reduce_precision(values, 8, 7)
    return high.astype(BF), (values - high).astype(BF)


def pack_kernel(hidden_ref, place_ref, gain_ref, gate_ref, up_ref, down_ref, wo_ref, wq_ref, wk_ref, wv_ref, wg_ref, out_ref):
    lanes = lax.broadcasted_iota(jnp.int32, (512, 384), 0)
    chosen = jnp.where(lanes == place_ref[0:1, :], 1.0, 0.0).astype(BF)
    moved = lax.dot_general(
        hidden_ref[...], chosen, (((1,), (1,)), ((), ())), preferred_element_type=F32
    )
    diagonal = lax.broadcasted_iota(jnp.int32, (32, 32), 0) == lax.broadcasted_iota(jnp.int32, (32, 32), 1)
    lane = lax.broadcasted_iota(jnp.int32, (32, 128), 1)
    extra = jnp.zeros((32, 128), F32)
    for which in range(3):
        rest = jnp.sum(jnp.where(diagonal, gain_ref[which : which + 1, :], 0.0), axis=1, keepdims=True)
        for digit in range(3):
            part = rest.astype(BF).astype(F32)
            extra = jnp.where(lane == 96 + which * 3 + digit, part, extra)
            rest = rest - part
    zeros = jnp.zeros((32, 64), BF)
    for y in range(4):
        tile = slice(y * 128, y * 128 + 128)
        start = 512 + y * 64
        side = slice(start, start + 64)
        out_ref[y, :, 0:128] = gate_ref[:, tile]
        out_ref[y, :, 128:256] = up_ref[:, tile]
        out_ref[y, :, 256:384] = down_ref[:, tile]
        out_ref[y, :, 384:640] = wo_ref[...]
        out_ref[y, :, 640:768] = jnp.concatenate([gate_ref[:, side], up_ref[:, side]], axis=1)
        out_ref[y, :, 768:896] = jnp.concatenate([down_ref[:, side], zeros], axis=1)
        out_ref[y, :, 896:1152] = wq_ref[...]
        out_ref[y, :, 1152:1280] = wk_ref[...]
        out_ref[y, :, 1280:1408] = wv_ref[...]
        out_ref[y, :, 1408:1664] = wg_ref[...]
        out_ref[y, :, 1664:1792] = (moved[:, tile] + extra).astype(BF)


def head_kernel(core_ref, temp_ref, tiles_ref, gain_ref, weight_ref, logits_ref, spot_ref, *, flip, width):
    rows = tiles_ref.shape[2]
    squares = jnp.zeros((rows, 128), F32)
    for column in range(16):
        tile = tiles_ref[column % 4, column // 4].astype(F32)
        squares = squares + tile * tile
    scale = lax.rsqrt(jnp.sum(squares, axis=1, keepdims=True) / width + EPSILON)
    total = jnp.zeros((rows, 256), F32)
    for pair in range(8):
        sides = []
        for column in (2 * pair, 2 * pair + 1):
            tile = tiles_ref[column % 4, column // 4].astype(F32)
            sides.append((tile * scale * gain_ref[column : column + 1, :]).astype(BF))
        total = total + jnp.dot(
            jnp.concatenate(sides, axis=1),
            weight_ref[pair * 256 : pair * 256 + 256, :],
            preferred_element_type=F32,
        )
    part = core_ref[0] if not flip else 1 - core_ref[0]
    row = lax.broadcasted_iota(jnp.int32, (rows, 1), 0)
    temps = jnp.zeros((rows, 1), F32)
    for request in range(4):
        here = (row >= request * 48) & (row < request * 48 + 48)
        temps = jnp.where(here, temp_ref[part * 4 + request], temps)
    logits = total * temps
    logits_ref[...] = logits
    top = jnp.max(logits, axis=1, keepdims=True)
    spot = top + jnp.log(jnp.sum(jnp.exp(logits - top), axis=1, keepdims=True))
    across = lax.broadcasted_iota(jnp.int32, (rows, 256), 0) == lax.broadcasted_iota(jnp.int32, (rows, 256), 1)
    spot_ref[...] = jnp.sum(jnp.where(across, spot, 0.0), axis=0, keepdims=True)


def head(core, temps, tiles, gains, weight, flip):
    rows = tiles.shape[2]
    vmem, smem = pl.BlockSpec(memory_space=pltpu.VMEM), pl.BlockSpec(memory_space=pltpu.SMEM)
    return pl.pallas_call(
        lambda *refs: head_kernel(*refs, flip=flip, width=2048),
        out_shape=(
            jax.ShapeDtypeStruct((rows, 256), F32),
            jax.ShapeDtypeStruct((1, 256), F32),
        ),
        in_specs=[smem, smem, vmem, vmem, vmem],
        out_specs=(vmem, vmem),
        cost_estimate=pl.CostEstimate(
            flops=2 * rows * 2048 * 256, bytes_accessed=2 * 2048 * (rows + 256), transcendentals=rows * 256
        ),
        name="head_flip" if flip else "head_own",
    )(core, temps, tiles, gains, weight)


def pack_state(peak, mass, weighted):
    count = peak.shape[0]
    mass_high, mass_low = split2(mass)
    stats = jnp.stack([peak.astype(BF), mass_high, mass_low], axis=1).reshape(count, 6, 24)
    stats = jnp.pad(stats, ((0, 0), (0, 2), (0, 104)))
    return jnp.concatenate([weighted.astype(BF).reshape(count, 48, 128), stats], axis=1)


def merge_state(packed):
    count = packed.shape[0]
    weighted = packed[:, :48].reshape(count, 2, 24, 128).astype(F32)
    stats = packed[:, 48:54, :24].astype(F32).reshape(count, 3, 2, 24)
    peaks, masses = stats[:, 0], stats[:, 1] + stats[:, 2]
    peak = jnp.max(peaks, axis=0)
    factor = jnp.exp(peaks - peak)
    return peak, jnp.sum(masses * factor, axis=0), jnp.sum(weighted * factor[..., None], axis=0)


def on_device(
    hidden, ln1_gain, wq, wk, wv, wg, q_gain, key_gain, wo, ln2_gain, w_gate, w_up, w_down,
    last_gain, head_weight, inv_temp, key_cache, value_cache, lengths, parents, accepted,
):
    z, y, x, c = (lax.axis_index(name) for name in ("z", "y", "x", "c"))
    seq = z * 4 + y
    requests, tree = parents.shape
    slot_count = key_cache.shape[1]
    width = 2048

    token = jnp.arange(384, dtype=jnp.int32)
    token_z = token % 192 // 12
    token_y = token // 192 * 2 + token % 12 // 6
    token_i = token % 6

    place = (token_y * 128 + token_z * 6 + token_i).reshape(1, 384)
    gains = jnp.stack([ln1_gain, ln2_gain, last_gain])
    vmem = pl.BlockSpec(memory_space=pltpu.VMEM)
    pieces = pl.pallas_call(
        pack_kernel,
        out_shape=jax.ShapeDtypeStruct((4, 32, 1792), BF),
        in_specs=[vmem] * 11,
        out_specs=vmem,
        name="pack",
    )(hidden.T, place, gains, w_gate, w_up, w_down.T, wo.T, wq, wk, wv, wg)
    mine = swap(pieces, "y").reshape(128, 1792)
    ffn = lax.all_gather(mine[:, :896], "z", axis=0, tiled=True)
    proj = mine[:, 896:1664]
    side = mine[:, 1664:]
    side_wide = side.astype(F32)
    ln1_row = side_wide[:, 96:97] + side_wide[:, 97:98] + side_wide[:, 98:99]
    scaled = (side_wide * ln1_row).astype(BF)
    partial = lax.dot_general(scaled, proj, (((0,), (0,)), ((), ())), preferred_element_type=F32)
    sent = jnp.concatenate([partial[:96].astype(BF), side.T[:96]], axis=1).reshape(16, 6, 896)
    got = swap(sent, "z")
    sums = jnp.sum(got[:, :, :768].astype(F32), axis=0)
    rows = got[:, :, 768:]
    rows_wide = rows.astype(F32)
    squares = jnp.sum(rows_wide * rows_wide, axis=(0, 2))
    sums = sums * lax.rsqrt(squares / width + EPSILON)[:, None]

    links = ancestry(parents)
    depth = jnp.sum((links > 0.5).astype(jnp.int32), axis=-1) - 1
    target = lengths[:, None] + depth
    first = y // 2 * 192 + z * 12 + y % 2 * 6
    my_places = lax.dynamic_slice(target.reshape(-1), (first,), (6,))
    inverse = ROPE_BASE ** (-jnp.arange(64, dtype=F32) / 64)
    angles = my_places.astype(F32)[:, None] * inverse[None, :]
    cosine, sine = jnp.cos(angles)[:, None, :], jnp.sin(angles)[:, None, :]
    query = rotate(head_norm(sums[:, :256].reshape(6, 2, 128), q_gain), cosine, sine) * 128 ** (-0.5)
    new_key = rotate(head_norm(sums[:, 256:384].reshape(6, 1, 128), key_gain), cosine, sine)
    outgate = jax.nn.sigmoid(sums[:, 512:]).astype(BF)
    block = jnp.concatenate(
        [
            query[:, 0], query[:, 1], new_key[:, 0], sums[:, 384:512],
            side[:, 99:105].T.astype(F32), jnp.zeros((2, 128), F32),
        ],
        axis=0,
    ).astype(BF)
    gathered = spread(block, "z", 16)
    gain_all = gathered[:, 24:30].astype(F32)
    ln2_all = gain_all[:, 0] + gain_all[:, 1] + gain_all[:, 2]
    last_all = gain_all[:, 3] + gain_all[:, 4] + gain_all[:, 5]
    pool = spread(gathered[:, :24].reshape(384, 128), "y", 4).reshape(1536, 128)
    origin = token_y * 384 + token_z * 24 + token_i
    origin = (jnp.arange(4, dtype=jnp.int32)[:, None] * 6 + origin[None, :]).reshape(1536)
    gather = (origin[:, None] == jnp.arange(1536, dtype=jnp.int32)[None, :]).astype(BF)
    tokens = jnp.dot(gather, pool, preferred_element_type=F32).astype(BF).reshape(4, requests, tree, 128)
    queries, tree_keys, tree_values = tokens[:2], tokens[2], tokens[3]

    slot_ids = seq * slot_count + jnp.arange(slot_count, dtype=jnp.int32)
    valid_slot = (slot_ids[None, :] < lengths[:, None])[:, None, None, :]
    valid_node = ((links > 0.5) & (seq == 0))[:, None, :, :]
    scores = jnp.einsum("grid,rcd->rgic", queries, key_cache, preferred_element_type=F32)
    tree_scores = jnp.einsum("grid,rjd->rgij", queries, tree_keys, preferred_element_type=F32)
    peak = jnp.maximum(
        jnp.max(jnp.where(valid_slot, scores, NEGATIVE), axis=-1),
        jnp.max(jnp.where(valid_node, tree_scores, NEGATIVE), axis=-1),
    )
    peak = lax.reduce_precision(peak, 8, 7)
    weights = jnp.where(valid_slot, jnp.exp(scores - peak[..., None]), 0.0)
    tree_weights = jnp.where(valid_node, jnp.exp(tree_scores - peak[..., None]), 0.0)
    mass = jnp.sum(weights, axis=-1) + jnp.sum(tree_weights, axis=-1)
    weighted = jnp.einsum(
        "rgic,rcd->rgid", weights.astype(BF), value_cache, preferred_element_type=F32
    ) + jnp.einsum("rgij,rjd->rgid", tree_weights.astype(BF), tree_values, preferred_element_type=F32)

    def by_z(values):
        rest = values.shape[3:]
        split = values.reshape((2, 4, 2, 4, 12) + rest)
        split = jnp.transpose(split, (1, 3, 2, 0, 4) + tuple(range(5, 5 + len(rest))))
        return split.reshape((16, 2, 24) + rest)

    outgoing = pack_state(by_z(peak), by_z(mass), by_z(weighted))
    state = merge_state(swap(outgoing, "z"))
    packed = pack_state(*(part[None] for part in state))[0]
    shared = jnp.concatenate([packed, rows.reshape(96, 128), outgate[:, :128], outgate[:, 128:]], axis=0)
    shared, ffn = lax.optimization_barrier((shared, ffn))
    both = spread(shared, "y", 4)
    peak, mass, weighted = merge_state(both[:, :56])
    my_gate = jnp.swapaxes(both[:, 152:].reshape(4, 2, 6, 128), 0, 1).reshape(2, 24, 128).astype(F32)
    gated = (weighted / mass[..., None] * my_gate).astype(BF)
    hidden_rows = jnp.swapaxes(both[:, 56:152].reshape(4, 16, 6, 128), 0, 1).reshape(16, 24, 128)

    attn = lax.dot_general(
        jnp.concatenate([gated[0], gated[1]], axis=1),
        ffn[:, 384:640],
        (((1,), (1,)), ((), ())),
        preferred_element_type=F32,
    )
    attn = jnp.sum(spread(attn.astype(BF), ("x", "c"), 8).astype(F32), axis=0)
    hidden_rows = jnp.swapaxes(hidden_rows, 0, 1).reshape(24, width)
    middle = (hidden_rows.astype(F32) + attn).astype(BF)
    middle_wide = middle.astype(F32)
    squares_mid = jnp.sum(middle_wide * middle_wide, axis=1)
    normed2 = (
        middle_wide * lax.rsqrt(squares_mid / width + EPSILON)[:, None] * ln2_all.reshape(1, width)
    ).astype(BF)
    units = jnp.dot(normed2, ffn[:, :256], preferred_element_type=F32)
    sides = jnp.dot(normed2, ffn[:, 640:768], preferred_element_type=F32)
    act = (jax.nn.silu(units[:, :128]) * units[:, 128:]).astype(BF)
    act_side = (jax.nn.silu(sides[:, :64]) * sides[:, 64:]).astype(BF)
    contract = (((1,), (1,)), ((), ()))
    down = lax.dot_general(act, ffn[:, 256:384], contract, preferred_element_type=F32) + lax.dot_general(
        act_side, ffn[:, 768:832], contract, preferred_element_type=F32
    )
    down = jnp.transpose(down.astype(BF).reshape(2, 12, 16, 128), (2, 0, 1, 3)).reshape(32, 12, 128)
    down = jnp.sum(swap(down, ("y", "x", "c")).astype(F32), axis=0)
    middle_mine = lax.dynamic_slice(middle, (c * 12, (y * 4 + x) * 128), (12, 128))
    following = (middle_mine.astype(F32) + down).astype(BF)

    half = spread(following, "z", 16).reshape(192, 128)
    half = spread(spread(half, "y", 4), "x", 4)
    other = lax.ppermute(half, "c", [(0, 1), (1, 0)])
    core = c.reshape(1)
    own_logits, own_spot = head(core, inv_temp, half, last_all, head_weight, False)
    other_logits, other_spot = head(core, inv_temp, other, last_all, head_weight, True)

    def in_order(mine_part, other_part):
        return jnp.concatenate(
            [jnp.where(c == 0, mine_part, other_part), jnp.where(c == 0, other_part, mine_part)], axis=0
        )

    def own_columns(tiles):
        return lax.dynamic_slice(tiles, (z % 4, z // 4, 0, 0), (1, 1, 192, 128)).reshape(192, 128)

    own = in_order(own_columns(half), own_columns(other))
    next_hidden = lax.dynamic_slice(own, (0, y * 32), (384, 32))
    spot = in_order(own_spot, other_spot).reshape(1, 512)
    for axis, count in ((("y", "x", "c"), 32), ("z", 16)):
        spots = spread(spot, axis, count)
        top = jnp.max(spots, axis=0)
        spot = top + jnp.log(jnp.sum(jnp.exp(spots - top), axis=0))
    spot = spot.reshape(2, 256)[:, :192].reshape(384, 1)
    logprobs = in_order(own_logits, other_logits) - spot

    accepted_rows = links[jnp.arange(requests), accepted]
    placed = (slot_ids[None, :, None] == target[:, None, :]).astype(F32) * accepted_rows[:, None, :]
    hits = (jnp.sum(placed, axis=2) > 0.5)[:, :, None]
    placed = placed.astype(BF)
    moved_keys = jnp.einsum("rca,rae->rce", placed, tree_keys, preferred_element_type=F32).astype(BF)
    moved_values = jnp.einsum("rca,rae->rce", placed, tree_values, preferred_element_type=F32).astype(BF)
    return (
        logprobs,
        next_hidden,
        jnp.where(hits, moved_keys, key_cache),
        jnp.where(hits, moved_values, value_cache),
    )


def solution(mesh):
    grid = Mesh(mesh.devices.reshape(16, 4, 4, 2), ("z", "y", "x", "c"))
    seq, tp = ("z", "y"), ("x", "c")
    in_specs = (
        P(None, seq), P(seq), P(seq, tp), P(seq, tp), P(seq, tp), P(seq, tp), P(), P(),
        P(tp, seq), P(seq), P(seq, tp), P(seq, tp), P(tp, seq), P(seq),
        P(None, seq + tp), P(), P(None, seq, tp), P(None, seq, tp), P(), P(), P(),
    )
    out_specs = (P(None, seq + tp), P(None, seq), P(None, seq, tp), P(None, seq, tp))
    return jax.shard_map(on_device, mesh=grid, in_specs=in_specs, out_specs=out_specs, check_vma=False)
```

time: 325 us -> 278 us (0.86)
  waiting for transfers between devices: 138 us -> 106 us
  starting transfers between devices: 94.6 us -> 74.3 us
  local copies, waits for them, and re-layouts: 30.7 us -> 12.2 us
  blocking collectives: 17.3 us -> 35.3 us
  Pallas kernels: 0 us -> 7.48 us
    all_gather x1, waiting for transfers between devices: 34.2 us -> 14.5 us  [on_device(): ffn = lax.all_gather(mine[:, :896], 'z', axis=0, tiled=True)]
    all_to_all x2 -> x3, blocking collectives: 17.3 us -> 35.3 us  [swap(): return lax.all_to_all(values, axis, 0, 0, tiled=True)]
    ppermute x2 -> x0, starting transfers between devices: 16.6 us -> none  [reduce_columns(): return part + lax.ppermute(part, 'c', [(0, 1), (1, 0)])]
    all_to_all x12 -> x10, waiting for transfers between devices: 102 us -> 91.8 us  [swap(): return lax.all_to_all(values, axis, 0, 0, tiled=True)]
    convert_element_type x5 -> x10, local copies, waits for them, and re-layouts: 10.7 us -> 0.57 us  [the longest x4 0.19 us: pack_state(): peak.astype(BF)]
    pallas_call x0 -> x3, Pallas kernels: none -> 7.48 us  [the longest x2 5.52 us: head(): pl.pallas_call(lambda *refs: head_kernel(*refs, flip=flip, width=2048), o...]
    all_to_all x12 -> x10, starting transfers between devices: 71 us -> 67.7 us  [swap(): return lax.all_to_all(values, axis, 0, 0, tiled=True)]
  transfers between devices with their start and end apart: 16 -> 12, of which waited for: 15 -> 11; matrix products, arithmetic and copies ran while one was open for 5% -> 7% of each run, Pallas kernels for 0% -> 1%
where the time goes in v2:
time: 278 us; the launch traced here: 276 us
  waiting for transfers between devices  106 us (38%)
  starting transfers between devices  74.3 us (27%)
  blocking collectives  35.3 us (13%)
  matrix products  15.9 us (6%)
  between operations  14.8 us (5%)
  local copies, waits for them, and re-layouts  12.2 us (4%)
  other arithmetic  9.76 us (4%)
  Pallas kernels  7.48 us (3%)
    all_to_all x10, waiting for transfers between devices, swap(): return lax.all_to_all(values, axis, 0, 0, tiled=True)  91.8 us
    all_to_all x10, starting transfers between devices, swap(): return lax.all_to_all(values, axis, 0, 0, tiled=True)  67.7 us
    all_to_all x3, blocking collectives, swap(): return lax.all_to_all(values, axis, 0, 0, tiled=True)  35.3 us
    all_gather x1, waiting for transfers between devices, on_device(): ffn = lax.all_gather(mine[:, :896], 'z', axis=0, tiled=True)  14.5 us
    ppermute x1, starting transfers between devices, on_device(): other = lax.ppermute(half, 'c', [(0, 1), (1, 0)])  6.59 us
  transfers between devices with their start and end apart: 12, of which 11 were waited for; matrix products, arithmetic and copies ran while one was open for 7% of the time, Pallas kernels for 1%

profile of v2, /device:TPU:1, one launch (start us, length us, event | category | flops | bytes accessed | tf_op | source)
XLA Modules:
  0.0 276.1 jit_solution(16805487082105822020)
XLA Ops:
  9.1 2.0 pack.1
  11.0 5.0 %all-to-all-start = ((bf16[4,32,1792]{2,1,0:T(8,128)(2,1)}), bf16[4,32,1792]{2,1,0:T(8,128)(2,1)S(1)}, u32[]{:S(2)}, u32[]{:S(2)}) async-start(bf16[4,32,1792]{2,1,0:T(8,128)(2,1)} %pack.1), calls=%async_computation | async-start | bytes 917504 | tf_op jit(solution)/shard_map/all_to_all | solution.py:39
  18.5 4.2 %all-to-all-done = bf16[4,32,1792]{2,1,0:T(8,128)(2,1)S(1)} async-done(((bf16[4,32,1792]{2,1,0:T(8,128)(2,1)}), bf16[4,32,1792]{2,1,0:T(8,128)(2,1)S(1)}, u32[]{:S(2)}, u32[]{:S(2)}) %all-to-all-start) | async-done | bytes 458784 | tf_op jit(solution)/shard_map/all_to_all | solution.py:39
  23.8 15.9 %all-to-all-start.1 = ((bf16[16,6,896]{2,1,0:T(8,128)(2,1)}), bf16[16,6,896]{2,1,0:T(8,128)(2,1)S(1)}, u32[]{:S(2)}, u32[]{:S(2)}) async-start(bf16[16,6,896]{2,1,0:T(8,128)(2,1)} %reshape.716), calls=%async_computation.1 | async-start | bytes 458752 | tf_op jit(solution)/shard_map/all_to_all | solution.py:39
  41.0 11.3 %all-to-all-done.1 = bf16[16,6,896]{2,1,0:T(8,128)(2,1)S(1)} async-done(((bf16[16,6,896]{2,1,0:T(8,128)(2,1)}), bf16[16,6,896]{2,1,0:T(8,128)(2,1)S(1)}, u32[]{:S(2)}, u32[]{:S(2)}) %all-to-all-start.1) | async-done | bytes 172064 | tf_op jit(solution)/shard_map/all_to_all | solution.py:39
  54.2 8.4 %all-to-all-start.2 = ((bf16[16,32,128]{2,1,0:T(8,128)(2,1)}), bf16[16,32,128]{2,1,0:T(8,128)(2,1)S(1)}, u32[]{:S(2)}, u32[]{:S(2)}) async-start(bf16[16,32,128]{2,1,0:T(8,128)(2,1)} %broadcast_in_dim.74), calls=%async_computation.2 | async-start | bytes 262144 | tf_op jit(solution)/shard_map/all_to_all | solution.py:39
  62.9 12.5 %all-to-all-done.2 = bf16[16,32,128]{2,1,0:T(8,128)(2,1)S(1)} async-done(((bf16[16,32,128]{2,1,0:T(8,128)(2,1)}), bf16[16,32,128]{2,1,0:T(8,128)(2,1)S(1)}, u32[]{:S(2)}, u32[]{:S(2)}) %all-to-all-start.2) | async-done | bytes 131104 | tf_op jit(solution)/shard_map/all_to_all | solution.py:39
  76.2 3.5 %all-to-all-start.3 = ((bf16[4,384,128]{2,1,0:T(8,128)(2,1)}), bf16[4,384,128]{2,1,0:T(8,128)(2,1)S(1)}, u32[]{:S(2)}, u32[]{:S(2)}) async-start(bf16[4,384,128]{2,1,0:T(8,128)(2,1)} %broadcast_in_dim.76), calls=%async_computation.3 | async-start | bytes 786432 | tf_op jit(solution)/shard_map/all_to_all | solution.py:39
  79.8 6.1 %all-to-all-done.3 = bf16[4,384,128]{2,1,0:T(8,128)(2,1)S(1)} async-done(((bf16[4,384,128]{2,1,0:T(8,128)(2,1)}), bf16[4,384,128]{2,1,0:T(8,128)(2,1)S(1)}, u32[]{:S(2)}, u32[]{:S(2)}) %all-to-all-start.3) | async-done | bytes 393248 | tf_op jit(solution)/shard_map/all_to_all | solution.py:39
  85.9 1.7 fusion.2
  91.0 6.0 %all-to-all-start.4 = ((bf16[16,56,128]{2,1,0:T(8,128)(2,1)}), bf16[16,56,128]{2,1,0:T(8,128)(2,1)S(1)}, u32[]{:S(2)}, u32[]{:S(2)}) async-start(bf16[16,56,128]{2,1,0:T(8,128)(2,1)} %copy.177), calls=%async_computation.4 | async-start | bytes 458752 | tf_op jit(solution)/shard_map/all_to_all | solution.py:39
  97.1 14.4 %all-to-all-done.4 = bf16[16,56,128]{2,1,0:T(8,128)(2,1)S(1)} async-done(((bf16[16,56,128]{2,1,0:T(8,128)(2,1)}), bf16[16,56,128]{2,1,0:T(8,128)(2,1)S(1)}, u32[]{:S(2)}, u32[]{:S(2)}) %all-to-all-start.4) | async-done | bytes 229408 | tf_op jit(solution)/shard_map/all_to_all | solution.py:39
  112.0 14.5 %all-gather.2.cloned.1.call-done = bf16[2048,896]{1,0:T(8,128)(2,1)} async-done(((bf16[128,896]{1,0:T(8,128)(2,1)}), bf16[2048,896]{1,0:T(8,128)(2,1)}) %all-gather.2.cloned.1.call-update) | async-done | bytes 3670032 | tf_op jit(solution)/shard_map/all_gather | solution.py:178
  126.5 9.3 %all_to_all.65 = bf16[4,164,128]{2,1,0:T(8,128)(2,1)S(1)} all-to-all(bf16[4,164,128]{2,1,0:T(8,128)(2,1)S(1)} %broadcast_in_dim.82), channel_id=1, replica_groups=mesh['z'=16,'y'=4,'x'=4,'c'=2] {'y'}, dimensions={0} | all-to-all | bytes 335872 | tf_op jit(solution)/shard_map/all_to_all | solution.py:39
  136.3 1.6 convolution_convert_fusion
  138.9 13.5 %all-to-all-start.6 = ((bf16[8,24,2048]{2,1,0:T(8,128)(2,1)}), bf16[8,24,2048]{2,1,0:T(8,128)(2,1)S(1)}, u32[]{:S(2)}, u32[]{:S(2)}) async-start(bf16[8,24,2048]{2,1,0:T(8,128)(2,1)} %broadcast_in_dim.83), calls=%async_computation.6 | async-start | bytes 1572864 | tf_op jit(solution)/shard_map/all_to_all | solution.py:39
  153.2 11.5 %all-to-all-done.6 = bf16[8,24,2048]{2,1,0:T(8,128)(2,1)S(1)} async-done(((bf16[8,24,2048]{2,1,0:T(8,128)(2,1)}), bf16[8,24,2048]{2,1,0:T(8,128)(2,1)S(1)}, u32[]{:S(2)}, u32[]{:S(2)}) %all-to-all-start.6) | async-done | bytes 786464 | tf_op jit(solution)/shard_map/all_to_all | solution.py:39
  171.6 4.4 %all-to-all-start.7 = ((bf16[32,12,128]{2,1,0:T(8,128)(2,1)}), bf16[32,12,128]{2,1,0:T(8,128)(2,1)S(1)}, u32[]{:S(2)}, u32[]{:S(2)}) async-start(bf16[32,12,128]{2,1,0:T(8,128)(2,1)} %copy.189), calls=%async_computation.7 | async-start | bytes 262144 | tf_op jit(solution)/shard_map/all_to_all | solution.py:39
  176.0 7.7 %all-to-all-done.7 = bf16[32,12,128]{2,1,0:T(8,128)(2,1)S(1)} async-done(((bf16[32,12,128]{2,1,0:T(8,128)(2,1)}), bf16[32,12,128]{2,1,0:T(8,128)(2,1)S(1)}, u32[]{:S(2)}, u32[]{:S(2)}) %all-to-all-start.7) | async-done | bytes 98336 | tf_op jit(solution)/shard_map/all_to_all | solution.py:39
  183.9 18.5 %all_to_all.66 = bf16[16,12,128]{2,1,0:T(8,128)(2,1)S(1)} all-to-all(bf16[16,12,128]{2,1,0:T(8,128)(2,1)S(1)} %broadcast_in_dim.84), channel_id=1, replica_groups=mesh['z'=16,'y'=4,'x'=4,'c'=2] {'z'}, dimensions={0} | all-to-all | bytes 98304 | tf_op jit(solution)/shard_map/all_to_all | solution.py:39
  202.4 7.5 %all_to_all.67 = bf16[4,192,128]{2,1,0:T(8,128)(2,1)S(1)} all-to-all(bf16[4,192,128]{2,1,0:T(8,128)(2,1)S(1)} %broadcast_in_dim.86), channel_id=1, replica_groups=mesh['z'=16,'y'=4,'x'=4,'c'=2] {'y'}, dimensions={0} | all-to-all | bytes 393216 | tf_op jit(solution)/shard_map/all_to_all | solution.py:39
  211.0 3.5 %all-to-all-start.10 = ((bf16[4,4,192,128]{3,2,1,0:T(8,128)(2,1)}), bf16[4,4,192,128]{3,2,1,0:T(8,128)(2,1)S(1)}, u32[]{:S(2)}, u32[]{:S(2)}) async-start(bf16[4,4,192,128]{3,2,1,0:T(8,128)(2,1)} %broadcast_in_dim.87), calls=%async_computation.10 | async-start | bytes 1572864 | tf_op jit(solution)/shard_map/all_to_all | solution.py:39
  215.1 8.1 %all-to-all-done.10.refs_2_ = bf16[4,4,192,128]{3,2,1,0:T(8,128)(2,1)S(1)} async-done(((bf16[4,4,192,128]{3,2,1,0:T(8,128)(2,1)}), bf16[4,4,192,128]{3,2,1,0:T(8,128)(2,1)S(1)}, u32[]{:S(2)}, u32[]{:S(2)}) %all-to-all-start.10) | async-done | bytes 786464 | tf_op jit(solution)/shard_map/all_to_all | solution.py:39
  223.2 6.6 %collective-permute-start = (bf16[4,4,192,128]{3,2,1,0:T(8,128)(2,1)S(1)}, bf16[4,4,192,128]{3,2,1,0:T(8,128)(2,1)S(1)}, u32[]{:S(2)}, u32[]{:S(2)}) collective-permute-start(bf16[4,4,192,128]{3,2,1,0:T(8,128)(2,1)S(1)} %all-to-all-done.10.refs_2_), channel_id=1, source_target_pairs={{0,1},{1,0},{2,3},{3,2},{4,5},{5,4},{6,7},{7,6},{8,9},{9,8},{10,11... | collective-permute-start | bytes 2359304 | tf_op jit(solution)/shard_map/ppermute | solution.py:285
  230.0 1.7 fusion.4
  231.7 1.6 fusion.5
  233.3 2.8 %head_own.1 = (f32[192,256]{1,0:T(8,128)}, f32[1,256]{1,0:T(1,128)}) custom-call(s32[1]{0:T(128)} %bitcast.refs_0_, f32[8]{0:T(128)} %refs_1_.3, bf16[4,4,192,128]{3,2,1,0:T(8,128)(2,1)} %copy-done, f32[16,128]{1,0:T(8,128)} %get-tuple-element.52.refs_3_, bf16[2048,256]{1,0:T(8,128)(2,1)} %refs_4_.3), custom_call_target="tpu_custom_call" | custom-call | flops 201326592 | bytes 1835008 | tf_op jit(solution)/shard_map/head_own/pallas_call | solution.py:119
  237.0 2.7 head_flip.1
  241.1 3.6 %all-to-all-start.11 = ((f32[32,1,512]{2,1,0:T(1,128)}), f32[32,1,512]{2,1,0:T(1,128)S(1)}, u32[]{:S(2)}, u32[]{:S(2)}) async-start(f32[32,1,512]{2,1,0:T(1,128)} %broadcast_in_dim.89), calls=%async_computation.11 | async-start | bytes 131072 | tf_op jit(solution)/shard_map/all_to_all | solution.py:39
  246.4 5.7 %all-to-all-done.11 = f32[32,1,512]{2,1,0:T(1,128)S(1)} async-done(((f32[32,1,512]{2,1,0:T(1,128)}), f32[32,1,512]{2,1,0:T(1,128)S(1)}, u32[]{:S(2)}, u32[]{:S(2)}) %all-to-all-start.11) | async-done | bytes 65568 | tf_op jit(solution)/shard_map/all_to_all | solution.py:39
  252.8 4.0 %all-to-all-start.12 = ((f32[16,1,512]{2,1,0:T(1,128)}), f32[16,1,512]{2,1,0:T(1,128)S(1)}, u32[]{:S(2)}, u32[]{:S(2)}) async-start(f32[16,1,512]{2,1,0:T(1,128)} %broadcast_in_dim.90), calls=%async_computation.12 | async-start | bytes 65536 | tf_op jit(solution)/shard_map/all_to_all | solution.py:39
  257.8 10.4 %all-to-all-done.12 = f32[16,1,512]{2,1,0:T(1,128)S(1)} async-done(((f32[16,1,512]{2,1,0:T(1,128)}), f32[16,1,512]{2,1,0:T(1,128)S(1)}, u32[]{:S(2)}, u32[]{:S(2)}) %all-to-all-start.12) | async-done | bytes 32800 | tf_op jit(solution)/shard_map/all_to_all | solution.py:39
  (178 shorter events, 31.3 us)
Async XLA Ops:
  7.2 32.6 %copy-start.4 = (s32[8]{0:T(128)S(1)}, s32[8]{0:T(128)}, u32[]{:S(2)}) copy-start(s32[8]{0:T(128)} %param.39) | copy-start | bytes 100
  7.2 45.5 %copy-start.5 = (f32[128]{0:T(128)S(1)}, f32[128]{0:T(128)}, u32[]{:S(2)}) copy-start(f32[128]{0:T(128)} %param.27) | copy-start | bytes 1540
  7.2 45.8 %copy-start.6 = (f32[128]{0:T(128)S(1)}, f32[128]{0:T(128)}, u32[]{:S(2)}) copy-start(f32[128]{0:T(128)} %param.28) | copy-start | bytes 1540
  11.0 11.6 %all-to-all-start = ((bf16[4,32,1792]{2,1,0:T(8,128)(2,1)}), bf16[4,32,1792]{2,1,0:T(8,128)(2,1)S(1)}, u32[]{:S(2)}, u32[]{:S(2)}) async-start(bf16[4,32,1792]{2,1,0:T(8,128)(2,1)} %pack.1), calls=%async_computation | async-start | bytes 917504 | tf_op jit(solution)/shard_map/all_to_all | solution.py:39
  23.8 28.5 %all-to-all-start.1 = ((bf16[16,6,896]{2,1,0:T(8,128)(2,1)}), bf16[16,6,896]{2,1,0:T(8,128)(2,1)S(1)}, u32[]{:S(2)}, u32[]{:S(2)}) async-start(bf16[16,6,896]{2,1,0:T(8,128)(2,1)} %reshape.716), calls=%async_computation.1 | async-start | bytes 458752 | tf_op jit(solution)/shard_map/all_to_all | solution.py:39
  39.7 86.8 %all-gather.2.cloned.1.call-start = ((), (), s32[]{:S(2)}) async-start(), calls=%async_computation.13 | async-start | bytes 3899392 | tf_op jit(solution)/shard_map/all_gather | solution.py:178
  54.2 21.2 %all-to-all-start.2 = ((bf16[16,32,128]{2,1,0:T(8,128)(2,1)}), bf16[16,32,128]{2,1,0:T(8,128)(2,1)S(1)}, u32[]{:S(2)}, u32[]{:S(2)}) async-start(bf16[16,32,128]{2,1,0:T(8,128)(2,1)} %broadcast_in_dim.74), calls=%async_computation.2 | async-start | bytes 262144 | tf_op jit(solution)/shard_map/all_to_all | solution.py:39
  76.2 9.7 %all-to-all-start.3 = ((bf16[4,384,128]{2,1,0:T(8,128)(2,1)}), bf16[4,384,128]{2,1,0:T(8,128)(2,1)S(1)}, u32[]{:S(2)}, u32[]{:S(2)}) async-start(bf16[4,384,128]{2,1,0:T(8,128)(2,1)} %broadcast_in_dim.76), calls=%async_computation.3 | async-start | bytes 786432 | tf_op jit(solution)/shard_map/all_to_all | solution.py:39
  85.9 2.1 copy-start.2
  85.9 2.6 copy-start.3
  91.0 20.4 %all-to-all-start.4 = ((bf16[16,56,128]{2,1,0:T(8,128)(2,1)}), bf16[16,56,128]{2,1,0:T(8,128)(2,1)S(1)}, u32[]{:S(2)}, u32[]{:S(2)}) async-start(bf16[16,56,128]{2,1,0:T(8,128)(2,1)} %copy.177), calls=%async_computation.4 | async-start | bytes 458752 | tf_op jit(solution)/shard_map/all_to_all | solution.py:39
  138.9 25.7 %all-to-all-start.6 = ((bf16[8,24,2048]{2,1,0:T(8,128)(2,1)}), bf16[8,24,2048]{2,1,0:T(8,128)(2,1)S(1)}, u32[]{:S(2)}, u32[]{:S(2)}) async-start(bf16[8,24,2048]{2,1,0:T(8,128)(2,1)} %broadcast_in_dim.83), calls=%async_computation.6 | async-start | bytes 1572864 | tf_op jit(solution)/shard_map/all_to_all | solution.py:39
  166.5 48.0 %copy-start.7 = (s32[8]{0:T(128)S(1)}, s32[8]{0:T(128)}, u32[]{:S(2)}) copy-start(s32[8]{0:T(128)} %param.41) | copy-start | bytes 100
  171.6 12.1 %all-to-all-start.7 = ((bf16[32,12,128]{2,1,0:T(8,128)(2,1)}), bf16[32,12,128]{2,1,0:T(8,128)(2,1)S(1)}, u32[]{:S(2)}, u32[]{:S(2)}) async-start(bf16[32,12,128]{2,1,0:T(8,128)(2,1)} %copy.189), calls=%async_computation.7 | async-start | bytes 262144 | tf_op jit(solution)/shard_map/all_to_all | solution.py:39
  211.0 12.2 %all-to-all-start.10 = ((bf16[4,4,192,128]{3,2,1,0:T(8,128)(2,1)}), bf16[4,4,192,128]{3,2,1,0:T(8,128)(2,1)S(1)}, u32[]{:S(2)}, u32[]{:S(2)}) async-start(bf16[4,4,192,128]{3,2,1,0:T(8,128)(2,1)} %broadcast_in_dim.87), calls=%async_computation.10 | async-start | bytes 1572864 | tf_op jit(solution)/shard_map/all_to_all | solution.py:39
  223.2 10.1 %copy-start = (bf16[4,4,192,128]{3,2,1,0:T(8,128)(2,1)}, bf16[4,4,192,128]{3,2,1,0:T(8,128)(2,1)S(1)}, u32[]{:S(2)}) copy-start(bf16[4,4,192,128]{3,2,1,0:T(8,128)(2,1)S(1)} %all-to-all-done.10.refs_2_) | copy-start | bytes 2359300
  223.2 12.9 %collective-permute-start = (bf16[4,4,192,128]{3,2,1,0:T(8,128)(2,1)S(1)}, bf16[4,4,192,128]{3,2,1,0:T(8,128)(2,1)S(1)}, u32[]{:S(2)}, u32[]{:S(2)}) collective-permute-start(bf16[4,4,192,128]{3,2,1,0:T(8,128)(2,1)S(1)} %all-to-all-done.10.refs_2_), channel_id=1, source_target_pairs={{0,1},{1,0},{2,3},{3,2},{4,5},{5,4},{6,7},{7,6},{8,9},{9,8},{10,11... | collective-permute-start | bytes 2359304 | tf_op jit(solution)/shard_map/ppermute | solution.py:285
  236.1 0.9 copy-start.1
  241.1 10.9 %all-to-all-start.11 = ((f32[32,1,512]{2,1,0:T(1,128)}), f32[32,1,512]{2,1,0:T(1,128)S(1)}, u32[]{:S(2)}, u32[]{:S(2)}) async-start(f32[32,1,512]{2,1,0:T(1,128)} %broadcast_in_dim.89), calls=%async_computation.11 | async-start | bytes 131072 | tf_op jit(solution)/shard_map/all_to_all | solution.py:39
  252.8 15.4 %all-to-all-start.12 = ((f32[16,1,512]{2,1,0:T(1,128)}), f32[16,1,512]{2,1,0:T(1,128)S(1)}, u32[]{:S(2)}, u32[]{:S(2)}) async-start(f32[16,1,512]{2,1,0:T(1,128)} %broadcast_in_dim.90), calls=%async_computation.12 | async-start | bytes 65536 | tf_op jit(solution)/shard_map/all_to_all | solution.py:39
Sparse Core Ops, SparseCore 0:
  43.2 83.2 all-gather.1

commit v3 on v2

--- a/solution.py
+++ b/solution.py
@@ -48,55 +48,53 @@
     return high.astype(BF), (values - high).astype(BF)
 
 
-def pack_kernel(hidden_ref, place_ref, gain_ref, gate_ref, up_ref, down_ref, wo_ref, wq_ref, wk_ref, wv_ref, wg_ref, out_ref):
-    lanes = lax.broadcasted_iota(jnp.int32, (512, 384), 0)
-    chosen = jnp.where(lanes == place_ref[0:1, :], 1.0, 0.0).astype(BF)
-    moved = lax.dot_general(
-        hidden_ref[...], chosen, (((1,), (1,)), ((), ())), preferred_element_type=F32
+def pack_kernel(hidden_ref, ln1_ref, ln2_ref, last_ref, wq_ref, wk_ref, wv_ref, wg_ref, out_ref):
+    lane = lax.broadcasted_iota(jnp.int32, (1, 512), 1)
+    first = lane // 128
+    local = lane - first * 128
+    first_z = local // 6
+    token = first // 2 * 192 + first_z * 12 + first % 2 * 6 + (local - first_z * 6)
+    token = jnp.where(local < 96, token, -1)
+    chosen = lax.broadcasted_iota(jnp.int32, (384, 512), 0) == token
+    moved = jnp.dot(
+        hidden_ref[...], jnp.where(chosen, 1.0, 0.0).astype(BF), preferred_element_type=F32
     )
     diagonal = lax.broadcasted_iota(jnp.int32, (32, 32), 0) == lax.broadcasted_iota(jnp.int32, (32, 32), 1)
     lane = lax.broadcasted_iota(jnp.int32, (32, 128), 1)
     extra = jnp.zeros((32, 128), F32)
-    for which in range(3):
-        rest = jnp.sum(jnp.where(diagonal, gain_ref[which : which + 1, :], 0.0), axis=1, keepdims=True)
+    for which, gain_ref in enumerate((ln1_ref, ln2_ref, last_ref)):
+        rest = jnp.sum(jnp.where(diagonal, gain_ref[...], 0.0), axis=1, keepdims=True)
         for digit in range(3):
             part = rest.astype(BF).astype(F32)
             extra = jnp.where(lane == 96 + which * 3 + digit, part, extra)
             rest = rest - part
-    zeros = jnp.zeros((32, 64), BF)
     for y in range(4):
-        tile = slice(y * 128, y * 128 + 128)
-        start = 512 + y * 64
-        side = slice(start, start + 64)
-        out_ref[y, :, 0:128] = gate_ref[:, tile]
-        out_ref[y, :, 128:256] = up_ref[:, tile]
-        out_ref[y, :, 256:384] = down_ref[:, tile]
-        out_ref[y, :, 384:640] = wo_ref[...]
-        out_ref[y, :, 640:768] = jnp.concatenate([gate_ref[:, side], up_ref[:, side]], axis=1)
-        out_ref[y, :, 768:896] = jnp.concatenate([down_ref[:, side], zeros], axis=1)
-        out_ref[y, :, 896:1152] = wq_ref[...]
-        out_ref[y, :, 1152:1280] = wk_ref[...]
-        out_ref[y, :, 1280:1408] = wv_ref[...]
-        out_ref[y, :, 1408:1664] = wg_ref[...]
-        out_ref[y, :, 1664:1792] = (moved[:, tile] + extra).astype(BF)
+        out_ref[y, :, 0:256] = wq_ref[...]
+        out_ref[y, :, 256:384] = wk_ref[...]
+        out_ref[y, :, 384:512] = wv_ref[...]
+        out_ref[y, :, 512:768] = wg_ref[...]
+        out_ref[y, :, 768:896] = (moved[:, y * 128 : y * 128 + 128] + extra).astype(BF)
 
 
 def head_kernel(core_ref, temp_ref, tiles_ref, gain_ref, weight_ref, logits_ref, spot_ref, *, flip, width):
     rows = tiles_ref.shape[2]
     squares = jnp.zeros((rows, 128), F32)
     for column in range(16):
-        tile = tiles_ref[column % 4, column // 4].astype(F32)
+        tile = tiles_ref[column // 4, column % 4].astype(F32)
         squares = squares + tile * tile
     scale = lax.rsqrt(jnp.sum(squares, axis=1, keepdims=True) / width + EPSILON)
     total = jnp.zeros((rows, 256), F32)
     for pair in range(8):
-        sides = []
+        sides, rights = [], []
         for column in (2 * pair, 2 * pair + 1):
-            tile = tiles_ref[column % 4, column // 4].astype(F32)
+            for quarter in range(4):
+                start = (column // 4 * 4 + quarter) * 128 + column % 4 * 32
+                rights.append(weight_ref[start : start + 32, :])
+            tile = tiles_ref[column // 4, column % 4].astype(F32)
             sides.append((tile * scale * gain_ref[column : column + 1, :]).astype(BF))
         total = total + jnp.dot(
             jnp.concatenate(sides, axis=1),
-            weight_ref[pair * 256 : pair * 256 + 256, :],
+            jnp.concatenate(rights, axis=0),
             preferred_element_type=F32,
         )
     part = core_ref[0] if not flip else 1 - core_ref[0]
@@ -164,20 +162,18 @@
     token_y = token // 192 * 2 + token % 12 // 6
     token_i = token % 6
 
-    place = (token_y * 128 + token_z * 6 + token_i).reshape(1, 384)
-    gains = jnp.stack([ln1_gain, ln2_gain, last_gain])
+    ffn = jnp.concatenate([w_gate, w_up, w_down.T, wo.T], axis=1)
+    ffn = lax.all_gather(ffn, "z", axis=0, tiled=True)
     vmem = pl.BlockSpec(memory_space=pltpu.VMEM)
     pieces = pl.pallas_call(
         pack_kernel,
-        out_shape=jax.ShapeDtypeStruct((4, 32, 1792), BF),
-        in_specs=[vmem] * 11,
+        out_shape=jax.ShapeDtypeStruct((4, 32, 896), BF),
+        in_specs=[vmem] * 8,
         out_specs=vmem,
         name="pack",
-    )(hidden.T, place, gains, w_gate, w_up, w_down.T, wo.T, wq, wk, wv, wg)
-    mine = swap(pieces, "y").reshape(128, 1792)
-    ffn = lax.all_gather(mine[:, :896], "z", axis=0, tiled=True)
-    proj = mine[:, 896:1664]
-    side = mine[:, 1664:]
+    )(hidden.T, *(gain.reshape(1, 32) for gain in (ln1_gain, ln2_gain, last_gain)), wq, wk, wv, wg)
+    mine = swap(pieces, "y").reshape(128, 896)
+    proj, side = mine[:, :768], mine[:, 768:]
     side_wide = side.astype(F32)
     ln1_row = side_wide[:, 96:97] + side_wide[:, 97:98] + side_wide[:, 98:99]
     scaled = (side_wide * ln1_row).astype(BF)
@@ -210,8 +206,10 @@
     ).astype(BF)
     gathered = spread(block, "z", 16)
     gain_all = gathered[:, 24:30].astype(F32)
-    ln2_all = gain_all[:, 0] + gain_all[:, 1] + gain_all[:, 2]
+    ln2_mine = gain_all[:, 0] + gain_all[:, 1] + gain_all[:, 2]
+    ln2_mine = lax.dynamic_slice(ln2_mine, (0, y * 32), (16, 32)).reshape(1, 512)
     last_all = gain_all[:, 3] + gain_all[:, 4] + gain_all[:, 5]
+    last_all = jnp.swapaxes(last_all.reshape(4, 4, 4, 32), 1, 2).reshape(16, 128)
     pool = spread(gathered[:, :24].reshape(384, 128), "y", 4).reshape(1536, 128)
     origin = token_y * 384 + token_z * 24 + token_i
     origin = (jnp.arange(4, dtype=jnp.int32)[:, None] * 6 + origin[None, :]).reshape(1536)
@@ -243,41 +241,44 @@
         return split.reshape((16, 2, 24) + rest)
 
     outgoing = pack_state(by_z(peak), by_z(mass), by_z(weighted))
+    outgoing, ffn = lax.optimization_barrier((outgoing, ffn))
     state = merge_state(swap(outgoing, "z"))
-    packed = pack_state(*(part[None] for part in state))[0]
-    shared = jnp.concatenate([packed, rows.reshape(96, 128), outgate[:, :128], outgate[:, 128:]], axis=0)
-    shared, ffn = lax.optimization_barrier((shared, ffn))
-    both = spread(shared, "y", 4)
+    packed = pack_state(*(part[None] for part in state))
+    residual = jnp.transpose(rows.reshape(4, 4, 6, 4, 32), (3, 0, 2, 1, 4)).reshape(4, 24, 128)
+    outgates = jnp.concatenate([outgate[:, :128], outgate[:, 128:]], axis=0)
+    shared = jnp.concatenate(
+        [jnp.broadcast_to(packed, (4, 56, 128)), residual, jnp.broadcast_to(outgates[None], (4, 12, 128))],
+        axis=1,
+    )
+    both = swap(shared, "y")
     peak, mass, weighted = merge_state(both[:, :56])
-    my_gate = jnp.swapaxes(both[:, 152:].reshape(4, 2, 6, 128), 0, 1).reshape(2, 24, 128).astype(F32)
+    my_gate = jnp.swapaxes(both[:, 80:].reshape(4, 2, 6, 128), 0, 1).reshape(2, 24, 128).astype(F32)
     gated = (weighted / mass[..., None] * my_gate).astype(BF)
-    hidden_rows = jnp.swapaxes(both[:, 56:152].reshape(4, 16, 6, 128), 0, 1).reshape(16, 24, 128)
-
+    hidden_rows = jnp.swapaxes(both[:, 56:80].reshape(4, 4, 6, 128), 1, 2).reshape(24, 512)
+
+    contract = (((1,), (1,)), ((), ()))
     attn = lax.dot_general(
         jnp.concatenate([gated[0], gated[1]], axis=1),
-        ffn[:, 384:640],
-        (((1,), (1,)), ((), ())),
+        ffn[:, 2304:],
+        contract,
         preferred_element_type=F32,
     )
     attn = jnp.sum(spread(attn.astype(BF), ("x", "c"), 8).astype(F32), axis=0)
-    hidden_rows = jnp.swapaxes(hidden_rows, 0, 1).reshape(24, width)
     middle = (hidden_rows.astype(F32) + attn).astype(BF)
     middle_wide = middle.astype(F32)
-    squares_mid = jnp.sum(middle_wide * middle_wide, axis=1)
-    normed2 = (
-        middle_wide * lax.rsqrt(squares_mid / width + EPSILON)[:, None] * ln2_all.reshape(1, width)
+    squares_mid = split2(jnp.sum(middle_wide * middle_wide, axis=1, keepdims=True))
+    units = jnp.dot(
+        (middle_wide * ln2_mine).astype(BF), ffn[:, :1536], preferred_element_type=F32
     ).astype(BF)
-    units = jnp.dot(normed2, ffn[:, :256], preferred_element_type=F32)
-    sides = jnp.dot(normed2, ffn[:, 640:768], preferred_element_type=F32)
-    act = (jax.nn.silu(units[:, :128]) * units[:, 128:]).astype(BF)
-    act_side = (jax.nn.silu(sides[:, :64]) * sides[:, 64:]).astype(BF)
-    contract = (((1,), (1,)), ((), ()))
-    down = lax.dot_general(act, ffn[:, 256:384], contract, preferred_element_type=F32) + lax.dot_general(
-        act_side, ffn[:, 768:832], contract, preferred_element_type=F32
-    )
-    down = jnp.transpose(down.astype(BF).reshape(2, 12, 16, 128), (2, 0, 1, 3)).reshape(32, 12, 128)
-    down = jnp.sum(swap(down, ("y", "x", "c")).astype(F32), axis=0)
-    middle_mine = lax.dynamic_slice(middle, (c * 12, (y * 4 + x) * 128), (12, 128))
+    squares_mid = jnp.pad(jnp.concatenate(squares_mid, axis=1), ((0, 0), (0, 126)))
+    units = spread(jnp.concatenate([units, squares_mid], axis=1), "y", 4)
+    units = jnp.sum(units.astype(F32), axis=0)
+    scale_mid = lax.rsqrt((units[:, 1536:1537] + units[:, 1537:1538]) / width + EPSILON)
+    act = (jax.nn.silu(units[:, :768] * scale_mid) * (units[:, 768:1536] * scale_mid)).astype(BF)
+    down = lax.dot_general(act, ffn[:, 1536:2304], contract, preferred_element_type=F32)
+    down = jnp.transpose(down.astype(BF).reshape(2, 12, 4, 128), (2, 0, 1, 3)).reshape(8, 12, 128)
+    down = jnp.sum(swap(down, ("x", "c")).astype(F32), axis=0)
+    middle_mine = lax.dynamic_slice(middle, (c * 12, x * 128), (12, 128))
     following = (middle_mine.astype(F32) + down).astype(BF)
 
     half = spread(following, "z", 16).reshape(192, 128)
@@ -293,10 +294,10 @@
         )
 
     def own_columns(tiles):
-        return lax.dynamic_slice(tiles, (z % 4, z // 4, 0, 0), (1, 1, 192, 128)).reshape(192, 128)
+        return lax.dynamic_slice(tiles, (z // 4, y, 0, 0), (1, 1, 192, 128)).reshape(192, 128)
 
     own = in_order(own_columns(half), own_columns(other))
-    next_hidden = lax.dynamic_slice(own, (0, y * 32), (384, 32))
+    next_hidden = lax.dynamic_slice(own, (0, z % 4 * 32), (384, 32))
     spot = in_order(own_spot, other_spot).reshape(1, 512)
     for axis, count in ((("y", "x", "c"), 32), ("z", 16)):
         spots = spread(spot, axis, count)

time: 278 us -> 264 us (0.950)
  waiting for transfers between devices: 106 us -> 91.4 us
  starting transfers between devices: 74.3 us -> 83.2 us
  matrix products: 15.9 us -> 10.2 us
    all_to_all x10 -> x11, waiting for transfers between devices: 91.8 us -> 81.6 us  [swap(): return lax.all_to_all(values, axis, 0, 0, tiled=True)]
    all_to_all x10 -> x11, starting transfers between devices: 67.7 us -> 76.5 us  [swap(): return lax.all_to_all(values, axis, 0, 0, tiled=True)]
    dot_general x5 -> x3, matrix products: 7.17 us -> 0.82 us  [the longest x1 0.34 us: on_device(): lax.dot_general(act, ffn[:, 1536:2304], contract, preferred_element_type=...]
    all_gather x1, waiting for transfers between devices: 14.5 us -> 9.81 us  [on_device(): ffn = lax.all_gather(ffn, 'z', axis=0, tiled=True)]
  transfers between devices with their start and end apart: 12 -> 13, of which waited for: 11 -> 12; matrix products, arithmetic and copies ran while one was open for 7% -> 9% of each run, Pallas kernels for 1% -> 1%
where the time goes in v3:
time: 264 us; the launch traced here: 262 us
  waiting for transfers between devices  91.4 us (35%)
  starting transfers between devices  83.2 us (32%)
  blocking collectives  32.7 us (12%)
  between operations  14.9 us (6%)
  local copies, waits for them, and re-layouts  13.2 us (5%)
  matrix products  10.2 us (4%)
  other arithmetic  9.52 us (4%)
  Pallas kernels  7.26 us (3%)
    all_to_all x11, waiting for transfers between devices, swap(): return lax.all_to_all(values, axis, 0, 0, tiled=True)  81.6 us
    all_to_all x11, starting transfers between devices, swap(): return lax.all_to_all(values, axis, 0, 0, tiled=True)  76.5 us
    all_to_all x3, blocking collectives, swap(): return lax.all_to_all(values, axis, 0, 0, tiled=True)  32.7 us
    all_gather x1, waiting for transfers between devices, on_device(): ffn = lax.all_gather(ffn, 'z', axis=0, tiled=True)  9.81 us
    ppermute x1, starting transfers between devices, on_device(): other = lax.ppermute(half, 'c', [(0, 1), (1, 0)])  6.63 us
    pallas_call x2, Pallas kernels, head(): pl.pallas_call(lambda *refs: head_kernel(*refs, flip=flip, width=2048), o...  5.52 us
  transfers between devices with their start and end apart: 13, of which 12 were waited for; matrix products, arithmetic and copies ran while one was open for 9% of the time, Pallas kernels for 1%

profile of v3, /device:TPU:1, one launch (start us, length us, event | category | flops | bytes accessed | tf_op | source)
XLA Modules:
  0.0 262.3 jit_solution(17823731226502149483)
XLA Ops:
  7.2 1.7 pack.1
  8.9 5.0 %all-to-all-start = ((bf16[4,32,896]{2,1,0:T(8,128)(2,1)}), bf16[4,32,896]{2,1,0:T(8,128)(2,1)S(1)}, u32[]{:S(2)}, u32[]{:S(2)}) async-start(bf16[4,32,896]{2,1,0:T(8,128)(2,1)} %pack.1), calls=%async_computation | async-start | bytes 458752 | tf_op jit(solution)/shard_map/all_to_all | solution.py:39
  20.5 14.9 %all-to-all-start.1 = ((bf16[16,6,896]{2,1,0:T(8,128)(2,1)}), bf16[16,6,896]{2,1,0:T(8,128)(2,1)S(1)}, u32[]{:S(2)}, u32[]{:S(2)}) async-start(bf16[16,6,896]{2,1,0:T(8,128)(2,1)} %reshape.648), calls=%async_computation.1 | async-start | bytes 458752 | tf_op jit(solution)/shard_map/all_to_all | solution.py:39
  35.9 12.1 %all-to-all-done.1 = bf16[16,6,896]{2,1,0:T(8,128)(2,1)S(1)} async-done(((bf16[16,6,896]{2,1,0:T(8,128)(2,1)}), bf16[16,6,896]{2,1,0:T(8,128)(2,1)S(1)}, u32[]{:S(2)}, u32[]{:S(2)}) %all-to-all-start.1) | async-done | bytes 172064 | tf_op jit(solution)/shard_map/all_to_all | solution.py:39
  50.0 9.3 %all-to-all-start.2 = ((bf16[16,32,128]{2,1,0:T(8,128)(2,1)}), bf16[16,32,128]{2,1,0:T(8,128)(2,1)S(1)}, u32[]{:S(2)}, u32[]{:S(2)}) async-start(bf16[16,32,128]{2,1,0:T(8,128)(2,1)} %broadcast_in_dim.80), calls=%async_computation.2 | async-start | bytes 262144 | tf_op jit(solution)/shard_map/all_to_all | solution.py:39
  59.6 12.2 %all-to-all-done.2 = bf16[16,32,128]{2,1,0:T(8,128)(2,1)S(1)} async-done(((bf16[16,32,128]{2,1,0:T(8,128)(2,1)}), bf16[16,32,128]{2,1,0:T(8,128)(2,1)S(1)}, u32[]{:S(2)}, u32[]{:S(2)}) %all-to-all-start.2) | async-done | bytes 131104 | tf_op jit(solution)/shard_map/all_to_all | solution.py:39
  72.5 5.2 %all-to-all-start.3 = ((bf16[4,384,128]{2,1,0:T(8,128)(2,1)}), bf16[4,384,128]{2,1,0:T(8,128)(2,1)S(1)}, u32[]{:S(2)}, u32[]{:S(2)}) async-start(bf16[4,384,128]{2,1,0:T(8,128)(2,1)} %broadcast_in_dim.82), calls=%async_computation.3 | async-start | bytes 786432 | tf_op jit(solution)/shard_map/all_to_all | solution.py:39
  77.8 6.2 %all-to-all-done.3 = bf16[4,384,128]{2,1,0:T(8,128)(2,1)S(1)} async-done(((bf16[4,384,128]{2,1,0:T(8,128)(2,1)}), bf16[4,384,128]{2,1,0:T(8,128)(2,1)S(1)}, u32[]{:S(2)}, u32[]{:S(2)}) %all-to-all-start.3) | async-done | bytes 393248 | tf_op jit(solution)/shard_map/all_to_all | solution.py:39
  83.9 1.7 fusion.2
  88.3 9.8 %all-gather.2.cloned.1.call-done = bf16[512,2560]{1,0:T(8,128)(2,1)} async-done(((bf16[32,2560]{1,0:T(8,128)(2,1)}), bf16[512,2560]{1,0:T(8,128)(2,1)}) %all-gather.2.cloned.1.call-update) | async-done | bytes 2621456 | tf_op jit(solution)/shard_map/all_gather | solution.py:166
  98.8 7.4 %all-to-all-start.4 = ((bf16[16,56,128]{2,1,0:T(8,128)(2,1)}), bf16[16,56,128]{2,1,0:T(8,128)(2,1)S(1)}, u32[]{:S(2)}, u32[]{:S(2)}) async-start(bf16[16,56,128]{2,1,0:T(8,128)(2,1)} %copy.278), calls=%async_computation.4 | async-start | bytes 458752 | tf_op jit(solution)/shard_map/all_to_all | solution.py:39
  106.6 12.3 %all-to-all-done.4 = bf16[16,56,128]{2,1,0:T(8,128)(2,1)S(1)} async-done(((bf16[16,56,128]{2,1,0:T(8,128)(2,1)}), bf16[16,56,128]{2,1,0:T(8,128)(2,1)S(1)}, u32[]{:S(2)}, u32[]{:S(2)}) %all-to-all-start.4) | async-done | bytes 229408 | tf_op jit(solution)/shard_map/all_to_all | solution.py:39
  120.1 4.1 %all-to-all-start.5 = ((bf16[4,92,128]{2,1,0:T(8,128)(2,1)}), bf16[4,92,128]{2,1,0:T(8,128)(2,1)S(1)}, u32[]{:S(2)}, u32[]{:S(2)}) async-start(bf16[4,92,128]{2,1,0:T(8,128)(2,1)} %pad_maximum_fusion.2), calls=%async_computation.5 | async-start | bytes 196608 | tf_op jit(solution)/shard_map/all_to_all | solution.py:39
  124.4 4.4 %all-to-all-done.5 = bf16[4,92,128]{2,1,0:T(8,128)(2,1)S(1)} async-done(((bf16[4,92,128]{2,1,0:T(8,128)(2,1)}), bf16[4,92,128]{2,1,0:T(8,128)(2,1)S(1)}, u32[]{:S(2)}, u32[]{:S(2)}) %all-to-all-start.5) | async-done | bytes 94240 | tf_op jit(solution)/shard_map/all_to_all | solution.py:39
  130.2 14.6 %all-to-all-start.6 = ((bf16[8,24,512]{2,1,0:T(8,128)(2,1)}), bf16[8,24,512]{2,1,0:T(8,128)(2,1)S(1)}, u32[]{:S(2)}, u32[]{:S(2)}) async-start(bf16[8,24,512]{2,1,0:T(8,128)(2,1)} %broadcast_in_dim.91), calls=%async_computation.6 | async-start | bytes 393216 | tf_op jit(solution)/shard_map/all_to_all | solution.py:39
  144.9 5.8 %all-to-all-done.6 = bf16[8,24,512]{2,1,0:T(8,128)(2,1)S(1)} async-done(((bf16[8,24,512]{2,1,0:T(8,128)(2,1)}), bf16[8,24,512]{2,1,0:T(8,128)(2,1)S(1)}, u32[]{:S(2)}, u32[]{:S(2)}) %all-to-all-start.6) | async-done | bytes 196640 | tf_op jit(solution)/shard_map/all_to_all | solution.py:39
  151.6 8.4 %all_to_all.70 = bf16[4,24,1664]{2,1,0:T(8,128)(2,1)S(1)} all-to-all(bf16[4,24,1664]{2,1,0:T(8,128)(2,1)S(1)} %broadcast_in_dim.92), channel_id=1, replica_groups=mesh['z'=16,'y'=4,'x'=4,'c'=2] {'y'}, dimensions={0} | all-to-all | bytes 638976 | tf_op jit(solution)/shard_map/all_to_all | solution.py:39
  161.3 5.4 %all-to-all-start.8 = ((bf16[8,12,128]{2,1,0:T(8,128)(2,1)}), bf16[8,12,128]{2,1,0:T(8,128)(2,1)S(1)}, u32[]{:S(2)}, u32[]{:S(2)}) async-start(bf16[8,12,128]{2,1,0:T(8,128)(2,1)} %copy.294), calls=%async_computation.8 | async-start | bytes 65536 | tf_op jit(solution)/shard_map/all_to_all | solution.py:39
  166.7 4.7 %all-to-all-done.8 = bf16[8,12,128]{2,1,0:T(8,128)(2,1)S(1)} async-done(((bf16[8,12,128]{2,1,0:T(8,128)(2,1)}), bf16[8,12,128]{2,1,0:T(8,128)(2,1)S(1)}, u32[]{:S(2)}, u32[]{:S(2)}) %all-to-all-start.8) | async-done | bytes 24608 | tf_op jit(solution)/shard_map/all_to_all | solution.py:39
  171.6 16.7 %all_to_all.71 = bf16[16,12,128]{2,1,0:T(8,128)(2,1)S(1)} all-to-all(bf16[16,12,128]{2,1,0:T(8,128)(2,1)S(1)} %broadcast_in_dim.93), channel_id=1, replica_groups=mesh['z'=16,'y'=4,'x'=4,'c'=2] {'z'}, dimensions={0} | all-to-all | bytes 98304 | tf_op jit(solution)/shard_map/all_to_all | solution.py:39
  188.3 7.5 %all_to_all.72 = bf16[4,192,128]{2,1,0:T(8,128)(2,1)S(1)} all-to-all(bf16[4,192,128]{2,1,0:T(8,128)(2,1)S(1)} %broadcast_in_dim.95), channel_id=1, replica_groups=mesh['z'=16,'y'=4,'x'=4,'c'=2] {'y'}, dimensions={0} | all-to-all | bytes 393216 | tf_op jit(solution)/shard_map/all_to_all | solution.py:39
  196.9 3.5 %all-to-all-start.11 = ((bf16[4,4,192,128]{3,2,1,0:T(8,128)(2,1)}), bf16[4,4,192,128]{3,2,1,0:T(8,128)(2,1)S(1)}, u32[]{:S(2)}, u32[]{:S(2)}) async-start(bf16[4,4,192,128]{3,2,1,0:T(8,128)(2,1)} %broadcast_in_dim.96), calls=%async_computation.11 | async-start | bytes 1572864 | tf_op jit(solution)/shard_map/all_to_all | solution.py:39
  201.9 7.1 %all-to-all-done.11.refs_2_ = bf16[4,4,192,128]{3,2,1,0:T(8,128)(2,1)S(1)} async-done(((bf16[4,4,192,128]{3,2,1,0:T(8,128)(2,1)}), bf16[4,4,192,128]{3,2,1,0:T(8,128)(2,1)S(1)}, u32[]{:S(2)}, u32[]{:S(2)}) %all-to-all-start.11) | async-done | bytes 786464 | tf_op jit(solution)/shard_map/all_to_all | solution.py:39
  209.1 6.6 %collective-permute-start = (bf16[4,4,192,128]{3,2,1,0:T(8,128)(2,1)S(1)}, bf16[4,4,192,128]{3,2,1,0:T(8,128)(2,1)S(1)}, u32[]{:S(2)}, u32[]{:S(2)}) collective-permute-start(bf16[4,4,192,128]{3,2,1,0:T(8,128)(2,1)S(1)} %all-to-all-done.11.refs_2_), channel_id=1, source_target_pairs={{0,1},{1,0},{2,3},{3,2},{4,5},{5,4},{6,7},{7,6},{8,9},{9,8},{10,11... | collective-permute-start | bytes 2359304 | tf_op jit(solution)/shard_map/ppermute | solution.py:286
  216.7 1.6 fusion.4
  218.4 1.6 fusion.5
  220.0 2.8 %head_own.1 = (f32[192,256]{1,0:T(8,128)}, f32[1,256]{1,0:T(1,128)}) custom-call(s32[1]{0:T(128)} %bitcast.refs_0_, f32[8]{0:T(128)} %refs_1_.3, bf16[4,4,192,128]{3,2,1,0:T(8,128)(2,1)} %copy-done, f32[16,128]{1,0:T(8,128)} %reshape.662.refs_3_, bf16[2048,256]{1,0:T(8,128)(2,1)} %refs_4_.3), custom_call_target="tpu_custom_call" | custom-call | flops 201326592 | bytes 1835008 | tf_op jit(solution)/shard_map/head_own/pallas_call | solution.py:117
  223.7 2.7 %head_flip.1 = (f32[192,256]{1,0:T(8,128)}, f32[1,256]{1,0:T(1,128)}) custom-call(s32[1]{0:T(128)} %bitcast.refs_0_, f32[8]{0:T(128)} %refs_1_.3, bf16[4,4,192,128]{3,2,1,0:T(8,128)(2,1)} %copy-done.2, f32[16,128]{1,0:T(8,128)} %reshape.662.refs_3_, bf16[2048,256]{1,0:T(8,128)(2,1)} %refs_4_.3), custom_call_target="tpu_custom_call" | custom-call | flops 201326592 | bytes 1835008 | tf_op jit(solution)/shard_map/head_flip/pallas_call | solution.py:117
  227.8 3.6 %all-to-all-start.12 = ((f32[32,1,512]{2,1,0:T(1,128)}), f32[32,1,512]{2,1,0:T(1,128)S(1)}, u32[]{:S(2)}, u32[]{:S(2)}) async-start(f32[32,1,512]{2,1,0:T(1,128)} %broadcast_in_dim.180), calls=%async_computation.12 | async-start | bytes 131072 | tf_op jit(solution)/shard_map/all_to_all | solution.py:39
  233.1 5.7 %all-to-all-done.12 = f32[32,1,512]{2,1,0:T(1,128)S(1)} async-done(((f32[32,1,512]{2,1,0:T(1,128)}), f32[32,1,512]{2,1,0:T(1,128)S(1)}, u32[]{:S(2)}, u32[]{:S(2)}) %all-to-all-start.12) | async-done | bytes 65568 | tf_op jit(solution)/shard_map/all_to_all | solution.py:39
  239.5 3.5 %all-to-all-start.13 = ((f32[16,1,512]{2,1,0:T(1,128)}), f32[16,1,512]{2,1,0:T(1,128)S(1)}, u32[]{:S(2)}, u32[]{:S(2)}) async-start(f32[16,1,512]{2,1,0:T(1,128)} %broadcast_in_dim.181), calls=%async_computation.13 | async-start | bytes 65536 | tf_op jit(solution)/shard_map/all_to_all | solution.py:39
  243.9 10.5 %all-to-all-done.13 = f32[16,1,512]{2,1,0:T(1,128)S(1)} async-done(((f32[16,1,512]{2,1,0:T(1,128)}), f32[16,1,512]{2,1,0:T(1,128)S(1)}, u32[]{:S(2)}, u32[]{:S(2)}) %all-to-all-start.13) | async-done | bytes 32800 | tf_op jit(solution)/shard_map/all_to_all | solution.py:39
  (207 shorter events, 28.7 us)
Async XLA Ops:
  7.2 28.2 %copy-start.10 = (s32[8]{0:T(128)S(1)}, s32[8]{0:T(128)}, u32[]{:S(2)}) copy-start(s32[8]{0:T(128)} %param.39) | copy-start | bytes 100
  7.2 41.2 %copy-start.11 = (f32[128]{0:T(128)S(1)}, f32[128]{0:T(128)}, u32[]{:S(2)}) copy-start(f32[128]{0:T(128)} %param.27) | copy-start | bytes 1540
  7.2 41.6 %copy-start.12 = (f32[128]{0:T(128)S(1)}, f32[128]{0:T(128)}, u32[]{:S(2)}) copy-start(f32[128]{0:T(128)} %param.28) | copy-start | bytes 1540
  8.9 10.4 %all-to-all-start = ((bf16[4,32,896]{2,1,0:T(8,128)(2,1)}), bf16[4,32,896]{2,1,0:T(8,128)(2,1)S(1)}, u32[]{:S(2)}, u32[]{:S(2)}) async-start(bf16[4,32,896]{2,1,0:T(8,128)(2,1)} %pack.1), calls=%async_computation | async-start | bytes 458752 | tf_op jit(solution)/shard_map/all_to_all | solution.py:39
  14.0 84.1 %all-gather.2.cloned.1.call-start = ((), (), s32[]{:S(2)}) async-start(), calls=%async_computation.14 | async-start | bytes 2785280 | tf_op jit(solution)/shard_map/all_gather | solution.py:166
  20.5 27.5 %all-to-all-start.1 = ((bf16[16,6,896]{2,1,0:T(8,128)(2,1)}), bf16[16,6,896]{2,1,0:T(8,128)(2,1)S(1)}, u32[]{:S(2)}, u32[]{:S(2)}) async-start(bf16[16,6,896]{2,1,0:T(8,128)(2,1)} %reshape.648), calls=%async_computation.1 | async-start | bytes 458752 | tf_op jit(solution)/shard_map/all_to_all | solution.py:39
  50.0 21.7 %all-to-all-start.2 = ((bf16[16,32,128]{2,1,0:T(8,128)(2,1)}), bf16[16,32,128]{2,1,0:T(8,128)(2,1)S(1)}, u32[]{:S(2)}, u32[]{:S(2)}) async-start(bf16[16,32,128]{2,1,0:T(8,128)(2,1)} %broadcast_in_dim.80), calls=%async_computation.2 | async-start | bytes 262144 | tf_op jit(solution)/shard_map/all_to_all | solution.py:39
  72.5 11.4 %all-to-all-start.3 = ((bf16[4,384,128]{2,1,0:T(8,128)(2,1)}), bf16[4,384,128]{2,1,0:T(8,128)(2,1)S(1)}, u32[]{:S(2)}, u32[]{:S(2)}) async-start(bf16[4,384,128]{2,1,0:T(8,128)(2,1)} %broadcast_in_dim.82), calls=%async_computation.3 | async-start | bytes 786432 | tf_op jit(solution)/shard_map/all_to_all | solution.py:39
  83.9 2.2 copy-start.3
  85.7 1.7 copy-start.5
  85.7 2.0 copy-start.7
  98.1 31.2 %copy-start.1 = (bf16[512,2560]{1,0:T(8,128)(2,1)S(1)}, bf16[512,2560]{1,0:T(8,128)(2,1)}, u32[]{:S(2)}) copy-start(bf16[512,2560]{1,0:T(8,128)(2,1)} %all-gather.2.cloned.1.call-done) | copy-start | bytes 7864324
  98.8 20.0 %all-to-all-start.4 = ((bf16[16,56,128]{2,1,0:T(8,128)(2,1)}), bf16[16,56,128]{2,1,0:T(8,128)(2,1)S(1)}, u32[]{:S(2)}, u32[]{:S(2)}) async-start(bf16[16,56,128]{2,1,0:T(8,128)(2,1)} %copy.278), calls=%async_computation.4 | async-start | bytes 458752 | tf_op jit(solution)/shard_map/all_to_all | solution.py:39
  120.1 8.7 %all-to-all-start.5 = ((bf16[4,92,128]{2,1,0:T(8,128)(2,1)}), bf16[4,92,128]{2,1,0:T(8,128)(2,1)S(1)}, u32[]{:S(2)}, u32[]{:S(2)}) async-start(bf16[4,92,128]{2,1,0:T(8,128)(2,1)} %pad_maximum_fusion.2), calls=%async_computation.5 | async-start | bytes 196608 | tf_op jit(solution)/shard_map/all_to_all | solution.py:39
  130.2 20.5 %all-to-all-start.6 = ((bf16[8,24,512]{2,1,0:T(8,128)(2,1)}), bf16[8,24,512]{2,1,0:T(8,128)(2,1)S(1)}, u32[]{:S(2)}, u32[]{:S(2)}) async-start(bf16[8,24,512]{2,1,0:T(8,128)(2,1)} %broadcast_in_dim.91), calls=%async_computation.6 | async-start | bytes 393216 | tf_op jit(solution)/shard_map/all_to_all | solution.py:39
  160.1 40.3 %copy-start.13 = (s32[8]{0:T(128)S(1)}, s32[8]{0:T(128)}, u32[]{:S(2)}) copy-start(s32[8]{0:T(128)} %param.41) | copy-start | bytes 100
  160.3 56.4 %copy-start.4 = (bf16[8,256,128]{2,1,0:T(8,128)(2,1)S(1)}, bf16[8,256,128]{2,1,0:T(8,128)(2,1)}, u32[]{:S(2)}) copy-start(bf16[8,256,128]{2,1,0:T(8,128)(2,1)} %param.37) | copy-start | bytes 1572868
  160.6 56.1 %copy-start.8 = (bf16[384,128]{1,0:T(8,128)(2,1)S(1)}, bf16[384,128]{1,0:T(8,128)(2,1)}, u32[]{:S(2)}) copy-start(bf16[384,128]{1,0:T(8,128)(2,1)} %copy-done.7) | copy-start | bytes 294916
  161.3 10.1 %all-to-all-start.8 = ((bf16[8,12,128]{2,1,0:T(8,128)(2,1)}), bf16[8,12,128]{2,1,0:T(8,128)(2,1)S(1)}, u32[]{:S(2)}, u32[]{:S(2)}) async-start(bf16[8,12,128]{2,1,0:T(8,128)(2,1)} %copy.294), calls=%async_computation.8 | async-start | bytes 65536 | tf_op jit(solution)/shard_map/all_to_all | solution.py:39
  166.7 51.6 %copy-start.6 = (bf16[8,256,128]{2,1,0:T(8,128)(2,1)S(1)}, bf16[8,256,128]{2,1,0:T(8,128)(2,1)}, u32[]{:S(2)}) copy-start(bf16[8,256,128]{2,1,0:T(8,128)(2,1)} %param.38) | copy-start | bytes 1572868
  196.9 12.2 %all-to-all-start.11 = ((bf16[4,4,192,128]{3,2,1,0:T(8,128)(2,1)}), bf16[4,4,192,128]{3,2,1,0:T(8,128)(2,1)S(1)}, u32[]{:S(2)}, u32[]{:S(2)}) async-start(bf16[4,4,192,128]{3,2,1,0:T(8,128)(2,1)} %broadcast_in_dim.96), calls=%async_computation.11 | async-start | bytes 1572864 | tf_op jit(solution)/shard_map/all_to_all | solution.py:39
  209.1 10.9 %copy-start = (bf16[4,4,192,128]{3,2,1,0:T(8,128)(2,1)}, bf16[4,4,192,128]{3,2,1,0:T(8,128)(2,1)S(1)}, u32[]{:S(2)}) copy-start(bf16[4,4,192,128]{3,2,1,0:T(8,128)(2,1)S(1)} %all-to-all-done.11.refs_2_) | copy-start | bytes 2359300
  209.1 13.7 %collective-permute-start = (bf16[4,4,192,128]{3,2,1,0:T(8,128)(2,1)S(1)}, bf16[4,4,192,128]{3,2,1,0:T(8,128)(2,1)S(1)}, u32[]{:S(2)}, u32[]{:S(2)}) collective-permute-start(bf16[4,4,192,128]{3,2,1,0:T(8,128)(2,1)S(1)} %all-to-all-done.11.refs_2_), channel_id=1, source_target_pairs={{0,1},{1,0},{2,3},{3,2},{4,5},{5,4},{6,7},{7,6},{8,9},{9,8},{10,11... | collective-permute-start | bytes 2359304 | tf_op jit(solution)/shard_map/ppermute | solution.py:286
  222.8 20.2 %copy-start.9 = (f32[192,256]{1,0:T(8,128)S(1)}, f32[192,256]{1,0:T(8,128)}, u32[]{:S(2)}) copy-start(f32[192,256]{1,0:T(8,128)} %get-tuple-element.12) | copy-start | bytes 589828
  222.8 0.9 copy-start.2
  227.8 10.9 %all-to-all-start.12 = ((f32[32,1,512]{2,1,0:T(1,128)}), f32[32,1,512]{2,1,0:T(1,128)S(1)}, u32[]{:S(2)}, u32[]{:S(2)}) async-start(f32[32,1,512]{2,1,0:T(1,128)} %broadcast_in_dim.180), calls=%async_computation.12 | async-start | bytes 131072 | tf_op jit(solution)/shard_map/all_to_all | solution.py:39
  239.5 15.0 %all-to-all-start.13 = ((f32[16,1,512]{2,1,0:T(1,128)}), f32[16,1,512]{2,1,0:T(1,128)S(1)}, u32[]{:S(2)}, u32[]{:S(2)}) async-start(f32[16,1,512]{2,1,0:T(1,128)} %broadcast_in_dim.181), calls=%async_computation.13 | async-start | bytes 65536 | tf_op jit(solution)/shard_map/all_to_all | solution.py:39
Sparse Core Ops, SparseCore 0:
  17.4 80.6 all-gather.1

commit v4 on v3

--- a/solution.py
+++ b/solution.py
@@ -77,10 +77,10 @@
 
 
 def head_kernel(core_ref, temp_ref, tiles_ref, gain_ref, weight_ref, logits_ref, spot_ref, *, flip, width):
-    rows = tiles_ref.shape[2]
+    rows = tiles_ref.shape[1]
     squares = jnp.zeros((rows, 128), F32)
     for column in range(16):
-        tile = tiles_ref[column // 4, column % 4].astype(F32)
+        tile = tiles_ref[column % 4 * 4 + column // 4].astype(F32)
         squares = squares + tile * tile
     scale = lax.rsqrt(jnp.sum(squares, axis=1, keepdims=True) / width + EPSILON)
     total = jnp.zeros((rows, 256), F32)
@@ -90,7 +90,7 @@
             for quarter in range(4):
                 start = (column // 4 * 4 + quarter) * 128 + column % 4 * 32
                 rights.append(weight_ref[start : start + 32, :])
-            tile = tiles_ref[column // 4, column % 4].astype(F32)
+            tile = tiles_ref[column % 4 * 4 + column // 4].astype(F32)
             sides.append((tile * scale * gain_ref[column : column + 1, :]).astype(BF))
         total = total + jnp.dot(
             jnp.concatenate(sides, axis=1),
@@ -112,7 +112,7 @@
 
 
 def head(core, temps, tiles, gains, weight, flip):
-    rows = tiles.shape[2]
+    rows = tiles.shape[1]
     vmem, smem = pl.BlockSpec(memory_space=pltpu.VMEM), pl.BlockSpec(memory_space=pltpu.SMEM)
     return pl.pallas_call(
         lambda *refs: head_kernel(*refs, flip=flip, width=2048),
@@ -241,8 +241,19 @@
         return split.reshape((16, 2, 24) + rest)
 
     outgoing = pack_state(by_z(peak), by_z(mass), by_z(weighted))
-    outgoing, ffn = lax.optimization_barrier((outgoing, ffn))
-    state = merge_state(swap(outgoing, "z"))
+    accepted_rows = links[jnp.arange(requests), accepted]
+    placed = (slot_ids[None, :, None] == target[:, None, :]).astype(F32) * accepted_rows[:, None, :]
+    hits = (jnp.sum(placed, axis=2) > 0.5)[:, :, None]
+    placed = placed.astype(BF)
+    moved_keys = jnp.einsum("rca,rae->rce", placed, tree_keys, preferred_element_type=F32).astype(BF)
+    moved_values = jnp.einsum("rca,rae->rce", placed, tree_values, preferred_element_type=F32).astype(BF)
+    updated_keys = jnp.where(hits, moved_keys, key_cache)
+    updated_values = jnp.where(hits, moved_values, value_cache)
+
+    arrived, ffn, updated_keys, updated_values = lax.optimization_barrier(
+        (swap(outgoing, "z"), ffn, updated_keys, updated_values)
+    )
+    state = merge_state(arrived)
     packed = pack_state(*(part[None] for part in state))
     residual = jnp.transpose(rows.reshape(4, 4, 6, 4, 32), (3, 0, 2, 1, 4)).reshape(4, 24, 128)
     outgates = jnp.concatenate([outgate[:, :128], outgate[:, 128:]], axis=0)
@@ -282,7 +293,7 @@
     following = (middle_mine.astype(F32) + down).astype(BF)
 
     half = spread(following, "z", 16).reshape(192, 128)
-    half = spread(spread(half, "y", 4), "x", 4)
+    half = spread(half, ("y", "x"), 16)
     other = lax.ppermute(half, "c", [(0, 1), (1, 0)])
     core = c.reshape(1)
     own_logits, own_spot = head(core, inv_temp, half, last_all, head_weight, False)
@@ -294,7 +305,7 @@
         )
 
     def own_columns(tiles):
-        return lax.dynamic_slice(tiles, (z // 4, y, 0, 0), (1, 1, 192, 128)).reshape(192, 128)
+        return lax.dynamic_slice(tiles, (y * 4 + z // 4, 0, 0), (1, 192, 128)).reshape(192, 128)
 
     own = in_order(own_columns(half), own_columns(other))
     next_hidden = lax.dynamic_slice(own, (0, z % 4 * 32), (384, 32))
@@ -306,18 +317,7 @@
     spot = spot.reshape(2, 256)[:, :192].reshape(384, 1)
     logprobs = in_order(own_logits, other_logits) - spot
 
-    accepted_rows = links[jnp.arange(requests), accepted]
-    placed = (slot_ids[None, :, None] == target[:, None, :]).astype(F32) * accepted_rows[:, None, :]
-    hits = (jnp.sum(placed, axis=2) > 0.5)[:, :, None]
-    placed = placed.astype(BF)
-    moved_keys = jnp.einsum("rca,rae->rce", placed, tree_keys, preferred_element_type=F32).astype(BF)
-    moved_values = jnp.einsum("rca,rae->rce", placed, tree_values, preferred_element_type=F32).astype(BF)
-    return (
-        logprobs,
-        next_hidden,
-        jnp.where(hits, moved_keys, key_cache),
-        jnp.where(hits, moved_values, value_cache),
-    )
+    return logprobs, next_hidden, updated_keys, updated_values
 
 
 def solution(mesh):

time: 264 us -> 240 us (0.909)
  waiting for transfers between devices: 91.4 us -> 70.4 us
  starting transfers between devices: 83.2 us -> 76.6 us
  blocking collectives: 32.7 us -> 37.8 us
    all_to_all x11 -> x10, waiting for transfers between devices: 81.6 us -> 70.4 us  [swap(): return lax.all_to_all(values, axis, 0, 0, tiled=True)]
    all_gather x1, waiting for transfers between devices: 9.81 us -> 0.01 us  [on_device(): ffn = lax.all_gather(ffn, 'z', axis=0, tiled=True)]
    all_to_all x11 -> x10, starting transfers between devices: 76.5 us -> 71.2 us  [swap(): return lax.all_to_all(values, axis, 0, 0, tiled=True)]
    all_to_all x3, blocking collectives: 32.7 us -> 37.8 us  [swap(): return lax.all_to_all(values, axis, 0, 0, tiled=True)]
  transfers between devices with their start and end apart: 13 -> 12, of which waited for: 12 -> 10; matrix products, arithmetic and copies ran while one was open for 9% -> 9% of each run, Pallas kernels for 1% -> 1%
where the time goes in v4:
time: 240 us; the launch traced here: 239 us
  starting transfers between devices  76.6 us (32%)
  waiting for transfers between devices  70.4 us (29%)
  blocking collectives  37.8 us (16%)
  between operations  14.9 us (6%)
  local copies, waits for them, and re-layouts  11.4 us (5%)
  matrix products  10.5 us (4%)
  other arithmetic  10.2 us (4%)
  Pallas kernels  7.25 us (3%)
    all_to_all x10, starting transfers between devices, swap(): return lax.all_to_all(values, axis, 0, 0, tiled=True)  71.2 us
    all_to_all x10, waiting for transfers between devices, swap(): return lax.all_to_all(values, axis, 0, 0, tiled=True)  70.4 us
    all_to_all x3, blocking collectives, swap(): return lax.all_to_all(values, axis, 0, 0, tiled=True)  37.8 us
    pallas_call x2, Pallas kernels, head(): pl.pallas_call(lambda *refs: head_kernel(*refs, flip=flip, width=2048), o...  5.52 us
    ppermute x1, starting transfers between devices, on_device(): other = lax.ppermute(half, 'c', [(0, 1), (1, 0)])  5.42 us
  transfers between devices with their start and end apart: 12, of which 10 were waited for; matrix products, arithmetic and copies ran while one was open for 9% of the time, Pallas kernels for 1%

profile of v4, /device:TPU:1, one launch (start us, length us, event | category | flops | bytes accessed | tf_op | source)
XLA Modules:
  0.0 239.0 jit_solution(13843212428123805126)
XLA Ops:
  7.2 1.7 pack.1
  8.9 5.1 %all-to-all-start = ((bf16[4,32,896]{2,1,0:T(8,128)(2,1)}), bf16[4,32,896]{2,1,0:T(8,128)(2,1)S(1)}, u32[]{:S(2)}, u32[]{:S(2)}) async-start(bf16[4,32,896]{2,1,0:T(8,128)(2,1)} %pack.1), calls=%async_computation | async-start | bytes 458752 | tf_op jit(solution)/shard_map/all_to_all | solution.py:39
  14.1 1.5 pad_maximum_fusion.1
  15.7 1.4 fusion.8
  20.6 14.9 %all-to-all-start.1 = ((bf16[16,6,896]{2,1,0:T(8,128)(2,1)}), bf16[16,6,896]{2,1,0:T(8,128)(2,1)S(1)}, u32[]{:S(2)}, u32[]{:S(2)}) async-start(bf16[16,6,896]{2,1,0:T(8,128)(2,1)} %reshape.647), calls=%async_computation.1 | async-start | bytes 458752 | tf_op jit(solution)/shard_map/all_to_all | solution.py:39
  36.1 12.0 %all-to-all-done.1 = bf16[16,6,896]{2,1,0:T(8,128)(2,1)S(1)} async-done(((bf16[16,6,896]{2,1,0:T(8,128)(2,1)}), bf16[16,6,896]{2,1,0:T(8,128)(2,1)S(1)}, u32[]{:S(2)}, u32[]{:S(2)}) %all-to-all-start.1) | async-done | bytes 172064 | tf_op jit(solution)/shard_map/all_to_all | solution.py:39
  50.0 9.3 %all-to-all-start.2 = ((bf16[16,32,128]{2,1,0:T(8,128)(2,1)}), bf16[16,32,128]{2,1,0:T(8,128)(2,1)S(1)}, u32[]{:S(2)}, u32[]{:S(2)}) async-start(bf16[16,32,128]{2,1,0:T(8,128)(2,1)} %broadcast_in_dim.81), calls=%async_computation.2 | async-start | bytes 262144 | tf_op jit(solution)/shard_map/all_to_all | solution.py:39
  60.0 11.8 %all-to-all-done.2 = bf16[16,32,128]{2,1,0:T(8,128)(2,1)S(1)} async-done(((bf16[16,32,128]{2,1,0:T(8,128)(2,1)}), bf16[16,32,128]{2,1,0:T(8,128)(2,1)S(1)}, u32[]{:S(2)}, u32[]{:S(2)}) %all-to-all-start.2) | async-done | bytes 131104 | tf_op jit(solution)/shard_map/all_to_all | solution.py:39
  72.6 6.3 %all-to-all-start.3 = ((bf16[4,384,128]{2,1,0:T(8,128)(2,1)}), bf16[4,384,128]{2,1,0:T(8,128)(2,1)S(1)}, u32[]{:S(2)}, u32[]{:S(2)}) async-start(bf16[4,384,128]{2,1,0:T(8,128)(2,1)} %broadcast_in_dim.83), calls=%async_computation.3 | async-start | bytes 786432 | tf_op jit(solution)/shard_map/all_to_all | solution.py:39
  79.1 6.1 %all-to-all-done.3 = bf16[4,384,128]{2,1,0:T(8,128)(2,1)S(1)} async-done(((bf16[4,384,128]{2,1,0:T(8,128)(2,1)}), bf16[4,384,128]{2,1,0:T(8,128)(2,1)S(1)}, u32[]{:S(2)}, u32[]{:S(2)}) %all-to-all-start.3) | async-done | bytes 393248 | tf_op jit(solution)/shard_map/all_to_all | solution.py:39
  85.2 1.7 fusion.2
  90.3 6.2 %all-to-all-start.4 = ((bf16[16,56,128]{2,1,0:T(8,128)(2,1)}), bf16[16,56,128]{2,1,0:T(8,128)(2,1)S(1)}, u32[]{:S(2)}, u32[]{:S(2)}) async-start(bf16[16,56,128]{2,1,0:T(8,128)(2,1)} %copy.278), calls=%async_computation.4 | async-start | bytes 458752 | tf_op jit(solution)/shard_map/all_to_all | solution.py:39
  96.8 1.7 fusion.4
  98.5 1.6 fusion.5
  100.1 9.0 %all-to-all-done.4 = bf16[16,56,128]{2,1,0:T(8,128)(2,1)S(1)} async-done(((bf16[16,56,128]{2,1,0:T(8,128)(2,1)}), bf16[16,56,128]{2,1,0:T(8,128)(2,1)S(1)}, u32[]{:S(2)}, u32[]{:S(2)}) %all-to-all-start.4) | async-done | bytes 229408 | tf_op jit(solution)/shard_map/all_to_all | solution.py:39
  110.4 3.4 %all-to-all-start.5 = ((bf16[4,92,128]{2,1,0:T(8,128)(2,1)}), bf16[4,92,128]{2,1,0:T(8,128)(2,1)S(1)}, u32[]{:S(2)}, u32[]{:S(2)}) async-start(bf16[4,92,128]{2,1,0:T(8,128)(2,1)} %pad_maximum_fusion.2), calls=%async_computation.5 | async-start | bytes 196608 | tf_op jit(solution)/shard_map/all_to_all | solution.py:39
  114.1 4.4 %all-to-all-done.5 = bf16[4,92,128]{2,1,0:T(8,128)(2,1)S(1)} async-done(((bf16[4,92,128]{2,1,0:T(8,128)(2,1)}), bf16[4,92,128]{2,1,0:T(8,128)(2,1)S(1)}, u32[]{:S(2)}, u32[]{:S(2)}) %all-to-all-start.5) | async-done | bytes 94240 | tf_op jit(solution)/shard_map/all_to_all | solution.py:39
  118.9 1.1 convolution_convert_fusion.4
  120.8 13.4 %all-to-all-start.6 = ((bf16[8,24,512]{2,1,0:T(8,128)(2,1)}), bf16[8,24,512]{2,1,0:T(8,128)(2,1)S(1)}, u32[]{:S(2)}, u32[]{:S(2)}) async-start(bf16[8,24,512]{2,1,0:T(8,128)(2,1)} %broadcast_in_dim.94), calls=%async_computation.6 | async-start | bytes 393216 | tf_op jit(solution)/shard_map/all_to_all | solution.py:39
  134.3 5.8 %all-to-all-done.6 = bf16[8,24,512]{2,1,0:T(8,128)(2,1)S(1)} async-done(((bf16[8,24,512]{2,1,0:T(8,128)(2,1)}), bf16[8,24,512]{2,1,0:T(8,128)(2,1)S(1)}, u32[]{:S(2)}, u32[]{:S(2)}) %all-to-all-start.6) | async-done | bytes 196640 | tf_op jit(solution)/shard_map/all_to_all | solution.py:39
  140.9 8.4 %all_to_all.65 = bf16[4,24,1664]{2,1,0:T(8,128)(2,1)S(1)} all-to-all(bf16[4,24,1664]{2,1,0:T(8,128)(2,1)S(1)} %broadcast_in_dim.95), channel_id=1, replica_groups=mesh['z'=16,'y'=4,'x'=4,'c'=2] {'y'}, dimensions={0} | all-to-all | bytes 638976 | tf_op jit(solution)/shard_map/all_to_all | solution.py:39
  150.7 5.4 %all-to-all-start.8 = ((bf16[8,12,128]{2,1,0:T(8,128)(2,1)}), bf16[8,12,128]{2,1,0:T(8,128)(2,1)S(1)}, u32[]{:S(2)}, u32[]{:S(2)}) async-start(bf16[8,12,128]{2,1,0:T(8,128)(2,1)} %copy.294), calls=%async_computation.8 | async-start | bytes 65536 | tf_op jit(solution)/shard_map/all_to_all | solution.py:39
  156.1 4.7 %all-to-all-done.8 = bf16[8,12,128]{2,1,0:T(8,128)(2,1)S(1)} async-done(((bf16[8,12,128]{2,1,0:T(8,128)(2,1)}), bf16[8,12,128]{2,1,0:T(8,128)(2,1)S(1)}, u32[]{:S(2)}, u32[]{:S(2)}) %all-to-all-start.8) | async-done | bytes 24608 | tf_op jit(solution)/shard_map/all_to_all | solution.py:39
  160.9 14.7 %all_to_all.66 = bf16[16,12,128]{2,1,0:T(8,128)(2,1)S(1)} all-to-all(bf16[16,12,128]{2,1,0:T(8,128)(2,1)S(1)} %broadcast_in_dim.96), channel_id=1, replica_groups=mesh['z'=16,'y'=4,'x'=4,'c'=2] {'z'}, dimensions={0} | all-to-all | bytes 98304 | tf_op jit(solution)/shard_map/all_to_all | solution.py:39
  175.8 14.7 %all_to_all.67.refs_2_ = bf16[16,192,128]{2,1,0:T(8,128)(2,1)S(1)} all-to-all(bf16[16,192,128]{2,1,0:T(8,128)(2,1)S(1)} %broadcast_in_dim.173), channel_id=1, replica_groups=mesh['z'=16,'y'=4,'x'=4,'c'=2] {'y','x'}, dimensions={0} | all-to-all | bytes 1572864 | tf_op jit(solution)/shard_map/all_to_all | solution.py:39
  190.4 5.4 %collective-permute-start = (bf16[16,192,128]{2,1,0:T(8,128)(2,1)S(1)}, bf16[16,192,128]{2,1,0:T(8,128)(2,1)S(1)}, u32[]{:S(2)}, u32[]{:S(2)}) collective-permute-start(bf16[16,192,128]{2,1,0:T(8,128)(2,1)S(1)} %all_to_all.67.refs_2_), channel_id=1, source_target_pairs={{0,1},{1,0},{2,3},{3,2},{4,5},{5,4},{6,7},{7,6},{8,9},{9,8},{10,11... | collective-permute-start | bytes 2359304 | tf_op jit(solution)/shard_map/ppermute | solution.py:297
  196.7 2.8 %head_own.1 = (f32[192,256]{1,0:T(8,128)}, f32[1,256]{1,0:T(1,128)}) custom-call(s32[1]{0:T(128)} %bitcast.refs_0_, f32[8]{0:T(128)} %refs_1_.3, bf16[16,192,128]{2,1,0:T(8,128)(2,1)} %copy-done, f32[16,128]{1,0:T(8,128)} %reshape.661.refs_3_, bf16[2048,256]{1,0:T(8,128)(2,1)} %refs_4_.3), custom_call_target="tpu_custom_call" | custom-call | flops 201326592 | bytes 1835008 | tf_op jit(solution)/shard_map/head_own/pallas_call | solution.py:117
  200.4 2.7 %head_flip.1 = (f32[192,256]{1,0:T(8,128)}, f32[1,256]{1,0:T(1,128)}) custom-call(s32[1]{0:T(128)} %bitcast.refs_0_, f32[8]{0:T(128)} %refs_1_.3, bf16[16,192,128]{2,1,0:T(8,128)(2,1)} %copy-done.2, f32[16,128]{1,0:T(8,128)} %reshape.661.refs_3_, bf16[2048,256]{1,0:T(8,128)(2,1)} %refs_4_.3), custom_call_target="tpu_custom_call" | custom-call | flops 201326592 | bytes 1835008 | tf_op jit(solution)/shard_map/head_flip/pallas_call | solution.py:117
  204.4 3.6 %all-to-all-start.11 = ((f32[32,1,512]{2,1,0:T(1,128)}), f32[32,1,512]{2,1,0:T(1,128)S(1)}, u32[]{:S(2)}, u32[]{:S(2)}) async-start(f32[32,1,512]{2,1,0:T(1,128)} %broadcast_in_dim.175), calls=%async_computation.11 | async-start | bytes 131072 | tf_op jit(solution)/shard_map/all_to_all | solution.py:39
  209.7 5.7 %all-to-all-done.11 = f32[32,1,512]{2,1,0:T(1,128)S(1)} async-done(((f32[32,1,512]{2,1,0:T(1,128)}), f32[32,1,512]{2,1,0:T(1,128)S(1)}, u32[]{:S(2)}, u32[]{:S(2)}) %all-to-all-start.11) | async-done | bytes 65568 | tf_op jit(solution)/shard_map/all_to_all | solution.py:39
  216.1 3.5 %all-to-all-start.12 = ((f32[16,1,512]{2,1,0:T(1,128)}), f32[16,1,512]{2,1,0:T(1,128)S(1)}, u32[]{:S(2)}, u32[]{:S(2)}) async-start(f32[16,1,512]{2,1,0:T(1,128)} %broadcast_in_dim.176), calls=%async_computation.12 | async-start | bytes 65536 | tf_op jit(solution)/shard_map/all_to_all | solution.py:39
  220.6 10.5 %all-to-all-done.12 = f32[16,1,512]{2,1,0:T(1,128)S(1)} async-done(((f32[16,1,512]{2,1,0:T(1,128)}), f32[16,1,512]{2,1,0:T(1,128)S(1)}, u32[]{:S(2)}, u32[]{:S(2)}) %all-to-all-start.12) | async-done | bytes 32800 | tf_op jit(solution)/shard_map/all_to_all | solution.py:39
  (196 shorter events, 23.4 us)
Async XLA Ops:
  8.9 39.7 %copy-start.7 = (f32[128]{0:T(128)S(1)}, f32[128]{0:T(128)}, u32[]{:S(2)}) copy-start(f32[128]{0:T(128)} %param.28) | copy-start | bytes 1540
  8.9 39.9 %copy-start.8 = (f32[128]{0:T(128)S(1)}, f32[128]{0:T(128)}, u32[]{:S(2)}) copy-start(f32[128]{0:T(128)} %param.27) | copy-start | bytes 1540
  8.9 10.5 %all-to-all-start = ((bf16[4,32,896]{2,1,0:T(8,128)(2,1)}), bf16[4,32,896]{2,1,0:T(8,128)(2,1)S(1)}, u32[]{:S(2)}, u32[]{:S(2)}) async-start(bf16[4,32,896]{2,1,0:T(8,128)(2,1)} %pack.1), calls=%async_computation | async-start | bytes 458752 | tf_op jit(solution)/shard_map/all_to_all | solution.py:39
  14.1 45.2 %copy-start.9 = (s32[8]{0:T(128)S(1)}, s32[8]{0:T(128)}, u32[]{:S(2)}) copy-start(s32[8]{0:T(128)} %param.41) | copy-start | bytes 100
  14.1 95.1 %all-gather.2.cloned.1.call-start = ((), (), s32[]{:S(2)}) async-start(), calls=%async_computation.13 | async-start | bytes 2785280 | tf_op jit(solution)/shard_map/all_gather | solution.py:166
  14.1 45.9 %copy-start.6 = (s32[8]{0:T(128)S(1)}, s32[8]{0:T(128)}, u32[]{:S(2)}) copy-start(s32[8]{0:T(128)} %param.39) | copy-start | bytes 100
  20.6 27.5 %all-to-all-start.1 = ((bf16[16,6,896]{2,1,0:T(8,128)(2,1)}), bf16[16,6,896]{2,1,0:T(8,128)(2,1)S(1)}, u32[]{:S(2)}, u32[]{:S(2)}) async-start(bf16[16,6,896]{2,1,0:T(8,128)(2,1)} %reshape.647), calls=%async_computation.1 | async-start | bytes 458752 | tf_op jit(solution)/shard_map/all_to_all | solution.py:39
  50.0 21.8 %all-to-all-start.2 = ((bf16[16,32,128]{2,1,0:T(8,128)(2,1)}), bf16[16,32,128]{2,1,0:T(8,128)(2,1)S(1)}, u32[]{:S(2)}, u32[]{:S(2)}) async-start(bf16[16,32,128]{2,1,0:T(8,128)(2,1)} %broadcast_in_dim.81), calls=%async_computation.2 | async-start | bytes 262144 | tf_op jit(solution)/shard_map/all_to_all | solution.py:39
  72.6 12.6 %all-to-all-start.3 = ((bf16[4,384,128]{2,1,0:T(8,128)(2,1)}), bf16[4,384,128]{2,1,0:T(8,128)(2,1)S(1)}, u32[]{:S(2)}, u32[]{:S(2)}) async-start(bf16[4,384,128]{2,1,0:T(8,128)(2,1)} %broadcast_in_dim.83), calls=%async_computation.3 | async-start | bytes 786432 | tf_op jit(solution)/shard_map/all_to_all | solution.py:39
  85.2 2.2 copy-start.3
  86.9 1.7 copy-start.4
  90.3 18.8 %all-to-all-start.4 = ((bf16[16,56,128]{2,1,0:T(8,128)(2,1)}), bf16[16,56,128]{2,1,0:T(8,128)(2,1)S(1)}, u32[]{:S(2)}, u32[]{:S(2)}) async-start(bf16[16,56,128]{2,1,0:T(8,128)(2,1)} %copy.278), calls=%async_computation.4 | async-start | bytes 458752 | tf_op jit(solution)/shard_map/all_to_all | solution.py:39
  109.1 31.4 %copy-start.1 = (bf16[512,2560]{1,0:T(8,128)(2,1)S(1)}, bf16[512,2560]{1,0:T(8,128)(2,1)}, u32[]{:S(2)}) copy-start(bf16[512,2560]{1,0:T(8,128)(2,1)} %all-gather.2.cloned.1.call-done) | copy-start | bytes 7864324
  110.4 8.1 %all-to-all-start.5 = ((bf16[4,92,128]{2,1,0:T(8,128)(2,1)}), bf16[4,92,128]{2,1,0:T(8,128)(2,1)S(1)}, u32[]{:S(2)}, u32[]{:S(2)}) async-start(bf16[4,92,128]{2,1,0:T(8,128)(2,1)} %pad_maximum_fusion.2), calls=%async_computation.5 | async-start | bytes 196608 | tf_op jit(solution)/shard_map/all_to_all | solution.py:39
  120.8 19.3 %all-to-all-start.6 = ((bf16[8,24,512]{2,1,0:T(8,128)(2,1)}), bf16[8,24,512]{2,1,0:T(8,128)(2,1)S(1)}, u32[]{:S(2)}, u32[]{:S(2)}) async-start(bf16[8,24,512]{2,1,0:T(8,128)(2,1)} %broadcast_in_dim.94), calls=%async_computation.6 | async-start | bytes 393216 | tf_op jit(solution)/shard_map/all_to_all | solution.py:39
  150.7 10.1 %all-to-all-start.8 = ((bf16[8,12,128]{2,1,0:T(8,128)(2,1)}), bf16[8,12,128]{2,1,0:T(8,128)(2,1)S(1)}, u32[]{:S(2)}, u32[]{:S(2)}) async-start(bf16[8,12,128]{2,1,0:T(8,128)(2,1)} %copy.294), calls=%async_computation.8 | async-start | bytes 65536 | tf_op jit(solution)/shard_map/all_to_all | solution.py:39
  190.4 6.3 %copy-start = (bf16[16,192,128]{2,1,0:T(8,128)(2,1)}, bf16[16,192,128]{2,1,0:T(8,128)(2,1)S(1)}, u32[]{:S(2)}) copy-start(bf16[16,192,128]{2,1,0:T(8,128)(2,1)S(1)} %all_to_all.67.refs_2_) | copy-start | bytes 2359300
  190.4 9.0 %collective-permute-start = (bf16[16,192,128]{2,1,0:T(8,128)(2,1)S(1)}, bf16[16,192,128]{2,1,0:T(8,128)(2,1)S(1)}, u32[]{:S(2)}, u32[]{:S(2)}) collective-permute-start(bf16[16,192,128]{2,1,0:T(8,128)(2,1)S(1)} %all_to_all.67.refs_2_), channel_id=1, source_target_pairs={{0,1},{1,0},{2,3},{3,2},{4,5},{5,4},{6,7},{7,6},{8,9},{9,8},{10,11... | collective-permute-start | bytes 2359304 | tf_op jit(solution)/shard_map/ppermute | solution.py:297
  199.4 20.2 %copy-start.5 = (f32[192,256]{1,0:T(8,128)S(1)}, f32[192,256]{1,0:T(8,128)}, u32[]{:S(2)}) copy-start(f32[192,256]{1,0:T(8,128)} %get-tuple-element.14) | copy-start | bytes 589828
  199.5 0.9 copy-start.2
  204.4 10.9 %all-to-all-start.11 = ((f32[32,1,512]{2,1,0:T(1,128)}), f32[32,1,512]{2,1,0:T(1,128)S(1)}, u32[]{:S(2)}, u32[]{:S(2)}) async-start(f32[32,1,512]{2,1,0:T(1,128)} %broadcast_in_dim.175), calls=%async_computation.11 | async-start | bytes 131072 | tf_op jit(solution)/shard_map/all_to_all | solution.py:39
  216.1 15.0 %all-to-all-start.12 = ((f32[16,1,512]{2,1,0:T(1,128)}), f32[16,1,512]{2,1,0:T(1,128)S(1)}, u32[]{:S(2)}, u32[]{:S(2)}) async-start(f32[16,1,512]{2,1,0:T(1,128)} %broadcast_in_dim.176), calls=%async_computation.12 | async-start | bytes 65536 | tf_op jit(solution)/shard_map/all_to_all | solution.py:39
Sparse Core Ops, SparseCore 0:
  17.0 81.1 all-gather.1

commit v5 on v4

--- a/solution.py
+++ b/solution.py
@@ -52,9 +52,7 @@
     lane = lax.broadcasted_iota(jnp.int32, (1, 512), 1)
     first = lane // 128
     local = lane - first * 128
-    first_z = local // 6
-    token = first // 2 * 192 + first_z * 12 + first % 2 * 6 + (local - first_z * 6)
-    token = jnp.where(local < 96, token, -1)
+    token = jnp.where(local < 96, first * 96 + local, -1)
     chosen = lax.broadcasted_iota(jnp.int32, (384, 512), 0) == token
     moved = jnp.dot(
         hidden_ref[...], jnp.where(chosen, 1.0, 0.0).astype(BF), preferred_element_type=F32
@@ -132,19 +130,18 @@
 def pack_state(peak, mass, weighted):
     count = peak.shape[0]
     mass_high, mass_low = split2(mass)
-    stats = jnp.stack([peak.astype(BF), mass_high, mass_low], axis=1).reshape(count, 6, 24)
-    stats = jnp.pad(stats, ((0, 0), (0, 2), (0, 104)))
-    return jnp.concatenate([weighted.astype(BF).reshape(count, 48, 128), stats], axis=1)
+    stats = jnp.stack([peak.astype(BF), mass_high, mass_low], axis=1).reshape(count, 6, 6)
+    stats = jnp.pad(stats, ((0, 0), (0, 0), (0, 122)))
+    return jnp.concatenate([weighted.astype(BF).reshape(count, 12, 128), stats], axis=1)
 
 
 def merge_state(packed):
     count = packed.shape[0]
-    weighted = packed[:, :48].reshape(count, 2, 24, 128).astype(F32)
-    stats = packed[:, 48:54, :24].astype(F32).reshape(count, 3, 2, 24)
+    weighted = packed[:, :12].reshape(count, 2, 6, 128).astype(F32)
+    stats = packed[:, 12:, :6].astype(F32).reshape(count, 3, 2, 6)
     peaks, masses = stats[:, 0], stats[:, 1] + stats[:, 2]
-    peak = jnp.max(peaks, axis=0)
-    factor = jnp.exp(peaks - peak)
-    return peak, jnp.sum(masses * factor, axis=0), jnp.sum(weighted * factor[..., None], axis=0)
+    factor = jnp.exp(peaks - jnp.max(peaks, axis=0))
+    return jnp.sum(masses * factor, axis=0), jnp.sum(weighted * factor[..., None], axis=0)
 
 
 def on_device(
@@ -157,10 +154,6 @@
     slot_count = key_cache.shape[1]
     width = 2048
 
-    token = jnp.arange(384, dtype=jnp.int32)
-    token_z = token % 192 // 12
-    token_y = token // 192 * 2 + token % 12 // 6
-    token_i = token % 6
 
     ffn = jnp.concatenate([w_gate, w_up, w_down.T, wo.T], axis=1)
     ffn = lax.all_gather(ffn, "z", axis=0, tiled=True)
@@ -189,7 +182,7 @@
     links = ancestry(parents)
     depth = jnp.sum((links > 0.5).astype(jnp.int32), axis=-1) - 1
     target = lengths[:, None] + depth
-    first = y // 2 * 192 + z * 12 + y % 2 * 6
+    first = y * 96 + z * 6
     my_places = lax.dynamic_slice(target.reshape(-1), (first,), (6,))
     inverse = ROPE_BASE ** (-jnp.arange(64, dtype=F32) / 64)
     angles = my_places.astype(F32)[:, None] * inverse[None, :]
@@ -204,23 +197,38 @@
         ],
         axis=0,
     ).astype(BF)
-    gathered = spread(block, "z", 16)
+    caches = jnp.stack([key_cache, value_cache])
+    parts = []
+    for shift in range(4):
+        part = lax.dynamic_slice(
+            caches, (0, (y + shift) % 4 * 2, 0, 0), (2, 2, slot_count, 128)
+        )
+        if shift:
+            part = lax.ppermute(part, "y", [(i, (i + shift) % 4) for i in range(4)])
+        parts.append(part)
+    moved = jnp.concatenate(parts, axis=2)
+    gathered, moved = lax.optimization_barrier((spread(block, "z", 16), moved))
     gain_all = gathered[:, 24:30].astype(F32)
     ln2_mine = gain_all[:, 0] + gain_all[:, 1] + gain_all[:, 2]
     ln2_mine = lax.dynamic_slice(ln2_mine, (0, y * 32), (16, 32)).reshape(1, 512)
     last_all = gain_all[:, 3] + gain_all[:, 4] + gain_all[:, 5]
     last_all = jnp.swapaxes(last_all.reshape(4, 4, 4, 32), 1, 2).reshape(16, 128)
-    pool = spread(gathered[:, :24].reshape(384, 128), "y", 4).reshape(1536, 128)
-    origin = token_y * 384 + token_z * 24 + token_i
-    origin = (jnp.arange(4, dtype=jnp.int32)[:, None] * 6 + origin[None, :]).reshape(1536)
-    gather = (origin[:, None] == jnp.arange(1536, dtype=jnp.int32)[None, :]).astype(BF)
-    tokens = jnp.dot(gather, pool, preferred_element_type=F32).astype(BF).reshape(4, requests, tree, 128)
-    queries, tree_keys, tree_values = tokens[:2], tokens[2], tokens[3]
-
-    slot_ids = seq * slot_count + jnp.arange(slot_count, dtype=jnp.int32)
-    valid_slot = (slot_ids[None, :] < lengths[:, None])[:, None, None, :]
-    valid_node = ((links > 0.5) & (seq == 0))[:, None, :, :]
-    scores = jnp.einsum("grid,rcd->rgic", queries, key_cache, preferred_element_type=F32)
+    spot96 = jnp.arange(96, dtype=jnp.int32)
+    origin = jnp.arange(4, dtype=jnp.int32)[:, None] * 6 + (spot96 // 6 * 24 + spot96 % 6)[None, :]
+    gather = (origin.reshape(384, 1) == jnp.arange(384, dtype=jnp.int32)[None, :]).astype(BF)
+    tokens = jnp.dot(gather, gathered[:, :24].reshape(384, 128), preferred_element_type=F32).astype(BF)
+    queries = tokens[:192].reshape(2, 2, tree, 128)
+    tree_keys = tokens[192:288].reshape(2, tree, 128)
+    tree_values = tokens[288:].reshape(2, tree, 128)
+
+    keys, values = moved[0], moved[1]
+    my_lengths = lax.dynamic_slice(lengths, (2 * y,), (2,))
+    my_links = lax.dynamic_slice(links, (2 * y, 0, 0), (2, tree, tree))
+    source = (y - jnp.arange(4, dtype=jnp.int32)) % 4 + z * 4
+    row_slots = (source[:, None] * slot_count + jnp.arange(slot_count, dtype=jnp.int32)).reshape(-1)
+    valid_slot = (row_slots[None, :] < my_lengths[:, None])[:, None, None, :]
+    valid_node = ((my_links > 0.5) & (z == 0))[:, None, :, :]
+    scores = jnp.einsum("grid,rcd->rgic", queries, keys, preferred_element_type=F32)
     tree_scores = jnp.einsum("grid,rjd->rgij", queries, tree_keys, preferred_element_type=F32)
     peak = jnp.maximum(
         jnp.max(jnp.where(valid_slot, scores, NEGATIVE), axis=-1),
@@ -231,16 +239,27 @@
     tree_weights = jnp.where(valid_node, jnp.exp(tree_scores - peak[..., None]), 0.0)
     mass = jnp.sum(weights, axis=-1) + jnp.sum(tree_weights, axis=-1)
     weighted = jnp.einsum(
-        "rgic,rcd->rgid", weights.astype(BF), value_cache, preferred_element_type=F32
+        "rgic,rcd->rgid", weights.astype(BF), values, preferred_element_type=F32
     ) + jnp.einsum("rgij,rjd->rgid", tree_weights.astype(BF), tree_values, preferred_element_type=F32)
 
     def by_z(values):
         rest = values.shape[3:]
-        split = values.reshape((2, 4, 2, 4, 12) + rest)
-        split = jnp.transpose(split, (1, 3, 2, 0, 4) + tuple(range(5, 5 + len(rest))))
-        return split.reshape((16, 2, 24) + rest)
+        return jnp.swapaxes(values.reshape((2, 2, 8, 6) + rest), 1, 2).reshape((16, 2, 6) + rest)
 
     outgoing = pack_state(by_z(peak), by_z(mass), by_z(weighted))
+    arrived, ffn = lax.optimization_barrier((swap(outgoing, "z"), ffn))
+    mass, weighted = merge_state(arrived)
+    my_gate = jnp.swapaxes(outgate.reshape(6, 2, 128), 0, 1).astype(F32)
+    gated = (weighted / mass[..., None] * my_gate).astype(BF).reshape(12, 128)
+    residual = jnp.transpose(rows.reshape(4, 4, 6, 4, 32), (3, 0, 2, 1, 4)).reshape(4, 24, 128)
+    same = jnp.concatenate([gated, tokens[192:]], axis=0)
+    both = swap(jnp.concatenate([residual, jnp.broadcast_to(same[None], (4, 204, 128))], axis=1), "y")
+    hidden_rows = jnp.swapaxes(both[:, :24].reshape(4, 4, 6, 128), 1, 2).reshape(24, 512)
+    gated = jnp.swapaxes(both[:, 24:36].reshape(4, 2, 6, 128), 0, 1).reshape(2, 24, 128)
+    tree_keys = both[:, 36:132].reshape(requests, tree, 128)
+    tree_values = both[:, 132:].reshape(requests, tree, 128)
+
+    slot_ids = seq * slot_count + jnp.arange(slot_count, dtype=jnp.int32)
     accepted_rows = links[jnp.arange(requests), accepted]
     placed = (slot_ids[None, :, None] == target[:, None, :]).astype(F32) * accepted_rows[:, None, :]
     hits = (jnp.sum(placed, axis=2) > 0.5)[:, :, None]
@@ -250,23 +269,6 @@
     updated_keys = jnp.where(hits, moved_keys, key_cache)
     updated_values = jnp.where(hits, moved_values, value_cache)
 
-    arrived, ffn, updated_keys, updated_values = lax.optimization_barrier(
-        (swap(outgoing, "z"), ffn, updated_keys, updated_values)
-    )
-    state = merge_state(arrived)
-    packed = pack_state(*(part[None] for part in state))
-    residual = jnp.transpose(rows.reshape(4, 4, 6, 4, 32), (3, 0, 2, 1, 4)).reshape(4, 24, 128)
-    outgates = jnp.concatenate([outgate[:, :128], outgate[:, 128:]], axis=0)
-    shared = jnp.concatenate(
-        [jnp.broadcast_to(packed, (4, 56, 128)), residual, jnp.broadcast_to(outgates[None], (4, 12, 128))],
-        axis=1,
-    )
-    both = swap(shared, "y")
-    peak, mass, weighted = merge_state(both[:, :56])
-    my_gate = jnp.swapaxes(both[:, 80:].reshape(4, 2, 6, 128), 0, 1).reshape(2, 24, 128).astype(F32)
-    gated = (weighted / mass[..., None] * my_gate).astype(BF)
-    hidden_rows = jnp.swapaxes(both[:, 56:80].reshape(4, 4, 6, 128), 1, 2).reshape(24, 512)
-
     contract = (((1,), (1,)), ((), ()))
     attn = lax.dot_general(
         jnp.concatenate([gated[0], gated[1]], axis=1),
@@ -274,7 +276,10 @@
         contract,
         preferred_element_type=F32,
     )
-    attn = jnp.sum(spread(attn.astype(BF), ("x", "c"), 8).astype(F32), axis=0)
+    attn, updated_keys, updated_values = lax.optimization_barrier(
+        (spread(attn.astype(BF), ("x", "c"), 8), updated_keys, updated_values)
+    )
+    attn = jnp.sum(attn.astype(F32), axis=0)
     middle = (hidden_rows.astype(F32) + attn).astype(BF)
     middle_wide = middle.astype(F32)
     squares_mid = split2(jnp.sum(middle_wide * middle_wide, axis=1, keepdims=True))
@@ -292,7 +297,8 @@
     middle_mine = lax.dynamic_slice(middle, (c * 12, x * 128), (12, 128))
     following = (middle_mine.astype(F32) + down).astype(BF)
 
-    half = spread(following, "z", 16).reshape(192, 128)
+    half = spread(following, "z", 16).reshape(16, 2, 6, 128)
+    half = jnp.swapaxes(half, 0, 1).reshape(192, 128)
     half = spread(half, ("y", "x"), 16)
     other = lax.ppermute(half, "c", [(0, 1), (1, 0)])
     core = c.reshape(1)

time: 240 us -> 252 us (1.050)
  blocking collectives: 37.8 us -> 45.1 us
    ppermute x0 -> x3, starting transfers between devices: none -> 11.5 us  [on_device(): part = lax.ppermute(part, 'y', [(i, (i + shift) % 4) for i in range(4)])]
    all_to_all x10 -> x9, starting transfers between devices: 71.2 us -> 61.7 us  [swap(): return lax.all_to_all(values, axis, 0, 0, tiled=True)]
    all_gather x1, waiting for transfers between devices: 0.01 us -> 7.5 us  [on_device(): ffn = lax.all_gather(ffn, 'z', axis=0, tiled=True)]
    all_to_all x3, blocking collectives: 37.8 us -> 45.1 us  [swap(): return lax.all_to_all(values, axis, 0, 0, tiled=True)]
    all_to_all x10 -> x9, waiting for transfers between devices: 70.4 us -> 64.6 us  [swap(): return lax.all_to_all(values, axis, 0, 0, tiled=True)]
  transfers between devices with their start and end apart: 12 -> 14, of which waited for: 10 -> 10; matrix products, arithmetic and copies ran while one was open for 9% -> 8% of each run, Pallas kernels for 1% -> 2%
where the time goes in v5:
time: 252 us; the launch traced here: 250 us
  starting transfers between devices  78.3 us (31%)
  waiting for transfers between devices  72.2 us (29%)
  blocking collectives  45.1 us (18%)
  between operations  15 us (6%)
  local copies, waits for them, and re-layouts  11.9 us (5%)
  other arithmetic  11.5 us (5%)
  matrix products  8.96 us (4%)
  Pallas kernels  7.24 us (3%)
    all_to_all x9, waiting for transfers between devices, swap(): return lax.all_to_all(values, axis, 0, 0, tiled=True)  64.6 us
    all_to_all x9, starting transfers between devices, swap(): return lax.all_to_all(values, axis, 0, 0, tiled=True)  61.7 us
    all_to_all x3, blocking collectives, swap(): return lax.all_to_all(values, axis, 0, 0, tiled=True)  45.1 us
    ppermute x3, starting transfers between devices, on_device(): part = lax.ppermute(part, 'y', [(i, (i + shift) % 4) for i in range(4)])  11.5 us
    all_gather x1, waiting for transfers between devices, on_device(): ffn = lax.all_gather(ffn, 'z', axis=0, tiled=True)  7.5 us
    pallas_call x2, Pallas kernels, head(): pl.pallas_call(lambda *refs: head_kernel(*refs, flip=flip, width=2048), o...  5.52 us
  transfers between devices with their start and end apart: 14, of which 10 were waited for; matrix products, arithmetic and copies ran while one was open for 8% of the time, Pallas kernels for 2%

profile of v5, /device:TPU:1, one launch (start us, length us, event | category | flops | bytes accessed | tf_op | source)
XLA Modules:
  0.0 250.1 jit_solution(4545308876580301939)
XLA Ops:
  7.3 1.4 fusion.26
  8.7 4.0 %collective-permute-start = (bf16[2,2,256,128]{3,2,1,0:T(8,128)(2,1)S(1)}, bf16[2,2,256,128]{3,2,1,0:T(8,128)(2,1)S(1)}, u32[]{:S(2)}, u32[]{:S(2)}) collective-permute-start(bf16[2,2,256,128]{3,2,1,0:T(8,128)(2,1)S(1)} %get-tuple-element.63), channel_id=1, source_target_pairs={{0,8},{8,16},{16,24},{24,0},{1,9},{9,17},{17,25},{25,1},{2,10},{10... | collective-permute-start | bytes 786440 | tf_op jit(solution)/shard_map/ppermute | solution.py:207
  12.7 4.5 %collective-permute-start.1 = (bf16[2,2,256,128]{3,2,1,0:T(8,128)(2,1)S(1)}, bf16[2,2,256,128]{3,2,1,0:T(8,128)(2,1)S(1)}, u32[]{:S(2)}, u32[]{:S(2)}) collective-permute-start(bf16[2,2,256,128]{3,2,1,0:T(8,128)(2,1)S(1)} %get-tuple-element.64), channel_id=1, source_target_pairs={{0,16},{8,24},{16,0},{24,8},{1,17},{9,25},{17,1},{25,9},{2,18},{10... | collective-permute-start | bytes 786440 | tf_op jit(solution)/shard_map/ppermute | solution.py:207
  17.3 3.0 %collective-permute-start.2 = (bf16[2,2,256,128]{3,2,1,0:T(8,128)(2,1)S(1)}, bf16[2,2,256,128]{3,2,1,0:T(8,128)(2,1)S(1)}, u32[]{:S(2)}, u32[]{:S(2)}) collective-permute-start(bf16[2,2,256,128]{3,2,1,0:T(8,128)(2,1)S(1)} %get-tuple-element.65), channel_id=1, source_target_pairs={{0,24},{8,0},{16,8},{24,16},{1,25},{9,1},{17,9},{25,17},{2,26},{10... | collective-permute-start | bytes 786440 | tf_op jit(solution)/shard_map/ppermute | solution.py:207
  20.2 1.7 pack.1
  22.0 3.4 %all-to-all-start = ((bf16[4,32,896]{2,1,0:T(8,128)(2,1)}), bf16[4,32,896]{2,1,0:T(8,128)(2,1)S(1)}, u32[]{:S(2)}, u32[]{:S(2)}) async-start(bf16[4,32,896]{2,1,0:T(8,128)(2,1)} %pack.1), calls=%async_computation | async-start | bytes 458752 | tf_op jit(solution)/shard_map/all_to_all | solution.py:39
  28.7 2.1 all-to-all-done
  31.9 14.8 %all-to-all-start.1 = ((bf16[16,6,896]{2,1,0:T(8,128)(2,1)}), bf16[16,6,896]{2,1,0:T(8,128)(2,1)S(1)}, u32[]{:S(2)}, u32[]{:S(2)}) async-start(bf16[16,6,896]{2,1,0:T(8,128)(2,1)} %reshape.592), calls=%async_computation.1 | async-start | bytes 458752 | tf_op jit(solution)/shard_map/all_to_all | solution.py:39
  47.2 12.1 %all-to-all-done.1 = bf16[16,6,896]{2,1,0:T(8,128)(2,1)S(1)} async-done(((bf16[16,6,896]{2,1,0:T(8,128)(2,1)}), bf16[16,6,896]{2,1,0:T(8,128)(2,1)S(1)}, u32[]{:S(2)}, u32[]{:S(2)}) %all-to-all-start.1) | async-done | bytes 172064 | tf_op jit(solution)/shard_map/all_to_all | solution.py:39
  61.2 8.6 %all-to-all-start.2 = ((bf16[16,32,128]{2,1,0:T(8,128)(2,1)}), bf16[16,32,128]{2,1,0:T(8,128)(2,1)S(1)}, u32[]{:S(2)}, u32[]{:S(2)}) async-start(bf16[16,32,128]{2,1,0:T(8,128)(2,1)} %broadcast_in_dim.73), calls=%async_computation.2 | async-start | bytes 262144 | tf_op jit(solution)/shard_map/all_to_all | solution.py:39
  70.5 12.2 %all-to-all-done.2 = bf16[16,32,128]{2,1,0:T(8,128)(2,1)S(1)} async-done(((bf16[16,32,128]{2,1,0:T(8,128)(2,1)}), bf16[16,32,128]{2,1,0:T(8,128)(2,1)S(1)}, u32[]{:S(2)}, u32[]{:S(2)}) %all-to-all-start.2) | async-done | bytes 131104 | tf_op jit(solution)/shard_map/all_to_all | solution.py:39
  86.0 4.6 %all-to-all-start.3 = ((bf16[16,18,128]{2,1,0:T(8,128)(2,1)}), bf16[16,18,128]{2,1,0:T(8,128)(2,1)S(1)}, u32[]{:S(2)}, u32[]{:S(2)}) async-start(bf16[16,18,128]{2,1,0:T(8,128)(2,1)} %copy.274), calls=%async_computation.3 | async-start | bytes 196608 | tf_op jit(solution)/shard_map/all_to_all | solution.py:39
  91.5 11.6 %all-to-all-done.3 = bf16[16,18,128]{2,1,0:T(8,128)(2,1)S(1)} async-done(((bf16[16,18,128]{2,1,0:T(8,128)(2,1)}), bf16[16,18,128]{2,1,0:T(8,128)(2,1)S(1)}, u32[]{:S(2)}, u32[]{:S(2)}) %all-to-all-start.3) | async-done | bytes 73760 | tf_op jit(solution)/shard_map/all_to_all | solution.py:39
  103.1 7.5 %all-gather.2.cloned.1.call-done = bf16[512,2560]{1,0:T(8,128)(2,1)} async-done(((bf16[32,2560]{1,0:T(8,128)(2,1)}), bf16[512,2560]{1,0:T(8,128)(2,1)}) %all-gather.2.cloned.1.call-update) | async-done | bytes 2621456 | tf_op jit(solution)/shard_map/all_gather | solution.py:159
  112.7 1.5 pad_maximum_fusion.1
  114.1 4.2 %all-to-all-start.4 = ((bf16[4,228,128]{2,1,0:T(8,128)(2,1)}), bf16[4,228,128]{2,1,0:T(8,128)(2,1)S(1)}, u32[]{:S(2)}, u32[]{:S(2)}) async-start(bf16[4,228,128]{2,1,0:T(8,128)(2,1)} %pad_maximum_fusion.1), calls=%async_computation.4 | async-start | bytes 475136 | tf_op jit(solution)/shard_map/all_to_all | solution.py:39
  118.6 5.1 %all-to-all-done.4 = bf16[4,228,128]{2,1,0:T(8,128)(2,1)S(1)} async-done(((bf16[4,228,128]{2,1,0:T(8,128)(2,1)}), bf16[4,228,128]{2,1,0:T(8,128)(2,1)S(1)}, u32[]{:S(2)}, u32[]{:S(2)}) %all-to-all-start.4) | async-done | bytes 233504 | tf_op jit(solution)/shard_map/all_to_all | solution.py:39
  124.7 13.0 %all-to-all-start.5 = ((bf16[8,24,512]{2,1,0:T(8,128)(2,1)}), bf16[8,24,512]{2,1,0:T(8,128)(2,1)S(1)}, u32[]{:S(2)}, u32[]{:S(2)}) async-start(bf16[8,24,512]{2,1,0:T(8,128)(2,1)} %broadcast_in_dim.80), calls=%async_computation.5 | async-start | bytes 393216 | tf_op jit(solution)/shard_map/all_to_all | solution.py:39
  137.9 2.6 %fusion.2 = bf16[8,256,128]{2,1,0:T(8,128)(2,1)} fusion(bf16[8,256,128]{2,1,0:T(8,128)(2,1)} %param.38, bf16[8,48,128]{2,1,0:T(8,128)(2,1)S(1)} %bitcast.167, pred[8,256]{1,0:T(8,128)(4,1)S(1)} %broadcast_compare_fusion, f32[8,48]{1,0:T(8,128)S(1)} %gather_fusion, s32[8,48]{1,0:T(8,128)S(1)} %add_add_fusion, s32[256]{0:T(256)S(1)} %iota_add_fusion), kind=kOutput, calls=%fused_computation.14 | convolution fusion | flops 25886720 | bytes 1153024 | tf_op jit(solution)/shard_map/rca,rae->rce/dot_general | solution.py:268
  140.5 2.6 %fusion.1 = bf16[8,256,128]{2,1,0:T(8,128)(2,1)} fusion(bf16[8,256,128]{2,1,0:T(8,128)(2,1)} %param.37, bf16[8,48,128]{2,1,0:T(8,128)(2,1)S(1)} %bitcast.166, pred[8,256]{1,0:T(8,128)(4,1)S(1)} %broadcast_compare_fusion, f32[8,48]{1,0:T(8,128)S(1)} %gather_fusion, s32[8,48]{1,0:T(8,128)S(1)} %add_add_fusion, s32[256]{0:T(256)S(1)} %iota_add_fusion), kind=kOutput, calls=%fused_computation.13 | convolution fusion | flops 25886720 | bytes 1153024 | tf_op jit(solution)/shard_map/rca,rae->rce/dot_general | solution.py:267
  144.5 8.4 %all_to_all.60 = bf16[4,24,1664]{2,1,0:T(8,128)(2,1)S(1)} all-to-all(bf16[4,24,1664]{2,1,0:T(8,128)(2,1)S(1)} %broadcast_in_dim.83), channel_id=1, replica_groups=mesh['z'=16,'y'=4,'x'=4,'c'=2] {'y'}, dimensions={0} | all-to-all | bytes 638976 | tf_op jit(solution)/shard_map/all_to_all | solution.py:39
  154.2 6.0 %all-to-all-start.7 = ((bf16[8,12,128]{2,1,0:T(8,128)(2,1)}), bf16[8,12,128]{2,1,0:T(8,128)(2,1)S(1)}, u32[]{:S(2)}, u32[]{:S(2)}) async-start(bf16[8,12,128]{2,1,0:T(8,128)(2,1)} %copy.292), calls=%async_computation.7 | async-start | bytes 65536 | tf_op jit(solution)/shard_map/all_to_all | solution.py:39
  160.2 4.7 %all-to-all-done.7 = bf16[8,12,128]{2,1,0:T(8,128)(2,1)S(1)} async-done(((bf16[8,12,128]{2,1,0:T(8,128)(2,1)}), bf16[8,12,128]{2,1,0:T(8,128)(2,1)S(1)}, u32[]{:S(2)}, u32[]{:S(2)}) %all-to-all-start.7) | async-done | bytes 24608 | tf_op jit(solution)/shard_map/all_to_all | solution.py:39
  165.1 21.1 %all_to_all.61 = bf16[16,12,128]{2,1,0:T(8,128)(2,1)S(1)} all-to-all(bf16[16,12,128]{2,1,0:T(8,128)(2,1)S(1)} %broadcast_in_dim.84), channel_id=1, replica_groups=mesh['z'=16,'y'=4,'x'=4,'c'=2] {'z'}, dimensions={0} | all-to-all | bytes 98304 | tf_op jit(solution)/shard_map/all_to_all | solution.py:39
  186.4 15.5 %all_to_all.62.refs_2_ = bf16[16,192,128]{2,1,0:T(8,128)(2,1)} all-to-all(bf16[16,192,128]{2,1,0:T(8,128)(2,1)S(1)} %broadcast_in_dim.86), channel_id=1, replica_groups=mesh['z'=16,'y'=4,'x'=4,'c'=2] {'y','x'}, dimensions={0} | all-to-all | bytes 1572864 | tf_op jit(solution)/shard_map/all_to_all | solution.py:39
  201.9 5.0 %collective-permute-start.3 = (bf16[16,192,128]{2,1,0:T(8,128)(2,1)}, bf16[16,192,128]{2,1,0:T(8,128)(2,1)S(1)}, u32[]{:S(2)}, u32[]{:S(2)}) collective-permute-start(bf16[16,192,128]{2,1,0:T(8,128)(2,1)} %all_to_all.62.refs_2_), channel_id=1, source_target_pairs={{0,1},{1,0},{2,3},{3,2},{4,5},{5,4},{6,7},{7,6},{8,9},{9,8},{10,11... | collective-permute-start | bytes 2359304 | tf_op jit(solution)/shard_map/ppermute | solution.py:303
  207.8 2.8 %head_own.1 = (f32[192,256]{1,0:T(8,128)}, f32[1,256]{1,0:T(1,128)}) custom-call(s32[1]{0:T(128)} %bitcast.refs_0_, f32[8]{0:T(128)} %refs_1_.3, bf16[16,192,128]{2,1,0:T(8,128)(2,1)} %all_to_all.62.refs_2_, f32[16,128]{1,0:T(8,128)} %reshape.611.refs_3_, bf16[2048,256]{1,0:T(8,128)(2,1)} %refs_4_.3), custom_call_target="tpu_custom_call" | custom-call | flops 201326592 | bytes 1835008 | tf_op jit(solution)/shard_map/head_own/pallas_call | solution.py:115
  211.5 2.7 %head_flip.1 = (f32[192,256]{1,0:T(8,128)}, f32[1,256]{1,0:T(1,128)}) custom-call(s32[1]{0:T(128)} %bitcast.refs_0_, f32[8]{0:T(128)} %refs_1_.3, bf16[16,192,128]{2,1,0:T(8,128)(2,1)} %copy-done.1, f32[16,128]{1,0:T(8,128)} %reshape.611.refs_3_, bf16[2048,256]{1,0:T(8,128)(2,1)} %refs_4_.3), custom_call_target="tpu_custom_call" | custom-call | flops 201326592 | bytes 1835008 | tf_op jit(solution)/shard_map/head_flip/pallas_call | solution.py:115
  215.6 3.6 %all-to-all-start.10 = ((f32[32,1,512]{2,1,0:T(1,128)}), f32[32,1,512]{2,1,0:T(1,128)S(1)}, u32[]{:S(2)}, u32[]{:S(2)}) async-start(f32[32,1,512]{2,1,0:T(1,128)} %broadcast_in_dim.153), calls=%async_computation.10 | async-start | bytes 131072 | tf_op jit(solution)/shard_map/all_to_all | solution.py:39
  220.9 5.7 %all-to-all-done.10 = f32[32,1,512]{2,1,0:T(1,128)S(1)} async-done(((f32[32,1,512]{2,1,0:T(1,128)}), f32[32,1,512]{2,1,0:T(1,128)S(1)}, u32[]{:S(2)}, u32[]{:S(2)}) %all-to-all-start.10) | async-done | bytes 65568 | tf_op jit(solution)/shard_map/all_to_all | solution.py:39
  227.2 3.5 %all-to-all-start.11 = ((f32[16,1,512]{2,1,0:T(1,128)}), f32[16,1,512]{2,1,0:T(1,128)S(1)}, u32[]{:S(2)}, u32[]{:S(2)}) async-start(f32[16,1,512]{2,1,0:T(1,128)} %broadcast_in_dim.154), calls=%async_computation.11 | async-start | bytes 65536 | tf_op jit(solution)/shard_map/all_to_all | solution.py:39
  231.7 10.5 %all-to-all-done.11 = f32[16,1,512]{2,1,0:T(1,128)S(1)} async-done(((f32[16,1,512]{2,1,0:T(1,128)}), f32[16,1,512]{2,1,0:T(1,128)S(1)}, u32[]{:S(2)}, u32[]{:S(2)}) %all-to-all-start.11) | async-done | bytes 32800 | tf_op jit(solution)/shard_map/all_to_all | solution.py:39
  (201 shorter events, 24.9 us)
Async XLA Ops:
  7.2 18.2 %copy-start.4 = (bf16[768,32]{0,1:T(8,128)(2,1)S(1)}, bf16[768,32]{0,1:T(8,128)(2,1)}, u32[]{:S(2)}) copy-start(bf16[768,32]{0,1:T(8,128)(2,1)} %param.33) | copy-start | bytes 147460
  7.2 18.2 %copy-start.7 = (bf16[256,32]{0,1:T(8,128)(2,1)S(1)}, bf16[256,32]{0,1:T(8,128)(2,1)}, u32[]{:S(2)}) copy-start(bf16[256,32]{0,1:T(8,128)(2,1)} %param.29) | copy-start | bytes 49156
  7.2 18.2 %copy-start.6 = (bf16[32,768]{1,0:T(8,128)(2,1)S(1)}, bf16[32,768]{1,0:T(8,128)(2,1)}, u32[]{:S(2)}) copy-start(bf16[32,768]{1,0:T(8,128)(2,1)} %param.31) | copy-start | bytes 147460
  7.2 18.2 %copy-start.5 = (bf16[32,768]{1,0:T(8,128)(2,1)S(1)}, bf16[32,768]{1,0:T(8,128)(2,1)}, u32[]{:S(2)}) copy-start(bf16[32,768]{1,0:T(8,128)(2,1)} %param.32) | copy-start | bytes 147460
  7.2 19.0 %copy-start.11 = (s32[8,48]{1,0:T(8,128)S(1)}, s32[8,48]{1,0:T(8,128)}, u32[]{:S(2)}) copy-start(s32[8,48]{1,0:T(8,128)} %param.40) | copy-start | bytes 4612
  7.3 20.6 %copy-start.10 = (s32[8]{0:T(128)S(1)}, s32[8]{0:T(128)}, u32[]{:S(2)}) copy-start(s32[8]{0:T(128)} %param.39) | copy-start | bytes 100
  7.3 20.7 %copy-start.12 = (s32[8]{0:T(128)S(1)}, s32[8]{0:T(128)}, u32[]{:S(2)}) copy-start(s32[8]{0:T(128)} %param.41) | copy-start | bytes 100
  8.7 61.7 %collective-permute-start = (bf16[2,2,256,128]{3,2,1,0:T(8,128)(2,1)S(1)}, bf16[2,2,256,128]{3,2,1,0:T(8,128)(2,1)S(1)}, u32[]{:S(2)}, u32[]{:S(2)}) collective-permute-start(bf16[2,2,256,128]{3,2,1,0:T(8,128)(2,1)S(1)} %get-tuple-element.63), channel_id=1, source_target_pairs={{0,8},{8,16},{16,24},{24,0},{1,9},{9,17},{17,25},{25,1},{2,10},{10... | collective-permute-start | bytes 786440 | tf_op jit(solution)/shard_map/ppermute | solution.py:207
  12.7 57.7 %collective-permute-start.1 = (bf16[2,2,256,128]{3,2,1,0:T(8,128)(2,1)S(1)}, bf16[2,2,256,128]{3,2,1,0:T(8,128)(2,1)S(1)}, u32[]{:S(2)}, u32[]{:S(2)}) collective-permute-start(bf16[2,2,256,128]{3,2,1,0:T(8,128)(2,1)S(1)} %get-tuple-element.64), channel_id=1, source_target_pairs={{0,16},{8,24},{16,0},{24,8},{1,17},{9,25},{17,1},{25,9},{2,18},{10... | collective-permute-start | bytes 786440 | tf_op jit(solution)/shard_map/ppermute | solution.py:207
  17.3 53.1 %collective-permute-start.2 = (bf16[2,2,256,128]{3,2,1,0:T(8,128)(2,1)S(1)}, bf16[2,2,256,128]{3,2,1,0:T(8,128)(2,1)S(1)}, u32[]{:S(2)}, u32[]{:S(2)}) collective-permute-start(bf16[2,2,256,128]{3,2,1,0:T(8,128)(2,1)S(1)} %get-tuple-element.65), channel_id=1, source_target_pairs={{0,24},{8,0},{16,8},{24,16},{1,25},{9,1},{17,9},{25,17},{2,26},{10... | collective-permute-start | bytes 786440 | tf_op jit(solution)/shard_map/ppermute | solution.py:207
  22.0 8.8 %all-to-all-start = ((bf16[4,32,896]{2,1,0:T(8,128)(2,1)}), bf16[4,32,896]{2,1,0:T(8,128)(2,1)S(1)}, u32[]{:S(2)}, u32[]{:S(2)}) async-start(bf16[4,32,896]{2,1,0:T(8,128)(2,1)} %pack.1), calls=%async_computation | async-start | bytes 458752 | tf_op jit(solution)/shard_map/all_to_all | solution.py:39
  25.4 85.3 %all-gather.2.cloned.1.call-start = ((), (), s32[]{:S(2)}) async-start(), calls=%async_computation.12 | async-start | bytes 2785280 | tf_op jit(solution)/shard_map/all_gather | solution.py:159
  26.1 33.5 %copy-start.8 = (f32[128]{0:T(128)S(1)}, f32[128]{0:T(128)}, u32[]{:S(2)}) copy-start(f32[128]{0:T(128)} %param.27) | copy-start | bytes 1540
  26.1 33.9 %copy-start.9 = (f32[128]{0:T(128)S(1)}, f32[128]{0:T(128)}, u32[]{:S(2)}) copy-start(f32[128]{0:T(128)} %param.28) | copy-start | bytes 1540
  31.9 27.4 %all-to-all-start.1 = ((bf16[16,6,896]{2,1,0:T(8,128)(2,1)}), bf16[16,6,896]{2,1,0:T(8,128)(2,1)S(1)}, u32[]{:S(2)}, u32[]{:S(2)}) async-start(bf16[16,6,896]{2,1,0:T(8,128)(2,1)} %reshape.592), calls=%async_computation.1 | async-start | bytes 458752 | tf_op jit(solution)/shard_map/all_to_all | solution.py:39
  59.6 10.8 %copy-start.3 = (f32[6,768]{1,0:T(8,128)}, f32[6,768]{1,0:T(8,128)S(1)}, u32[]{:S(2)}) copy-start(f32[6,768]{1,0:T(8,128)S(1)} %broadcast_multiply_fusion) | copy-start | bytes 55300
  61.2 21.5 %all-to-all-start.2 = ((bf16[16,32,128]{2,1,0:T(8,128)(2,1)}), bf16[16,32,128]{2,1,0:T(8,128)(2,1)S(1)}, u32[]{:S(2)}, u32[]{:S(2)}) async-start(bf16[16,32,128]{2,1,0:T(8,128)(2,1)} %broadcast_in_dim.73), calls=%async_computation.2 | async-start | bytes 262144 | tf_op jit(solution)/shard_map/all_to_all | solution.py:39
  86.0 17.1 %all-to-all-start.3 = ((bf16[16,18,128]{2,1,0:T(8,128)(2,1)}), bf16[16,18,128]{2,1,0:T(8,128)(2,1)S(1)}, u32[]{:S(2)}, u32[]{:S(2)}) async-start(bf16[16,18,128]{2,1,0:T(8,128)(2,1)} %copy.274), calls=%async_computation.3 | async-start | bytes 196608 | tf_op jit(solution)/shard_map/all_to_all | solution.py:39
  110.6 13.2 %copy-start = (bf16[512,2560]{1,0:T(8,128)(2,1)S(1)}, bf16[512,2560]{1,0:T(8,128)(2,1)}, u32[]{:S(2)}) copy-start(bf16[512,2560]{1,0:T(8,128)(2,1)} %all-gather.2.cloned.1.call-done) | copy-start | bytes 7864324
  114.1 9.6 %all-to-all-start.4 = ((bf16[4,228,128]{2,1,0:T(8,128)(2,1)}), bf16[4,228,128]{2,1,0:T(8,128)(2,1)S(1)}, u32[]{:S(2)}, u32[]{:S(2)}) async-start(bf16[4,228,128]{2,1,0:T(8,128)(2,1)} %pad_maximum_fusion.1), calls=%async_computation.4 | async-start | bytes 475136 | tf_op jit(solution)/shard_map/all_to_all | solution.py:39
  124.7 18.9 %all-to-all-start.5 = ((bf16[8,24,512]{2,1,0:T(8,128)(2,1)}), bf16[8,24,512]{2,1,0:T(8,128)(2,1)S(1)}, u32[]{:S(2)}, u32[]{:S(2)}) async-start(bf16[8,24,512]{2,1,0:T(8,128)(2,1)} %broadcast_in_dim.80), calls=%async_computation.5 | async-start | bytes 393216 | tf_op jit(solution)/shard_map/all_to_all | solution.py:39
  154.2 10.8 %all-to-all-start.7 = ((bf16[8,12,128]{2,1,0:T(8,128)(2,1)}), bf16[8,12,128]{2,1,0:T(8,128)(2,1)S(1)}, u32[]{:S(2)}, u32[]{:S(2)}) async-start(bf16[8,12,128]{2,1,0:T(8,128)(2,1)} %copy.292), calls=%async_computation.7 | async-start | bytes 65536 | tf_op jit(solution)/shard_map/all_to_all | solution.py:39
  201.9 8.6 %collective-permute-start.3 = (bf16[16,192,128]{2,1,0:T(8,128)(2,1)}, bf16[16,192,128]{2,1,0:T(8,128)(2,1)S(1)}, u32[]{:S(2)}, u32[]{:S(2)}) collective-permute-start(bf16[16,192,128]{2,1,0:T(8,128)(2,1)} %all_to_all.62.refs_2_), channel_id=1, source_target_pairs={{0,1},{1,0},{2,3},{3,2},{4,5},{5,4},{6,7},{7,6},{8,9},{9,8},{10,11... | collective-permute-start | bytes 2359304 | tf_op jit(solution)/shard_map/ppermute | solution.py:303
  210.6 20.2 %copy-start.2 = (f32[192,256]{1,0:T(8,128)S(1)}, f32[192,256]{1,0:T(8,128)}, u32[]{:S(2)}) copy-start(f32[192,256]{1,0:T(8,128)} %get-tuple-element.20) | copy-start | bytes 589828
  210.6 0.9 copy-start.1
  215.6 10.9 %all-to-all-start.10 = ((f32[32,1,512]{2,1,0:T(1,128)}), f32[32,1,512]{2,1,0:T(1,128)S(1)}, u32[]{:S(2)}, u32[]{:S(2)}) async-start(f32[32,1,512]{2,1,0:T(1,128)} %broadcast_in_dim.153), calls=%async_computation.10 | async-start | bytes 131072 | tf_op jit(solution)/shard_map/all_to_all | solution.py:39
  227.2 15.0 %all-to-all-start.11 = ((f32[16,1,512]{2,1,0:T(1,128)}), f32[16,1,512]{2,1,0:T(1,128)S(1)}, u32[]{:S(2)}, u32[]{:S(2)}) async-start(f32[16,1,512]{2,1,0:T(1,128)} %broadcast_in_dim.154), calls=%async_computation.11 | async-start | bytes 65536 | tf_op jit(solution)/shard_map/all_to_all | solution.py:39
Sparse Core Ops, SparseCore 0:
  28.9 81.7 all-gather.1

commit v6 on v5

--- a/solution.py
+++ b/solution.py
@@ -172,7 +172,16 @@
     scaled = (side_wide * ln1_row).astype(BF)
     partial = lax.dot_general(scaled, proj, (((0,), (0,)), ((), ())), preferred_element_type=F32)
     sent = jnp.concatenate([partial[:96].astype(BF), side.T[:96]], axis=1).reshape(16, 6, 896)
+    caches = jnp.stack([key_cache, value_cache])
+    parts = [
+        lax.dynamic_slice(caches, (0, (y + shift) % 4 * 2, 0, 0), (2, 2, slot_count, 128))
+        for shift in range(4)
+    ]
+    sent, parts = lax.optimization_barrier((sent, parts))
     got = swap(sent, "z")
+    for shift in range(1, 4):
+        parts[shift] = lax.ppermute(parts[shift], "y", [(i, (i + shift) % 4) for i in range(4)])
+    moved = jnp.concatenate(parts, axis=2)
     sums = jnp.sum(got[:, :, :768].astype(F32), axis=0)
     rows = got[:, :, 768:]
     rows_wide = rows.astype(F32)
@@ -197,17 +206,8 @@
         ],
         axis=0,
     ).astype(BF)
-    caches = jnp.stack([key_cache, value_cache])
-    parts = []
-    for shift in range(4):
-        part = lax.dynamic_slice(
-            caches, (0, (y + shift) % 4 * 2, 0, 0), (2, 2, slot_count, 128)
-        )
-        if shift:
-            part = lax.ppermute(part, "y", [(i, (i + shift) % 4) for i in range(4)])
-        parts.append(part)
-    moved = jnp.concatenate(parts, axis=2)
-    gathered, moved = lax.optimization_barrier((spread(block, "z", 16), moved))
+    block, moved = lax.optimization_barrier((block, moved))
+    gathered = spread(block, "z", 16)
     gain_all = gathered[:, 24:30].astype(F32)
     ln2_mine = gain_all[:, 0] + gain_all[:, 1] + gain_all[:, 2]
     ln2_mine = lax.dynamic_slice(ln2_mine, (0, y * 32), (16, 32)).reshape(1, 512)

time: 252 us -> 238 us (0.944)
  waiting for transfers between devices: 72.2 us -> 54.9 us
  starting transfers between devices: 78.3 us -> 81.4 us
    all_to_all x9, waiting for transfers between devices: 64.6 us -> 48 us  [swap(): return lax.all_to_all(values, axis, 0, 0, tiled=True)]
    all_gather x1, waiting for transfers between devices: 7.5 us -> 0.01 us  [on_device(): ffn = lax.all_gather(ffn, 'z', axis=0, tiled=True)]
    ppermute x3, waiting for transfers between devices: 0.01 us -> 6.91 us  [on_device(): lax.ppermute(parts[shift], 'y', [(i, (i + shift) % 4) for i in range(4)])]
    all_to_all x9, starting transfers between devices: 61.7 us -> 65.6 us  [swap(): return lax.all_to_all(values, axis, 0, 0, tiled=True)]
  transfers between devices with their start and end apart: 14 -> 14, of which waited for: 10 -> 9; matrix products, arithmetic and copies ran while one was open for 8% -> 11% of each run, Pallas kernels for 2% -> 1%
where the time goes in v6:
time: 238 us; the launch traced here: 237 us
  starting transfers between devices  81.4 us (34%)
  waiting for transfers between devices  54.9 us (23%)
  blocking collectives  43.1 us (18%)
  between operations  14.9 us (6%)
  local copies, waits for them, and re-layouts  13.3 us (6%)
  other arithmetic  12.1 us (5%)
  matrix products  9.8 us (4%)
  Pallas kernels  7.3 us (3%)
    all_to_all x9, starting transfers between devices, swap(): return lax.all_to_all(values, axis, 0, 0, tiled=True)  65.6 us
    all_to_all x9, waiting for transfers between devices, swap(): return lax.all_to_all(values, axis, 0, 0, tiled=True)  48 us
    all_to_all x3, blocking collectives, swap(): return lax.all_to_all(values, axis, 0, 0, tiled=True)  43.1 us
    ppermute x3, starting transfers between devices, on_device(): lax.ppermute(parts[shift], 'y', [(i, (i + shift) % 4) for i in range(4)])  10.8 us
    ppermute x3, waiting for transfers between devices, on_device(): lax.ppermute(parts[shift], 'y', [(i, (i + shift) % 4) for i in range(4)])  6.91 us
    pallas_call x2, Pallas kernels, head(): pl.pallas_call(lambda *refs: head_kernel(*refs, flip=flip, width=2048), o...  5.52 us
    ppermute x1, starting transfers between devices, on_device(): other = lax.ppermute(half, 'c', [(0, 1), (1, 0)])  5.02 us
  transfers between devices with their start and end apart: 14, of which 9 were waited for; matrix products, arithmetic and copies ran while one was open for 11% of the time, Pallas kernels for 1%

profile of v6, /device:TPU:1, one launch (start us, length us, event | category | flops | bytes accessed | tf_op | source)
XLA Modules:
  0.0 236.9 jit_solution(17187310822385603339)
XLA Ops:
  7.2 1.8 pack.1
  9.0 5.0 %all-to-all-start = ((bf16[4,32,896]{2,1,0:T(8,128)(2,1)}), bf16[4,32,896]{2,1,0:T(8,128)(2,1)S(1)}, u32[]{:S(2)}, u32[]{:S(2)}) async-start(bf16[4,32,896]{2,1,0:T(8,128)(2,1)} %pack.1), calls=%async_computation | async-start | bytes 458752 | tf_op jit(solution)/shard_map/all_to_all | solution.py:39
  14.0 1.5 pad_maximum_fusion.3
  15.6 1.4 fusion.4
  20.9 14.9 %all-to-all-start.1 = ((bf16[16,6,896]{2,1,0:T(8,128)(2,1)}), bf16[16,6,896]{2,1,0:T(8,128)(2,1)S(1)}, u32[]{:S(2)}, u32[]{:S(2)}) async-start(bf16[16,6,896]{2,1,0:T(8,128)(2,1)} %reshape.547), calls=%async_computation.1 | async-start | bytes 458752 | tf_op jit(solution)/shard_map/all_to_all | solution.py:39
  35.8 3.4 %collective-permute-start = (bf16[2,2,256,128]{3,2,1,0:T(8,128)(2,1)S(1)}, bf16[2,2,256,128]{3,2,1,0:T(8,128)(2,1)S(1)}, u32[]{:S(2)}, u32[]{:S(2)}) collective-permute-start(bf16[2,2,256,128]{3,2,1,0:T(8,128)(2,1)S(1)} %get-tuple-element.22), channel_id=1, source_target_pairs={{0,8},{8,16},{16,24},{24,0},{1,9},{9,17},{17,25},{25,1},{2,10},{10... | collective-permute-start | bytes 786440 | tf_op jit(solution)/shard_map/ppermute | solution.py:183
  39.2 4.3 %collective-permute-start.1 = (bf16[2,2,256,128]{3,2,1,0:T(8,128)(2,1)S(1)}, bf16[2,2,256,128]{3,2,1,0:T(8,128)(2,1)S(1)}, u32[]{:S(2)}, u32[]{:S(2)}) collective-permute-start(bf16[2,2,256,128]{3,2,1,0:T(8,128)(2,1)S(1)} %get-tuple-element.23), channel_id=1, source_target_pairs={{0,16},{8,24},{16,0},{24,8},{1,17},{9,25},{17,1},{25,9},{2,18},{10... | collective-permute-start | bytes 786440 | tf_op jit(solution)/shard_map/ppermute | solution.py:183
  43.5 3.1 %collective-permute-start.2 = (bf16[2,2,256,128]{3,2,1,0:T(8,128)(2,1)S(1)}, bf16[2,2,256,128]{3,2,1,0:T(8,128)(2,1)S(1)}, u32[]{:S(2)}, u32[]{:S(2)}) collective-permute-start(bf16[2,2,256,128]{3,2,1,0:T(8,128)(2,1)S(1)} %get-tuple-element.24), channel_id=1, source_target_pairs={{0,24},{8,0},{16,8},{24,16},{1,25},{9,1},{17,9},{25,17},{2,26},{10... | collective-permute-start | bytes 786440 | tf_op jit(solution)/shard_map/ppermute | solution.py:183
  47.0 5.1 %collective-permute-done.1 = bf16[2,2,256,128]{3,2,1,0:T(8,128)(2,1)S(1)} collective-permute-done((bf16[2,2,256,128]{3,2,1,0:T(8,128)(2,1)S(1)}, bf16[2,2,256,128]{3,2,1,0:T(8,128)(2,1)S(1)}, u32[]{:S(2)}, u32[]{:S(2)}) %collective-permute-start.1) | collective-permute-done | bytes 262176 | tf_op jit(solution)/shard_map/ppermute | solution.py:183
  52.0 1.8 collective-permute-done.2
  57.2 11.4 %all-to-all-start.2 = ((bf16[16,32,128]{2,1,0:T(8,128)(2,1)}), bf16[16,32,128]{2,1,0:T(8,128)(2,1)S(1)}, u32[]{:S(2)}, u32[]{:S(2)}) async-start(bf16[16,32,128]{2,1,0:T(8,128)(2,1)} %broadcast_in_dim.73), calls=%async_computation.2 | async-start | bytes 262144 | tf_op jit(solution)/shard_map/all_to_all | solution.py:39
  71.8 9.2 %all-to-all-done.2 = bf16[16,32,128]{2,1,0:T(8,128)(2,1)S(1)} async-done(((bf16[16,32,128]{2,1,0:T(8,128)(2,1)}), bf16[16,32,128]{2,1,0:T(8,128)(2,1)S(1)}, u32[]{:S(2)}, u32[]{:S(2)}) %all-to-all-start.2) | async-done | bytes 131104 | tf_op jit(solution)/shard_map/all_to_all | solution.py:39
  84.4 6.3 %all-to-all-start.3 = ((bf16[16,18,128]{2,1,0:T(8,128)(2,1)}), bf16[16,18,128]{2,1,0:T(8,128)(2,1)S(1)}, u32[]{:S(2)}, u32[]{:S(2)}) async-start(bf16[16,18,128]{2,1,0:T(8,128)(2,1)} %copy.274), calls=%async_computation.3 | async-start | bytes 196608 | tf_op jit(solution)/shard_map/all_to_all | solution.py:39
  91.0 12.2 %all-to-all-done.3 = bf16[16,18,128]{2,1,0:T(8,128)(2,1)S(1)} async-done(((bf16[16,18,128]{2,1,0:T(8,128)(2,1)}), bf16[16,18,128]{2,1,0:T(8,128)(2,1)S(1)}, u32[]{:S(2)}, u32[]{:S(2)}) %all-to-all-start.3) | async-done | bytes 73760 | tf_op jit(solution)/shard_map/all_to_all | solution.py:39
  105.3 5.1 %all-to-all-start.4 = ((bf16[4,228,128]{2,1,0:T(8,128)(2,1)}), bf16[4,228,128]{2,1,0:T(8,128)(2,1)S(1)}, u32[]{:S(2)}, u32[]{:S(2)}) async-start(bf16[4,228,128]{2,1,0:T(8,128)(2,1)} %pad_maximum_fusion.1), calls=%async_computation.4 | async-start | bytes 475136 | tf_op jit(solution)/shard_map/all_to_all | solution.py:39
  110.7 5.1 %all-to-all-done.4 = bf16[4,228,128]{2,1,0:T(8,128)(2,1)S(1)} async-done(((bf16[4,228,128]{2,1,0:T(8,128)(2,1)}), bf16[4,228,128]{2,1,0:T(8,128)(2,1)S(1)}, u32[]{:S(2)}, u32[]{:S(2)}) %all-to-all-start.4) | async-done | bytes 233504 | tf_op jit(solution)/shard_map/all_to_all | solution.py:39
  116.8 9.7 %all-to-all-start.5 = ((bf16[8,24,512]{2,1,0:T(8,128)(2,1)}), bf16[8,24,512]{2,1,0:T(8,128)(2,1)S(1)}, u32[]{:S(2)}, u32[]{:S(2)}) async-start(bf16[8,24,512]{2,1,0:T(8,128)(2,1)} %broadcast_in_dim.80), calls=%async_computation.5 | async-start | bytes 393216 | tf_op jit(solution)/shard_map/all_to_all | solution.py:39
  126.6 2.6 %fusion.2 = bf16[8,256,128]{2,1,0:T(8,128)(2,1)} fusion(bf16[8,256,128]{2,1,0:T(8,128)(2,1)} %param.38, bf16[8,48,128]{2,1,0:T(8,128)(2,1)S(1)} %bitcast.167, pred[8,256]{1,0:T(8,128)(4,1)S(1)} %broadcast_compare_fusion, f32[8,48]{1,0:T(8,128)S(1)} %gather_fusion, s32[8,48]{1,0:T(8,128)S(1)} %add_add_fusion, s32[256]{0:T(256)S(1)} %iota_add_fusion), kind=kOutput, calls=%fused_computation.14 | convolution fusion | flops 25886720 | bytes 1153024 | tf_op jit(solution)/shard_map/rca,rae->rce/dot_general | solution.py:268
  129.2 2.6 %fusion.1 = bf16[8,256,128]{2,1,0:T(8,128)(2,1)} fusion(bf16[8,256,128]{2,1,0:T(8,128)(2,1)} %param.37, bf16[8,48,128]{2,1,0:T(8,128)(2,1)S(1)} %bitcast.166, pred[8,256]{1,0:T(8,128)(4,1)S(1)} %broadcast_compare_fusion, f32[8,48]{1,0:T(8,128)S(1)} %gather_fusion, s32[8,48]{1,0:T(8,128)S(1)} %add_add_fusion, s32[256]{0:T(256)S(1)} %iota_add_fusion), kind=kOutput, calls=%fused_computation.13 | convolution fusion | flops 25886720 | bytes 1153024 | tf_op jit(solution)/shard_map/rca,rae->rce/dot_general | solution.py:267
  133.2 8.4 %all_to_all.60 = bf16[4,24,1664]{2,1,0:T(8,128)(2,1)S(1)} all-to-all(bf16[4,24,1664]{2,1,0:T(8,128)(2,1)S(1)} %broadcast_in_dim.83), channel_id=1, replica_groups=mesh['z'=16,'y'=4,'x'=4,'c'=2] {'y'}, dimensions={0} | all-to-all | bytes 638976 | tf_op jit(solution)/shard_map/all_to_all | solution.py:39
  142.9 6.0 %all-to-all-start.7 = ((bf16[8,12,128]{2,1,0:T(8,128)(2,1)}), bf16[8,12,128]{2,1,0:T(8,128)(2,1)S(1)}, u32[]{:S(2)}, u32[]{:S(2)}) async-start(bf16[8,12,128]{2,1,0:T(8,128)(2,1)} %copy.292), calls=%async_computation.7 | async-start | bytes 65536 | tf_op jit(solution)/shard_map/all_to_all | solution.py:39
  149.0 4.7 %all-to-all-done.7 = bf16[8,12,128]{2,1,0:T(8,128)(2,1)S(1)} async-done(((bf16[8,12,128]{2,1,0:T(8,128)(2,1)}), bf16[8,12,128]{2,1,0:T(8,128)(2,1)S(1)}, u32[]{:S(2)}, u32[]{:S(2)}) %all-to-all-start.7) | async-done | bytes 24608 | tf_op jit(solution)/shard_map/all_to_all | solution.py:39
  153.8 19.2 %all_to_all.61 = bf16[16,12,128]{2,1,0:T(8,128)(2,1)S(1)} all-to-all(bf16[16,12,128]{2,1,0:T(8,128)(2,1)S(1)} %broadcast_in_dim.84), channel_id=1, replica_groups=mesh['z'=16,'y'=4,'x'=4,'c'=2] {'z'}, dimensions={0} | all-to-all | bytes 98304 | tf_op jit(solution)/shard_map/all_to_all | solution.py:39
  173.2 15.5 %all_to_all.62.refs_2_ = bf16[16,192,128]{2,1,0:T(8,128)(2,1)} all-to-all(bf16[16,192,128]{2,1,0:T(8,128)(2,1)S(1)} %broadcast_in_dim.86), channel_id=1, replica_groups=mesh['z'=16,'y'=4,'x'=4,'c'=2] {'y','x'}, dimensions={0} | all-to-all | bytes 1572864 | tf_op jit(solution)/shard_map/all_to_all | solution.py:39
  188.7 5.0 %collective-permute-start.3 = (bf16[16,192,128]{2,1,0:T(8,128)(2,1)}, bf16[16,192,128]{2,1,0:T(8,128)(2,1)S(1)}, u32[]{:S(2)}, u32[]{:S(2)}) collective-permute-start(bf16[16,192,128]{2,1,0:T(8,128)(2,1)} %all_to_all.62.refs_2_), channel_id=1, source_target_pairs={{0,1},{1,0},{2,3},{3,2},{4,5},{5,4},{6,7},{7,6},{8,9},{9,8},{10,11... | collective-permute-start | bytes 2359304 | tf_op jit(solution)/shard_map/ppermute | solution.py:303
  194.5 2.8 %head_own.1 = (f32[192,256]{1,0:T(8,128)}, f32[1,256]{1,0:T(1,128)}) custom-call(s32[1]{0:T(128)} %bitcast.refs_0_, f32[8]{0:T(128)} %refs_1_.3, bf16[16,192,128]{2,1,0:T(8,128)(2,1)} %all_to_all.62.refs_2_, f32[16,128]{1,0:T(8,128)} %reshape.566.refs_3_, bf16[2048,256]{1,0:T(8,128)(2,1)} %refs_4_.3), custom_call_target="tpu_custom_call" | custom-call | flops 201326592 | bytes 1835008 | tf_op jit(solution)/shard_map/head_own/pallas_call | solution.py:115
  198.2 2.7 %head_flip.1 = (f32[192,256]{1,0:T(8,128)}, f32[1,256]{1,0:T(1,128)}) custom-call(s32[1]{0:T(128)} %bitcast.refs_0_, f32[8]{0:T(128)} %refs_1_.3, bf16[16,192,128]{2,1,0:T(8,128)(2,1)} %copy-done.1, f32[16,128]{1,0:T(8,128)} %reshape.566.refs_3_, bf16[2048,256]{1,0:T(8,128)(2,1)} %refs_4_.3), custom_call_target="tpu_custom_call" | custom-call | flops 201326592 | bytes 1835008 | tf_op jit(solution)/shard_map/head_flip/pallas_call | solution.py:115
  202.3 3.6 %all-to-all-start.10 = ((f32[32,1,512]{2,1,0:T(1,128)}), f32[32,1,512]{2,1,0:T(1,128)S(1)}, u32[]{:S(2)}, u32[]{:S(2)}) async-start(f32[32,1,512]{2,1,0:T(1,128)} %broadcast_in_dim.153), calls=%async_computation.10 | async-start | bytes 131072 | tf_op jit(solution)/shard_map/all_to_all | solution.py:39
  207.6 5.7 %all-to-all-done.10 = f32[32,1,512]{2,1,0:T(1,128)S(1)} async-done(((f32[32,1,512]{2,1,0:T(1,128)}), f32[32,1,512]{2,1,0:T(1,128)S(1)}, u32[]{:S(2)}, u32[]{:S(2)}) %all-to-all-start.10) | async-done | bytes 65568 | tf_op jit(solution)/shard_map/all_to_all | solution.py:39
  214.0 3.5 %all-to-all-start.11 = ((f32[16,1,512]{2,1,0:T(1,128)}), f32[16,1,512]{2,1,0:T(1,128)S(1)}, u32[]{:S(2)}, u32[]{:S(2)}) async-start(f32[16,1,512]{2,1,0:T(1,128)} %broadcast_in_dim.154), calls=%async_computation.11 | async-start | bytes 65536 | tf_op jit(solution)/shard_map/all_to_all | solution.py:39
  217.5 1.0 broadcast_select_fusion.1
  218.5 10.5 %all-to-all-done.11 = f32[16,1,512]{2,1,0:T(1,128)S(1)} async-done(((f32[16,1,512]{2,1,0:T(1,128)}), f32[16,1,512]{2,1,0:T(1,128)S(1)}, u32[]{:S(2)}, u32[]{:S(2)}) %all-to-all-start.11) | async-done | bytes 32800 | tf_op jit(solution)/shard_map/all_to_all | solution.py:39
  (198 shorter events, 26.8 us)
Async XLA Ops:
  7.2 11.5 %copy-start.9 = (s32[8]{0:T(128)S(1)}, s32[8]{0:T(128)}, u32[]{:S(2)}) copy-start(s32[8]{0:T(128)} %param.39) | copy-start | bytes 100
  7.2 12.4 %copy-start.3 = (bf16[8,256,128]{2,1,0:T(8,128)(2,1)S(1)}, bf16[8,256,128]{2,1,0:T(8,128)(2,1)}, u32[]{:S(2)}) copy-start(bf16[8,256,128]{2,1,0:T(8,128)(2,1)} %param.37) | copy-start | bytes 1572868
  7.2 12.4 %copy-start.2 = (bf16[8,256,128]{2,1,0:T(8,128)(2,1)S(1)}, bf16[8,256,128]{2,1,0:T(8,128)(2,1)}, u32[]{:S(2)}) copy-start(bf16[8,256,128]{2,1,0:T(8,128)(2,1)} %param.38) | copy-start | bytes 1572868
  9.0 10.7 %all-to-all-start = ((bf16[4,32,896]{2,1,0:T(8,128)(2,1)}), bf16[4,32,896]{2,1,0:T(8,128)(2,1)S(1)}, u32[]{:S(2)}, u32[]{:S(2)}) async-start(bf16[4,32,896]{2,1,0:T(8,128)(2,1)} %pack.1), calls=%async_computation | async-start | bytes 458752 | tf_op jit(solution)/shard_map/all_to_all | solution.py:39
  14.0 89.2 %all-gather.2.cloned.1.call-start = ((), (), s32[]{:S(2)}) async-start(), calls=%async_computation.12 | async-start | bytes 2785280 | tf_op jit(solution)/shard_map/all_gather | solution.py:159
  19.4 27.3 %copy-start.5 = (f32[64]{0:T(128)}, f32[64]{0:T(128)S(1)}, u32[]{:S(2)}) copy-start(f32[64]{0:T(128)S(1)} %multiply_power_fusion) | copy-start | bytes 772
  19.6 16.2 %copy-start.10 = (s32[8]{0:T(128)S(1)}, s32[8]{0:T(128)}, u32[]{:S(2)}) copy-start(s32[8]{0:T(128)} %param.41) | copy-start | bytes 100
  20.9 33.1 %all-to-all-start.1 = ((bf16[16,6,896]{2,1,0:T(8,128)(2,1)}), bf16[16,6,896]{2,1,0:T(8,128)(2,1)S(1)}, u32[]{:S(2)}, u32[]{:S(2)}) async-start(bf16[16,6,896]{2,1,0:T(8,128)(2,1)} %reshape.547), calls=%async_computation.1 | async-start | bytes 458752 | tf_op jit(solution)/shard_map/all_to_all | solution.py:39
  35.8 11.1 %collective-permute-start = (bf16[2,2,256,128]{3,2,1,0:T(8,128)(2,1)S(1)}, bf16[2,2,256,128]{3,2,1,0:T(8,128)(2,1)S(1)}, u32[]{:S(2)}, u32[]{:S(2)}) collective-permute-start(bf16[2,2,256,128]{3,2,1,0:T(8,128)(2,1)S(1)} %get-tuple-element.22), channel_id=1, source_target_pairs={{0,8},{8,16},{16,24},{24,0},{1,9},{9,17},{17,25},{25,1},{2,10},{10... | collective-permute-start | bytes 786440 | tf_op jit(solution)/shard_map/ppermute | solution.py:183
  39.2 12.8 %collective-permute-start.1 = (bf16[2,2,256,128]{3,2,1,0:T(8,128)(2,1)S(1)}, bf16[2,2,256,128]{3,2,1,0:T(8,128)(2,1)S(1)}, u32[]{:S(2)}, u32[]{:S(2)}) collective-permute-start(bf16[2,2,256,128]{3,2,1,0:T(8,128)(2,1)S(1)} %get-tuple-element.23), channel_id=1, source_target_pairs={{0,16},{8,24},{16,0},{24,8},{1,17},{9,25},{17,1},{25,9},{2,18},{10... | collective-permute-start | bytes 786440 | tf_op jit(solution)/shard_map/ppermute | solution.py:183
  43.5 10.4 %collective-permute-start.2 = (bf16[2,2,256,128]{3,2,1,0:T(8,128)(2,1)S(1)}, bf16[2,2,256,128]{3,2,1,0:T(8,128)(2,1)S(1)}, u32[]{:S(2)}, u32[]{:S(2)}) collective-permute-start(bf16[2,2,256,128]{3,2,1,0:T(8,128)(2,1)S(1)} %get-tuple-element.24), channel_id=1, source_target_pairs={{0,24},{8,0},{16,8},{24,16},{1,25},{9,1},{17,9},{25,17},{2,26},{10... | collective-permute-start | bytes 786440 | tf_op jit(solution)/shard_map/ppermute | solution.py:183
  46.7 5.3 %copy-start.7 = (f32[6]{0:T(128)}, f32[6]{0:T(128)S(1)}, u32[]{:S(2)}) copy-start(f32[6]{0:T(128)S(1)} %dynamic-slice_convert_fusion) | copy-start | bytes 76
  46.9 8.2 %copy-start.6 = (f32[64]{0:T(128)S(1)}, f32[64]{0:T(128)}, u32[]{:S(2)}) copy-start(f32[64]{0:T(128)} %copy-done.5) | copy-start | bytes 772
  53.9 1.2 copy-start.8
  57.2 23.8 %all-to-all-start.2 = ((bf16[16,32,128]{2,1,0:T(8,128)(2,1)}), bf16[16,32,128]{2,1,0:T(8,128)(2,1)S(1)}, u32[]{:S(2)}, u32[]{:S(2)}) async-start(bf16[16,32,128]{2,1,0:T(8,128)(2,1)} %broadcast_in_dim.73), calls=%async_computation.2 | async-start | bytes 262144 | tf_op jit(solution)/shard_map/all_to_all | solution.py:39
  84.4 18.9 %all-to-all-start.3 = ((bf16[16,18,128]{2,1,0:T(8,128)(2,1)}), bf16[16,18,128]{2,1,0:T(8,128)(2,1)S(1)}, u32[]{:S(2)}, u32[]{:S(2)}) async-start(bf16[16,18,128]{2,1,0:T(8,128)(2,1)} %copy.274), calls=%async_computation.3 | async-start | bytes 196608 | tf_op jit(solution)/shard_map/all_to_all | solution.py:39
  103.2 12.7 %copy-start = (bf16[512,2560]{1,0:T(8,128)(2,1)S(1)}, bf16[512,2560]{1,0:T(8,128)(2,1)}, u32[]{:S(2)}) copy-start(bf16[512,2560]{1,0:T(8,128)(2,1)} %all-gather.2.cloned.1.call-done) | copy-start | bytes 7864324
  105.3 10.5 %all-to-all-start.4 = ((bf16[4,228,128]{2,1,0:T(8,128)(2,1)}), bf16[4,228,128]{2,1,0:T(8,128)(2,1)S(1)}, u32[]{:S(2)}, u32[]{:S(2)}) async-start(bf16[4,228,128]{2,1,0:T(8,128)(2,1)} %pad_maximum_fusion.1), calls=%async_computation.4 | async-start | bytes 475136 | tf_op jit(solution)/shard_map/all_to_all | solution.py:39
  116.8 15.6 %all-to-all-start.5 = ((bf16[8,24,512]{2,1,0:T(8,128)(2,1)}), bf16[8,24,512]{2,1,0:T(8,128)(2,1)S(1)}, u32[]{:S(2)}, u32[]{:S(2)}) async-start(bf16[8,24,512]{2,1,0:T(8,128)(2,1)} %broadcast_in_dim.80), calls=%async_computation.5 | async-start | bytes 393216 | tf_op jit(solution)/shard_map/all_to_all | solution.py:39
  142.9 10.8 %all-to-all-start.7 = ((bf16[8,12,128]{2,1,0:T(8,128)(2,1)}), bf16[8,12,128]{2,1,0:T(8,128)(2,1)S(1)}, u32[]{:S(2)}, u32[]{:S(2)}) async-start(bf16[8,12,128]{2,1,0:T(8,128)(2,1)} %copy.292), calls=%async_computation.7 | async-start | bytes 65536 | tf_op jit(solution)/shard_map/all_to_all | solution.py:39
  188.7 8.6 %collective-permute-start.3 = (bf16[16,192,128]{2,1,0:T(8,128)(2,1)}, bf16[16,192,128]{2,1,0:T(8,128)(2,1)S(1)}, u32[]{:S(2)}, u32[]{:S(2)}) collective-permute-start(bf16[16,192,128]{2,1,0:T(8,128)(2,1)} %all_to_all.62.refs_2_), channel_id=1, source_target_pairs={{0,1},{1,0},{2,3},{3,2},{4,5},{5,4},{6,7},{7,6},{8,9},{9,8},{10,11... | collective-permute-start | bytes 2359304 | tf_op jit(solution)/shard_map/ppermute | solution.py:303
  197.3 20.2 %copy-start.4 = (f32[192,256]{1,0:T(8,128)S(1)}, f32[192,256]{1,0:T(8,128)}, u32[]{:S(2)}) copy-start(f32[192,256]{1,0:T(8,128)} %get-tuple-element.30) | copy-start | bytes 589828
  197.3 0.9 copy-start.1
  202.3 10.9 %all-to-all-start.10 = ((f32[32,1,512]{2,1,0:T(1,128)}), f32[32,1,512]{2,1,0:T(1,128)S(1)}, u32[]{:S(2)}, u32[]{:S(2)}) async-start(f32[32,1,512]{2,1,0:T(1,128)} %broadcast_in_dim.153), calls=%async_computation.10 | async-start | bytes 131072 | tf_op jit(solution)/shard_map/all_to_all | solution.py:39
  214.0 15.0 %all-to-all-start.11 = ((f32[16,1,512]{2,1,0:T(1,128)}), f32[16,1,512]{2,1,0:T(1,128)S(1)}, u32[]{:S(2)}, u32[]{:S(2)}) async-start(f32[16,1,512]{2,1,0:T(1,128)} %broadcast_in_dim.154), calls=%async_computation.11 | async-start | bytes 65536 | tf_op jit(solution)/shard_map/all_to_all | solution.py:39
Sparse Core Ops, SparseCore 0:
  17.5 82.2 all-gather.1

commit v7 on v6

--- a/solution.py
+++ b/solution.py
@@ -181,7 +181,6 @@
     got = swap(sent, "z")
     for shift in range(1, 4):
         parts[shift] = lax.ppermute(parts[shift], "y", [(i, (i + shift) % 4) for i in range(4)])
-    moved = jnp.concatenate(parts, axis=2)
     sums = jnp.sum(got[:, :, :768].astype(F32), axis=0)
     rows = got[:, :, 768:]
     rows_wide = rows.astype(F32)
@@ -206,8 +205,8 @@
         ],
         axis=0,
     ).astype(BF)
-    block, moved = lax.optimization_barrier((block, moved))
-    gathered = spread(block, "z", 16)
+    block, parts[1], parts[3] = lax.optimization_barrier((block, parts[1], parts[3]))
+    gathered, moved = lax.optimization_barrier((spread(block, "z", 16), jnp.concatenate(parts, axis=2)))
     gain_all = gathered[:, 24:30].astype(F32)
     ln2_mine = gain_all[:, 0] + gain_all[:, 1] + gain_all[:, 2]
     ln2_mine = lax.dynamic_slice(ln2_mine, (0, y * 32), (16, 32)).reshape(1, 512)
@@ -247,8 +246,7 @@
         return jnp.swapaxes(values.reshape((2, 2, 8, 6) + rest), 1, 2).reshape((16, 2, 6) + rest)
 
     outgoing = pack_state(by_z(peak), by_z(mass), by_z(weighted))
-    arrived, ffn = lax.optimization_barrier((swap(outgoing, "z"), ffn))
-    mass, weighted = merge_state(arrived)
+    mass, weighted = merge_state(swap(outgoing, "z"))
     my_gate = jnp.swapaxes(outgate.reshape(6, 2, 128), 0, 1).astype(F32)
     gated = (weighted / mass[..., None] * my_gate).astype(BF).reshape(12, 128)
     residual = jnp.transpose(rows.reshape(4, 4, 6, 4, 32), (3, 0, 2, 1, 4)).reshape(4, 24, 128)
@@ -256,8 +254,17 @@
     both = swap(jnp.concatenate([residual, jnp.broadcast_to(same[None], (4, 204, 128))], axis=1), "y")
     hidden_rows = jnp.swapaxes(both[:, :24].reshape(4, 4, 6, 128), 1, 2).reshape(24, 512)
     gated = jnp.swapaxes(both[:, 24:36].reshape(4, 2, 6, 128), 0, 1).reshape(2, 24, 128)
-    tree_keys = both[:, 36:132].reshape(requests, tree, 128)
-    tree_values = both[:, 132:].reshape(requests, tree, 128)
+
+    contract = (((1,), (1,)), ((), ()))
+    attn = lax.dot_general(
+        jnp.concatenate([gated[0], gated[1]], axis=1),
+        ffn[:, 2304:],
+        contract,
+        preferred_element_type=F32,
+    )
+    attn, fresh = lax.optimization_barrier((attn.astype(BF), both[:, 36:]))
+    tree_keys = fresh[:, :96].reshape(requests, tree, 128)
+    tree_values = fresh[:, 96:].reshape(requests, tree, 128)
 
     slot_ids = seq * slot_count + jnp.arange(slot_count, dtype=jnp.int32)
     accepted_rows = links[jnp.arange(requests), accepted]
@@ -269,15 +276,8 @@
     updated_keys = jnp.where(hits, moved_keys, key_cache)
     updated_values = jnp.where(hits, moved_values, value_cache)
 
-    contract = (((1,), (1,)), ((), ()))
-    attn = lax.dot_general(
-        jnp.concatenate([gated[0], gated[1]], axis=1),
-        ffn[:, 2304:],
-        contract,
-        preferred_element_type=F32,
-    )
     attn, updated_keys, updated_values = lax.optimization_barrier(
-        (spread(attn.astype(BF), ("x", "c"), 8), updated_keys, updated_values)
+        (spread(attn, ("x", "c"), 8), updated_keys, updated_values)
     )
     attn = jnp.sum(attn.astype(F32), axis=0)
     middle = (hidden_rows.astype(F32) + attn).astype(BF)

time: 238 us -> 230 us (0.966)
  waiting for transfers between devices: 54.9 us -> 48.6 us
  blocking collectives: 43.1 us -> 38.8 us
  starting transfers between devices: 81.4 us -> 85.4 us
    all_to_all x3, blocking collectives: 43.1 us -> 38.8 us  [swap(): return lax.all_to_all(values, axis, 0, 0, tiled=True)]
    ppermute x3, waiting for transfers between devices: 6.91 us -> 3.66 us  [on_device(): lax.ppermute(parts[shift], 'y', [(i, (i + shift) % 4) for i in range(4)])]
    all_to_all x9, waiting for transfers between devices: 48 us -> 44.9 us  [swap(): return lax.all_to_all(values, axis, 0, 0, tiled=True)]
  transfers between devices with their start and end apart: 14 -> 14, of which waited for: 9 -> 10; matrix products, arithmetic and copies ran while one was open for 11% -> 11% of each run, Pallas kernels for 1% -> 1%
where the time goes in v7:
time: 230 us; the launch traced here: 229 us
  starting transfers between devices  85.4 us (37%)
  waiting for transfers between devices  48.6 us (21%)
  blocking collectives  38.8 us (17%)
  between operations  14.9 us (6%)
  local copies, waits for them, and re-layouts  12.3 us (5%)
  matrix products  11.2 us (5%)
  other arithmetic  10.2 us (4%)
  Pallas kernels  7.31 us (3%)
    all_to_all x9, starting transfers between devices, swap(): return lax.all_to_all(values, axis, 0, 0, tiled=True)  67.2 us
    all_to_all x9, waiting for transfers between devices, swap(): return lax.all_to_all(values, axis, 0, 0, tiled=True)  44.9 us
    all_to_all x3, blocking collectives, swap(): return lax.all_to_all(values, axis, 0, 0, tiled=True)  38.8 us
    ppermute x3, starting transfers between devices, on_device(): lax.ppermute(parts[shift], 'y', [(i, (i + shift) % 4) for i in range(4)])  13.1 us
    pallas_call x2, Pallas kernels, head(): pl.pallas_call(lambda *refs: head_kernel(*refs, flip=flip, width=2048), o...  5.52 us
    ppermute x1, starting transfers between devices, on_device(): other = lax.ppermute(half, 'c', [(0, 1), (1, 0)])  5.02 us
  transfers between devices with their start and end apart: 14, of which 10 were waited for; matrix products, arithmetic and copies ran while one was open for 11% of the time, Pallas kernels for 1%

profile of v7, /device:TPU:1, one launch (start us, length us, event | category | flops | bytes accessed | tf_op | source)
XLA Modules:
  0.0 228.7 jit_solution(4143087875533894437)
XLA Ops:
  7.2 1.8 pack.1
  9.0 5.0 %all-to-all-start = ((bf16[4,32,896]{2,1,0:T(8,128)(2,1)}), bf16[4,32,896]{2,1,0:T(8,128)(2,1)S(1)}, u32[]{:S(2)}, u32[]{:S(2)}) async-start(bf16[4,32,896]{2,1,0:T(8,128)(2,1)} %pack.1), calls=%async_computation | async-start | bytes 458752 | tf_op jit(solution)/shard_map/all_to_all | solution.py:39
  14.0 1.5 pad_maximum_fusion.3
  15.7 1.4 fusion.4
  20.5 14.9 %all-to-all-start.1 = ((bf16[16,6,896]{2,1,0:T(8,128)(2,1)}), bf16[16,6,896]{2,1,0:T(8,128)(2,1)S(1)}, u32[]{:S(2)}, u32[]{:S(2)}) async-start(bf16[16,6,896]{2,1,0:T(8,128)(2,1)} %reshape.547), calls=%async_computation.1 | async-start | bytes 458752 | tf_op jit(solution)/shard_map/all_to_all | solution.py:39
  35.9 3.1 %collective-permute-start = (bf16[2,2,256,128]{3,2,1,0:T(8,128)(2,1)S(1)}, bf16[2,2,256,128]{3,2,1,0:T(8,128)(2,1)S(1)}, u32[]{:S(2)}, u32[]{:S(2)}) collective-permute-start(bf16[2,2,256,128]{3,2,1,0:T(8,128)(2,1)S(1)} %get-tuple-element.24), channel_id=1, source_target_pairs={{0,8},{8,16},{16,24},{24,0},{1,9},{9,17},{17,25},{25,1},{2,10},{10... | collective-permute-start | bytes 786440 | tf_op jit(solution)/shard_map/ppermute | solution.py:183
  39.0 3.4 %collective-permute-start.1 = (bf16[2,2,256,128]{3,2,1,0:T(8,128)(2,1)S(1)}, bf16[2,2,256,128]{3,2,1,0:T(8,128)(2,1)S(1)}, u32[]{:S(2)}, u32[]{:S(2)}) collective-permute-start(bf16[2,2,256,128]{3,2,1,0:T(8,128)(2,1)S(1)} %get-tuple-element.25), channel_id=1, source_target_pairs={{0,24},{8,0},{16,8},{24,16},{1,25},{9,1},{17,9},{25,17},{2,26},{10... | collective-permute-start | bytes 786440 | tf_op jit(solution)/shard_map/ppermute | solution.py:183
  42.4 5.7 %all-to-all-done.1 = bf16[16,6,896]{2,1,0:T(8,128)(2,1)S(1)} async-done(((bf16[16,6,896]{2,1,0:T(8,128)(2,1)}), bf16[16,6,896]{2,1,0:T(8,128)(2,1)S(1)}, u32[]{:S(2)}, u32[]{:S(2)}) %all-to-all-start.1) | async-done | bytes 172064 | tf_op jit(solution)/shard_map/all_to_all | solution.py:39
  50.0 9.3 %all-to-all-start.2 = ((bf16[16,32,128]{2,1,0:T(8,128)(2,1)}), bf16[16,32,128]{2,1,0:T(8,128)(2,1)S(1)}, u32[]{:S(2)}, u32[]{:S(2)}) async-start(bf16[16,32,128]{2,1,0:T(8,128)(2,1)} %broadcast_in_dim.73), calls=%async_computation.2 | async-start | bytes 262144 | tf_op jit(solution)/shard_map/all_to_all | solution.py:39
  59.5 6.6 %collective-permute-start.2 = (bf16[2,2,256,128]{3,2,1,0:T(8,128)(2,1)S(1)}, bf16[2,2,256,128]{3,2,1,0:T(8,128)(2,1)S(1)}, u32[]{:S(2)}, u32[]{:S(2)}) collective-permute-start(bf16[2,2,256,128]{3,2,1,0:T(8,128)(2,1)S(1)} %get-tuple-element.29), channel_id=1, source_target_pairs={{0,16},{8,24},{16,0},{24,8},{1,17},{9,25},{17,1},{25,9},{2,18},{10... | collective-permute-start | bytes 786440 | tf_op jit(solution)/shard_map/ppermute | solution.py:183
  66.5 3.7 %collective-permute-done.2 = bf16[2,2,256,128]{3,2,1,0:T(8,128)(2,1)S(1)} collective-permute-done((bf16[2,2,256,128]{3,2,1,0:T(8,128)(2,1)S(1)}, bf16[2,2,256,128]{3,2,1,0:T(8,128)(2,1)S(1)}, u32[]{:S(2)}, u32[]{:S(2)}) %collective-permute-start.2) | collective-permute-done | bytes 262176 | tf_op jit(solution)/shard_map/ppermute | solution.py:183
  70.2 1.7 all-to-all-done.2
  75.2 9.5 %all-to-all-start.3 = ((bf16[16,18,128]{2,1,0:T(8,128)(2,1)}), bf16[16,18,128]{2,1,0:T(8,128)(2,1)S(1)}, u32[]{:S(2)}, u32[]{:S(2)}) async-start(bf16[16,18,128]{2,1,0:T(8,128)(2,1)} %copy.274), calls=%async_computation.3 | async-start | bytes 196608 | tf_op jit(solution)/shard_map/all_to_all | solution.py:39
  85.7 10.9 %all-to-all-done.3 = bf16[16,18,128]{2,1,0:T(8,128)(2,1)S(1)} async-done(((bf16[16,18,128]{2,1,0:T(8,128)(2,1)}), bf16[16,18,128]{2,1,0:T(8,128)(2,1)S(1)}, u32[]{:S(2)}, u32[]{:S(2)}) %all-to-all-start.3) | async-done | bytes 73760 | tf_op jit(solution)/shard_map/all_to_all | solution.py:39
  98.4 5.4 %all-to-all-start.4 = ((bf16[4,228,128]{2,1,0:T(8,128)(2,1)}), bf16[4,228,128]{2,1,0:T(8,128)(2,1)S(1)}, u32[]{:S(2)}, u32[]{:S(2)}) async-start(bf16[4,228,128]{2,1,0:T(8,128)(2,1)} %pad_maximum_fusion.1), calls=%async_computation.4 | async-start | bytes 475136 | tf_op jit(solution)/shard_map/all_to_all | solution.py:39
  104.7 4.5 %all-to-all-done.4 = bf16[4,228,128]{2,1,0:T(8,128)(2,1)S(1)} async-done(((bf16[4,228,128]{2,1,0:T(8,128)(2,1)}), bf16[4,228,128]{2,1,0:T(8,128)(2,1)S(1)}, u32[]{:S(2)}, u32[]{:S(2)}) %all-to-all-start.4) | async-done | bytes 233504 | tf_op jit(solution)/shard_map/all_to_all | solution.py:39
  109.5 1.1 convolution_convert_fusion.5
  112.0 10.2 %all-to-all-start.5 = ((bf16[8,24,512]{2,1,0:T(8,128)(2,1)}), bf16[8,24,512]{2,1,0:T(8,128)(2,1)S(1)}, u32[]{:S(2)}, u32[]{:S(2)}) async-start(bf16[8,24,512]{2,1,0:T(8,128)(2,1)} %broadcast_in_dim.80), calls=%async_computation.5 | async-start | bytes 393216 | tf_op jit(solution)/shard_map/all_to_all | solution.py:39
  122.2 2.4 %fusion.2 = bf16[8,256,128]{2,1,0:T(8,128)(2,1)} fusion(bf16[8,256,128]{2,1,0:T(8,128)(2,1)S(1)} %copy-done.2, bf16[8,48,128]{2,1,0:T(8,128)(2,1)} %bitcast.167, pred[8,256]{1,0:T(8,128)(4,1)} %broadcast_compare_fusion, f32[8,48]{1,0:T(8,128)S(1)} %gather_fusion, s32[8,48]{1,0:T(8,128)S(1)} %add_add_fusion, s32[256]{0:T(256)} %copy-done.5), kind=kOutput, calls=%fused_computation.14 | convolution fusion | flops 25886720 | bytes 1153024 | tf_op jit(solution)/shard_map/rca,rae->rce/dot_general | solution.py:275
  124.6 2.6 %fusion.1 = bf16[8,256,128]{2,1,0:T(8,128)(2,1)} fusion(bf16[8,256,128]{2,1,0:T(8,128)(2,1)} %param.37, bf16[8,48,128]{2,1,0:T(8,128)(2,1)S(1)} %bitcast.166, pred[8,256]{1,0:T(8,128)(4,1)} %broadcast_compare_fusion, f32[8,48]{1,0:T(8,128)S(1)} %gather_fusion, s32[8,48]{1,0:T(8,128)S(1)} %add_add_fusion, s32[256]{0:T(256)} %copy-done.5), kind=kOutput, calls=%fused_computation.13 | convolution fusion | flops 25886720 | bytes 1153024 | tf_op jit(solution)/shard_map/rca,rae->rce/dot_general | solution.py:274
  129.6 8.4 %all_to_all.60 = bf16[4,24,1664]{2,1,0:T(8,128)(2,1)S(1)} all-to-all(bf16[4,24,1664]{2,1,0:T(8,128)(2,1)S(1)} %broadcast_in_dim.83), channel_id=1, replica_groups=mesh['z'=16,'y'=4,'x'=4,'c'=2] {'y'}, dimensions={0} | all-to-all | bytes 638976 | tf_op jit(solution)/shard_map/all_to_all | solution.py:39
  139.3 5.7 %all-to-all-start.7 = ((bf16[8,12,128]{2,1,0:T(8,128)(2,1)}), bf16[8,12,128]{2,1,0:T(8,128)(2,1)S(1)}, u32[]{:S(2)}, u32[]{:S(2)}) async-start(bf16[8,12,128]{2,1,0:T(8,128)(2,1)} %copy.292), calls=%async_computation.7 | async-start | bytes 65536 | tf_op jit(solution)/shard_map/all_to_all | solution.py:39
  145.0 4.7 %all-to-all-done.7 = bf16[8,12,128]{2,1,0:T(8,128)(2,1)S(1)} async-done(((bf16[8,12,128]{2,1,0:T(8,128)(2,1)}), bf16[8,12,128]{2,1,0:T(8,128)(2,1)S(1)}, u32[]{:S(2)}, u32[]{:S(2)}) %all-to-all-start.7) | async-done | bytes 24608 | tf_op jit(solution)/shard_map/all_to_all | solution.py:39
  149.8 14.9 %all_to_all.61 = bf16[16,12,128]{2,1,0:T(8,128)(2,1)S(1)} all-to-all(bf16[16,12,128]{2,1,0:T(8,128)(2,1)S(1)} %broadcast_in_dim.84), channel_id=1, replica_groups=mesh['z'=16,'y'=4,'x'=4,'c'=2] {'z'}, dimensions={0} | all-to-all | bytes 98304 | tf_op jit(solution)/shard_map/all_to_all | solution.py:39
  165.0 15.5 %all_to_all.62.refs_2_ = bf16[16,192,128]{2,1,0:T(8,128)(2,1)} all-to-all(bf16[16,192,128]{2,1,0:T(8,128)(2,1)S(1)} %broadcast_in_dim.86), channel_id=1, replica_groups=mesh['z'=16,'y'=4,'x'=4,'c'=2] {'y','x'}, dimensions={0} | all-to-all | bytes 1572864 | tf_op jit(solution)/shard_map/all_to_all | solution.py:39
  180.5 5.0 %collective-permute-start.3 = (bf16[16,192,128]{2,1,0:T(8,128)(2,1)}, bf16[16,192,128]{2,1,0:T(8,128)(2,1)S(1)}, u32[]{:S(2)}, u32[]{:S(2)}) collective-permute-start(bf16[16,192,128]{2,1,0:T(8,128)(2,1)} %all_to_all.62.refs_2_), channel_id=1, source_target_pairs={{0,1},{1,0},{2,3},{3,2},{4,5},{5,4},{6,7},{7,6},{8,9},{9,8},{10,11... | collective-permute-start | bytes 2359304 | tf_op jit(solution)/shard_map/ppermute | solution.py:303
  186.3 2.8 %head_own.1 = (f32[192,256]{1,0:T(8,128)}, f32[1,256]{1,0:T(1,128)}) custom-call(s32[1]{0:T(128)} %bitcast.refs_0_, f32[8]{0:T(128)} %refs_1_.3, bf16[16,192,128]{2,1,0:T(8,128)(2,1)} %all_to_all.62.refs_2_, f32[16,128]{1,0:T(8,128)} %reshape.566.refs_3_, bf16[2048,256]{1,0:T(8,128)(2,1)} %refs_4_.3), custom_call_target="tpu_custom_call" | custom-call | flops 201326592 | bytes 1835008 | tf_op jit(solution)/shard_map/head_own/pallas_call | solution.py:115
  190.0 2.7 %head_flip.1 = (f32[192,256]{1,0:T(8,128)}, f32[1,256]{1,0:T(1,128)}) custom-call(s32[1]{0:T(128)} %bitcast.refs_0_, f32[8]{0:T(128)} %refs_1_.3, bf16[16,192,128]{2,1,0:T(8,128)(2,1)} %copy-done.1, f32[16,128]{1,0:T(8,128)} %reshape.566.refs_3_, bf16[2048,256]{1,0:T(8,128)(2,1)} %refs_4_.3), custom_call_target="tpu_custom_call" | custom-call | flops 201326592 | bytes 1835008 | tf_op jit(solution)/shard_map/head_flip/pallas_call | solution.py:115
  194.1 3.6 %all-to-all-start.10 = ((f32[32,1,512]{2,1,0:T(1,128)}), f32[32,1,512]{2,1,0:T(1,128)S(1)}, u32[]{:S(2)}, u32[]{:S(2)}) async-start(f32[32,1,512]{2,1,0:T(1,128)} %broadcast_in_dim.153), calls=%async_computation.10 | async-start | bytes 131072 | tf_op jit(solution)/shard_map/all_to_all | solution.py:39
  199.4 5.7 %all-to-all-done.10 = f32[32,1,512]{2,1,0:T(1,128)S(1)} async-done(((f32[32,1,512]{2,1,0:T(1,128)}), f32[32,1,512]{2,1,0:T(1,128)S(1)}, u32[]{:S(2)}, u32[]{:S(2)}) %all-to-all-start.10) | async-done | bytes 65568 | tf_op jit(solution)/shard_map/all_to_all | solution.py:39
  205.8 3.5 %all-to-all-start.11 = ((f32[16,1,512]{2,1,0:T(1,128)}), f32[16,1,512]{2,1,0:T(1,128)S(1)}, u32[]{:S(2)}, u32[]{:S(2)}) async-start(f32[16,1,512]{2,1,0:T(1,128)} %broadcast_in_dim.154), calls=%async_computation.11 | async-start | bytes 65536 | tf_op jit(solution)/shard_map/all_to_all | solution.py:39
  210.3 10.5 %all-to-all-done.11 = f32[16,1,512]{2,1,0:T(1,128)S(1)} async-done(((f32[16,1,512]{2,1,0:T(1,128)}), f32[16,1,512]{2,1,0:T(1,128)S(1)}, u32[]{:S(2)}, u32[]{:S(2)}) %all-to-all-start.11) | async-done | bytes 32800 | tf_op jit(solution)/shard_map/all_to_all | solution.py:39
  (197 shorter events, 25.9 us)
Async XLA Ops:
  7.2 10.9 %copy-start.8 = (s32[8]{0:T(128)S(1)}, s32[8]{0:T(128)}, u32[]{:S(2)}) copy-start(s32[8]{0:T(128)} %param.39) | copy-start | bytes 100
  7.2 11.1 %copy-start.9 = (s32[8]{0:T(128)S(1)}, s32[8]{0:T(128)}, u32[]{:S(2)}) copy-start(s32[8]{0:T(128)} %param.41) | copy-start | bytes 100
  7.2 11.8 %copy-start.3 = (bf16[8,256,128]{2,1,0:T(8,128)(2,1)S(1)}, bf16[8,256,128]{2,1,0:T(8,128)(2,1)}, u32[]{:S(2)}) copy-start(bf16[8,256,128]{2,1,0:T(8,128)(2,1)} %param.37) | copy-start | bytes 1572868
  7.2 11.8 %copy-start.2 = (bf16[8,256,128]{2,1,0:T(8,128)(2,1)S(1)}, bf16[8,256,128]{2,1,0:T(8,128)(2,1)}, u32[]{:S(2)}) copy-start(bf16[8,256,128]{2,1,0:T(8,128)(2,1)} %param.38) | copy-start | bytes 1572868
  9.0 10.4 %all-to-all-start = ((bf16[4,32,896]{2,1,0:T(8,128)(2,1)}), bf16[4,32,896]{2,1,0:T(8,128)(2,1)S(1)}, u32[]{:S(2)}, u32[]{:S(2)}) async-start(bf16[4,32,896]{2,1,0:T(8,128)(2,1)} %pack.1), calls=%async_computation | async-start | bytes 458752 | tf_op jit(solution)/shard_map/all_to_all | solution.py:39
  14.0 95.5 %all-gather.2.cloned.1.call-start = ((), (), s32[]{:S(2)}) async-start(), calls=%async_computation.12 | async-start | bytes 2785280 | tf_op jit(solution)/shard_map/all_gather | solution.py:159
  18.3 41.0 %copy-start.5 = (s32[256]{0:T(256)}, s32[256]{0:T(256)S(1)}, u32[]{:S(2)}) copy-start(s32[256]{0:T(256)S(1)} %iota_add_fusion) | copy-start | bytes 3076
  19.0 29.6 %copy-start.6 = (f32[128]{0:T(128)S(1)}, f32[128]{0:T(128)}, u32[]{:S(2)}) copy-start(f32[128]{0:T(128)} %param.28) | copy-start | bytes 1540
  19.0 29.8 %copy-start.7 = (f32[128]{0:T(128)S(1)}, f32[128]{0:T(128)}, u32[]{:S(2)}) copy-start(f32[128]{0:T(128)} %param.27) | copy-start | bytes 1540
  20.5 27.5 %all-to-all-start.1 = ((bf16[16,6,896]{2,1,0:T(8,128)(2,1)}), bf16[16,6,896]{2,1,0:T(8,128)(2,1)S(1)}, u32[]{:S(2)}, u32[]{:S(2)}) async-start(bf16[16,6,896]{2,1,0:T(8,128)(2,1)} %reshape.547), calls=%async_computation.1 | async-start | bytes 458752 | tf_op jit(solution)/shard_map/all_to_all | solution.py:39
  35.9 13.5 %collective-permute-start = (bf16[2,2,256,128]{3,2,1,0:T(8,128)(2,1)S(1)}, bf16[2,2,256,128]{3,2,1,0:T(8,128)(2,1)S(1)}, u32[]{:S(2)}, u32[]{:S(2)}) collective-permute-start(bf16[2,2,256,128]{3,2,1,0:T(8,128)(2,1)S(1)} %get-tuple-element.24), channel_id=1, source_target_pairs={{0,8},{8,16},{16,24},{24,0},{1,9},{9,17},{17,25},{25,1},{2,10},{10... | collective-permute-start | bytes 786440 | tf_op jit(solution)/shard_map/ppermute | solution.py:183
  39.0 10.3 %collective-permute-start.1 = (bf16[2,2,256,128]{3,2,1,0:T(8,128)(2,1)S(1)}, bf16[2,2,256,128]{3,2,1,0:T(8,128)(2,1)S(1)}, u32[]{:S(2)}, u32[]{:S(2)}) collective-permute-start(bf16[2,2,256,128]{3,2,1,0:T(8,128)(2,1)S(1)} %get-tuple-element.25), channel_id=1, source_target_pairs={{0,24},{8,0},{16,8},{24,16},{1,25},{9,1},{17,9},{25,17},{2,26},{10... | collective-permute-start | bytes 786440 | tf_op jit(solution)/shard_map/ppermute | solution.py:183
  50.0 21.9 %all-to-all-start.2 = ((bf16[16,32,128]{2,1,0:T(8,128)(2,1)}), bf16[16,32,128]{2,1,0:T(8,128)(2,1)S(1)}, u32[]{:S(2)}, u32[]{:S(2)}) async-start(bf16[16,32,128]{2,1,0:T(8,128)(2,1)} %broadcast_in_dim.73), calls=%async_computation.2 | async-start | bytes 262144 | tf_op jit(solution)/shard_map/all_to_all | solution.py:39
  59.5 10.7 %collective-permute-start.2 = (bf16[2,2,256,128]{3,2,1,0:T(8,128)(2,1)S(1)}, bf16[2,2,256,128]{3,2,1,0:T(8,128)(2,1)S(1)}, u32[]{:S(2)}, u32[]{:S(2)}) collective-permute-start(bf16[2,2,256,128]{3,2,1,0:T(8,128)(2,1)S(1)} %get-tuple-element.29), channel_id=1, source_target_pairs={{0,16},{8,24},{16,0},{24,8},{1,17},{9,25},{17,1},{25,9},{2,18},{10... | collective-permute-start | bytes 786440 | tf_op jit(solution)/shard_map/ppermute | solution.py:183
  75.2 21.3 %all-to-all-start.3 = ((bf16[16,18,128]{2,1,0:T(8,128)(2,1)}), bf16[16,18,128]{2,1,0:T(8,128)(2,1)S(1)}, u32[]{:S(2)}, u32[]{:S(2)}) async-start(bf16[16,18,128]{2,1,0:T(8,128)(2,1)} %copy.274), calls=%async_computation.3 | async-start | bytes 196608 | tf_op jit(solution)/shard_map/all_to_all | solution.py:39
  98.4 10.8 %all-to-all-start.4 = ((bf16[4,228,128]{2,1,0:T(8,128)(2,1)}), bf16[4,228,128]{2,1,0:T(8,128)(2,1)S(1)}, u32[]{:S(2)}, u32[]{:S(2)}) async-start(bf16[4,228,128]{2,1,0:T(8,128)(2,1)} %pad_maximum_fusion.1), calls=%async_computation.4 | async-start | bytes 475136 | tf_op jit(solution)/shard_map/all_to_all | solution.py:39
  111.3 17.3 %copy-start = (bf16[512,2560]{1,0:T(8,128)(2,1)S(1)}, bf16[512,2560]{1,0:T(8,128)(2,1)}, u32[]{:S(2)}) copy-start(bf16[512,2560]{1,0:T(8,128)(2,1)} %all-gather.2.cloned.1.call-done) | copy-start | bytes 7864324
  112.0 16.1 %all-to-all-start.5 = ((bf16[8,24,512]{2,1,0:T(8,128)(2,1)}), bf16[8,24,512]{2,1,0:T(8,128)(2,1)S(1)}, u32[]{:S(2)}, u32[]{:S(2)}) async-start(bf16[8,24,512]{2,1,0:T(8,128)(2,1)} %broadcast_in_dim.80), calls=%async_computation.5 | async-start | bytes 393216 | tf_op jit(solution)/shard_map/all_to_all | solution.py:39
  139.3 10.4 %all-to-all-start.7 = ((bf16[8,12,128]{2,1,0:T(8,128)(2,1)}), bf16[8,12,128]{2,1,0:T(8,128)(2,1)S(1)}, u32[]{:S(2)}, u32[]{:S(2)}) async-start(bf16[8,12,128]{2,1,0:T(8,128)(2,1)} %copy.292), calls=%async_computation.7 | async-start | bytes 65536 | tf_op jit(solution)/shard_map/all_to_all | solution.py:39
  180.5 8.6 %collective-permute-start.3 = (bf16[16,192,128]{2,1,0:T(8,128)(2,1)}, bf16[16,192,128]{2,1,0:T(8,128)(2,1)S(1)}, u32[]{:S(2)}, u32[]{:S(2)}) collective-permute-start(bf16[16,192,128]{2,1,0:T(8,128)(2,1)} %all_to_all.62.refs_2_), channel_id=1, source_target_pairs={{0,1},{1,0},{2,3},{3,2},{4,5},{5,4},{6,7},{7,6},{8,9},{9,8},{10,11... | collective-permute-start | bytes 2359304 | tf_op jit(solution)/shard_map/ppermute | solution.py:303
  189.1 20.2 %copy-start.4 = (f32[192,256]{1,0:T(8,128)S(1)}, f32[192,256]{1,0:T(8,128)}, u32[]{:S(2)}) copy-start(f32[192,256]{1,0:T(8,128)} %get-tuple-element.36) | copy-start | bytes 589828
  189.1 0.9 copy-start.1
  194.1 10.9 %all-to-all-start.10 = ((f32[32,1,512]{2,1,0:T(1,128)}), f32[32,1,512]{2,1,0:T(1,128)S(1)}, u32[]{:S(2)}, u32[]{:S(2)}) async-start(f32[32,1,512]{2,1,0:T(1,128)} %broadcast_in_dim.153), calls=%async_computation.10 | async-start | bytes 131072 | tf_op jit(solution)/shard_map/all_to_all | solution.py:39
  205.8 15.0 %all-to-all-start.11 = ((f32[16,1,512]{2,1,0:T(1,128)}), f32[16,1,512]{2,1,0:T(1,128)S(1)}, u32[]{:S(2)}, u32[]{:S(2)}) async-start(f32[16,1,512]{2,1,0:T(1,128)} %broadcast_in_dim.154), calls=%async_computation.11 | async-start | bytes 65536 | tf_op jit(solution)/shard_map/all_to_all | solution.py:39
Sparse Core Ops, SparseCore 0:
  17.5 82.4 all-gather.1

commit v8 on v7

--- a/solution.py
+++ b/solution.py
@@ -74,7 +74,8 @@
         out_ref[y, :, 768:896] = (moved[:, y * 128 : y * 128 + 128] + extra).astype(BF)
 
 
-def head_kernel(core_ref, temp_ref, tiles_ref, gain_ref, weight_ref, logits_ref, spot_ref, *, flip, width):
+def head_kernel(core_ref, temp_ref, tiles_ref, gain_ref, weight_ref, *refs, flip, width):
+    logits_ref, spot_ref = refs[-2:]
     rows = tiles_ref.shape[1]
     squares = jnp.zeros((rows, 128), F32)
     for column in range(16):
@@ -106,25 +107,35 @@
     top = jnp.max(logits, axis=1, keepdims=True)
     spot = top + jnp.log(jnp.sum(jnp.exp(logits - top), axis=1, keepdims=True))
     across = lax.broadcasted_iota(jnp.int32, (rows, 256), 0) == lax.broadcasted_iota(jnp.int32, (rows, 256), 1)
-    spot_ref[...] = jnp.sum(jnp.where(across, spot, 0.0), axis=0, keepdims=True)
-
-
-def head(core, temps, tiles, gains, weight, flip):
+    mine = jnp.sum(jnp.where(across, spot, 0.0), axis=0, keepdims=True)
+    if not flip:
+        spot_ref[...] = mine
+    else:
+        first = refs[0][...]
+        low, high = jnp.where(part == 1, first, mine), jnp.where(part == 1, mine, first)
+        for copy in range(spot_ref.shape[0]):
+            spot_ref[copy, :, 0:256] = low
+            spot_ref[copy, :, 256:512] = high
+
+
+def head(core, temps, tiles, gains, weight, first=None):
     rows = tiles.shape[1]
+    flip = first is not None
     vmem, smem = pl.BlockSpec(memory_space=pltpu.VMEM), pl.BlockSpec(memory_space=pltpu.SMEM)
+    extra = (first,) if flip else ()
     return pl.pallas_call(
         lambda *refs: head_kernel(*refs, flip=flip, width=2048),
         out_shape=(
             jax.ShapeDtypeStruct((rows, 256), F32),
-            jax.ShapeDtypeStruct((1, 256), F32),
+            jax.ShapeDtypeStruct((32, 1, 512) if flip else (1, 256), F32),
         ),
-        in_specs=[smem, smem, vmem, vmem, vmem],
+        in_specs=[smem, smem, vmem, vmem, vmem] + [vmem] * len(extra),
         out_specs=(vmem, vmem),
         cost_estimate=pl.CostEstimate(
             flops=2 * rows * 2048 * 256, bytes_accessed=2 * 2048 * (rows + 256), transcendentals=rows * 256
         ),
         name="head_flip" if flip else "head_own",
-    )(core, temps, tiles, gains, weight)
+    )(core, temps, tiles, gains, weight, *extra)
 
 
 def pack_state(peak, mass, weighted):
@@ -171,7 +182,13 @@
     ln1_row = side_wide[:, 96:97] + side_wide[:, 97:98] + side_wide[:, 98:99]
     scaled = (side_wide * ln1_row).astype(BF)
     partial = lax.dot_general(scaled, proj, (((0,), (0,)), ((), ())), preferred_element_type=F32)
-    sent = jnp.concatenate([partial[:96].astype(BF), side.T[:96]], axis=1).reshape(16, 6, 896)
+    partial = partial[:96].astype(BF)
+
+    def by_tile(values):
+        split = values.reshape(16, 6, values.shape[1] // 128, 128)
+        return jnp.swapaxes(split, 1, 2).reshape(16, -1, 128)
+
+    sent = by_tile(jnp.concatenate([partial[:, :512], side.T[:96]], axis=1))
     caches = jnp.stack([key_cache, value_cache])
     parts = [
         lax.dynamic_slice(caches, (0, (y + shift) % 4 * 2, 0, 0), (2, 2, slot_count, 128))
@@ -181,11 +198,12 @@
     got = swap(sent, "z")
     for shift in range(1, 4):
         parts[shift] = lax.ppermute(parts[shift], "y", [(i, (i + shift) % 4) for i in range(4)])
-    sums = jnp.sum(got[:, :, :768].astype(F32), axis=0)
-    rows = got[:, :, 768:]
+    sums = jnp.sum(got[:, :24].astype(F32), axis=0).reshape(4, 6, 128)
+    rows = got[:, 24:]
     rows_wide = rows.astype(F32)
     squares = jnp.sum(rows_wide * rows_wide, axis=(0, 2))
-    sums = sums * lax.rsqrt(squares / width + EPSILON)[:, None]
+    scale1 = lax.rsqrt(squares / width + EPSILON)[:, None]
+    sums = sums * scale1
 
     links = ancestry(parents)
     depth = jnp.sum((links > 0.5).astype(jnp.int32), axis=-1) - 1
@@ -194,13 +212,12 @@
     my_places = lax.dynamic_slice(target.reshape(-1), (first,), (6,))
     inverse = ROPE_BASE ** (-jnp.arange(64, dtype=F32) / 64)
     angles = my_places.astype(F32)[:, None] * inverse[None, :]
-    cosine, sine = jnp.cos(angles)[:, None, :], jnp.sin(angles)[:, None, :]
-    query = rotate(head_norm(sums[:, :256].reshape(6, 2, 128), q_gain), cosine, sine) * 128 ** (-0.5)
-    new_key = rotate(head_norm(sums[:, 256:384].reshape(6, 1, 128), key_gain), cosine, sine)
-    outgate = jax.nn.sigmoid(sums[:, 512:]).astype(BF)
+    cosine, sine = jnp.cos(angles), jnp.sin(angles)
+    query = rotate(head_norm(sums[:2], q_gain), cosine, sine) * 128 ** (-0.5)
+    new_key = rotate(head_norm(sums[2], key_gain), cosine, sine)
     block = jnp.concatenate(
         [
-            query[:, 0], query[:, 1], new_key[:, 0], sums[:, 384:512],
+            query.reshape(12, 128), new_key, sums[3],
             side[:, 99:105].T.astype(F32), jnp.zeros((2, 128), F32),
         ],
         axis=0,
@@ -246,9 +263,12 @@
         return jnp.swapaxes(values.reshape((2, 2, 8, 6) + rest), 1, 2).reshape((16, 2, 6) + rest)
 
     outgoing = pack_state(by_z(peak), by_z(mass), by_z(weighted))
-    mass, weighted = merge_state(swap(outgoing, "z"))
-    my_gate = jnp.swapaxes(outgate.reshape(6, 2, 128), 0, 1).astype(F32)
-    gated = (weighted / mass[..., None] * my_gate).astype(BF).reshape(12, 128)
+    outgoing = jnp.concatenate([outgoing, by_tile(partial[:, 512:])], axis=1)
+    arrived, last_all = lax.optimization_barrier((swap(outgoing, "z"), last_all))
+    mass, weighted = merge_state(arrived[:, :18])
+    gate = jnp.sum(arrived[:, 18:].astype(F32), axis=0).reshape(2, 6, 128)
+    gated = weighted / mass[..., None] * jax.nn.sigmoid(gate * scale1)
+    gated = gated.astype(BF).reshape(12, 128)
     residual = jnp.transpose(rows.reshape(4, 4, 6, 4, 32), (3, 0, 2, 1, 4)).reshape(4, 24, 128)
     same = jnp.concatenate([gated, tokens[192:]], axis=0)
     both = swap(jnp.concatenate([residual, jnp.broadcast_to(same[None], (4, 204, 128))], axis=1), "y")
@@ -302,8 +322,8 @@
     half = spread(half, ("y", "x"), 16)
     other = lax.ppermute(half, "c", [(0, 1), (1, 0)])
     core = c.reshape(1)
-    own_logits, own_spot = head(core, inv_temp, half, last_all, head_weight, False)
-    other_logits, other_spot = head(core, inv_temp, other, last_all, head_weight, True)
+    own_logits, own_spot = head(core, inv_temp, half, last_all, head_weight)
+    other_logits, spots = head(core, inv_temp, other, last_all, head_weight, own_spot)
 
     def in_order(mine_part, other_part):
         return jnp.concatenate(
@@ -315,11 +335,12 @@
 
     own = in_order(own_columns(half), own_columns(other))
     next_hidden = lax.dynamic_slice(own, (0, z % 4 * 32), (384, 32))
-    spot = in_order(own_spot, other_spot).reshape(1, 512)
-    for axis, count in ((("y", "x", "c"), 32), ("z", 16)):
-        spots = spread(spot, axis, count)
-        top = jnp.max(spots, axis=0)
-        spot = top + jnp.log(jnp.sum(jnp.exp(spots - top), axis=0))
+    spots = swap(spots, ("y", "x", "c"))
+    top = jnp.max(spots, axis=0)
+    spot = top + jnp.log(jnp.sum(jnp.exp(spots - top), axis=0))
+    spots = spread(spot, "z", 16)
+    top = jnp.max(spots, axis=0)
+    spot = top + jnp.log(jnp.sum(jnp.exp(spots - top), axis=0))
     spot = spot.reshape(2, 256)[:, :192].reshape(384, 1)
     logprobs = in_order(own_logits, other_logits) - spot
 

time: 230 us -> 227 us (0.987)
  starting transfers between devices: 85.4 us -> 83 us
    all_to_all x9, waiting for transfers between devices: 44.9 us -> 47.5 us  [swap(): return lax.all_to_all(values, axis, 0, 0, tiled=True)]
  transfers between devices with their start and end apart: 14 -> 14, of which waited for: 10 -> 10; matrix products, arithmetic and copies ran while one was open for 11% -> 10% of each run, Pallas kernels for 1% -> 1%
where the time goes in v8:
time: 227 us; the launch traced here: 226 us
  starting transfers between devices  83 us (37%)
  waiting for transfers between devices  50.7 us (22%)
  blocking collectives  38.6 us (17%)
  between operations  14.9 us (7%)
  local copies, waits for them, and re-layouts  11.7 us (5%)
  matrix products  10.5 us (5%)
  other arithmetic  8.91 us (4%)
  Pallas kernels  7.42 us (3%)
    all_to_all x9, starting transfers between devices, swap(): return lax.all_to_all(values, axis, 0, 0, tiled=True)  66.8 us
    all_to_all x9, waiting for transfers between devices, swap(): return lax.all_to_all(values, axis, 0, 0, tiled=True)  47.5 us
    all_to_all x3, blocking collectives, swap(): return lax.all_to_all(values, axis, 0, 0, tiled=True)  38.6 us
    ppermute x3, starting transfers between devices, on_device(): lax.ppermute(parts[shift], 'y', [(i, (i + shift) % 4) for i in range(4)])  11 us
    pallas_call x2, Pallas kernels, head(): pl.pallas_call(lambda *refs: head_kernel(*refs, flip=flip, width=2048), o...  5.63 us
    ppermute x1, starting transfers between devices, on_device(): other = lax.ppermute(half, 'c', [(0, 1), (1, 0)])  5.24 us
  transfers between devices with their start and end apart: 14, of which 10 were waited for; matrix products, arithmetic and copies ran while one was open for 10% of the time, Pallas kernels for 1%

profile of v8, /device:TPU:1, one launch (start us, length us, event | category | flops | bytes accessed | tf_op | source)
XLA Modules:
  0.0 225.7 jit_solution(9310472920055154684)
XLA Ops:
  7.2 1.8 pack.1
  9.0 5.0 %all-to-all-start = ((bf16[4,32,896]{2,1,0:T(8,128)(2,1)}), bf16[4,32,896]{2,1,0:T(8,128)(2,1)S(1)}, u32[]{:S(2)}, u32[]{:S(2)}) async-start(bf16[4,32,896]{2,1,0:T(8,128)(2,1)} %pack.1), calls=%async_computation | async-start | bytes 458752 | tf_op jit(solution)/shard_map/all_to_all | solution.py:39
  14.0 1.5 pad_maximum_fusion.2
  15.6 1.4 fusion.4
  20.7 14.9 %all-to-all-start.1 = ((bf16[16,30,128]{2,1,0:T(8,128)(2,1)}), bf16[16,30,128]{2,1,0:T(8,128)(2,1)S(1)}, u32[]{:S(2)}, u32[]{:S(2)}) async-start(bf16[16,30,128]{2,1,0:T(8,128)(2,1)} %copy.265), calls=%async_computation.1 | async-start | bytes 262144 | tf_op jit(solution)/shard_map/all_to_all | solution.py:39
  36.0 2.5 %collective-permute-start = (bf16[2,2,256,128]{3,2,1,0:T(8,128)(2,1)S(1)}, bf16[2,2,256,128]{3,2,1,0:T(8,128)(2,1)S(1)}, u32[]{:S(2)}, u32[]{:S(2)}) collective-permute-start(bf16[2,2,256,128]{3,2,1,0:T(8,128)(2,1)S(1)} %get-tuple-element.26), channel_id=1, source_target_pairs={{0,8},{8,16},{16,24},{24,0},{1,9},{9,17},{17,25},{25,1},{2,10},{10... | collective-permute-start | bytes 786440 | tf_op jit(solution)/shard_map/ppermute | solution.py:200
  38.4 4.0 %collective-permute-start.1 = (bf16[2,2,256,128]{3,2,1,0:T(8,128)(2,1)S(1)}, bf16[2,2,256,128]{3,2,1,0:T(8,128)(2,1)S(1)}, u32[]{:S(2)}, u32[]{:S(2)}) collective-permute-start(bf16[2,2,256,128]{3,2,1,0:T(8,128)(2,1)S(1)} %get-tuple-element.27), channel_id=1, source_target_pairs={{0,24},{8,0},{16,8},{24,16},{1,25},{9,1},{17,9},{25,17},{2,26},{10... | collective-permute-start | bytes 786440 | tf_op jit(solution)/shard_map/ppermute | solution.py:200
  42.5 5.1 %all-to-all-done.1 = bf16[16,30,128]{2,1,0:T(8,128)(2,1)S(1)} async-done(((bf16[16,30,128]{2,1,0:T(8,128)(2,1)}), bf16[16,30,128]{2,1,0:T(8,128)(2,1)S(1)}, u32[]{:S(2)}, u32[]{:S(2)}) %all-to-all-start.1) | async-done | bytes 122912 | tf_op jit(solution)/shard_map/all_to_all | solution.py:39
  49.4 8.6 %all-to-all-start.2 = ((bf16[16,32,128]{2,1,0:T(8,128)(2,1)}), bf16[16,32,128]{2,1,0:T(8,128)(2,1)S(1)}, u32[]{:S(2)}, u32[]{:S(2)}) async-start(bf16[16,32,128]{2,1,0:T(8,128)(2,1)} %broadcast_in_dim.69), calls=%async_computation.2 | async-start | bytes 262144 | tf_op jit(solution)/shard_map/all_to_all | solution.py:39
  58.0 4.5 %collective-permute-start.2 = (bf16[2,2,256,128]{3,2,1,0:T(8,128)(2,1)S(1)}, bf16[2,2,256,128]{3,2,1,0:T(8,128)(2,1)S(1)}, u32[]{:S(2)}, u32[]{:S(2)}) collective-permute-start(bf16[2,2,256,128]{3,2,1,0:T(8,128)(2,1)S(1)} %get-tuple-element.31), channel_id=1, source_target_pairs={{0,16},{8,24},{16,0},{24,8},{1,17},{9,25},{17,1},{25,9},{2,18},{10... | collective-permute-start | bytes 786440 | tf_op jit(solution)/shard_map/ppermute | solution.py:200
  63.5 3.1 %collective-permute-done.2 = bf16[2,2,256,128]{3,2,1,0:T(8,128)(2,1)S(1)} collective-permute-done((bf16[2,2,256,128]{3,2,1,0:T(8,128)(2,1)S(1)}, bf16[2,2,256,128]{3,2,1,0:T(8,128)(2,1)S(1)}, u32[]{:S(2)}, u32[]{:S(2)}) %collective-permute-start.2) | collective-permute-done | bytes 262176 | tf_op jit(solution)/shard_map/ppermute | solution.py:200
  66.7 3.2 %all-to-all-done.2 = bf16[16,32,128]{2,1,0:T(8,128)(2,1)S(1)} async-done(((bf16[16,32,128]{2,1,0:T(8,128)(2,1)}), bf16[16,32,128]{2,1,0:T(8,128)(2,1)S(1)}, u32[]{:S(2)}, u32[]{:S(2)}) %all-to-all-start.2) | async-done | bytes 131104 | tf_op jit(solution)/shard_map/all_to_all | solution.py:39
  73.3 8.5 %all-to-all-start.3 = ((bf16[16,30,128]{2,1,0:T(8,128)(2,1)}), bf16[16,30,128]{2,1,0:T(8,128)(2,1)S(1)}, u32[]{:S(2)}, u32[]{:S(2)}) async-start(bf16[16,30,128]{2,1,0:T(8,128)(2,1)} %copy.282), calls=%async_computation.3 | async-start | bytes 262144 | tf_op jit(solution)/shard_map/all_to_all | solution.py:39
  83.3 11.3 %all-to-all-done.3 = bf16[16,30,128]{2,1,0:T(8,128)(2,1)S(1)} async-done(((bf16[16,30,128]{2,1,0:T(8,128)(2,1)}), bf16[16,30,128]{2,1,0:T(8,128)(2,1)S(1)}, u32[]{:S(2)}, u32[]{:S(2)}) %all-to-all-start.3) | async-done | bytes 122912 | tf_op jit(solution)/shard_map/all_to_all | solution.py:39
  96.8 4.5 %all-to-all-start.4 = ((bf16[4,228,128]{2,1,0:T(8,128)(2,1)}), bf16[4,228,128]{2,1,0:T(8,128)(2,1)S(1)}, u32[]{:S(2)}, u32[]{:S(2)}) async-start(bf16[4,228,128]{2,1,0:T(8,128)(2,1)} %pad_maximum_fusion.1), calls=%async_computation.4 | async-start | bytes 475136 | tf_op jit(solution)/shard_map/all_to_all | solution.py:39
  101.6 5.2 %all-to-all-done.4 = bf16[4,228,128]{2,1,0:T(8,128)(2,1)S(1)} async-done(((bf16[4,228,128]{2,1,0:T(8,128)(2,1)}), bf16[4,228,128]{2,1,0:T(8,128)(2,1)S(1)}, u32[]{:S(2)}, u32[]{:S(2)}) %all-to-all-start.4) | async-done | bytes 233504 | tf_op jit(solution)/shard_map/all_to_all | solution.py:39
  107.0 1.1 convolution_convert_fusion.6
  109.5 12.4 %all-to-all-start.5 = ((bf16[8,24,512]{2,1,0:T(8,128)(2,1)}), bf16[8,24,512]{2,1,0:T(8,128)(2,1)S(1)}, u32[]{:S(2)}, u32[]{:S(2)}) async-start(bf16[8,24,512]{2,1,0:T(8,128)(2,1)} %broadcast_in_dim.76), calls=%async_computation.5 | async-start | bytes 393216 | tf_op jit(solution)/shard_map/all_to_all | solution.py:39
  121.9 2.4 %fusion.2 = bf16[8,256,128]{2,1,0:T(8,128)(2,1)} fusion(bf16[8,256,128]{2,1,0:T(8,128)(2,1)S(1)} %copy-done.3, bf16[8,48,128]{2,1,0:T(8,128)(2,1)} %bitcast.156, pred[8,256]{1,0:T(8,128)(4,1)S(1)} %broadcast_compare_fusion, f32[8,48]{1,0:T(8,128)S(1)} %gather_fusion, s32[8,48]{1,0:T(8,128)S(1)} %add_add_fusion, s32[256]{0:T(256)} %copy-done.6), kind=kOutput, calls=%fused_computation.14 | convolution fusion | flops 25886720 | bytes 1153024 | tf_op jit(solution)/shard_map/rca,rae->rce/dot_general | solution.py:295
  124.3 2.6 %fusion.1 = bf16[8,256,128]{2,1,0:T(8,128)(2,1)} fusion(bf16[8,256,128]{2,1,0:T(8,128)(2,1)} %param.37, bf16[8,48,128]{2,1,0:T(8,128)(2,1)S(1)} %bitcast.155, pred[8,256]{1,0:T(8,128)(4,1)S(1)} %broadcast_compare_fusion, f32[8,48]{1,0:T(8,128)S(1)} %gather_fusion, s32[8,48]{1,0:T(8,128)S(1)} %add_add_fusion, s32[256]{0:T(256)} %copy-done.6), kind=kOutput, calls=%fused_computation.13 | convolution fusion | flops 25886720 | bytes 1153024 | tf_op jit(solution)/shard_map/rca,rae->rce/dot_general | solution.py:294
  128.6 8.4 %all_to_all.60 = bf16[4,24,1664]{2,1,0:T(8,128)(2,1)S(1)} all-to-all(bf16[4,24,1664]{2,1,0:T(8,128)(2,1)S(1)} %broadcast_in_dim.79), channel_id=1, replica_groups=mesh['z'=16,'y'=4,'x'=4,'c'=2] {'y'}, dimensions={0} | all-to-all | bytes 638976 | tf_op jit(solution)/shard_map/all_to_all | solution.py:39
  138.3 5.7 %all-to-all-start.7 = ((bf16[8,12,128]{2,1,0:T(8,128)(2,1)}), bf16[8,12,128]{2,1,0:T(8,128)(2,1)S(1)}, u32[]{:S(2)}, u32[]{:S(2)}) async-start(bf16[8,12,128]{2,1,0:T(8,128)(2,1)} %copy.300), calls=%async_computation.7 | async-start | bytes 65536 | tf_op jit(solution)/shard_map/all_to_all | solution.py:39
  144.0 4.7 %all-to-all-done.7 = bf16[8,12,128]{2,1,0:T(8,128)(2,1)S(1)} async-done(((bf16[8,12,128]{2,1,0:T(8,128)(2,1)}), bf16[8,12,128]{2,1,0:T(8,128)(2,1)S(1)}, u32[]{:S(2)}, u32[]{:S(2)}) %all-to-all-start.7) | async-done | bytes 24608 | tf_op jit(solution)/shard_map/all_to_all | solution.py:39
  148.9 15.5 %all_to_all.61 = bf16[16,12,128]{2,1,0:T(8,128)(2,1)S(1)} all-to-all(bf16[16,12,128]{2,1,0:T(8,128)(2,1)S(1)} %broadcast_in_dim.80), channel_id=1, replica_groups=mesh['z'=16,'y'=4,'x'=4,'c'=2] {'z'}, dimensions={0} | all-to-all | bytes 98304 | tf_op jit(solution)/shard_map/all_to_all | solution.py:39
  164.6 14.7 %all_to_all.62.refs_2_ = bf16[16,192,128]{2,1,0:T(8,128)(2,1)S(1)} all-to-all(bf16[16,192,128]{2,1,0:T(8,128)(2,1)S(1)} %broadcast_in_dim.82), channel_id=1, replica_groups=mesh['z'=16,'y'=4,'x'=4,'c'=2] {'y','x'}, dimensions={0} | all-to-all | bytes 1572864 | tf_op jit(solution)/shard_map/all_to_all | solution.py:39
  179.3 5.2 %collective-permute-start.3 = (bf16[16,192,128]{2,1,0:T(8,128)(2,1)S(1)}, bf16[16,192,128]{2,1,0:T(8,128)(2,1)S(1)}, u32[]{:S(2)}, u32[]{:S(2)}) collective-permute-start(bf16[16,192,128]{2,1,0:T(8,128)(2,1)S(1)} %all_to_all.62.refs_2_), channel_id=1, source_target_pairs={{0,1},{1,0},{2,3},{3,2},{4,5},{5,4},{6,7},{7,6},{8,9},{9,8},{10,11... | collective-permute-start | bytes 2359304 | tf_op jit(solution)/shard_map/ppermute | solution.py:323
  184.6 2.8 %head_own.1 = (f32[192,256]{1,0:T(8,128)}, f32[1,256]{1,0:T(1,128)}) custom-call(s32[1]{0:T(128)} %bitcast.refs_0_, f32[8]{0:T(128)} %refs_1_.3, bf16[16,192,128]{2,1,0:T(8,128)(2,1)} %copy-done, f32[16,128]{1,0:T(8,128)} %reshape.519.refs_3_, bf16[2048,256]{1,0:T(8,128)(2,1)} %refs_4_.3), custom_call_target="tpu_custom_call" | custom-call | flops 201326592 | bytes 1835008 | tf_op jit(solution)/shard_map/head_own/pallas_call | solution.py:126
  188.3 2.8 %head_flip.1 = (f32[192,256]{1,0:T(8,128)}, f32[32,1,512]{2,1,0:T(1,128)}) custom-call(s32[1]{0:T(128)} %bitcast.refs_0_, f32[8]{0:T(128)} %refs_1_.3, bf16[16,192,128]{2,1,0:T(8,128)(2,1)} %copy-done.2, f32[16,128]{1,0:T(8,128)} %reshape.519.refs_3_, bf16[2048,256]{1,0:T(8,128)(2,1)} %refs_4_.3, f32[1,256]{1,0:T(1,128)} %get-tuple-element.41.refs_5_), custom_call_target="tpu_custom_call" | custom-call | flops 201326592 | bytes 1835008 | tf_op jit(solution)/shard_map/head_flip/pallas_call | solution.py:126
  191.1 3.6 %all-to-all-start.10 = ((f32[32,1,512]{2,1,0:T(1,128)}), f32[32,1,512]{2,1,0:T(1,128)S(1)}, u32[]{:S(2)}, u32[]{:S(2)}) async-start(f32[32,1,512]{2,1,0:T(1,128)} %get-tuple-element.43), calls=%async_computation.10 | async-start | bytes 131072 | tf_op jit(solution)/shard_map/all_to_all | solution.py:39
  196.4 5.7 %all-to-all-done.10 = f32[32,1,512]{2,1,0:T(1,128)S(1)} async-done(((f32[32,1,512]{2,1,0:T(1,128)}), f32[32,1,512]{2,1,0:T(1,128)S(1)}, u32[]{:S(2)}, u32[]{:S(2)}) %all-to-all-start.10) | async-done | bytes 65568 | tf_op jit(solution)/shard_map/all_to_all | solution.py:39
  202.9 3.5 %all-to-all-start.11 = ((f32[16,1,512]{2,1,0:T(1,128)}), f32[16,1,512]{2,1,0:T(1,128)S(1)}, u32[]{:S(2)}, u32[]{:S(2)}) async-start(f32[16,1,512]{2,1,0:T(1,128)} %broadcast_in_dim.83), calls=%async_computation.11 | async-start | bytes 65536 | tf_op jit(solution)/shard_map/all_to_all | solution.py:39
  207.3 10.5 %all-to-all-done.11 = f32[16,1,512]{2,1,0:T(1,128)S(1)} async-done(((f32[16,1,512]{2,1,0:T(1,128)}), f32[16,1,512]{2,1,0:T(1,128)S(1)}, u32[]{:S(2)}, u32[]{:S(2)}) %all-to-all-start.11) | async-done | bytes 32800 | tf_op jit(solution)/shard_map/all_to_all | solution.py:39
  (202 shorter events, 23.9 us)
Async XLA Ops:
  7.2 10.9 %copy-start.10 = (s32[8]{0:T(128)S(1)}, s32[8]{0:T(128)}, u32[]{:S(2)}) copy-start(s32[8]{0:T(128)} %param.41) | copy-start | bytes 100
  7.2 10.9 %copy-start.9 = (s32[8]{0:T(128)S(1)}, s32[8]{0:T(128)}, u32[]{:S(2)}) copy-start(s32[8]{0:T(128)} %param.39) | copy-start | bytes 100
  7.2 11.1 %copy-start.4 = (bf16[8,256,128]{2,1,0:T(8,128)(2,1)S(1)}, bf16[8,256,128]{2,1,0:T(8,128)(2,1)}, u32[]{:S(2)}) copy-start(bf16[8,256,128]{2,1,0:T(8,128)(2,1)} %param.37) | copy-start | bytes 1572868
  7.2 11.1 %copy-start.3 = (bf16[8,256,128]{2,1,0:T(8,128)(2,1)S(1)}, bf16[8,256,128]{2,1,0:T(8,128)(2,1)}, u32[]{:S(2)}) copy-start(bf16[8,256,128]{2,1,0:T(8,128)(2,1)} %param.38) | copy-start | bytes 1572868
  9.0 10.4 %all-to-all-start = ((bf16[4,32,896]{2,1,0:T(8,128)(2,1)}), bf16[4,32,896]{2,1,0:T(8,128)(2,1)S(1)}, u32[]{:S(2)}, u32[]{:S(2)}) async-start(bf16[4,32,896]{2,1,0:T(8,128)(2,1)} %pack.1), calls=%async_computation | async-start | bytes 458752 | tf_op jit(solution)/shard_map/all_to_all | solution.py:39
  14.0 93.0 %all-gather.2.cloned.1.call-start = ((), (), s32[]{:S(2)}) async-start(), calls=%async_computation.12 | async-start | bytes 2785280 | tf_op jit(solution)/shard_map/all_gather | solution.py:170
  18.3 29.8 %copy-start.7 = (f32[128]{0:T(128)S(1)}, f32[128]{0:T(128)}, u32[]{:S(2)}) copy-start(f32[128]{0:T(128)} %param.28) | copy-start | bytes 1540
  18.3 29.8 %copy-start.8 = (f32[128]{0:T(128)S(1)}, f32[128]{0:T(128)}, u32[]{:S(2)}) copy-start(f32[128]{0:T(128)} %param.27) | copy-start | bytes 1540
  20.7 26.9 %all-to-all-start.1 = ((bf16[16,30,128]{2,1,0:T(8,128)(2,1)}), bf16[16,30,128]{2,1,0:T(8,128)(2,1)S(1)}, u32[]{:S(2)}, u32[]{:S(2)}) async-start(bf16[16,30,128]{2,1,0:T(8,128)(2,1)} %copy.265), calls=%async_computation.1 | async-start | bytes 262144 | tf_op jit(solution)/shard_map/all_to_all | solution.py:39
  36.0 12.8 %collective-permute-start = (bf16[2,2,256,128]{3,2,1,0:T(8,128)(2,1)S(1)}, bf16[2,2,256,128]{3,2,1,0:T(8,128)(2,1)S(1)}, u32[]{:S(2)}, u32[]{:S(2)}) collective-permute-start(bf16[2,2,256,128]{3,2,1,0:T(8,128)(2,1)S(1)} %get-tuple-element.26), channel_id=1, source_target_pairs={{0,8},{8,16},{16,24},{24,0},{1,9},{9,17},{17,25},{25,1},{2,10},{10... | collective-permute-start | bytes 786440 | tf_op jit(solution)/shard_map/ppermute | solution.py:200
  38.4 10.3 %collective-permute-start.1 = (bf16[2,2,256,128]{3,2,1,0:T(8,128)(2,1)S(1)}, bf16[2,2,256,128]{3,2,1,0:T(8,128)(2,1)S(1)}, u32[]{:S(2)}, u32[]{:S(2)}) collective-permute-start(bf16[2,2,256,128]{3,2,1,0:T(8,128)(2,1)S(1)} %get-tuple-element.27), channel_id=1, source_target_pairs={{0,24},{8,0},{16,8},{24,16},{1,25},{9,1},{17,9},{25,17},{2,26},{10... | collective-permute-start | bytes 786440 | tf_op jit(solution)/shard_map/ppermute | solution.py:200
  49.4 20.5 %all-to-all-start.2 = ((bf16[16,32,128]{2,1,0:T(8,128)(2,1)}), bf16[16,32,128]{2,1,0:T(8,128)(2,1)S(1)}, u32[]{:S(2)}, u32[]{:S(2)}) async-start(bf16[16,32,128]{2,1,0:T(8,128)(2,1)} %broadcast_in_dim.69), calls=%async_computation.2 | async-start | bytes 262144 | tf_op jit(solution)/shard_map/all_to_all | solution.py:39
  58.0 8.6 %collective-permute-start.2 = (bf16[2,2,256,128]{3,2,1,0:T(8,128)(2,1)S(1)}, bf16[2,2,256,128]{3,2,1,0:T(8,128)(2,1)S(1)}, u32[]{:S(2)}, u32[]{:S(2)}) collective-permute-start(bf16[2,2,256,128]{3,2,1,0:T(8,128)(2,1)S(1)} %get-tuple-element.31), channel_id=1, source_target_pairs={{0,16},{8,24},{16,0},{24,8},{1,17},{9,25},{17,1},{25,9},{2,18},{10... | collective-permute-start | bytes 786440 | tf_op jit(solution)/shard_map/ppermute | solution.py:200
  62.5 19.3 %copy-start.6 = (s32[256]{0:T(256)}, s32[256]{0:T(256)S(1)}, u32[]{:S(2)}) copy-start(s32[256]{0:T(256)S(1)} %iota_add_fusion) | copy-start | bytes 3076
  73.3 21.3 %all-to-all-start.3 = ((bf16[16,30,128]{2,1,0:T(8,128)(2,1)}), bf16[16,30,128]{2,1,0:T(8,128)(2,1)S(1)}, u32[]{:S(2)}, u32[]{:S(2)}) async-start(bf16[16,30,128]{2,1,0:T(8,128)(2,1)} %copy.282), calls=%async_computation.3 | async-start | bytes 262144 | tf_op jit(solution)/shard_map/all_to_all | solution.py:39
  96.8 9.9 %all-to-all-start.4 = ((bf16[4,228,128]{2,1,0:T(8,128)(2,1)}), bf16[4,228,128]{2,1,0:T(8,128)(2,1)S(1)}, u32[]{:S(2)}, u32[]{:S(2)}) async-start(bf16[4,228,128]{2,1,0:T(8,128)(2,1)} %pad_maximum_fusion.1), calls=%async_computation.4 | async-start | bytes 475136 | tf_op jit(solution)/shard_map/all_to_all | solution.py:39
  108.8 19.5 %copy-start.1 = (bf16[512,2560]{1,0:T(8,128)(2,1)S(1)}, bf16[512,2560]{1,0:T(8,128)(2,1)}, u32[]{:S(2)}) copy-start(bf16[512,2560]{1,0:T(8,128)(2,1)} %all-gather.2.cloned.1.call-done) | copy-start | bytes 7864324
  109.5 18.3 %all-to-all-start.5 = ((bf16[8,24,512]{2,1,0:T(8,128)(2,1)}), bf16[8,24,512]{2,1,0:T(8,128)(2,1)S(1)}, u32[]{:S(2)}, u32[]{:S(2)}) async-start(bf16[8,24,512]{2,1,0:T(8,128)(2,1)} %broadcast_in_dim.76), calls=%async_computation.5 | async-start | bytes 393216 | tf_op jit(solution)/shard_map/all_to_all | solution.py:39
  138.3 10.4 %all-to-all-start.7 = ((bf16[8,12,128]{2,1,0:T(8,128)(2,1)}), bf16[8,12,128]{2,1,0:T(8,128)(2,1)S(1)}, u32[]{:S(2)}, u32[]{:S(2)}) async-start(bf16[8,12,128]{2,1,0:T(8,128)(2,1)} %copy.300), calls=%async_computation.7 | async-start | bytes 65536 | tf_op jit(solution)/shard_map/all_to_all | solution.py:39
  179.3 5.3 %copy-start = (bf16[16,192,128]{2,1,0:T(8,128)(2,1)}, bf16[16,192,128]{2,1,0:T(8,128)(2,1)S(1)}, u32[]{:S(2)}) copy-start(bf16[16,192,128]{2,1,0:T(8,128)(2,1)S(1)} %all_to_all.62.refs_2_) | copy-start | bytes 2359300
  179.3 8.1 %collective-permute-start.3 = (bf16[16,192,128]{2,1,0:T(8,128)(2,1)S(1)}, bf16[16,192,128]{2,1,0:T(8,128)(2,1)S(1)}, u32[]{:S(2)}, u32[]{:S(2)}) collective-permute-start(bf16[16,192,128]{2,1,0:T(8,128)(2,1)S(1)} %all_to_all.62.refs_2_), channel_id=1, source_target_pairs={{0,1},{1,0},{2,3},{3,2},{4,5},{5,4},{6,7},{7,6},{8,9},{9,8},{10,11... | collective-permute-start | bytes 2359304 | tf_op jit(solution)/shard_map/ppermute | solution.py:323
  187.4 19.0 %copy-start.5 = (f32[192,256]{1,0:T(8,128)S(1)}, f32[192,256]{1,0:T(8,128)}, u32[]{:S(2)}) copy-start(f32[192,256]{1,0:T(8,128)} %get-tuple-element.40) | copy-start | bytes 589828
  187.4 0.9 copy-start.2
  191.1 10.9 %all-to-all-start.10 = ((f32[32,1,512]{2,1,0:T(1,128)}), f32[32,1,512]{2,1,0:T(1,128)S(1)}, u32[]{:S(2)}, u32[]{:S(2)}) async-start(f32[32,1,512]{2,1,0:T(1,128)} %get-tuple-element.43), calls=%async_computation.10 | async-start | bytes 131072 | tf_op jit(solution)/shard_map/all_to_all | solution.py:39
  202.9 15.0 %all-to-all-start.11 = ((f32[16,1,512]{2,1,0:T(1,128)}), f32[16,1,512]{2,1,0:T(1,128)S(1)}, u32[]{:S(2)}, u32[]{:S(2)}) async-start(f32[16,1,512]{2,1,0:T(1,128)} %broadcast_in_dim.83), calls=%async_computation.11 | async-start | bytes 65536 | tf_op jit(solution)/shard_map/all_to_all | solution.py:39
Sparse Core Ops, SparseCore 0:
  17.5 79.1 all-gather.1

commit v9 on v8

--- a/solution.py
+++ b/solution.py
@@ -191,13 +191,13 @@
     sent = by_tile(jnp.concatenate([partial[:, :512], side.T[:96]], axis=1))
     caches = jnp.stack([key_cache, value_cache])
     parts = [
-        lax.dynamic_slice(caches, (0, (y + shift) % 4 * 2, 0, 0), (2, 2, slot_count, 128))
+        lax.dynamic_slice(caches, (0, (y ^ shift) * 2, 0, 0), (2, 2, slot_count, 128))
         for shift in range(4)
     ]
     sent, parts = lax.optimization_barrier((sent, parts))
     got = swap(sent, "z")
     for shift in range(1, 4):
-        parts[shift] = lax.ppermute(parts[shift], "y", [(i, (i + shift) % 4) for i in range(4)])
+        parts[shift] = lax.ppermute(parts[shift], "y", [(i, i ^ shift) for i in range(4)])
     sums = jnp.sum(got[:, :24].astype(F32), axis=0).reshape(4, 6, 128)
     rows = got[:, 24:]
     rows_wide = rows.astype(F32)
@@ -240,7 +240,7 @@
     keys, values = moved[0], moved[1]
     my_lengths = lax.dynamic_slice(lengths, (2 * y,), (2,))
     my_links = lax.dynamic_slice(links, (2 * y, 0, 0), (2, tree, tree))
-    source = (y - jnp.arange(4, dtype=jnp.int32)) % 4 + z * 4
+    source = (y ^ jnp.arange(4, dtype=jnp.int32)) + z * 4
     row_slots = (source[:, None] * slot_count + jnp.arange(slot_count, dtype=jnp.int32)).reshape(-1)
     valid_slot = (row_slots[None, :] < my_lengths[:, None])[:, None, None, :]
     valid_node = ((my_links > 0.5) & (z == 0))[:, None, :, :]
@@ -282,7 +282,8 @@
         contract,
         preferred_element_type=F32,
     )
-    attn, fresh = lax.optimization_barrier((attn.astype(BF), both[:, 36:]))
+    attn = jnp.broadcast_to(attn.astype(BF)[None], (8, 24, 512))
+    attn, fresh = lax.optimization_barrier((attn, both[:, 36:]))
     tree_keys = fresh[:, :96].reshape(requests, tree, 128)
     tree_values = fresh[:, 96:].reshape(requests, tree, 128)
 
@@ -297,7 +298,7 @@
     updated_values = jnp.where(hits, moved_values, value_cache)
 
     attn, updated_keys, updated_values = lax.optimization_barrier(
-        (spread(attn, ("x", "c"), 8), updated_keys, updated_values)
+        (swap(attn, ("x", "c")), updated_keys, updated_values)
     )
     attn = jnp.sum(attn.astype(F32), axis=0)
     middle = (hidden_rows.astype(F32) + attn).astype(BF)

time: 227 us -> 227 us (level)
  no operation moved by 1% of the time
where the time goes in v9:
time: 227 us; the launch traced here: 225 us
  starting transfers between devices  81 us (36%)
  waiting for transfers between devices  52.3 us (23%)
  blocking collectives  38.5 us (17%)
  between operations  14.9 us (7%)
  local copies, waits for them, and re-layouts  11.6 us (5%)
  matrix products  10.5 us (5%)
  other arithmetic  8.91 us (4%)
  Pallas kernels  7.42 us (3%)
    all_to_all x9, starting transfers between devices, swap(): return lax.all_to_all(values, axis, 0, 0, tiled=True)  66.5 us
    all_to_all x9, waiting for transfers between devices, swap(): return lax.all_to_all(values, axis, 0, 0, tiled=True)  47.8 us
    all_to_all x3, blocking collectives, swap(): return lax.all_to_all(values, axis, 0, 0, tiled=True)  38.5 us
    ppermute x3, starting transfers between devices, on_device(): lax.ppermute(parts[shift], 'y', [(i, i ^ shift) for i in range(4)])  9.27 us
    pallas_call x2, Pallas kernels, head(): pl.pallas_call(lambda *refs: head_kernel(*refs, flip=flip, width=2048), o...  5.63 us
    ppermute x1, starting transfers between devices, on_device(): other = lax.ppermute(half, 'c', [(0, 1), (1, 0)])  5.24 us
  transfers between devices with their start and end apart: 14, of which 10 were waited for; matrix products, arithmetic and copies ran while one was open for 10% of the time, Pallas kernels for 1%

profile of v9, /device:TPU:1, one launch (start us, length us, event | category | flops | bytes accessed | tf_op | source)
XLA Modules:
  0.0 225.2 jit_solution(11083164426357497061)
XLA Ops:
  7.2 1.8 pack.1
  9.0 5.0 %all-to-all-start = ((bf16[4,32,896]{2,1,0:T(8,128)(2,1)}), bf16[4,32,896]{2,1,0:T(8,128)(2,1)S(1)}, u32[]{:S(2)}, u32[]{:S(2)}) async-start(bf16[4,32,896]{2,1,0:T(8,128)(2,1)} %pack.1), calls=%async_computation | async-start | bytes 458752 | tf_op jit(solution)/shard_map/all_to_all | solution.py:39
  14.0 1.5 pad_maximum_fusion.2
  15.6 1.4 fusion.4
  20.7 14.9 %all-to-all-start.1 = ((bf16[16,30,128]{2,1,0:T(8,128)(2,1)}), bf16[16,30,128]{2,1,0:T(8,128)(2,1)S(1)}, u32[]{:S(2)}, u32[]{:S(2)}) async-start(bf16[16,30,128]{2,1,0:T(8,128)(2,1)} %copy.265), calls=%async_computation.1 | async-start | bytes 262144 | tf_op jit(solution)/shard_map/all_to_all | solution.py:39
  36.0 2.4 %collective-permute-start = (bf16[2,2,256,128]{3,2,1,0:T(8,128)(2,1)S(1)}, bf16[2,2,256,128]{3,2,1,0:T(8,128)(2,1)S(1)}, u32[]{:S(2)}, u32[]{:S(2)}) collective-permute-start(bf16[2,2,256,128]{3,2,1,0:T(8,128)(2,1)S(1)} %get-tuple-element.26), channel_id=1, source_target_pairs={{0,8},{8,0},{16,24},{24,16},{1,9},{9,1},{17,25},{25,17},{2,10},{10... | collective-permute-start | bytes 786440 | tf_op jit(solution)/shard_map/ppermute | solution.py:200
  38.4 3.7 %collective-permute-start.1 = (bf16[2,2,256,128]{3,2,1,0:T(8,128)(2,1)S(1)}, bf16[2,2,256,128]{3,2,1,0:T(8,128)(2,1)S(1)}, u32[]{:S(2)}, u32[]{:S(2)}) collective-permute-start(bf16[2,2,256,128]{3,2,1,0:T(8,128)(2,1)S(1)} %get-tuple-element.27), channel_id=1, source_target_pairs={{0,24},{8,16},{16,8},{24,0},{1,25},{9,17},{17,9},{25,1},{2,26},{10... | collective-permute-start | bytes 786440 | tf_op jit(solution)/shard_map/ppermute | solution.py:200
  42.1 5.5 %all-to-all-done.1 = bf16[16,30,128]{2,1,0:T(8,128)(2,1)S(1)} async-done(((bf16[16,30,128]{2,1,0:T(8,128)(2,1)}), bf16[16,30,128]{2,1,0:T(8,128)(2,1)S(1)}, u32[]{:S(2)}, u32[]{:S(2)}) %all-to-all-start.1) | async-done | bytes 122912 | tf_op jit(solution)/shard_map/all_to_all | solution.py:39
  49.4 9.8 %all-to-all-start.2 = ((bf16[16,32,128]{2,1,0:T(8,128)(2,1)}), bf16[16,32,128]{2,1,0:T(8,128)(2,1)S(1)}, u32[]{:S(2)}, u32[]{:S(2)}) async-start(bf16[16,32,128]{2,1,0:T(8,128)(2,1)} %broadcast_in_dim.69), calls=%async_computation.2 | async-start | bytes 262144 | tf_op jit(solution)/shard_map/all_to_all | solution.py:39
  59.3 3.1 %collective-permute-start.2 = (bf16[2,2,256,128]{3,2,1,0:T(8,128)(2,1)S(1)}, bf16[2,2,256,128]{3,2,1,0:T(8,128)(2,1)S(1)}, u32[]{:S(2)}, u32[]{:S(2)}) collective-permute-start(bf16[2,2,256,128]{3,2,1,0:T(8,128)(2,1)S(1)} %get-tuple-element.31), channel_id=1, source_target_pairs={{0,16},{8,24},{16,0},{24,8},{1,17},{9,25},{17,1},{25,9},{2,18},{10... | collective-permute-start | bytes 786440 | tf_op jit(solution)/shard_map/ppermute | solution.py:200
  63.5 4.5 %collective-permute-done.2 = bf16[2,2,256,128]{3,2,1,0:T(8,128)(2,1)S(1)} collective-permute-done((bf16[2,2,256,128]{3,2,1,0:T(8,128)(2,1)S(1)}, bf16[2,2,256,128]{3,2,1,0:T(8,128)(2,1)S(1)}, u32[]{:S(2)}, u32[]{:S(2)}) %collective-permute-start.2) | collective-permute-done | bytes 262176 | tf_op jit(solution)/shard_map/ppermute | solution.py:200
  68.0 3.4 %all-to-all-done.2 = bf16[16,32,128]{2,1,0:T(8,128)(2,1)S(1)} async-done(((bf16[16,32,128]{2,1,0:T(8,128)(2,1)}), bf16[16,32,128]{2,1,0:T(8,128)(2,1)S(1)}, u32[]{:S(2)}, u32[]{:S(2)}) %all-to-all-start.2) | async-done | bytes 131104 | tf_op jit(solution)/shard_map/all_to_all | solution.py:39
  74.7 8.3 %all-to-all-start.3 = ((bf16[16,30,128]{2,1,0:T(8,128)(2,1)}), bf16[16,30,128]{2,1,0:T(8,128)(2,1)S(1)}, u32[]{:S(2)}, u32[]{:S(2)}) async-start(bf16[16,30,128]{2,1,0:T(8,128)(2,1)} %copy.282), calls=%async_computation.3 | async-start | bytes 262144 | tf_op jit(solution)/shard_map/all_to_all | solution.py:39
  84.5 11.0 %all-to-all-done.3 = bf16[16,30,128]{2,1,0:T(8,128)(2,1)S(1)} async-done(((bf16[16,30,128]{2,1,0:T(8,128)(2,1)}), bf16[16,30,128]{2,1,0:T(8,128)(2,1)S(1)}, u32[]{:S(2)}, u32[]{:S(2)}) %all-to-all-start.3) | async-done | bytes 122912 | tf_op jit(solution)/shard_map/all_to_all | solution.py:39
  97.8 3.4 %all-to-all-start.4 = ((bf16[4,228,128]{2,1,0:T(8,128)(2,1)}), bf16[4,228,128]{2,1,0:T(8,128)(2,1)S(1)}, u32[]{:S(2)}, u32[]{:S(2)}) async-start(bf16[4,228,128]{2,1,0:T(8,128)(2,1)} %pad_maximum_fusion.1), calls=%async_computation.4 | async-start | bytes 475136 | tf_op jit(solution)/shard_map/all_to_all | solution.py:39
  101.5 5.1 %all-to-all-done.4 = bf16[4,228,128]{2,1,0:T(8,128)(2,1)S(1)} async-done(((bf16[4,228,128]{2,1,0:T(8,128)(2,1)}), bf16[4,228,128]{2,1,0:T(8,128)(2,1)S(1)}, u32[]{:S(2)}, u32[]{:S(2)}) %all-to-all-start.4) | async-done | bytes 233504 | tf_op jit(solution)/shard_map/all_to_all | solution.py:39
  106.8 1.1 convolution_convert_fusion.6
  109.3 12.2 %all-to-all-start.5 = ((bf16[8,24,512]{2,1,0:T(8,128)(2,1)}), bf16[8,24,512]{2,1,0:T(8,128)(2,1)S(1)}, u32[]{:S(2)}, u32[]{:S(2)}) async-start(bf16[8,24,512]{2,1,0:T(8,128)(2,1)} %broadcast_in_dim.76), calls=%async_computation.5 | async-start | bytes 393216 | tf_op jit(solution)/shard_map/all_to_all | solution.py:39
  121.5 2.4 %fusion.2 = bf16[8,256,128]{2,1,0:T(8,128)(2,1)} fusion(bf16[8,256,128]{2,1,0:T(8,128)(2,1)S(1)} %copy-done.3, bf16[8,48,128]{2,1,0:T(8,128)(2,1)} %bitcast.156, pred[8,256]{1,0:T(8,128)(4,1)S(1)} %broadcast_compare_fusion, f32[8,48]{1,0:T(8,128)S(1)} %gather_fusion, s32[8,48]{1,0:T(8,128)S(1)} %add_add_fusion, s32[256]{0:T(256)} %copy-done.6), kind=kOutput, calls=%fused_computation.14 | convolution fusion | flops 25886720 | bytes 1153024 | tf_op jit(solution)/shard_map/rca,rae->rce/dot_general | solution.py:296
  123.9 2.6 %fusion.1 = bf16[8,256,128]{2,1,0:T(8,128)(2,1)} fusion(bf16[8,256,128]{2,1,0:T(8,128)(2,1)} %param.37, bf16[8,48,128]{2,1,0:T(8,128)(2,1)S(1)} %bitcast.155, pred[8,256]{1,0:T(8,128)(4,1)S(1)} %broadcast_compare_fusion, f32[8,48]{1,0:T(8,128)S(1)} %gather_fusion, s32[8,48]{1,0:T(8,128)S(1)} %add_add_fusion, s32[256]{0:T(256)} %copy-done.6), kind=kOutput, calls=%fused_computation.13 | convolution fusion | flops 25886720 | bytes 1153024 | tf_op jit(solution)/shard_map/rca,rae->rce/dot_general | solution.py:295
  128.2 8.4 %all_to_all.60 = bf16[4,24,1664]{2,1,0:T(8,128)(2,1)S(1)} all-to-all(bf16[4,24,1664]{2,1,0:T(8,128)(2,1)S(1)} %broadcast_in_dim.79), channel_id=1, replica_groups=mesh['z'=16,'y'=4,'x'=4,'c'=2] {'y'}, dimensions={0} | all-to-all | bytes 638976 | tf_op jit(solution)/shard_map/all_to_all | solution.py:39
  137.9 5.7 %all-to-all-start.7 = ((bf16[8,12,128]{2,1,0:T(8,128)(2,1)}), bf16[8,12,128]{2,1,0:T(8,128)(2,1)S(1)}, u32[]{:S(2)}, u32[]{:S(2)}) async-start(bf16[8,12,128]{2,1,0:T(8,128)(2,1)} %copy.300), calls=%async_computation.7 | async-start | bytes 65536 | tf_op jit(solution)/shard_map/all_to_all | solution.py:39
  143.6 4.7 %all-to-all-done.7 = bf16[8,12,128]{2,1,0:T(8,128)(2,1)S(1)} async-done(((bf16[8,12,128]{2,1,0:T(8,128)(2,1)}), bf16[8,12,128]{2,1,0:T(8,128)(2,1)S(1)}, u32[]{:S(2)}, u32[]{:S(2)}) %all-to-all-start.7) | async-done | bytes 24608 | tf_op jit(solution)/shard_map/all_to_all | solution.py:39
  148.5 15.4 %all_to_all.61 = bf16[16,12,128]{2,1,0:T(8,128)(2,1)S(1)} all-to-all(bf16[16,12,128]{2,1,0:T(8,128)(2,1)S(1)} %broadcast_in_dim.80), channel_id=1, replica_groups=mesh['z'=16,'y'=4,'x'=4,'c'=2] {'z'}, dimensions={0} | all-to-all | bytes 98304 | tf_op jit(solution)/shard_map/all_to_all | solution.py:39
  164.1 14.7 %all_to_all.62.refs_2_ = bf16[16,192,128]{2,1,0:T(8,128)(2,1)S(1)} all-to-all(bf16[16,192,128]{2,1,0:T(8,128)(2,1)S(1)} %broadcast_in_dim.82), channel_id=1, replica_groups=mesh['z'=16,'y'=4,'x'=4,'c'=2] {'y','x'}, dimensions={0} | all-to-all | bytes 1572864 | tf_op jit(solution)/shard_map/all_to_all | solution.py:39
  178.8 5.2 %collective-permute-start.3 = (bf16[16,192,128]{2,1,0:T(8,128)(2,1)S(1)}, bf16[16,192,128]{2,1,0:T(8,128)(2,1)S(1)}, u32[]{:S(2)}, u32[]{:S(2)}) collective-permute-start(bf16[16,192,128]{2,1,0:T(8,128)(2,1)S(1)} %all_to_all.62.refs_2_), channel_id=1, source_target_pairs={{0,1},{1,0},{2,3},{3,2},{4,5},{5,4},{6,7},{7,6},{8,9},{9,8},{10,11... | collective-permute-start | bytes 2359304 | tf_op jit(solution)/shard_map/ppermute | solution.py:324
  184.0 2.8 %head_own.1 = (f32[192,256]{1,0:T(8,128)}, f32[1,256]{1,0:T(1,128)}) custom-call(s32[1]{0:T(128)} %bitcast.refs_0_, f32[8]{0:T(128)} %refs_1_.3, bf16[16,192,128]{2,1,0:T(8,128)(2,1)} %copy-done, f32[16,128]{1,0:T(8,128)} %reshape.508.refs_3_, bf16[2048,256]{1,0:T(8,128)(2,1)} %refs_4_.3), custom_call_target="tpu_custom_call" | custom-call | flops 201326592 | bytes 1835008 | tf_op jit(solution)/shard_map/head_own/pallas_call | solution.py:126
  187.8 2.8 %head_flip.1 = (f32[192,256]{1,0:T(8,128)}, f32[32,1,512]{2,1,0:T(1,128)}) custom-call(s32[1]{0:T(128)} %bitcast.refs_0_, f32[8]{0:T(128)} %refs_1_.3, bf16[16,192,128]{2,1,0:T(8,128)(2,1)} %copy-done.2, f32[16,128]{1,0:T(8,128)} %reshape.508.refs_3_, bf16[2048,256]{1,0:T(8,128)(2,1)} %refs_4_.3, f32[1,256]{1,0:T(1,128)} %get-tuple-element.41.refs_5_), custom_call_target="tpu_custom_call" | custom-call | flops 201326592 | bytes 1835008 | tf_op jit(solution)/shard_map/head_flip/pallas_call | solution.py:126
  190.6 3.6 %all-to-all-start.10 = ((f32[32,1,512]{2,1,0:T(1,128)}), f32[32,1,512]{2,1,0:T(1,128)S(1)}, u32[]{:S(2)}, u32[]{:S(2)}) async-start(f32[32,1,512]{2,1,0:T(1,128)} %get-tuple-element.43), calls=%async_computation.10 | async-start | bytes 131072 | tf_op jit(solution)/shard_map/all_to_all | solution.py:39
  195.9 5.7 %all-to-all-done.10 = f32[32,1,512]{2,1,0:T(1,128)S(1)} async-done(((f32[32,1,512]{2,1,0:T(1,128)}), f32[32,1,512]{2,1,0:T(1,128)S(1)}, u32[]{:S(2)}, u32[]{:S(2)}) %all-to-all-start.10) | async-done | bytes 65568 | tf_op jit(solution)/shard_map/all_to_all | solution.py:39
  202.4 3.5 %all-to-all-start.11 = ((f32[16,1,512]{2,1,0:T(1,128)}), f32[16,1,512]{2,1,0:T(1,128)S(1)}, u32[]{:S(2)}, u32[]{:S(2)}) async-start(f32[16,1,512]{2,1,0:T(1,128)} %broadcast_in_dim.83), calls=%async_computation.11 | async-start | bytes 65536 | tf_op jit(solution)/shard_map/all_to_all | solution.py:39
  206.8 10.5 %all-to-all-done.11 = f32[16,1,512]{2,1,0:T(1,128)S(1)} async-done(((f32[16,1,512]{2,1,0:T(1,128)}), f32[16,1,512]{2,1,0:T(1,128)S(1)}, u32[]{:S(2)}, u32[]{:S(2)}) %all-to-all-start.11) | async-done | bytes 32800 | tf_op jit(solution)/shard_map/all_to_all | solution.py:39
  (202 shorter events, 24.0 us)
Async XLA Ops:
  7.2 10.9 %copy-start.10 = (s32[8]{0:T(128)S(1)}, s32[8]{0:T(128)}, u32[]{:S(2)}) copy-start(s32[8]{0:T(128)} %param.41) | copy-start | bytes 100
  7.2 10.9 %copy-start.9 = (s32[8]{0:T(128)S(1)}, s32[8]{0:T(128)}, u32[]{:S(2)}) copy-start(s32[8]{0:T(128)} %param.39) | copy-start | bytes 100
  7.2 11.1 %copy-start.4 = (bf16[8,256,128]{2,1,0:T(8,128)(2,1)S(1)}, bf16[8,256,128]{2,1,0:T(8,128)(2,1)}, u32[]{:S(2)}) copy-start(bf16[8,256,128]{2,1,0:T(8,128)(2,1)} %param.37) | copy-start | bytes 1572868
  7.2 11.0 %copy-start.3 = (bf16[8,256,128]{2,1,0:T(8,128)(2,1)S(1)}, bf16[8,256,128]{2,1,0:T(8,128)(2,1)}, u32[]{:S(2)}) copy-start(bf16[8,256,128]{2,1,0:T(8,128)(2,1)} %param.38) | copy-start | bytes 1572868
  9.0 10.4 %all-to-all-start = ((bf16[4,32,896]{2,1,0:T(8,128)(2,1)}), bf16[4,32,896]{2,1,0:T(8,128)(2,1)S(1)}, u32[]{:S(2)}, u32[]{:S(2)}) async-start(bf16[4,32,896]{2,1,0:T(8,128)(2,1)} %pack.1), calls=%async_computation | async-start | bytes 458752 | tf_op jit(solution)/shard_map/all_to_all | solution.py:39
  14.0 92.8 %all-gather.2.cloned.1.call-start = ((), (), s32[]{:S(2)}) async-start(), calls=%async_computation.12 | async-start | bytes 2785280 | tf_op jit(solution)/shard_map/all_gather | solution.py:170
  18.3 29.8 %copy-start.7 = (f32[128]{0:T(128)S(1)}, f32[128]{0:T(128)}, u32[]{:S(2)}) copy-start(f32[128]{0:T(128)} %param.28) | copy-start | bytes 1540
  18.3 29.9 %copy-start.8 = (f32[128]{0:T(128)S(1)}, f32[128]{0:T(128)}, u32[]{:S(2)}) copy-start(f32[128]{0:T(128)} %param.27) | copy-start | bytes 1540
  20.7 26.9 %all-to-all-start.1 = ((bf16[16,30,128]{2,1,0:T(8,128)(2,1)}), bf16[16,30,128]{2,1,0:T(8,128)(2,1)S(1)}, u32[]{:S(2)}, u32[]{:S(2)}) async-start(bf16[16,30,128]{2,1,0:T(8,128)(2,1)} %copy.265), calls=%async_computation.1 | async-start | bytes 262144 | tf_op jit(solution)/shard_map/all_to_all | solution.py:39
  36.0 12.8 %collective-permute-start = (bf16[2,2,256,128]{3,2,1,0:T(8,128)(2,1)S(1)}, bf16[2,2,256,128]{3,2,1,0:T(8,128)(2,1)S(1)}, u32[]{:S(2)}, u32[]{:S(2)}) collective-permute-start(bf16[2,2,256,128]{3,2,1,0:T(8,128)(2,1)S(1)} %get-tuple-element.26), channel_id=1, source_target_pairs={{0,8},{8,0},{16,24},{24,16},{1,9},{9,1},{17,25},{25,17},{2,10},{10... | collective-permute-start | bytes 786440 | tf_op jit(solution)/shard_map/ppermute | solution.py:200
  38.4 10.4 %collective-permute-start.1 = (bf16[2,2,256,128]{3,2,1,0:T(8,128)(2,1)S(1)}, bf16[2,2,256,128]{3,2,1,0:T(8,128)(2,1)S(1)}, u32[]{:S(2)}, u32[]{:S(2)}) collective-permute-start(bf16[2,2,256,128]{3,2,1,0:T(8,128)(2,1)S(1)} %get-tuple-element.27), channel_id=1, source_target_pairs={{0,24},{8,16},{16,8},{24,0},{1,25},{9,17},{17,9},{25,1},{2,26},{10... | collective-permute-start | bytes 786440 | tf_op jit(solution)/shard_map/ppermute | solution.py:200
  49.4 22.0 %all-to-all-start.2 = ((bf16[16,32,128]{2,1,0:T(8,128)(2,1)}), bf16[16,32,128]{2,1,0:T(8,128)(2,1)S(1)}, u32[]{:S(2)}, u32[]{:S(2)}) async-start(bf16[16,32,128]{2,1,0:T(8,128)(2,1)} %broadcast_in_dim.69), calls=%async_computation.2 | async-start | bytes 262144 | tf_op jit(solution)/shard_map/all_to_all | solution.py:39
  59.3 8.7 %collective-permute-start.2 = (bf16[2,2,256,128]{3,2,1,0:T(8,128)(2,1)S(1)}, bf16[2,2,256,128]{3,2,1,0:T(8,128)(2,1)S(1)}, u32[]{:S(2)}, u32[]{:S(2)}) collective-permute-start(bf16[2,2,256,128]{3,2,1,0:T(8,128)(2,1)S(1)} %get-tuple-element.31), channel_id=1, source_target_pairs={{0,16},{8,24},{16,0},{24,8},{1,17},{9,25},{17,1},{25,9},{2,18},{10... | collective-permute-start | bytes 786440 | tf_op jit(solution)/shard_map/ppermute | solution.py:200
  62.5 20.6 %copy-start.6 = (s32[256]{0:T(256)}, s32[256]{0:T(256)S(1)}, u32[]{:S(2)}) copy-start(s32[256]{0:T(256)S(1)} %iota_add_fusion) | copy-start | bytes 3076
  74.7 20.8 %all-to-all-start.3 = ((bf16[16,30,128]{2,1,0:T(8,128)(2,1)}), bf16[16,30,128]{2,1,0:T(8,128)(2,1)S(1)}, u32[]{:S(2)}, u32[]{:S(2)}) async-start(bf16[16,30,128]{2,1,0:T(8,128)(2,1)} %copy.282), calls=%async_computation.3 | async-start | bytes 262144 | tf_op jit(solution)/shard_map/all_to_all | solution.py:39
  97.8 8.8 %all-to-all-start.4 = ((bf16[4,228,128]{2,1,0:T(8,128)(2,1)}), bf16[4,228,128]{2,1,0:T(8,128)(2,1)S(1)}, u32[]{:S(2)}, u32[]{:S(2)}) async-start(bf16[4,228,128]{2,1,0:T(8,128)(2,1)} %pad_maximum_fusion.1), calls=%async_computation.4 | async-start | bytes 475136 | tf_op jit(solution)/shard_map/all_to_all | solution.py:39
  108.7 19.2 %copy-start.1 = (bf16[512,2560]{1,0:T(8,128)(2,1)S(1)}, bf16[512,2560]{1,0:T(8,128)(2,1)}, u32[]{:S(2)}) copy-start(bf16[512,2560]{1,0:T(8,128)(2,1)} %all-gather.2.cloned.1.call-done) | copy-start | bytes 7864324
  109.3 18.1 %all-to-all-start.5 = ((bf16[8,24,512]{2,1,0:T(8,128)(2,1)}), bf16[8,24,512]{2,1,0:T(8,128)(2,1)S(1)}, u32[]{:S(2)}, u32[]{:S(2)}) async-start(bf16[8,24,512]{2,1,0:T(8,128)(2,1)} %broadcast_in_dim.76), calls=%async_computation.5 | async-start | bytes 393216 | tf_op jit(solution)/shard_map/all_to_all | solution.py:39
  137.9 10.4 %all-to-all-start.7 = ((bf16[8,12,128]{2,1,0:T(8,128)(2,1)}), bf16[8,12,128]{2,1,0:T(8,128)(2,1)S(1)}, u32[]{:S(2)}, u32[]{:S(2)}) async-start(bf16[8,12,128]{2,1,0:T(8,128)(2,1)} %copy.300), calls=%async_computation.7 | async-start | bytes 65536 | tf_op jit(solution)/shard_map/all_to_all | solution.py:39
  178.7 5.3 %copy-start = (bf16[16,192,128]{2,1,0:T(8,128)(2,1)}, bf16[16,192,128]{2,1,0:T(8,128)(2,1)S(1)}, u32[]{:S(2)}) copy-start(bf16[16,192,128]{2,1,0:T(8,128)(2,1)S(1)} %all_to_all.62.refs_2_) | copy-start | bytes 2359300
  178.8 8.1 %collective-permute-start.3 = (bf16[16,192,128]{2,1,0:T(8,128)(2,1)S(1)}, bf16[16,192,128]{2,1,0:T(8,128)(2,1)S(1)}, u32[]{:S(2)}, u32[]{:S(2)}) collective-permute-start(bf16[16,192,128]{2,1,0:T(8,128)(2,1)S(1)} %all_to_all.62.refs_2_), channel_id=1, source_target_pairs={{0,1},{1,0},{2,3},{3,2},{4,5},{5,4},{6,7},{7,6},{8,9},{9,8},{10,11... | collective-permute-start | bytes 2359304 | tf_op jit(solution)/shard_map/ppermute | solution.py:324
  186.8 19.0 %copy-start.5 = (f32[192,256]{1,0:T(8,128)S(1)}, f32[192,256]{1,0:T(8,128)}, u32[]{:S(2)}) copy-start(f32[192,256]{1,0:T(8,128)} %get-tuple-element.40) | copy-start | bytes 589828
  186.8 0.9 copy-start.2
  190.6 10.9 %all-to-all-start.10 = ((f32[32,1,512]{2,1,0:T(1,128)}), f32[32,1,512]{2,1,0:T(1,128)S(1)}, u32[]{:S(2)}, u32[]{:S(2)}) async-start(f32[32,1,512]{2,1,0:T(1,128)} %get-tuple-element.43), calls=%async_computation.10 | async-start | bytes 131072 | tf_op jit(solution)/shard_map/all_to_all | solution.py:39
  202.4 15.0 %all-to-all-start.11 = ((f32[16,1,512]{2,1,0:T(1,128)}), f32[16,1,512]{2,1,0:T(1,128)S(1)}, u32[]{:S(2)}, u32[]{:S(2)}) async-start(f32[16,1,512]{2,1,0:T(1,128)} %broadcast_in_dim.83), calls=%async_computation.11 | async-start | bytes 65536 | tf_op jit(solution)/shard_map/all_to_all | solution.py:39
Sparse Core Ops, SparseCore 0:
  17.5 80.3 all-gather.1

commit v10 on v9

--- a/solution.py
+++ b/solution.py
@@ -222,7 +222,7 @@
         ],
         axis=0,
     ).astype(BF)
-    block, parts[1], parts[3] = lax.optimization_barrier((block, parts[1], parts[3]))
+    block, parts[2] = lax.optimization_barrier((block, parts[2]))
     gathered, moved = lax.optimization_barrier((spread(block, "z", 16), jnp.concatenate(parts, axis=2)))
     gain_all = gathered[:, 24:30].astype(F32)
     ln2_mine = gain_all[:, 0] + gain_all[:, 1] + gain_all[:, 2]

time: 227 us -> 227 us (level)
  no operation moved by 1% of the time
where the time goes in v10:
time: 227 us; the launch traced here: 225 us
  starting transfers between devices  81.6 us (36%)
  waiting for transfers between devices  51.9 us (23%)
  blocking collectives  38.6 us (17%)
  between operations  14.9 us (7%)
  local copies, waits for them, and re-layouts  11.6 us (5%)
  matrix products  10.5 us (5%)
  other arithmetic  8.9 us (4%)
  Pallas kernels  7.42 us (3%)
    all_to_all x9, starting transfers between devices, swap(): return lax.all_to_all(values, axis, 0, 0, tiled=True)  65.5 us
    all_to_all x9, waiting for transfers between devices, swap(): return lax.all_to_all(values, axis, 0, 0, tiled=True)  48.4 us
    all_to_all x3, blocking collectives, swap(): return lax.all_to_all(values, axis, 0, 0, tiled=True)  38.6 us
    ppermute x3, starting transfers between devices, on_device(): lax.ppermute(parts[shift], 'y', [(i, i ^ shift) for i in range(4)])  10.8 us
    pallas_call x2, Pallas kernels, head(): pl.pallas_call(lambda *refs: head_kernel(*refs, flip=flip, width=2048), o...  5.63 us
    ppermute x1, starting transfers between devices, on_device(): other = lax.ppermute(half, 'c', [(0, 1), (1, 0)])  5.24 us
  transfers between devices with their start and end apart: 14, of which 10 were waited for; matrix products, arithmetic and copies ran while one was open for 10% of the time, Pallas kernels for 1%

profile of v10, /device:TPU:1, one launch (start us, length us, event | category | flops | bytes accessed | tf_op | source)
XLA Modules:
  0.0 225.5 jit_solution(14548167315369208142)
XLA Ops:
  7.2 1.8 pack.1
  9.0 5.0 %all-to-all-start = ((bf16[4,32,896]{2,1,0:T(8,128)(2,1)}), bf16[4,32,896]{2,1,0:T(8,128)(2,1)S(1)}, u32[]{:S(2)}, u32[]{:S(2)}) async-start(bf16[4,32,896]{2,1,0:T(8,128)(2,1)} %pack.1), calls=%async_computation | async-start | bytes 458752 | tf_op jit(solution)/shard_map/all_to_all | solution.py:39
  14.0 1.5 pad_maximum_fusion.2
  15.6 1.4 fusion.4
  20.7 14.9 %all-to-all-start.1 = ((bf16[16,30,128]{2,1,0:T(8,128)(2,1)}), bf16[16,30,128]{2,1,0:T(8,128)(2,1)S(1)}, u32[]{:S(2)}, u32[]{:S(2)}) async-start(bf16[16,30,128]{2,1,0:T(8,128)(2,1)} %copy.265), calls=%async_computation.1 | async-start | bytes 262144 | tf_op jit(solution)/shard_map/all_to_all | solution.py:39
  36.0 3.9 %collective-permute-start = (bf16[2,2,256,128]{3,2,1,0:T(8,128)(2,1)S(1)}, bf16[2,2,256,128]{3,2,1,0:T(8,128)(2,1)S(1)}, u32[]{:S(2)}, u32[]{:S(2)}) collective-permute-start(bf16[2,2,256,128]{3,2,1,0:T(8,128)(2,1)S(1)} %get-tuple-element.25), channel_id=1, source_target_pairs={{0,16},{8,24},{16,0},{24,8},{1,17},{9,25},{17,1},{25,9},{2,18},{10... | collective-permute-start | bytes 786440 | tf_op jit(solution)/shard_map/ppermute | solution.py:200
  39.9 7.7 %all-to-all-done.1 = bf16[16,30,128]{2,1,0:T(8,128)(2,1)S(1)} async-done(((bf16[16,30,128]{2,1,0:T(8,128)(2,1)}), bf16[16,30,128]{2,1,0:T(8,128)(2,1)S(1)}, u32[]{:S(2)}, u32[]{:S(2)}) %all-to-all-start.1) | async-done | bytes 122912 | tf_op jit(solution)/shard_map/all_to_all | solution.py:39
  49.4 7.3 %all-to-all-start.2 = ((bf16[16,32,128]{2,1,0:T(8,128)(2,1)}), bf16[16,32,128]{2,1,0:T(8,128)(2,1)S(1)}, u32[]{:S(2)}, u32[]{:S(2)}) async-start(bf16[16,32,128]{2,1,0:T(8,128)(2,1)} %broadcast_in_dim.69), calls=%async_computation.2 | async-start | bytes 262144 | tf_op jit(solution)/shard_map/all_to_all | solution.py:39
  56.8 2.6 %collective-permute-start.1 = (bf16[2,2,256,128]{3,2,1,0:T(8,128)(2,1)S(1)}, bf16[2,2,256,128]{3,2,1,0:T(8,128)(2,1)S(1)}, u32[]{:S(2)}, u32[]{:S(2)}) collective-permute-start(bf16[2,2,256,128]{3,2,1,0:T(8,128)(2,1)S(1)} %get-tuple-element.28), channel_id=1, source_target_pairs={{0,8},{8,0},{16,24},{24,16},{1,9},{9,1},{17,25},{25,17},{2,10},{10... | collective-permute-start | bytes 786440 | tf_op jit(solution)/shard_map/ppermute | solution.py:200
  59.4 4.3 %collective-permute-start.2 = (bf16[2,2,256,128]{3,2,1,0:T(8,128)(2,1)S(1)}, bf16[2,2,256,128]{3,2,1,0:T(8,128)(2,1)S(1)}, u32[]{:S(2)}, u32[]{:S(2)}) collective-permute-start(bf16[2,2,256,128]{3,2,1,0:T(8,128)(2,1)S(1)} %get-tuple-element.30), channel_id=1, source_target_pairs={{0,24},{8,16},{16,8},{24,0},{1,25},{9,17},{17,9},{25,1},{2,26},{10... | collective-permute-start | bytes 786440 | tf_op jit(solution)/shard_map/ppermute | solution.py:200
  64.7 3.4 %collective-permute-done.2 = bf16[2,2,256,128]{3,2,1,0:T(8,128)(2,1)S(1)} collective-permute-done((bf16[2,2,256,128]{3,2,1,0:T(8,128)(2,1)S(1)}, bf16[2,2,256,128]{3,2,1,0:T(8,128)(2,1)S(1)}, u32[]{:S(2)}, u32[]{:S(2)}) %collective-permute-start.2) | collective-permute-done | bytes 262176 | tf_op jit(solution)/shard_map/ppermute | solution.py:200
  68.2 1.4 all-to-all-done.2
  73.0 9.8 %all-to-all-start.3 = ((bf16[16,30,128]{2,1,0:T(8,128)(2,1)}), bf16[16,30,128]{2,1,0:T(8,128)(2,1)S(1)}, u32[]{:S(2)}, u32[]{:S(2)}) async-start(bf16[16,30,128]{2,1,0:T(8,128)(2,1)} %copy.282), calls=%async_computation.3 | async-start | bytes 262144 | tf_op jit(solution)/shard_map/all_to_all | solution.py:39
  84.2 11.3 %all-to-all-done.3 = bf16[16,30,128]{2,1,0:T(8,128)(2,1)S(1)} async-done(((bf16[16,30,128]{2,1,0:T(8,128)(2,1)}), bf16[16,30,128]{2,1,0:T(8,128)(2,1)S(1)}, u32[]{:S(2)}, u32[]{:S(2)}) %all-to-all-start.3) | async-done | bytes 122912 | tf_op jit(solution)/shard_map/all_to_all | solution.py:39
  97.8 3.8 %all-to-all-start.4 = ((bf16[4,228,128]{2,1,0:T(8,128)(2,1)}), bf16[4,228,128]{2,1,0:T(8,128)(2,1)S(1)}, u32[]{:S(2)}, u32[]{:S(2)}) async-start(bf16[4,228,128]{2,1,0:T(8,128)(2,1)} %pad_maximum_fusion.1), calls=%async_computation.4 | async-start | bytes 475136 | tf_op jit(solution)/shard_map/all_to_all | solution.py:39
  101.8 5.2 %all-to-all-done.4 = bf16[4,228,128]{2,1,0:T(8,128)(2,1)S(1)} async-done(((bf16[4,228,128]{2,1,0:T(8,128)(2,1)}), bf16[4,228,128]{2,1,0:T(8,128)(2,1)S(1)}, u32[]{:S(2)}, u32[]{:S(2)}) %all-to-all-start.4) | async-done | bytes 233504 | tf_op jit(solution)/shard_map/all_to_all | solution.py:39
  107.2 1.1 convolution_convert_fusion.6
  109.7 11.9 %all-to-all-start.5 = ((bf16[8,24,512]{2,1,0:T(8,128)(2,1)}), bf16[8,24,512]{2,1,0:T(8,128)(2,1)S(1)}, u32[]{:S(2)}, u32[]{:S(2)}) async-start(bf16[8,24,512]{2,1,0:T(8,128)(2,1)} %broadcast_in_dim.76), calls=%async_computation.5 | async-start | bytes 393216 | tf_op jit(solution)/shard_map/all_to_all | solution.py:39
  121.6 2.4 %fusion.2 = bf16[8,256,128]{2,1,0:T(8,128)(2,1)} fusion(bf16[8,256,128]{2,1,0:T(8,128)(2,1)S(1)} %copy-done.3, bf16[8,48,128]{2,1,0:T(8,128)(2,1)} %bitcast.156, pred[8,256]{1,0:T(8,128)(4,1)S(1)} %broadcast_compare_fusion, f32[8,48]{1,0:T(8,128)S(1)} %gather_fusion, s32[8,48]{1,0:T(8,128)S(1)} %add_add_fusion, s32[256]{0:T(256)} %copy-done.6), kind=kOutput, calls=%fused_computation.14 | convolution fusion | flops 25886720 | bytes 1153024 | tf_op jit(solution)/shard_map/rca,rae->rce/dot_general | solution.py:296
  123.9 2.6 %fusion.1 = bf16[8,256,128]{2,1,0:T(8,128)(2,1)} fusion(bf16[8,256,128]{2,1,0:T(8,128)(2,1)} %param.37, bf16[8,48,128]{2,1,0:T(8,128)(2,1)S(1)} %bitcast.155, pred[8,256]{1,0:T(8,128)(4,1)S(1)} %broadcast_compare_fusion, f32[8,48]{1,0:T(8,128)S(1)} %gather_fusion, s32[8,48]{1,0:T(8,128)S(1)} %add_add_fusion, s32[256]{0:T(256)} %copy-done.6), kind=kOutput, calls=%fused_computation.13 | convolution fusion | flops 25886720 | bytes 1153024 | tf_op jit(solution)/shard_map/rca,rae->rce/dot_general | solution.py:295
  128.3 8.4 %all_to_all.60 = bf16[4,24,1664]{2,1,0:T(8,128)(2,1)S(1)} all-to-all(bf16[4,24,1664]{2,1,0:T(8,128)(2,1)S(1)} %broadcast_in_dim.79), channel_id=1, replica_groups=mesh['z'=16,'y'=4,'x'=4,'c'=2] {'y'}, dimensions={0} | all-to-all | bytes 638976 | tf_op jit(solution)/shard_map/all_to_all | solution.py:39
  138.0 5.7 %all-to-all-start.7 = ((bf16[8,12,128]{2,1,0:T(8,128)(2,1)}), bf16[8,12,128]{2,1,0:T(8,128)(2,1)S(1)}, u32[]{:S(2)}, u32[]{:S(2)}) async-start(bf16[8,12,128]{2,1,0:T(8,128)(2,1)} %copy.300), calls=%async_computation.7 | async-start | bytes 65536 | tf_op jit(solution)/shard_map/all_to_all | solution.py:39
  143.7 4.7 %all-to-all-done.7 = bf16[8,12,128]{2,1,0:T(8,128)(2,1)S(1)} async-done(((bf16[8,12,128]{2,1,0:T(8,128)(2,1)}), bf16[8,12,128]{2,1,0:T(8,128)(2,1)S(1)}, u32[]{:S(2)}, u32[]{:S(2)}) %all-to-all-start.7) | async-done | bytes 24608 | tf_op jit(solution)/shard_map/all_to_all | solution.py:39
  148.6 15.5 %all_to_all.61 = bf16[16,12,128]{2,1,0:T(8,128)(2,1)S(1)} all-to-all(bf16[16,12,128]{2,1,0:T(8,128)(2,1)S(1)} %broadcast_in_dim.80), channel_id=1, replica_groups=mesh['z'=16,'y'=4,'x'=4,'c'=2] {'z'}, dimensions={0} | all-to-all | bytes 98304 | tf_op jit(solution)/shard_map/all_to_all | solution.py:39
  164.3 14.7 %all_to_all.62.refs_2_ = bf16[16,192,128]{2,1,0:T(8,128)(2,1)S(1)} all-to-all(bf16[16,192,128]{2,1,0:T(8,128)(2,1)S(1)} %broadcast_in_dim.82), channel_id=1, replica_groups=mesh['z'=16,'y'=4,'x'=4,'c'=2] {'y','x'}, dimensions={0} | all-to-all | bytes 1572864 | tf_op jit(solution)/shard_map/all_to_all | solution.py:39
  179.0 5.2 %collective-permute-start.3 = (bf16[16,192,128]{2,1,0:T(8,128)(2,1)S(1)}, bf16[16,192,128]{2,1,0:T(8,128)(2,1)S(1)}, u32[]{:S(2)}, u32[]{:S(2)}) collective-permute-start(bf16[16,192,128]{2,1,0:T(8,128)(2,1)S(1)} %all_to_all.62.refs_2_), channel_id=1, source_target_pairs={{0,1},{1,0},{2,3},{3,2},{4,5},{5,4},{6,7},{7,6},{8,9},{9,8},{10,11... | collective-permute-start | bytes 2359304 | tf_op jit(solution)/shard_map/ppermute | solution.py:324
  184.3 2.8 %head_own.1 = (f32[192,256]{1,0:T(8,128)}, f32[1,256]{1,0:T(1,128)}) custom-call(s32[1]{0:T(128)} %bitcast.refs_0_, f32[8]{0:T(128)} %refs_1_.3, bf16[16,192,128]{2,1,0:T(8,128)(2,1)} %copy-done, f32[16,128]{1,0:T(8,128)} %reshape.508.refs_3_, bf16[2048,256]{1,0:T(8,128)(2,1)} %refs_4_.3), custom_call_target="tpu_custom_call" | custom-call | flops 201326592 | bytes 1835008 | tf_op jit(solution)/shard_map/head_own/pallas_call | solution.py:126
  188.0 2.8 %head_flip.1 = (f32[192,256]{1,0:T(8,128)}, f32[32,1,512]{2,1,0:T(1,128)}) custom-call(s32[1]{0:T(128)} %bitcast.refs_0_, f32[8]{0:T(128)} %refs_1_.3, bf16[16,192,128]{2,1,0:T(8,128)(2,1)} %copy-done.2, f32[16,128]{1,0:T(8,128)} %reshape.508.refs_3_, bf16[2048,256]{1,0:T(8,128)(2,1)} %refs_4_.3, f32[1,256]{1,0:T(1,128)} %get-tuple-element.39.refs_5_), custom_call_target="tpu_custom_call" | custom-call | flops 201326592 | bytes 1835008 | tf_op jit(solution)/shard_map/head_flip/pallas_call | solution.py:126
  190.8 3.6 %all-to-all-start.10 = ((f32[32,1,512]{2,1,0:T(1,128)}), f32[32,1,512]{2,1,0:T(1,128)S(1)}, u32[]{:S(2)}, u32[]{:S(2)}) async-start(f32[32,1,512]{2,1,0:T(1,128)} %get-tuple-element.41), calls=%async_computation.10 | async-start | bytes 131072 | tf_op jit(solution)/shard_map/all_to_all | solution.py:39
  196.1 5.7 %all-to-all-done.10 = f32[32,1,512]{2,1,0:T(1,128)S(1)} async-done(((f32[32,1,512]{2,1,0:T(1,128)}), f32[32,1,512]{2,1,0:T(1,128)S(1)}, u32[]{:S(2)}, u32[]{:S(2)}) %all-to-all-start.10) | async-done | bytes 65568 | tf_op jit(solution)/shard_map/all_to_all | solution.py:39
  202.6 3.5 %all-to-all-start.11 = ((f32[16,1,512]{2,1,0:T(1,128)}), f32[16,1,512]{2,1,0:T(1,128)S(1)}, u32[]{:S(2)}, u32[]{:S(2)}) async-start(f32[16,1,512]{2,1,0:T(1,128)} %broadcast_in_dim.83), calls=%async_computation.11 | async-start | bytes 65536 | tf_op jit(solution)/shard_map/all_to_all | solution.py:39
  207.1 10.5 %all-to-all-done.11 = f32[16,1,512]{2,1,0:T(1,128)S(1)} async-done(((f32[16,1,512]{2,1,0:T(1,128)}), f32[16,1,512]{2,1,0:T(1,128)S(1)}, u32[]{:S(2)}, u32[]{:S(2)}) %all-to-all-start.11) | async-done | bytes 32800 | tf_op jit(solution)/shard_map/all_to_all | solution.py:39
  (202 shorter events, 24.0 us)
Async XLA Ops:
  7.2 10.9 %copy-start.10 = (s32[8]{0:T(128)S(1)}, s32[8]{0:T(128)}, u32[]{:S(2)}) copy-start(s32[8]{0:T(128)} %param.41) | copy-start | bytes 100
  7.2 10.9 %copy-start.9 = (s32[8]{0:T(128)S(1)}, s32[8]{0:T(128)}, u32[]{:S(2)}) copy-start(s32[8]{0:T(128)} %param.39) | copy-start | bytes 100
  7.2 11.1 %copy-start.4 = (bf16[8,256,128]{2,1,0:T(8,128)(2,1)S(1)}, bf16[8,256,128]{2,1,0:T(8,128)(2,1)}, u32[]{:S(2)}) copy-start(bf16[8,256,128]{2,1,0:T(8,128)(2,1)} %param.37) | copy-start | bytes 1572868
  7.2 11.0 %copy-start.3 = (bf16[8,256,128]{2,1,0:T(8,128)(2,1)S(1)}, bf16[8,256,128]{2,1,0:T(8,128)(2,1)}, u32[]{:S(2)}) copy-start(bf16[8,256,128]{2,1,0:T(8,128)(2,1)} %param.38) | copy-start | bytes 1572868
  9.0 10.4 %all-to-all-start = ((bf16[4,32,896]{2,1,0:T(8,128)(2,1)}), bf16[4,32,896]{2,1,0:T(8,128)(2,1)S(1)}, u32[]{:S(2)}, u32[]{:S(2)}) async-start(bf16[4,32,896]{2,1,0:T(8,128)(2,1)} %pack.1), calls=%async_computation | async-start | bytes 458752 | tf_op jit(solution)/shard_map/all_to_all | solution.py:39
  14.0 93.2 %all-gather.2.cloned.1.call-start = ((), (), s32[]{:S(2)}) async-start(), calls=%async_computation.12 | async-start | bytes 2785280 | tf_op jit(solution)/shard_map/all_gather | solution.py:170
  18.3 29.8 %copy-start.7 = (f32[128]{0:T(128)S(1)}, f32[128]{0:T(128)}, u32[]{:S(2)}) copy-start(f32[128]{0:T(128)} %param.28) | copy-start | bytes 1540
  18.3 29.9 %copy-start.8 = (f32[128]{0:T(128)S(1)}, f32[128]{0:T(128)}, u32[]{:S(2)}) copy-start(f32[128]{0:T(128)} %param.27) | copy-start | bytes 1540
  20.7 26.9 %all-to-all-start.1 = ((bf16[16,30,128]{2,1,0:T(8,128)(2,1)}), bf16[16,30,128]{2,1,0:T(8,128)(2,1)S(1)}, u32[]{:S(2)}, u32[]{:S(2)}) async-start(bf16[16,30,128]{2,1,0:T(8,128)(2,1)} %copy.265), calls=%async_computation.1 | async-start | bytes 262144 | tf_op jit(solution)/shard_map/all_to_all | solution.py:39
  36.0 12.8 %collective-permute-start = (bf16[2,2,256,128]{3,2,1,0:T(8,128)(2,1)S(1)}, bf16[2,2,256,128]{3,2,1,0:T(8,128)(2,1)S(1)}, u32[]{:S(2)}, u32[]{:S(2)}) collective-permute-start(bf16[2,2,256,128]{3,2,1,0:T(8,128)(2,1)S(1)} %get-tuple-element.25), channel_id=1, source_target_pairs={{0,16},{8,24},{16,0},{24,8},{1,17},{9,25},{17,1},{25,9},{2,18},{10... | collective-permute-start | bytes 786440 | tf_op jit(solution)/shard_map/ppermute | solution.py:200
  49.4 20.2 %all-to-all-start.2 = ((bf16[16,32,128]{2,1,0:T(8,128)(2,1)}), bf16[16,32,128]{2,1,0:T(8,128)(2,1)S(1)}, u32[]{:S(2)}, u32[]{:S(2)}) async-start(bf16[16,32,128]{2,1,0:T(8,128)(2,1)} %broadcast_in_dim.69), calls=%async_computation.2 | async-start | bytes 262144 | tf_op jit(solution)/shard_map/all_to_all | solution.py:39
  56.8 7.9 %collective-permute-start.1 = (bf16[2,2,256,128]{3,2,1,0:T(8,128)(2,1)S(1)}, bf16[2,2,256,128]{3,2,1,0:T(8,128)(2,1)S(1)}, u32[]{:S(2)}, u32[]{:S(2)}) collective-permute-start(bf16[2,2,256,128]{3,2,1,0:T(8,128)(2,1)S(1)} %get-tuple-element.28), channel_id=1, source_target_pairs={{0,8},{8,0},{16,24},{24,16},{1,9},{9,1},{17,25},{25,17},{2,10},{10... | collective-permute-start | bytes 786440 | tf_op jit(solution)/shard_map/ppermute | solution.py:200
  59.4 8.7 %collective-permute-start.2 = (bf16[2,2,256,128]{3,2,1,0:T(8,128)(2,1)S(1)}, bf16[2,2,256,128]{3,2,1,0:T(8,128)(2,1)S(1)}, u32[]{:S(2)}, u32[]{:S(2)}) collective-permute-start(bf16[2,2,256,128]{3,2,1,0:T(8,128)(2,1)S(1)} %get-tuple-element.30), channel_id=1, source_target_pairs={{0,24},{8,16},{16,8},{24,0},{1,25},{9,17},{17,9},{25,1},{2,26},{10... | collective-permute-start | bytes 786440 | tf_op jit(solution)/shard_map/ppermute | solution.py:200
  63.7 19.1 %copy-start.6 = (s32[256]{0:T(256)}, s32[256]{0:T(256)S(1)}, u32[]{:S(2)}) copy-start(s32[256]{0:T(256)S(1)} %iota_add_fusion) | copy-start | bytes 3076
  73.0 22.5 %all-to-all-start.3 = ((bf16[16,30,128]{2,1,0:T(8,128)(2,1)}), bf16[16,30,128]{2,1,0:T(8,128)(2,1)S(1)}, u32[]{:S(2)}, u32[]{:S(2)}) async-start(bf16[16,30,128]{2,1,0:T(8,128)(2,1)} %copy.282), calls=%async_computation.3 | async-start | bytes 262144 | tf_op jit(solution)/shard_map/all_to_all | solution.py:39
  97.8 9.2 %all-to-all-start.4 = ((bf16[4,228,128]{2,1,0:T(8,128)(2,1)}), bf16[4,228,128]{2,1,0:T(8,128)(2,1)S(1)}, u32[]{:S(2)}, u32[]{:S(2)}) async-start(bf16[4,228,128]{2,1,0:T(8,128)(2,1)} %pad_maximum_fusion.1), calls=%async_computation.4 | async-start | bytes 475136 | tf_op jit(solution)/shard_map/all_to_all | solution.py:39
  109.0 18.9 %copy-start.1 = (bf16[512,2560]{1,0:T(8,128)(2,1)S(1)}, bf16[512,2560]{1,0:T(8,128)(2,1)}, u32[]{:S(2)}) copy-start(bf16[512,2560]{1,0:T(8,128)(2,1)} %all-gather.2.cloned.1.call-done) | copy-start | bytes 7864324
  109.7 17.8 %all-to-all-start.5 = ((bf16[8,24,512]{2,1,0:T(8,128)(2,1)}), bf16[8,24,512]{2,1,0:T(8,128)(2,1)S(1)}, u32[]{:S(2)}, u32[]{:S(2)}) async-start(bf16[8,24,512]{2,1,0:T(8,128)(2,1)} %broadcast_in_dim.76), calls=%async_computation.5 | async-start | bytes 393216 | tf_op jit(solution)/shard_map/all_to_all | solution.py:39
  138.0 10.4 %all-to-all-start.7 = ((bf16[8,12,128]{2,1,0:T(8,128)(2,1)}), bf16[8,12,128]{2,1,0:T(8,128)(2,1)S(1)}, u32[]{:S(2)}, u32[]{:S(2)}) async-start(bf16[8,12,128]{2,1,0:T(8,128)(2,1)} %copy.300), calls=%async_computation.7 | async-start | bytes 65536 | tf_op jit(solution)/shard_map/all_to_all | solution.py:39
  179.0 5.3 %copy-start = (bf16[16,192,128]{2,1,0:T(8,128)(2,1)}, bf16[16,192,128]{2,1,0:T(8,128)(2,1)S(1)}, u32[]{:S(2)}) copy-start(bf16[16,192,128]{2,1,0:T(8,128)(2,1)S(1)} %all_to_all.62.refs_2_) | copy-start | bytes 2359300
  179.0 8.1 %collective-permute-start.3 = (bf16[16,192,128]{2,1,0:T(8,128)(2,1)S(1)}, bf16[16,192,128]{2,1,0:T(8,128)(2,1)S(1)}, u32[]{:S(2)}, u32[]{:S(2)}) collective-permute-start(bf16[16,192,128]{2,1,0:T(8,128)(2,1)S(1)} %all_to_all.62.refs_2_), channel_id=1, source_target_pairs={{0,1},{1,0},{2,3},{3,2},{4,5},{5,4},{6,7},{7,6},{8,9},{9,8},{10,11... | collective-permute-start | bytes 2359304 | tf_op jit(solution)/shard_map/ppermute | solution.py:324
  187.1 19.0 %copy-start.5 = (f32[192,256]{1,0:T(8,128)S(1)}, f32[192,256]{1,0:T(8,128)}, u32[]{:S(2)}) copy-start(f32[192,256]{1,0:T(8,128)} %get-tuple-element.38) | copy-start | bytes 589828
  187.1 0.9 copy-start.2
  190.8 10.9 %all-to-all-start.10 = ((f32[32,1,512]{2,1,0:T(1,128)}), f32[32,1,512]{2,1,0:T(1,128)S(1)}, u32[]{:S(2)}, u32[]{:S(2)}) async-start(f32[32,1,512]{2,1,0:T(1,128)} %get-tuple-element.41), calls=%async_computation.10 | async-start | bytes 131072 | tf_op jit(solution)/shard_map/all_to_all | solution.py:39
  202.6 15.0 %all-to-all-start.11 = ((f32[16,1,512]{2,1,0:T(1,128)}), f32[16,1,512]{2,1,0:T(1,128)S(1)}, u32[]{:S(2)}, u32[]{:S(2)}) async-start(f32[16,1,512]{2,1,0:T(1,128)} %broadcast_in_dim.83), calls=%async_computation.11 | async-start | bytes 65536 | tf_op jit(solution)/shard_map/all_to_all | solution.py:39
Sparse Core Ops, SparseCore 0:
  17.5 80.3 all-gather.1

commit v11 on v9

--- a/solution.py
+++ b/solution.py
@@ -127,7 +127,7 @@
         lambda *refs: head_kernel(*refs, flip=flip, width=2048),
         out_shape=(
             jax.ShapeDtypeStruct((rows, 256), F32),
-            jax.ShapeDtypeStruct((32, 1, 512) if flip else (1, 256), F32),
+            jax.ShapeDtypeStruct((8, 1, 512) if flip else (1, 256), F32),
         ),
         in_specs=[smem, smem, vmem, vmem, vmem] + [vmem] * len(extra),
         out_specs=(vmem, vmem),
@@ -272,6 +272,7 @@
     residual = jnp.transpose(rows.reshape(4, 4, 6, 4, 32), (3, 0, 2, 1, 4)).reshape(4, 24, 128)
     same = jnp.concatenate([gated, tokens[192:]], axis=0)
     both = swap(jnp.concatenate([residual, jnp.broadcast_to(same[None], (4, 204, 128))], axis=1), "y")
+    both, ffn = lax.optimization_barrier((both, ffn))
     hidden_rows = jnp.swapaxes(both[:, :24].reshape(4, 4, 6, 128), 1, 2).reshape(24, 512)
     gated = jnp.swapaxes(both[:, 24:36].reshape(4, 2, 6, 128), 0, 1).reshape(2, 24, 128)
 
@@ -336,10 +337,10 @@
 
     own = in_order(own_columns(half), own_columns(other))
     next_hidden = lax.dynamic_slice(own, (0, z % 4 * 32), (384, 32))
-    spots = swap(spots, ("y", "x", "c"))
+    spots = swap(spots, ("x", "c"))
     top = jnp.max(spots, axis=0)
     spot = top + jnp.log(jnp.sum(jnp.exp(spots - top), axis=0))
-    spots = spread(spot, "z", 16)
+    spots = spread(spot, ("z", "y"), 64)
     top = jnp.max(spots, axis=0)
     spot = top + jnp.log(jnp.sum(jnp.exp(spots - top), axis=0))
     spot = spot.reshape(2, 256)[:, :192].reshape(384, 1)

time: 227 us -> 231 us (1.018)
  blocking collectives: 38.5 us -> 47.3 us
  waiting for transfers between devices: 52.3 us -> 48.9 us
    all_to_all x3 -> x4, blocking collectives: 38.5 us -> 47.3 us  [swap(): return lax.all_to_all(values, axis, 0, 0, tiled=True)]
    all_to_all x9 -> x8, waiting for transfers between devices: 47.8 us -> 43.5 us  [swap(): return lax.all_to_all(values, axis, 0, 0, tiled=True)]
    all_to_all x9 -> x8, starting transfers between devices: 66.5 us -> 64.9 us  [swap(): return lax.all_to_all(values, axis, 0, 0, tiled=True)]
  transfers between devices with their start and end apart: 14 -> 13, of which waited for: 10 -> 9; matrix products, arithmetic and copies ran while one was open for 10% -> 10% of each run, Pallas kernels for 1% -> 1%
where the time goes in v11:
time: 231 us; the launch traced here: 229 us
  starting transfers between devices  79.2 us (34%)
  waiting for transfers between devices  48.9 us (21%)
  blocking collectives  47.3 us (20%)
  between operations  14.8 us (6%)
  local copies, waits for them, and re-layouts  11.7 us (5%)
  matrix products  10.5 us (5%)
  other arithmetic  8.88 us (4%)
  Pallas kernels  7.38 us (3%)
    all_to_all x8, starting transfers between devices, swap(): return lax.all_to_all(values, axis, 0, 0, tiled=True)  64.9 us
    all_to_all x4, blocking collectives, swap(): return lax.all_to_all(values, axis, 0, 0, tiled=True)  47.3 us
    all_to_all x8, waiting for transfers between devices, swap(): return lax.all_to_all(values, axis, 0, 0, tiled=True)  43.5 us
    ppermute x3, starting transfers between devices, on_device(): lax.ppermute(parts[shift], 'y', [(i, i ^ shift) for i in range(4)])  9.27 us
    pallas_call x2, Pallas kernels, head(): pl.pallas_call(lambda *refs: head_kernel(*refs, flip=flip, width=2048), o...  5.59 us
    ppermute x3, waiting for transfers between devices, on_device(): lax.ppermute(parts[shift], 'y', [(i, i ^ shift) for i in range(4)])  5.32 us
    ppermute x1, starting transfers between devices, on_device(): other = lax.ppermute(half, 'c', [(0, 1), (1, 0)])  5.02 us
  transfers between devices with their start and end apart: 13, of which 9 were waited for; matrix products, arithmetic and copies ran while one was open for 10% of the time, Pallas kernels for 1%

profile of v11, /device:TPU:1, one launch (start us, length us, event | category | flops | bytes accessed | tf_op | source)
XLA Modules:
  0.0 228.7 jit_solution(17778554454806503292)
XLA Ops:
  7.2 1.8 pack.1
  9.0 5.0 %all-to-all-start = ((bf16[4,32,896]{2,1,0:T(8,128)(2,1)}), bf16[4,32,896]{2,1,0:T(8,128)(2,1)S(1)}, u32[]{:S(2)}, u32[]{:S(2)}) async-start(bf16[4,32,896]{2,1,0:T(8,128)(2,1)} %pack.1), calls=%async_computation | async-start | bytes 458752 | tf_op jit(solution)/shard_map/all_to_all | solution.py:39
  14.0 1.5 pad_maximum_fusion.2
  15.6 1.4 fusion.4
  18.4 1.0 all-to-all-done
  20.7 14.9 %all-to-all-start.1 = ((bf16[16,30,128]{2,1,0:T(8,128)(2,1)}), bf16[16,30,128]{2,1,0:T(8,128)(2,1)S(1)}, u32[]{:S(2)}, u32[]{:S(2)}) async-start(bf16[16,30,128]{2,1,0:T(8,128)(2,1)} %copy.265), calls=%async_computation.1 | async-start | bytes 262144 | tf_op jit(solution)/shard_map/all_to_all | solution.py:39
  36.0 2.4 %collective-permute-start = (bf16[2,2,256,128]{3,2,1,0:T(8,128)(2,1)S(1)}, bf16[2,2,256,128]{3,2,1,0:T(8,128)(2,1)S(1)}, u32[]{:S(2)}, u32[]{:S(2)}) collective-permute-start(bf16[2,2,256,128]{3,2,1,0:T(8,128)(2,1)S(1)} %get-tuple-element.28), channel_id=1, source_target_pairs={{0,8},{8,0},{16,24},{24,16},{1,9},{9,1},{17,25},{25,17},{2,10},{10... | collective-permute-start | bytes 786440 | tf_op jit(solution)/shard_map/ppermute | solution.py:200
  38.4 3.7 %collective-permute-start.1 = (bf16[2,2,256,128]{3,2,1,0:T(8,128)(2,1)S(1)}, bf16[2,2,256,128]{3,2,1,0:T(8,128)(2,1)S(1)}, u32[]{:S(2)}, u32[]{:S(2)}) collective-permute-start(bf16[2,2,256,128]{3,2,1,0:T(8,128)(2,1)S(1)} %get-tuple-element.29), channel_id=1, source_target_pairs={{0,24},{8,16},{16,8},{24,0},{1,25},{9,17},{17,9},{25,1},{2,26},{10... | collective-permute-start | bytes 786440 | tf_op jit(solution)/shard_map/ppermute | solution.py:200
  42.1 5.5 %all-to-all-done.1 = bf16[16,30,128]{2,1,0:T(8,128)(2,1)S(1)} async-done(((bf16[16,30,128]{2,1,0:T(8,128)(2,1)}), bf16[16,30,128]{2,1,0:T(8,128)(2,1)S(1)}, u32[]{:S(2)}, u32[]{:S(2)}) %all-to-all-start.1) | async-done | bytes 122912 | tf_op jit(solution)/shard_map/all_to_all | solution.py:39
  49.4 9.8 %all-to-all-start.2 = ((bf16[16,32,128]{2,1,0:T(8,128)(2,1)}), bf16[16,32,128]{2,1,0:T(8,128)(2,1)S(1)}, u32[]{:S(2)}, u32[]{:S(2)}) async-start(bf16[16,32,128]{2,1,0:T(8,128)(2,1)} %broadcast_in_dim.69), calls=%async_computation.2 | async-start | bytes 262144 | tf_op jit(solution)/shard_map/all_to_all | solution.py:39
  60.1 3.1 %collective-permute-start.2 = (bf16[2,2,256,128]{3,2,1,0:T(8,128)(2,1)S(1)}, bf16[2,2,256,128]{3,2,1,0:T(8,128)(2,1)S(1)}, u32[]{:S(2)}, u32[]{:S(2)}) collective-permute-start(bf16[2,2,256,128]{3,2,1,0:T(8,128)(2,1)S(1)} %get-tuple-element.33), channel_id=1, source_target_pairs={{0,16},{8,24},{16,0},{24,8},{1,17},{9,25},{17,1},{25,9},{2,18},{10... | collective-permute-start | bytes 786440 | tf_op jit(solution)/shard_map/ppermute | solution.py:200
  63.4 5.3 %collective-permute-done.2 = bf16[2,2,256,128]{3,2,1,0:T(8,128)(2,1)S(1)} collective-permute-done((bf16[2,2,256,128]{3,2,1,0:T(8,128)(2,1)S(1)}, bf16[2,2,256,128]{3,2,1,0:T(8,128)(2,1)S(1)}, u32[]{:S(2)}, u32[]{:S(2)}) %collective-permute-start.2) | collective-permute-done | bytes 262176 | tf_op jit(solution)/shard_map/ppermute | solution.py:200
  68.8 2.5 %all-to-all-done.2 = bf16[16,32,128]{2,1,0:T(8,128)(2,1)S(1)} async-done(((bf16[16,32,128]{2,1,0:T(8,128)(2,1)}), bf16[16,32,128]{2,1,0:T(8,128)(2,1)S(1)}, u32[]{:S(2)}, u32[]{:S(2)}) %all-to-all-start.2) | async-done | bytes 131104 | tf_op jit(solution)/shard_map/all_to_all | solution.py:39
  74.7 9.1 %all-to-all-start.3 = ((bf16[16,30,128]{2,1,0:T(8,128)(2,1)}), bf16[16,30,128]{2,1,0:T(8,128)(2,1)S(1)}, u32[]{:S(2)}, u32[]{:S(2)}) async-start(bf16[16,30,128]{2,1,0:T(8,128)(2,1)} %copy.282), calls=%async_computation.3 | async-start | bytes 262144 | tf_op jit(solution)/shard_map/all_to_all | solution.py:39
  85.2 10.8 %all-to-all-done.3 = bf16[16,30,128]{2,1,0:T(8,128)(2,1)S(1)} async-done(((bf16[16,30,128]{2,1,0:T(8,128)(2,1)}), bf16[16,30,128]{2,1,0:T(8,128)(2,1)S(1)}, u32[]{:S(2)}, u32[]{:S(2)}) %all-to-all-start.3) | async-done | bytes 122912 | tf_op jit(solution)/shard_map/all_to_all | solution.py:39
  98.3 3.9 %all-to-all-start.4 = ((bf16[4,228,128]{2,1,0:T(8,128)(2,1)}), bf16[4,228,128]{2,1,0:T(8,128)(2,1)S(1)}, u32[]{:S(2)}, u32[]{:S(2)}) async-start(bf16[4,228,128]{2,1,0:T(8,128)(2,1)} %pad_maximum_fusion.1), calls=%async_computation.4 | async-start | bytes 475136 | tf_op jit(solution)/shard_map/all_to_all | solution.py:39
  102.4 5.2 %all-to-all-done.4 = bf16[4,228,128]{2,1,0:T(8,128)(2,1)S(1)} async-done(((bf16[4,228,128]{2,1,0:T(8,128)(2,1)}), bf16[4,228,128]{2,1,0:T(8,128)(2,1)S(1)}, u32[]{:S(2)}, u32[]{:S(2)}) %all-to-all-start.4) | async-done | bytes 233504 | tf_op jit(solution)/shard_map/all_to_all | solution.py:39
  107.8 1.1 convolution_convert_fusion.6
  110.2 11.8 %all-to-all-start.5 = ((bf16[8,24,512]{2,1,0:T(8,128)(2,1)}), bf16[8,24,512]{2,1,0:T(8,128)(2,1)S(1)}, u32[]{:S(2)}, u32[]{:S(2)}) async-start(bf16[8,24,512]{2,1,0:T(8,128)(2,1)} %broadcast_in_dim.76), calls=%async_computation.5 | async-start | bytes 393216 | tf_op jit(solution)/shard_map/all_to_all | solution.py:39
  122.1 2.4 %fusion.2 = bf16[8,256,128]{2,1,0:T(8,128)(2,1)} fusion(bf16[8,256,128]{2,1,0:T(8,128)(2,1)S(1)} %copy-done.2, bf16[8,48,128]{2,1,0:T(8,128)(2,1)} %bitcast.156, pred[8,256]{1,0:T(8,128)(4,1)S(1)} %broadcast_compare_fusion, f32[8,48]{1,0:T(8,128)S(1)} %gather_fusion, s32[8,48]{1,0:T(8,128)S(1)} %add_add_fusion, s32[256]{0:T(256)} %copy-done.5), kind=kOutput, calls=%fused_computation.14 | convolution fusion | flops 25886720 | bytes 1153024 | tf_op jit(solution)/shard_map/rca,rae->rce/dot_general | solution.py:297
  124.5 2.6 %fusion.1 = bf16[8,256,128]{2,1,0:T(8,128)(2,1)} fusion(bf16[8,256,128]{2,1,0:T(8,128)(2,1)} %param.37, bf16[8,48,128]{2,1,0:T(8,128)(2,1)S(1)} %bitcast.155, pred[8,256]{1,0:T(8,128)(4,1)S(1)} %broadcast_compare_fusion, f32[8,48]{1,0:T(8,128)S(1)} %gather_fusion, s32[8,48]{1,0:T(8,128)S(1)} %add_add_fusion, s32[256]{0:T(256)} %copy-done.5), kind=kOutput, calls=%fused_computation.13 | convolution fusion | flops 25886720 | bytes 1153024 | tf_op jit(solution)/shard_map/rca,rae->rce/dot_general | solution.py:296
  128.8 8.4 %all_to_all.60 = bf16[4,24,1664]{2,1,0:T(8,128)(2,1)S(1)} all-to-all(bf16[4,24,1664]{2,1,0:T(8,128)(2,1)S(1)} %broadcast_in_dim.79), channel_id=1, replica_groups=mesh['z'=16,'y'=4,'x'=4,'c'=2] {'y'}, dimensions={0} | all-to-all | bytes 638976 | tf_op jit(solution)/shard_map/all_to_all | solution.py:39
  138.5 5.7 %all-to-all-start.7 = ((bf16[8,12,128]{2,1,0:T(8,128)(2,1)}), bf16[8,12,128]{2,1,0:T(8,128)(2,1)S(1)}, u32[]{:S(2)}, u32[]{:S(2)}) async-start(bf16[8,12,128]{2,1,0:T(8,128)(2,1)} %copy.300), calls=%async_computation.7 | async-start | bytes 65536 | tf_op jit(solution)/shard_map/all_to_all | solution.py:39
  144.3 4.7 %all-to-all-done.7 = bf16[8,12,128]{2,1,0:T(8,128)(2,1)S(1)} async-done(((bf16[8,12,128]{2,1,0:T(8,128)(2,1)}), bf16[8,12,128]{2,1,0:T(8,128)(2,1)S(1)}, u32[]{:S(2)}, u32[]{:S(2)}) %all-to-all-start.7) | async-done | bytes 24608 | tf_op jit(solution)/shard_map/all_to_all | solution.py:39
  149.1 15.4 %all_to_all.61 = bf16[16,12,128]{2,1,0:T(8,128)(2,1)S(1)} all-to-all(bf16[16,12,128]{2,1,0:T(8,128)(2,1)S(1)} %broadcast_in_dim.80), channel_id=1, replica_groups=mesh['z'=16,'y'=4,'x'=4,'c'=2] {'z'}, dimensions={0} | all-to-all | bytes 98304 | tf_op jit(solution)/shard_map/all_to_all | solution.py:39
  164.7 15.5 %all_to_all.62.refs_2_ = bf16[16,192,128]{2,1,0:T(8,128)(2,1)} all-to-all(bf16[16,192,128]{2,1,0:T(8,128)(2,1)S(1)} %broadcast_in_dim.82), channel_id=1, replica_groups=mesh['z'=16,'y'=4,'x'=4,'c'=2] {'y','x'}, dimensions={0} | all-to-all | bytes 1572864 | tf_op jit(solution)/shard_map/all_to_all | solution.py:39
  180.3 5.0 %collective-permute-start.3 = (bf16[16,192,128]{2,1,0:T(8,128)(2,1)}, bf16[16,192,128]{2,1,0:T(8,128)(2,1)S(1)}, u32[]{:S(2)}, u32[]{:S(2)}) collective-permute-start(bf16[16,192,128]{2,1,0:T(8,128)(2,1)} %all_to_all.62.refs_2_), channel_id=1, source_target_pairs={{0,1},{1,0},{2,3},{3,2},{4,5},{5,4},{6,7},{7,6},{8,9},{9,8},{10,11... | collective-permute-start | bytes 2359304 | tf_op jit(solution)/shard_map/ppermute | solution.py:325
  185.3 2.8 %head_own.1 = (f32[192,256]{1,0:T(8,128)}, f32[1,256]{1,0:T(1,128)}) custom-call(s32[1]{0:T(128)} %bitcast.refs_0_, f32[8]{0:T(128)} %refs_1_.3, bf16[16,192,128]{2,1,0:T(8,128)(2,1)} %all_to_all.62.refs_2_, f32[16,128]{1,0:T(8,128)} %reshape.508.refs_3_, bf16[2048,256]{1,0:T(8,128)(2,1)} %refs_4_.3), custom_call_target="tpu_custom_call" | custom-call | flops 201326592 | bytes 1835008 | tf_op jit(solution)/shard_map/head_own/pallas_call | solution.py:126
  189.0 2.8 %head_flip.1 = (f32[192,256]{1,0:T(8,128)}, f32[8,1,512]{2,1,0:T(1,128)}) custom-call(s32[1]{0:T(128)} %bitcast.refs_0_, f32[8]{0:T(128)} %refs_1_.3, bf16[16,192,128]{2,1,0:T(8,128)(2,1)} %copy-done.1, f32[16,128]{1,0:T(8,128)} %reshape.508.refs_3_, bf16[2048,256]{1,0:T(8,128)(2,1)} %refs_4_.3, f32[1,256]{1,0:T(1,128)} %get-tuple-element.45.refs_5_), custom_call_target="tpu_custom_call" | custom-call | flops 201326592 | bytes 1835008 | tf_op jit(solution)/shard_map/head_flip/pallas_call | solution.py:126
  191.8 7.9 %all_to_all.63 = f32[8,1,512]{2,1,0:T(1,128)S(1)} all-to-all(f32[8,1,512]{2,1,0:T(1,128)} %get-tuple-element.47), channel_id=1, replica_groups=mesh['z'=16,'y'=4,'x'=4,'c'=2] {'x','c'}, dimensions={0} | all-to-all | bytes 32768 | tf_op jit(solution)/shard_map/all_to_all | solution.py:39
  200.5 4.6 %all-to-all-start.11 = ((f32[64,1,512]{2,1,0:T(1,128)}), f32[64,1,512]{2,1,0:T(1,128)S(1)}, u32[]{:S(2)}, u32[]{:S(2)}) async-start(f32[64,1,512]{2,1,0:T(1,128)} %broadcast_in_dim.83), calls=%async_computation.11 | async-start | bytes 262144 | tf_op jit(solution)/shard_map/all_to_all | solution.py:39
  207.7 12.9 %all-to-all-done.11 = f32[64,1,512]{2,1,0:T(1,128)S(1)} async-done(((f32[64,1,512]{2,1,0:T(1,128)}), f32[64,1,512]{2,1,0:T(1,128)S(1)}, u32[]{:S(2)}, u32[]{:S(2)}) %all-to-all-start.11) | async-done | bytes 131104 | tf_op jit(solution)/shard_map/all_to_all | solution.py:39
  (199 shorter events, 23.0 us)
Async XLA Ops:
  7.2 10.9 %copy-start.9 = (s32[8]{0:T(128)S(1)}, s32[8]{0:T(128)}, u32[]{:S(2)}) copy-start(s32[8]{0:T(128)} %param.41) | copy-start | bytes 100
  7.2 10.9 %copy-start.8 = (s32[8]{0:T(128)S(1)}, s32[8]{0:T(128)}, u32[]{:S(2)}) copy-start(s32[8]{0:T(128)} %param.39) | copy-start | bytes 100
  7.2 11.1 %copy-start.3 = (bf16[8,256,128]{2,1,0:T(8,128)(2,1)S(1)}, bf16[8,256,128]{2,1,0:T(8,128)(2,1)}, u32[]{:S(2)}) copy-start(bf16[8,256,128]{2,1,0:T(8,128)(2,1)} %param.37) | copy-start | bytes 1572868
  7.2 11.0 %copy-start.2 = (bf16[8,256,128]{2,1,0:T(8,128)(2,1)S(1)}, bf16[8,256,128]{2,1,0:T(8,128)(2,1)}, u32[]{:S(2)}) copy-start(bf16[8,256,128]{2,1,0:T(8,128)(2,1)} %param.38) | copy-start | bytes 1572868
  9.0 10.4 %all-to-all-start = ((bf16[4,32,896]{2,1,0:T(8,128)(2,1)}), bf16[4,32,896]{2,1,0:T(8,128)(2,1)S(1)}, u32[]{:S(2)}, u32[]{:S(2)}) async-start(bf16[4,32,896]{2,1,0:T(8,128)(2,1)} %pack.1), calls=%async_computation | async-start | bytes 458752 | tf_op jit(solution)/shard_map/all_to_all | solution.py:39
  14.0 93.6 %all-gather.2.cloned.1.call-start = ((), (), s32[]{:S(2)}) async-start(), calls=%async_computation.12 | async-start | bytes 2785280 | tf_op jit(solution)/shard_map/all_gather | solution.py:170
  18.3 29.8 %copy-start.6 = (f32[128]{0:T(128)S(1)}, f32[128]{0:T(128)}, u32[]{:S(2)}) copy-start(f32[128]{0:T(128)} %param.28) | copy-start | bytes 1540
  18.3 29.9 %copy-start.7 = (f32[128]{0:T(128)S(1)}, f32[128]{0:T(128)}, u32[]{:S(2)}) copy-start(f32[128]{0:T(128)} %param.27) | copy-start | bytes 1540
  20.7 26.9 %all-to-all-start.1 = ((bf16[16,30,128]{2,1,0:T(8,128)(2,1)}), bf16[16,30,128]{2,1,0:T(8,128)(2,1)S(1)}, u32[]{:S(2)}, u32[]{:S(2)}) async-start(bf16[16,30,128]{2,1,0:T(8,128)(2,1)} %copy.265), calls=%async_computation.1 | async-start | bytes 262144 | tf_op jit(solution)/shard_map/all_to_all | solution.py:39
  36.0 12.8 %collective-permute-start = (bf16[2,2,256,128]{3,2,1,0:T(8,128)(2,1)S(1)}, bf16[2,2,256,128]{3,2,1,0:T(8,128)(2,1)S(1)}, u32[]{:S(2)}, u32[]{:S(2)}) collective-permute-start(bf16[2,2,256,128]{3,2,1,0:T(8,128)(2,1)S(1)} %get-tuple-element.28), channel_id=1, source_target_pairs={{0,8},{8,0},{16,24},{24,16},{1,9},{9,1},{17,25},{25,17},{2,10},{10... | collective-permute-start | bytes 786440 | tf_op jit(solution)/shard_map/ppermute | solution.py:200
  38.4 10.4 %collective-permute-start.1 = (bf16[2,2,256,128]{3,2,1,0:T(8,128)(2,1)S(1)}, bf16[2,2,256,128]{3,2,1,0:T(8,128)(2,1)S(1)}, u32[]{:S(2)}, u32[]{:S(2)}) collective-permute-start(bf16[2,2,256,128]{3,2,1,0:T(8,128)(2,1)S(1)} %get-tuple-element.29), channel_id=1, source_target_pairs={{0,24},{8,16},{16,8},{24,0},{1,25},{9,17},{17,9},{25,1},{2,26},{10... | collective-permute-start | bytes 786440 | tf_op jit(solution)/shard_map/ppermute | solution.py:200
  49.4 21.9 %all-to-all-start.2 = ((bf16[16,32,128]{2,1,0:T(8,128)(2,1)}), bf16[16,32,128]{2,1,0:T(8,128)(2,1)S(1)}, u32[]{:S(2)}, u32[]{:S(2)}) async-start(bf16[16,32,128]{2,1,0:T(8,128)(2,1)} %broadcast_in_dim.69), calls=%async_computation.2 | async-start | bytes 262144 | tf_op jit(solution)/shard_map/all_to_all | solution.py:39
  60.1 8.6 %collective-permute-start.2 = (bf16[2,2,256,128]{3,2,1,0:T(8,128)(2,1)S(1)}, bf16[2,2,256,128]{3,2,1,0:T(8,128)(2,1)S(1)}, u32[]{:S(2)}, u32[]{:S(2)}) collective-permute-start(bf16[2,2,256,128]{3,2,1,0:T(8,128)(2,1)S(1)} %get-tuple-element.33), channel_id=1, source_target_pairs={{0,16},{8,24},{16,0},{24,8},{1,17},{9,25},{17,1},{25,9},{2,18},{10... | collective-permute-start | bytes 786440 | tf_op jit(solution)/shard_map/ppermute | solution.py:200
  63.4 44.2 %copy-start.5 = (s32[256]{0:T(256)}, s32[256]{0:T(256)S(1)}, u32[]{:S(2)}) copy-start(s32[256]{0:T(256)S(1)} %iota_add_fusion) | copy-start | bytes 3076
  74.7 21.4 %all-to-all-start.3 = ((bf16[16,30,128]{2,1,0:T(8,128)(2,1)}), bf16[16,30,128]{2,1,0:T(8,128)(2,1)S(1)}, u32[]{:S(2)}, u32[]{:S(2)}) async-start(bf16[16,30,128]{2,1,0:T(8,128)(2,1)} %copy.282), calls=%async_computation.3 | async-start | bytes 262144 | tf_op jit(solution)/shard_map/all_to_all | solution.py:39
  98.3 9.3 %all-to-all-start.4 = ((bf16[4,228,128]{2,1,0:T(8,128)(2,1)}), bf16[4,228,128]{2,1,0:T(8,128)(2,1)S(1)}, u32[]{:S(2)}, u32[]{:S(2)}) async-start(bf16[4,228,128]{2,1,0:T(8,128)(2,1)} %pad_maximum_fusion.1), calls=%async_computation.4 | async-start | bytes 475136 | tf_op jit(solution)/shard_map/all_to_all | solution.py:39
  109.6 18.8 %copy-start = (bf16[512,2560]{1,0:T(8,128)(2,1)S(1)}, bf16[512,2560]{1,0:T(8,128)(2,1)}, u32[]{:S(2)}) copy-start(bf16[512,2560]{1,0:T(8,128)(2,1)} %all-gather.2.cloned.1.call-done) | copy-start | bytes 7864324
  110.2 17.7 %all-to-all-start.5 = ((bf16[8,24,512]{2,1,0:T(8,128)(2,1)}), bf16[8,24,512]{2,1,0:T(8,128)(2,1)S(1)}, u32[]{:S(2)}, u32[]{:S(2)}) async-start(bf16[8,24,512]{2,1,0:T(8,128)(2,1)} %broadcast_in_dim.76), calls=%async_computation.5 | async-start | bytes 393216 | tf_op jit(solution)/shard_map/all_to_all | solution.py:39
  138.5 10.5 %all-to-all-start.7 = ((bf16[8,12,128]{2,1,0:T(8,128)(2,1)}), bf16[8,12,128]{2,1,0:T(8,128)(2,1)S(1)}, u32[]{:S(2)}, u32[]{:S(2)}) async-start(bf16[8,12,128]{2,1,0:T(8,128)(2,1)} %copy.300), calls=%async_computation.7 | async-start | bytes 65536 | tf_op jit(solution)/shard_map/all_to_all | solution.py:39
  180.3 7.8 %collective-permute-start.3 = (bf16[16,192,128]{2,1,0:T(8,128)(2,1)}, bf16[16,192,128]{2,1,0:T(8,128)(2,1)S(1)}, u32[]{:S(2)}, u32[]{:S(2)}) collective-permute-start(bf16[16,192,128]{2,1,0:T(8,128)(2,1)} %all_to_all.62.refs_2_), channel_id=1, source_target_pairs={{0,1},{1,0},{2,3},{3,2},{4,5},{5,4},{6,7},{7,6},{8,9},{9,8},{10,11... | collective-permute-start | bytes 2359304 | tf_op jit(solution)/shard_map/ppermute | solution.py:325
  188.1 18.7 %copy-start.4 = (f32[192,256]{1,0:T(8,128)S(1)}, f32[192,256]{1,0:T(8,128)}, u32[]{:S(2)}) copy-start(f32[192,256]{1,0:T(8,128)} %get-tuple-element.44) | copy-start | bytes 589828
  188.1 0.9 copy-start.1
  200.5 20.2 %all-to-all-start.11 = ((f32[64,1,512]{2,1,0:T(1,128)}), f32[64,1,512]{2,1,0:T(1,128)S(1)}, u32[]{:S(2)}, u32[]{:S(2)}) async-start(f32[64,1,512]{2,1,0:T(1,128)} %broadcast_in_dim.83), calls=%async_computation.11 | async-start | bytes 262144 | tf_op jit(solution)/shard_map/all_to_all | solution.py:39
Sparse Core Ops, SparseCore 0:
  17.5 79.0 all-gather.1

commit v12 on v9

--- a/solution.py
+++ b/solution.py
@@ -48,7 +48,14 @@
     return high.astype(BF), (values - high).astype(BF)
 
 
-def pack_kernel(hidden_ref, ln1_ref, ln2_ref, last_ref, wq_ref, wk_ref, wv_ref, wg_ref, out_ref):
+def pack_kernel(
+    hidden_ref, ln1_ref, ln2_ref, last_ref, wq_ref, wk_ref, wv_ref, wg_ref,
+    gate_ref, up_ref, down_ref, wo_ref, out_ref, joined_ref,
+):
+    joined_ref[:, 0:768] = gate_ref[...]
+    joined_ref[:, 768:1536] = up_ref[...]
+    joined_ref[:, 1536:2304] = down_ref[...]
+    joined_ref[:, 2304:2560] = wo_ref[...]
     lane = lax.broadcasted_iota(jnp.int32, (1, 512), 1)
     first = lane // 128
     local = lane - first * 128
@@ -166,16 +173,18 @@
     width = 2048
 
 
-    ffn = jnp.concatenate([w_gate, w_up, w_down.T, wo.T], axis=1)
+    vmem = pl.BlockSpec(memory_space=pltpu.VMEM)
+    pieces, ffn = pl.pallas_call(
+        pack_kernel,
+        out_shape=(jax.ShapeDtypeStruct((4, 32, 896), BF), jax.ShapeDtypeStruct((32, 2560), BF)),
+        in_specs=[vmem] * 12,
+        out_specs=(vmem, vmem),
+        name="pack",
+    )(
+        hidden.T, *(gain.reshape(1, 32) for gain in (ln1_gain, ln2_gain, last_gain)), wq, wk, wv, wg,
+        w_gate, w_up, w_down.T, wo.T,
+    )
     ffn = lax.all_gather(ffn, "z", axis=0, tiled=True)
-    vmem = pl.BlockSpec(memory_space=pltpu.VMEM)
-    pieces = pl.pallas_call(
-        pack_kernel,
-        out_shape=jax.ShapeDtypeStruct((4, 32, 896), BF),
-        in_specs=[vmem] * 8,
-        out_specs=vmem,
-        name="pack",
-    )(hidden.T, *(gain.reshape(1, 32) for gain in (ln1_gain, ln2_gain, last_gain)), wq, wk, wv, wg)
     mine = swap(pieces, "y").reshape(128, 896)
     proj, side = mine[:, :768], mine[:, 768:]
     side_wide = side.astype(F32)

time: 227 us -> 227 us (level)
  no operation moved by 1% of the time
where the time goes in v12:
time: 227 us; the launch traced here: 225 us
  starting transfers between devices  81.6 us (36%)
  waiting for transfers between devices  52 us (23%)
  blocking collectives  38.6 us (17%)
  between operations  14.9 us (7%)
  local copies, waits for them, and re-layouts  11.6 us (5%)
  matrix products  10.5 us (5%)
  other arithmetic  8.68 us (4%)
  Pallas kernels  7.54 us (3%)
    all_to_all x9, starting transfers between devices, swap(): return lax.all_to_all(values, axis, 0, 0, tiled=True)  66.2 us
    all_to_all x9, waiting for transfers between devices, swap(): return lax.all_to_all(values, axis, 0, 0, tiled=True)  47.2 us
    all_to_all x3, blocking collectives, swap(): return lax.all_to_all(values, axis, 0, 0, tiled=True)  38.6 us
    ppermute x3, starting transfers between devices, on_device(): lax.ppermute(parts[shift], 'y', [(i, i ^ shift) for i in range(4)])  10.2 us
    pallas_call x2, Pallas kernels, head(): pl.pallas_call(lambda *refs: head_kernel(*refs, flip=flip, width=2048), o...  5.63 us
    ppermute x1, starting transfers between devices, on_device(): other = lax.ppermute(half, 'c', [(0, 1), (1, 0)])  5.24 us
  transfers between devices with their start and end apart: 14, of which 10 were waited for; matrix products, arithmetic and copies ran while one was open for 10% of the time, Pallas kernels for 1%

profile of v12, /device:TPU:1, one launch (start us, length us, event | category | flops | bytes accessed | tf_op | source)
XLA Modules:
  0.0 225.4 jit_solution(6387923992909960894)
XLA Ops:
  7.2 1.9 pack.1
  9.1 5.0 %all-to-all-start = ((bf16[4,32,896]{2,1,0:T(8,128)(2,1)}), bf16[4,32,896]{2,1,0:T(8,128)(2,1)S(1)}, u32[]{:S(2)}, u32[]{:S(2)}) async-start(bf16[4,32,896]{2,1,0:T(8,128)(2,1)} %get-tuple-element.27), calls=%async_computation | async-start | bytes 458752 | tf_op jit(solution)/shard_map/all_to_all | solution.py:39
  14.9 1.4 fusion.4
  20.8 14.9 %all-to-all-start.1 = ((bf16[16,30,128]{2,1,0:T(8,128)(2,1)}), bf16[16,30,128]{2,1,0:T(8,128)(2,1)S(1)}, u32[]{:S(2)}, u32[]{:S(2)}) async-start(bf16[16,30,128]{2,1,0:T(8,128)(2,1)} %copy.265), calls=%async_computation.1 | async-start | bytes 262144 | tf_op jit(solution)/shard_map/all_to_all | solution.py:39
  36.1 2.9 %collective-permute-start = (bf16[2,2,256,128]{3,2,1,0:T(8,128)(2,1)S(1)}, bf16[2,2,256,128]{3,2,1,0:T(8,128)(2,1)S(1)}, u32[]{:S(2)}, u32[]{:S(2)}) collective-permute-start(bf16[2,2,256,128]{3,2,1,0:T(8,128)(2,1)S(1)} %get-tuple-element.29), channel_id=1, source_target_pairs={{0,8},{8,0},{16,24},{24,16},{1,9},{9,1},{17,25},{25,17},{2,10},{10... | collective-permute-start | bytes 786440 | tf_op jit(solution)/shard_map/ppermute | solution.py:209
  38.9 3.7 %collective-permute-start.1 = (bf16[2,2,256,128]{3,2,1,0:T(8,128)(2,1)S(1)}, bf16[2,2,256,128]{3,2,1,0:T(8,128)(2,1)S(1)}, u32[]{:S(2)}, u32[]{:S(2)}) collective-permute-start(bf16[2,2,256,128]{3,2,1,0:T(8,128)(2,1)S(1)} %get-tuple-element.30), channel_id=1, source_target_pairs={{0,24},{8,16},{16,8},{24,0},{1,25},{9,17},{17,9},{25,1},{2,26},{10... | collective-permute-start | bytes 786440 | tf_op jit(solution)/shard_map/ppermute | solution.py:209
  42.7 5.1 %all-to-all-done.1 = bf16[16,30,128]{2,1,0:T(8,128)(2,1)S(1)} async-done(((bf16[16,30,128]{2,1,0:T(8,128)(2,1)}), bf16[16,30,128]{2,1,0:T(8,128)(2,1)S(1)}, u32[]{:S(2)}, u32[]{:S(2)}) %all-to-all-start.1) | async-done | bytes 122912 | tf_op jit(solution)/shard_map/all_to_all | solution.py:39
  49.5 9.9 %all-to-all-start.2 = ((bf16[16,32,128]{2,1,0:T(8,128)(2,1)}), bf16[16,32,128]{2,1,0:T(8,128)(2,1)S(1)}, u32[]{:S(2)}, u32[]{:S(2)}) async-start(bf16[16,32,128]{2,1,0:T(8,128)(2,1)} %broadcast_in_dim.69), calls=%async_computation.2 | async-start | bytes 262144 | tf_op jit(solution)/shard_map/all_to_all | solution.py:39
  59.4 3.6 %collective-permute-start.2 = (bf16[2,2,256,128]{3,2,1,0:T(8,128)(2,1)S(1)}, bf16[2,2,256,128]{3,2,1,0:T(8,128)(2,1)S(1)}, u32[]{:S(2)}, u32[]{:S(2)}) collective-permute-start(bf16[2,2,256,128]{3,2,1,0:T(8,128)(2,1)S(1)} %get-tuple-element.34), channel_id=1, source_target_pairs={{0,16},{8,24},{16,0},{24,8},{1,17},{9,25},{17,1},{25,9},{2,18},{10... | collective-permute-start | bytes 786440 | tf_op jit(solution)/shard_map/ppermute | solution.py:209
  64.1 4.1 %collective-permute-done.2 = bf16[2,2,256,128]{3,2,1,0:T(8,128)(2,1)S(1)} collective-permute-done((bf16[2,2,256,128]{3,2,1,0:T(8,128)(2,1)S(1)}, bf16[2,2,256,128]{3,2,1,0:T(8,128)(2,1)S(1)}, u32[]{:S(2)}, u32[]{:S(2)}) %collective-permute-start.2) | collective-permute-done | bytes 262176 | tf_op jit(solution)/shard_map/ppermute | solution.py:209
  68.2 3.4 %all-to-all-done.2 = bf16[16,32,128]{2,1,0:T(8,128)(2,1)S(1)} async-done(((bf16[16,32,128]{2,1,0:T(8,128)(2,1)}), bf16[16,32,128]{2,1,0:T(8,128)(2,1)S(1)}, u32[]{:S(2)}, u32[]{:S(2)}) %all-to-all-start.2) | async-done | bytes 131104 | tf_op jit(solution)/shard_map/all_to_all | solution.py:39
  74.9 8.3 %all-to-all-start.3 = ((bf16[16,30,128]{2,1,0:T(8,128)(2,1)}), bf16[16,30,128]{2,1,0:T(8,128)(2,1)S(1)}, u32[]{:S(2)}, u32[]{:S(2)}) async-start(bf16[16,30,128]{2,1,0:T(8,128)(2,1)} %copy.282), calls=%async_computation.3 | async-start | bytes 262144 | tf_op jit(solution)/shard_map/all_to_all | solution.py:39
  84.7 11.3 %all-to-all-done.3 = bf16[16,30,128]{2,1,0:T(8,128)(2,1)S(1)} async-done(((bf16[16,30,128]{2,1,0:T(8,128)(2,1)}), bf16[16,30,128]{2,1,0:T(8,128)(2,1)S(1)}, u32[]{:S(2)}, u32[]{:S(2)}) %all-to-all-start.3) | async-done | bytes 122912 | tf_op jit(solution)/shard_map/all_to_all | solution.py:39
  98.2 3.4 %all-to-all-start.4 = ((bf16[4,228,128]{2,1,0:T(8,128)(2,1)}), bf16[4,228,128]{2,1,0:T(8,128)(2,1)S(1)}, u32[]{:S(2)}, u32[]{:S(2)}) async-start(bf16[4,228,128]{2,1,0:T(8,128)(2,1)} %pad_maximum_fusion.1), calls=%async_computation.4 | async-start | bytes 475136 | tf_op jit(solution)/shard_map/all_to_all | solution.py:39
  101.9 5.1 %all-to-all-done.4 = bf16[4,228,128]{2,1,0:T(8,128)(2,1)S(1)} async-done(((bf16[4,228,128]{2,1,0:T(8,128)(2,1)}), bf16[4,228,128]{2,1,0:T(8,128)(2,1)S(1)}, u32[]{:S(2)}, u32[]{:S(2)}) %all-to-all-start.4) | async-done | bytes 233504 | tf_op jit(solution)/shard_map/all_to_all | solution.py:39
  107.2 1.1 convolution_convert_fusion.6
  109.7 11.8 %all-to-all-start.5 = ((bf16[8,24,512]{2,1,0:T(8,128)(2,1)}), bf16[8,24,512]{2,1,0:T(8,128)(2,1)S(1)}, u32[]{:S(2)}, u32[]{:S(2)}) async-start(bf16[8,24,512]{2,1,0:T(8,128)(2,1)} %broadcast_in_dim.76), calls=%async_computation.5 | async-start | bytes 393216 | tf_op jit(solution)/shard_map/all_to_all | solution.py:39
  121.5 2.4 %fusion.2 = bf16[8,256,128]{2,1,0:T(8,128)(2,1)} fusion(bf16[8,256,128]{2,1,0:T(8,128)(2,1)S(1)} %copy-done.3, bf16[8,48,128]{2,1,0:T(8,128)(2,1)} %bitcast.156, pred[8,256]{1,0:T(8,128)(4,1)S(1)} %broadcast_compare_fusion, f32[8,48]{1,0:T(8,128)S(1)} %gather_fusion, s32[8,48]{1,0:T(8,128)S(1)} %add_add_fusion, s32[256]{0:T(256)} %copy-done.6), kind=kOutput, calls=%fused_computation.14 | convolution fusion | flops 25886720 | bytes 1153024 | tf_op jit(solution)/shard_map/rca,rae->rce/dot_general | solution.py:305
  123.9 2.6 %fusion.1 = bf16[8,256,128]{2,1,0:T(8,128)(2,1)} fusion(bf16[8,256,128]{2,1,0:T(8,128)(2,1)} %param.37, bf16[8,48,128]{2,1,0:T(8,128)(2,1)S(1)} %bitcast.155, pred[8,256]{1,0:T(8,128)(4,1)S(1)} %broadcast_compare_fusion, f32[8,48]{1,0:T(8,128)S(1)} %gather_fusion, s32[8,48]{1,0:T(8,128)S(1)} %add_add_fusion, s32[256]{0:T(256)} %copy-done.6), kind=kOutput, calls=%fused_computation.13 | convolution fusion | flops 25886720 | bytes 1153024 | tf_op jit(solution)/shard_map/rca,rae->rce/dot_general | solution.py:304
  128.3 8.4 %all_to_all.60 = bf16[4,24,1664]{2,1,0:T(8,128)(2,1)S(1)} all-to-all(bf16[4,24,1664]{2,1,0:T(8,128)(2,1)S(1)} %broadcast_in_dim.79), channel_id=1, replica_groups=mesh['z'=16,'y'=4,'x'=4,'c'=2] {'y'}, dimensions={0} | all-to-all | bytes 638976 | tf_op jit(solution)/shard_map/all_to_all | solution.py:39
  138.0 5.7 %all-to-all-start.7 = ((bf16[8,12,128]{2,1,0:T(8,128)(2,1)}), bf16[8,12,128]{2,1,0:T(8,128)(2,1)S(1)}, u32[]{:S(2)}, u32[]{:S(2)}) async-start(bf16[8,12,128]{2,1,0:T(8,128)(2,1)} %copy.300), calls=%async_computation.7 | async-start | bytes 65536 | tf_op jit(solution)/shard_map/all_to_all | solution.py:39
  143.7 4.7 %all-to-all-done.7 = bf16[8,12,128]{2,1,0:T(8,128)(2,1)S(1)} async-done(((bf16[8,12,128]{2,1,0:T(8,128)(2,1)}), bf16[8,12,128]{2,1,0:T(8,128)(2,1)S(1)}, u32[]{:S(2)}, u32[]{:S(2)}) %all-to-all-start.7) | async-done | bytes 24608 | tf_op jit(solution)/shard_map/all_to_all | solution.py:39
  148.5 15.5 %all_to_all.61 = bf16[16,12,128]{2,1,0:T(8,128)(2,1)S(1)} all-to-all(bf16[16,12,128]{2,1,0:T(8,128)(2,1)S(1)} %broadcast_in_dim.80), channel_id=1, replica_groups=mesh['z'=16,'y'=4,'x'=4,'c'=2] {'z'}, dimensions={0} | all-to-all | bytes 98304 | tf_op jit(solution)/shard_map/all_to_all | solution.py:39
  164.2 14.7 %all_to_all.62.refs_2_ = bf16[16,192,128]{2,1,0:T(8,128)(2,1)S(1)} all-to-all(bf16[16,192,128]{2,1,0:T(8,128)(2,1)S(1)} %broadcast_in_dim.82), channel_id=1, replica_groups=mesh['z'=16,'y'=4,'x'=4,'c'=2] {'y','x'}, dimensions={0} | all-to-all | bytes 1572864 | tf_op jit(solution)/shard_map/all_to_all | solution.py:39
  178.9 5.2 %collective-permute-start.3 = (bf16[16,192,128]{2,1,0:T(8,128)(2,1)S(1)}, bf16[16,192,128]{2,1,0:T(8,128)(2,1)S(1)}, u32[]{:S(2)}, u32[]{:S(2)}) collective-permute-start(bf16[16,192,128]{2,1,0:T(8,128)(2,1)S(1)} %all_to_all.62.refs_2_), channel_id=1, source_target_pairs={{0,1},{1,0},{2,3},{3,2},{4,5},{5,4},{6,7},{7,6},{8,9},{9,8},{10,11... | collective-permute-start | bytes 2359304 | tf_op jit(solution)/shard_map/ppermute | solution.py:333
  184.2 2.8 %head_own.1 = (f32[192,256]{1,0:T(8,128)}, f32[1,256]{1,0:T(1,128)}) custom-call(s32[1]{0:T(128)} %bitcast.refs_0_, f32[8]{0:T(128)} %refs_1_.3, bf16[16,192,128]{2,1,0:T(8,128)(2,1)} %copy-done, f32[16,128]{1,0:T(8,128)} %reshape.508.refs_3_, bf16[2048,256]{1,0:T(8,128)(2,1)} %refs_4_.3), custom_call_target="tpu_custom_call" | custom-call | flops 201326592 | bytes 1835008 | tf_op jit(solution)/shard_map/head_own/pallas_call | solution.py:133
  187.9 2.8 %head_flip.1 = (f32[192,256]{1,0:T(8,128)}, f32[32,1,512]{2,1,0:T(1,128)}) custom-call(s32[1]{0:T(128)} %bitcast.refs_0_, f32[8]{0:T(128)} %refs_1_.3, bf16[16,192,128]{2,1,0:T(8,128)(2,1)} %copy-done.2, f32[16,128]{1,0:T(8,128)} %reshape.508.refs_3_, bf16[2048,256]{1,0:T(8,128)(2,1)} %refs_4_.3, f32[1,256]{1,0:T(1,128)} %get-tuple-element.45.refs_5_), custom_call_target="tpu_custom_call" | custom-call | flops 201326592 | bytes 1835008 | tf_op jit(solution)/shard_map/head_flip/pallas_call | solution.py:133
  190.8 3.6 %all-to-all-start.10 = ((f32[32,1,512]{2,1,0:T(1,128)}), f32[32,1,512]{2,1,0:T(1,128)S(1)}, u32[]{:S(2)}, u32[]{:S(2)}) async-start(f32[32,1,512]{2,1,0:T(1,128)} %get-tuple-element.47), calls=%async_computation.10 | async-start | bytes 131072 | tf_op jit(solution)/shard_map/all_to_all | solution.py:39
  196.0 5.7 %all-to-all-done.10 = f32[32,1,512]{2,1,0:T(1,128)S(1)} async-done(((f32[32,1,512]{2,1,0:T(1,128)}), f32[32,1,512]{2,1,0:T(1,128)S(1)}, u32[]{:S(2)}, u32[]{:S(2)}) %all-to-all-start.10) | async-done | bytes 65568 | tf_op jit(solution)/shard_map/all_to_all | solution.py:39
  202.5 3.5 %all-to-all-start.11 = ((f32[16,1,512]{2,1,0:T(1,128)}), f32[16,1,512]{2,1,0:T(1,128)S(1)}, u32[]{:S(2)}, u32[]{:S(2)}) async-start(f32[16,1,512]{2,1,0:T(1,128)} %broadcast_in_dim.83), calls=%async_computation.11 | async-start | bytes 65536 | tf_op jit(solution)/shard_map/all_to_all | solution.py:39
  206.0 1.0 broadcast_select_fusion.1
  207.0 10.5 %all-to-all-done.11 = f32[16,1,512]{2,1,0:T(1,128)S(1)} async-done(((f32[16,1,512]{2,1,0:T(1,128)}), f32[16,1,512]{2,1,0:T(1,128)S(1)}, u32[]{:S(2)}, u32[]{:S(2)}) %all-to-all-start.11) | async-done | bytes 32800 | tf_op jit(solution)/shard_map/all_to_all | solution.py:39
  (199 shorter events, 24.6 us)
Async XLA Ops:
  7.2 11.6 %copy-start.4 = (bf16[8,256,128]{2,1,0:T(8,128)(2,1)S(1)}, bf16[8,256,128]{2,1,0:T(8,128)(2,1)}, u32[]{:S(2)}) copy-start(bf16[8,256,128]{2,1,0:T(8,128)(2,1)} %param.37) | copy-start | bytes 1572868
  7.2 11.6 %copy-start.3 = (bf16[8,256,128]{2,1,0:T(8,128)(2,1)S(1)}, bf16[8,256,128]{2,1,0:T(8,128)(2,1)}, u32[]{:S(2)}) copy-start(bf16[8,256,128]{2,1,0:T(8,128)(2,1)} %param.38) | copy-start | bytes 1572868
  9.1 10.4 %all-to-all-start = ((bf16[4,32,896]{2,1,0:T(8,128)(2,1)}), bf16[4,32,896]{2,1,0:T(8,128)(2,1)S(1)}, u32[]{:S(2)}, u32[]{:S(2)}) async-start(bf16[4,32,896]{2,1,0:T(8,128)(2,1)} %get-tuple-element.27), calls=%async_computation | async-start | bytes 458752 | tf_op jit(solution)/shard_map/all_to_all | solution.py:39
  14.1 93.1 %all-gather.2.cloned.1.call-start = ((), (), s32[]{:S(2)}) async-start(), calls=%async_computation.12 | async-start | bytes 2785280 | tf_op jit(solution)/shard_map/all_gather | solution.py:187
  18.8 29.4 %copy-start.7 = (f32[128]{0:T(128)S(1)}, f32[128]{0:T(128)}, u32[]{:S(2)}) copy-start(f32[128]{0:T(128)} %param.28) | copy-start | bytes 1540
  18.8 29.5 %copy-start.8 = (f32[128]{0:T(128)S(1)}, f32[128]{0:T(128)}, u32[]{:S(2)}) copy-start(f32[128]{0:T(128)} %param.27) | copy-start | bytes 1540
  18.9 44.1 %copy-start.9 = (s32[8]{0:T(128)S(1)}, s32[8]{0:T(128)}, u32[]{:S(2)}) copy-start(s32[8]{0:T(128)} %param.39) | copy-start | bytes 100
  20.8 26.9 %all-to-all-start.1 = ((bf16[16,30,128]{2,1,0:T(8,128)(2,1)}), bf16[16,30,128]{2,1,0:T(8,128)(2,1)S(1)}, u32[]{:S(2)}, u32[]{:S(2)}) async-start(bf16[16,30,128]{2,1,0:T(8,128)(2,1)} %copy.265), calls=%async_computation.1 | async-start | bytes 262144 | tf_op jit(solution)/shard_map/all_to_all | solution.py:39
  36.1 12.8 %collective-permute-start = (bf16[2,2,256,128]{3,2,1,0:T(8,128)(2,1)S(1)}, bf16[2,2,256,128]{3,2,1,0:T(8,128)(2,1)S(1)}, u32[]{:S(2)}, u32[]{:S(2)}) collective-permute-start(bf16[2,2,256,128]{3,2,1,0:T(8,128)(2,1)S(1)} %get-tuple-element.29), channel_id=1, source_target_pairs={{0,8},{8,0},{16,24},{24,16},{1,9},{9,1},{17,25},{25,17},{2,10},{10... | collective-permute-start | bytes 786440 | tf_op jit(solution)/shard_map/ppermute | solution.py:209
  38.9 9.9 %collective-permute-start.1 = (bf16[2,2,256,128]{3,2,1,0:T(8,128)(2,1)S(1)}, bf16[2,2,256,128]{3,2,1,0:T(8,128)(2,1)S(1)}, u32[]{:S(2)}, u32[]{:S(2)}) collective-permute-start(bf16[2,2,256,128]{3,2,1,0:T(8,128)(2,1)S(1)} %get-tuple-element.30), channel_id=1, source_target_pairs={{0,24},{8,16},{16,8},{24,0},{1,25},{9,17},{17,9},{25,1},{2,26},{10... | collective-permute-start | bytes 786440 | tf_op jit(solution)/shard_map/ppermute | solution.py:209
  49.5 22.0 %all-to-all-start.2 = ((bf16[16,32,128]{2,1,0:T(8,128)(2,1)}), bf16[16,32,128]{2,1,0:T(8,128)(2,1)S(1)}, u32[]{:S(2)}, u32[]{:S(2)}) async-start(bf16[16,32,128]{2,1,0:T(8,128)(2,1)} %broadcast_in_dim.69), calls=%async_computation.2 | async-start | bytes 262144 | tf_op jit(solution)/shard_map/all_to_all | solution.py:39
  59.4 8.7 %collective-permute-start.2 = (bf16[2,2,256,128]{3,2,1,0:T(8,128)(2,1)S(1)}, bf16[2,2,256,128]{3,2,1,0:T(8,128)(2,1)S(1)}, u32[]{:S(2)}, u32[]{:S(2)}) collective-permute-start(bf16[2,2,256,128]{3,2,1,0:T(8,128)(2,1)S(1)} %get-tuple-element.34), channel_id=1, source_target_pairs={{0,16},{8,24},{16,0},{24,8},{1,17},{9,25},{17,1},{25,9},{2,18},{10... | collective-permute-start | bytes 786440 | tf_op jit(solution)/shard_map/ppermute | solution.py:209
  63.1 20.2 %copy-start.6 = (s32[256]{0:T(256)}, s32[256]{0:T(256)S(1)}, u32[]{:S(2)}) copy-start(s32[256]{0:T(256)S(1)} %iota_add_fusion) | copy-start | bytes 3076
  74.9 21.0 %all-to-all-start.3 = ((bf16[16,30,128]{2,1,0:T(8,128)(2,1)}), bf16[16,30,128]{2,1,0:T(8,128)(2,1)S(1)}, u32[]{:S(2)}, u32[]{:S(2)}) async-start(bf16[16,30,128]{2,1,0:T(8,128)(2,1)} %copy.282), calls=%async_computation.3 | async-start | bytes 262144 | tf_op jit(solution)/shard_map/all_to_all | solution.py:39
  98.2 8.8 %all-to-all-start.4 = ((bf16[4,228,128]{2,1,0:T(8,128)(2,1)}), bf16[4,228,128]{2,1,0:T(8,128)(2,1)S(1)}, u32[]{:S(2)}, u32[]{:S(2)}) async-start(bf16[4,228,128]{2,1,0:T(8,128)(2,1)} %pad_maximum_fusion.1), calls=%async_computation.4 | async-start | bytes 475136 | tf_op jit(solution)/shard_map/all_to_all | solution.py:39
  109.1 18.8 %copy-start.1 = (bf16[512,2560]{1,0:T(8,128)(2,1)S(1)}, bf16[512,2560]{1,0:T(8,128)(2,1)}, u32[]{:S(2)}) copy-start(bf16[512,2560]{1,0:T(8,128)(2,1)} %all-gather.2.cloned.1.call-done) | copy-start | bytes 7864324
  109.7 17.7 %all-to-all-start.5 = ((bf16[8,24,512]{2,1,0:T(8,128)(2,1)}), bf16[8,24,512]{2,1,0:T(8,128)(2,1)S(1)}, u32[]{:S(2)}, u32[]{:S(2)}) async-start(bf16[8,24,512]{2,1,0:T(8,128)(2,1)} %broadcast_in_dim.76), calls=%async_computation.5 | async-start | bytes 393216 | tf_op jit(solution)/shard_map/all_to_all | solution.py:39
  138.0 10.4 %all-to-all-start.7 = ((bf16[8,12,128]{2,1,0:T(8,128)(2,1)}), bf16[8,12,128]{2,1,0:T(8,128)(2,1)S(1)}, u32[]{:S(2)}, u32[]{:S(2)}) async-start(bf16[8,12,128]{2,1,0:T(8,128)(2,1)} %copy.300), calls=%async_computation.7 | async-start | bytes 65536 | tf_op jit(solution)/shard_map/all_to_all | solution.py:39
  178.9 5.3 %copy-start = (bf16[16,192,128]{2,1,0:T(8,128)(2,1)}, bf16[16,192,128]{2,1,0:T(8,128)(2,1)S(1)}, u32[]{:S(2)}) copy-start(bf16[16,192,128]{2,1,0:T(8,128)(2,1)S(1)} %all_to_all.62.refs_2_) | copy-start | bytes 2359300
  178.9 8.1 %collective-permute-start.3 = (bf16[16,192,128]{2,1,0:T(8,128)(2,1)S(1)}, bf16[16,192,128]{2,1,0:T(8,128)(2,1)S(1)}, u32[]{:S(2)}, u32[]{:S(2)}) collective-permute-start(bf16[16,192,128]{2,1,0:T(8,128)(2,1)S(1)} %all_to_all.62.refs_2_), channel_id=1, source_target_pairs={{0,1},{1,0},{2,3},{3,2},{4,5},{5,4},{6,7},{7,6},{8,9},{9,8},{10,11... | collective-permute-start | bytes 2359304 | tf_op jit(solution)/shard_map/ppermute | solution.py:333
  187.0 19.0 %copy-start.5 = (f32[192,256]{1,0:T(8,128)S(1)}, f32[192,256]{1,0:T(8,128)}, u32[]{:S(2)}) copy-start(f32[192,256]{1,0:T(8,128)} %get-tuple-element.44) | copy-start | bytes 589828
  187.0 0.9 copy-start.2
  190.8 10.9 %all-to-all-start.10 = ((f32[32,1,512]{2,1,0:T(1,128)}), f32[32,1,512]{2,1,0:T(1,128)S(1)}, u32[]{:S(2)}, u32[]{:S(2)}) async-start(f32[32,1,512]{2,1,0:T(1,128)} %get-tuple-element.47), calls=%async_computation.10 | async-start | bytes 131072 | tf_op jit(solution)/shard_map/all_to_all | solution.py:39
  202.5 15.0 %all-to-all-start.11 = ((f32[16,1,512]{2,1,0:T(1,128)}), f32[16,1,512]{2,1,0:T(1,128)S(1)}, u32[]{:S(2)}, u32[]{:S(2)}) async-start(f32[16,1,512]{2,1,0:T(1,128)} %broadcast_in_dim.83), calls=%async_computation.11 | async-start | bytes 65536 | tf_op jit(solution)/shard_map/all_to_all | solution.py:39
Sparse Core Ops, SparseCore 0:
  17.6 79.8 all-gather.1

commit v13 on v12

--- a/solution.py
+++ b/solution.py
@@ -285,13 +285,15 @@
     gated = jnp.swapaxes(both[:, 24:36].reshape(4, 2, 6, 128), 0, 1).reshape(2, 24, 128)
 
     contract = (((1,), (1,)), ((), ()))
+    repeated = jnp.broadcast_to(jnp.concatenate([gated[0], gated[1]], axis=1)[None], (8, 24, 256))
+    repeated = lax.optimization_barrier(repeated.reshape(192, 256))
     attn = lax.dot_general(
-        jnp.concatenate([gated[0], gated[1]], axis=1),
+        repeated,
         ffn[:, 2304:],
         contract,
         preferred_element_type=F32,
     )
-    attn = jnp.broadcast_to(attn.astype(BF)[None], (8, 24, 512))
+    attn = attn.astype(BF).reshape(8, 24, 512)
     attn, fresh = lax.optimization_barrier((attn, both[:, 36:]))
     tree_keys = fresh[:, :96].reshape(requests, tree, 128)
     tree_values = fresh[:, 96:].reshape(requests, tree, 128)

time: 227 us -> 227 us (level)
  no operation moved by 1% of the time
where the time goes in v13:
time: 227 us; the launch traced here: 225 us
  starting transfers between devices  81.6 us (36%)
  waiting for transfers between devices  52 us (23%)
  blocking collectives  38.6 us (17%)
  between operations  14.9 us (7%)
  matrix products  11.3 us (5%)
  local copies, waits for them, and re-layouts  10.9 us (5%)
  other arithmetic  8.69 us (4%)
  Pallas kernels  7.54 us (3%)
    all_to_all x9, starting transfers between devices, swap(): return lax.all_to_all(values, axis, 0, 0, tiled=True)  66.2 us
    all_to_all x9, waiting for transfers between devices, swap(): return lax.all_to_all(values, axis, 0, 0, tiled=True)  47.2 us
    all_to_all x3, blocking collectives, swap(): return lax.all_to_all(values, axis, 0, 0, tiled=True)  38.6 us
    ppermute x3, starting transfers between devices, on_device(): lax.ppermute(parts[shift], 'y', [(i, i ^ shift) for i in range(4)])  10.2 us
    pallas_call x2, Pallas kernels, head(): pl.pallas_call(lambda *refs: head_kernel(*refs, flip=flip, width=2048), o...  5.63 us
    ppermute x1, starting transfers between devices, on_device(): other = lax.ppermute(half, 'c', [(0, 1), (1, 0)])  5.24 us
  transfers between devices with their start and end apart: 14, of which 10 were waited for; matrix products, arithmetic and copies ran while one was open for 10% of the time, Pallas kernels for 1%

profile of v13, /device:TPU:1, one launch (start us, length us, event | category | flops | bytes accessed | tf_op | source)
XLA Modules:
  0.0 225.5 jit_solution(16238148945584403232)
XLA Ops:
  7.2 1.9 pack.1
  9.1 5.0 %all-to-all-start = ((bf16[4,32,896]{2,1,0:T(8,128)(2,1)}), bf16[4,32,896]{2,1,0:T(8,128)(2,1)S(1)}, u32[]{:S(2)}, u32[]{:S(2)}) async-start(bf16[4,32,896]{2,1,0:T(8,128)(2,1)} %get-tuple-element.27), calls=%async_computation | async-start | bytes 458752 | tf_op jit(solution)/shard_map/all_to_all | solution.py:39
  14.9 1.4 fusion.4
  20.8 14.9 %all-to-all-start.1 = ((bf16[16,30,128]{2,1,0:T(8,128)(2,1)}), bf16[16,30,128]{2,1,0:T(8,128)(2,1)S(1)}, u32[]{:S(2)}, u32[]{:S(2)}) async-start(bf16[16,30,128]{2,1,0:T(8,128)(2,1)} %copy.265), calls=%async_computation.1 | async-start | bytes 262144 | tf_op jit(solution)/shard_map/all_to_all | solution.py:39
  36.1 2.9 %collective-permute-start = (bf16[2,2,256,128]{3,2,1,0:T(8,128)(2,1)S(1)}, bf16[2,2,256,128]{3,2,1,0:T(8,128)(2,1)S(1)}, u32[]{:S(2)}, u32[]{:S(2)}) collective-permute-start(bf16[2,2,256,128]{3,2,1,0:T(8,128)(2,1)S(1)} %get-tuple-element.29), channel_id=1, source_target_pairs={{0,8},{8,0},{16,24},{24,16},{1,9},{9,1},{17,25},{25,17},{2,10},{10... | collective-permute-start | bytes 786440 | tf_op jit(solution)/shard_map/ppermute | solution.py:209
  38.9 3.7 %collective-permute-start.1 = (bf16[2,2,256,128]{3,2,1,0:T(8,128)(2,1)S(1)}, bf16[2,2,256,128]{3,2,1,0:T(8,128)(2,1)S(1)}, u32[]{:S(2)}, u32[]{:S(2)}) collective-permute-start(bf16[2,2,256,128]{3,2,1,0:T(8,128)(2,1)S(1)} %get-tuple-element.30), channel_id=1, source_target_pairs={{0,24},{8,16},{16,8},{24,0},{1,25},{9,17},{17,9},{25,1},{2,26},{10... | collective-permute-start | bytes 786440 | tf_op jit(solution)/shard_map/ppermute | solution.py:209
  42.7 5.1 %all-to-all-done.1 = bf16[16,30,128]{2,1,0:T(8,128)(2,1)S(1)} async-done(((bf16[16,30,128]{2,1,0:T(8,128)(2,1)}), bf16[16,30,128]{2,1,0:T(8,128)(2,1)S(1)}, u32[]{:S(2)}, u32[]{:S(2)}) %all-to-all-start.1) | async-done | bytes 122912 | tf_op jit(solution)/shard_map/all_to_all | solution.py:39
  49.5 9.9 %all-to-all-start.2 = ((bf16[16,32,128]{2,1,0:T(8,128)(2,1)}), bf16[16,32,128]{2,1,0:T(8,128)(2,1)S(1)}, u32[]{:S(2)}, u32[]{:S(2)}) async-start(bf16[16,32,128]{2,1,0:T(8,128)(2,1)} %broadcast_in_dim.69), calls=%async_computation.2 | async-start | bytes 262144 | tf_op jit(solution)/shard_map/all_to_all | solution.py:39
  59.4 3.6 %collective-permute-start.2 = (bf16[2,2,256,128]{3,2,1,0:T(8,128)(2,1)S(1)}, bf16[2,2,256,128]{3,2,1,0:T(8,128)(2,1)S(1)}, u32[]{:S(2)}, u32[]{:S(2)}) collective-permute-start(bf16[2,2,256,128]{3,2,1,0:T(8,128)(2,1)S(1)} %get-tuple-element.34), channel_id=1, source_target_pairs={{0,16},{8,24},{16,0},{24,8},{1,17},{9,25},{17,1},{25,9},{2,18},{10... | collective-permute-start | bytes 786440 | tf_op jit(solution)/shard_map/ppermute | solution.py:209
  64.1 4.1 %collective-permute-done.2 = bf16[2,2,256,128]{3,2,1,0:T(8,128)(2,1)S(1)} collective-permute-done((bf16[2,2,256,128]{3,2,1,0:T(8,128)(2,1)S(1)}, bf16[2,2,256,128]{3,2,1,0:T(8,128)(2,1)S(1)}, u32[]{:S(2)}, u32[]{:S(2)}) %collective-permute-start.2) | collective-permute-done | bytes 262176 | tf_op jit(solution)/shard_map/ppermute | solution.py:209
  68.2 3.4 %all-to-all-done.2 = bf16[16,32,128]{2,1,0:T(8,128)(2,1)S(1)} async-done(((bf16[16,32,128]{2,1,0:T(8,128)(2,1)}), bf16[16,32,128]{2,1,0:T(8,128)(2,1)S(1)}, u32[]{:S(2)}, u32[]{:S(2)}) %all-to-all-start.2) | async-done | bytes 131104 | tf_op jit(solution)/shard_map/all_to_all | solution.py:39
  74.9 8.3 %all-to-all-start.3 = ((bf16[16,30,128]{2,1,0:T(8,128)(2,1)}), bf16[16,30,128]{2,1,0:T(8,128)(2,1)S(1)}, u32[]{:S(2)}, u32[]{:S(2)}) async-start(bf16[16,30,128]{2,1,0:T(8,128)(2,1)} %copy.282), calls=%async_computation.3 | async-start | bytes 262144 | tf_op jit(solution)/shard_map/all_to_all | solution.py:39
  84.7 11.3 %all-to-all-done.3 = bf16[16,30,128]{2,1,0:T(8,128)(2,1)S(1)} async-done(((bf16[16,30,128]{2,1,0:T(8,128)(2,1)}), bf16[16,30,128]{2,1,0:T(8,128)(2,1)S(1)}, u32[]{:S(2)}, u32[]{:S(2)}) %all-to-all-start.3) | async-done | bytes 122912 | tf_op jit(solution)/shard_map/all_to_all | solution.py:39
  98.2 3.4 %all-to-all-start.4 = ((bf16[4,228,128]{2,1,0:T(8,128)(2,1)}), bf16[4,228,128]{2,1,0:T(8,128)(2,1)S(1)}, u32[]{:S(2)}, u32[]{:S(2)}) async-start(bf16[4,228,128]{2,1,0:T(8,128)(2,1)} %pad_maximum_fusion.1), calls=%async_computation.4 | async-start | bytes 475136 | tf_op jit(solution)/shard_map/all_to_all | solution.py:39
  101.9 5.1 %all-to-all-done.4 = bf16[4,228,128]{2,1,0:T(8,128)(2,1)S(1)} async-done(((bf16[4,228,128]{2,1,0:T(8,128)(2,1)}), bf16[4,228,128]{2,1,0:T(8,128)(2,1)S(1)}, u32[]{:S(2)}, u32[]{:S(2)}) %all-to-all-start.4) | async-done | bytes 233504 | tf_op jit(solution)/shard_map/all_to_all | solution.py:39
  107.2 1.9 convolution_convert_fusion.3
  109.8 11.8 %all-to-all-start.5 = ((bf16[8,24,512]{2,1,0:T(8,128)(2,1)}), bf16[8,24,512]{2,1,0:T(8,128)(2,1)S(1)}, u32[]{:S(2)}, u32[]{:S(2)}) async-start(bf16[8,24,512]{2,1,0:T(8,128)(2,1)} %bitcast.51), calls=%async_computation.5 | async-start | bytes 393216 | tf_op jit(solution)/shard_map/all_to_all | solution.py:39
  121.6 2.4 %fusion.2 = bf16[8,256,128]{2,1,0:T(8,128)(2,1)} fusion(bf16[8,256,128]{2,1,0:T(8,128)(2,1)S(1)} %copy-done.3, bf16[8,48,128]{2,1,0:T(8,128)(2,1)} %bitcast.160, pred[8,256]{1,0:T(8,128)(4,1)S(1)} %broadcast_compare_fusion, f32[8,48]{1,0:T(8,128)S(1)} %gather_fusion, s32[8,48]{1,0:T(8,128)S(1)} %add_add_fusion, s32[256]{0:T(256)} %copy-done.6), kind=kOutput, calls=%fused_computation.14 | convolution fusion | flops 25886720 | bytes 1153024 | tf_op jit(solution)/shard_map/rca,rae->rce/dot_general | solution.py:307
  124.0 2.6 %fusion.1 = bf16[8,256,128]{2,1,0:T(8,128)(2,1)} fusion(bf16[8,256,128]{2,1,0:T(8,128)(2,1)} %param.37, bf16[8,48,128]{2,1,0:T(8,128)(2,1)S(1)} %bitcast.159, pred[8,256]{1,0:T(8,128)(4,1)S(1)} %broadcast_compare_fusion, f32[8,48]{1,0:T(8,128)S(1)} %gather_fusion, s32[8,48]{1,0:T(8,128)S(1)} %add_add_fusion, s32[256]{0:T(256)} %copy-done.6), kind=kOutput, calls=%fused_computation.13 | convolution fusion | flops 25886720 | bytes 1153024 | tf_op jit(solution)/shard_map/rca,rae->rce/dot_general | solution.py:306
  128.3 8.4 %all_to_all.60 = bf16[4,24,1664]{2,1,0:T(8,128)(2,1)S(1)} all-to-all(bf16[4,24,1664]{2,1,0:T(8,128)(2,1)S(1)} %broadcast_in_dim.79), channel_id=1, replica_groups=mesh['z'=16,'y'=4,'x'=4,'c'=2] {'y'}, dimensions={0} | all-to-all | bytes 638976 | tf_op jit(solution)/shard_map/all_to_all | solution.py:39
  138.1 5.7 %all-to-all-start.7 = ((bf16[8,12,128]{2,1,0:T(8,128)(2,1)}), bf16[8,12,128]{2,1,0:T(8,128)(2,1)S(1)}, u32[]{:S(2)}, u32[]{:S(2)}) async-start(bf16[8,12,128]{2,1,0:T(8,128)(2,1)} %copy.300), calls=%async_computation.7 | async-start | bytes 65536 | tf_op jit(solution)/shard_map/all_to_all | solution.py:39
  143.8 4.7 %all-to-all-done.7 = bf16[8,12,128]{2,1,0:T(8,128)(2,1)S(1)} async-done(((bf16[8,12,128]{2,1,0:T(8,128)(2,1)}), bf16[8,12,128]{2,1,0:T(8,128)(2,1)S(1)}, u32[]{:S(2)}, u32[]{:S(2)}) %all-to-all-start.7) | async-done | bytes 24608 | tf_op jit(solution)/shard_map/all_to_all | solution.py:39
  148.6 15.5 %all_to_all.61 = bf16[16,12,128]{2,1,0:T(8,128)(2,1)S(1)} all-to-all(bf16[16,12,128]{2,1,0:T(8,128)(2,1)S(1)} %broadcast_in_dim.80), channel_id=1, replica_groups=mesh['z'=16,'y'=4,'x'=4,'c'=2] {'z'}, dimensions={0} | all-to-all | bytes 98304 | tf_op jit(solution)/shard_map/all_to_all | solution.py:39
  164.3 14.7 %all_to_all.62.refs_2_ = bf16[16,192,128]{2,1,0:T(8,128)(2,1)S(1)} all-to-all(bf16[16,192,128]{2,1,0:T(8,128)(2,1)S(1)} %broadcast_in_dim.82), channel_id=1, replica_groups=mesh['z'=16,'y'=4,'x'=4,'c'=2] {'y','x'}, dimensions={0} | all-to-all | bytes 1572864 | tf_op jit(solution)/shard_map/all_to_all | solution.py:39
  179.0 5.2 %collective-permute-start.3 = (bf16[16,192,128]{2,1,0:T(8,128)(2,1)S(1)}, bf16[16,192,128]{2,1,0:T(8,128)(2,1)S(1)}, u32[]{:S(2)}, u32[]{:S(2)}) collective-permute-start(bf16[16,192,128]{2,1,0:T(8,128)(2,1)S(1)} %all_to_all.62.refs_2_), channel_id=1, source_target_pairs={{0,1},{1,0},{2,3},{3,2},{4,5},{5,4},{6,7},{7,6},{8,9},{9,8},{10,11... | collective-permute-start | bytes 2359304 | tf_op jit(solution)/shard_map/ppermute | solution.py:335
  184.3 2.8 %head_own.1 = (f32[192,256]{1,0:T(8,128)}, f32[1,256]{1,0:T(1,128)}) custom-call(s32[1]{0:T(128)} %bitcast.refs_0_, f32[8]{0:T(128)} %refs_1_.3, bf16[16,192,128]{2,1,0:T(8,128)(2,1)} %copy-done, f32[16,128]{1,0:T(8,128)} %reshape.514.refs_3_, bf16[2048,256]{1,0:T(8,128)(2,1)} %refs_4_.3), custom_call_target="tpu_custom_call" | custom-call | flops 201326592 | bytes 1835008 | tf_op jit(solution)/shard_map/head_own/pallas_call | solution.py:133
  188.0 2.8 %head_flip.1 = (f32[192,256]{1,0:T(8,128)}, f32[32,1,512]{2,1,0:T(1,128)}) custom-call(s32[1]{0:T(128)} %bitcast.refs_0_, f32[8]{0:T(128)} %refs_1_.3, bf16[16,192,128]{2,1,0:T(8,128)(2,1)} %copy-done.2, f32[16,128]{1,0:T(8,128)} %reshape.514.refs_3_, bf16[2048,256]{1,0:T(8,128)(2,1)} %refs_4_.3, f32[1,256]{1,0:T(1,128)} %get-tuple-element.45.refs_5_), custom_call_target="tpu_custom_call" | custom-call | flops 201326592 | bytes 1835008 | tf_op jit(solution)/shard_map/head_flip/pallas_call | solution.py:133
  190.8 3.6 %all-to-all-start.10 = ((f32[32,1,512]{2,1,0:T(1,128)}), f32[32,1,512]{2,1,0:T(1,128)S(1)}, u32[]{:S(2)}, u32[]{:S(2)}) async-start(f32[32,1,512]{2,1,0:T(1,128)} %get-tuple-element.47), calls=%async_computation.10 | async-start | bytes 131072 | tf_op jit(solution)/shard_map/all_to_all | solution.py:39
  196.1 5.7 %all-to-all-done.10 = f32[32,1,512]{2,1,0:T(1,128)S(1)} async-done(((f32[32,1,512]{2,1,0:T(1,128)}), f32[32,1,512]{2,1,0:T(1,128)S(1)}, u32[]{:S(2)}, u32[]{:S(2)}) %all-to-all-start.10) | async-done | bytes 65568 | tf_op jit(solution)/shard_map/all_to_all | solution.py:39
  202.6 3.5 %all-to-all-start.11 = ((f32[16,1,512]{2,1,0:T(1,128)}), f32[16,1,512]{2,1,0:T(1,128)S(1)}, u32[]{:S(2)}, u32[]{:S(2)}) async-start(f32[16,1,512]{2,1,0:T(1,128)} %broadcast_in_dim.83), calls=%async_computation.11 | async-start | bytes 65536 | tf_op jit(solution)/shard_map/all_to_all | solution.py:39
  206.1 1.0 broadcast_select_fusion.1
  207.1 10.5 %all-to-all-done.11 = f32[16,1,512]{2,1,0:T(1,128)S(1)} async-done(((f32[16,1,512]{2,1,0:T(1,128)}), f32[16,1,512]{2,1,0:T(1,128)S(1)}, u32[]{:S(2)}, u32[]{:S(2)}) %all-to-all-start.11) | async-done | bytes 32800 | tf_op jit(solution)/shard_map/all_to_all | solution.py:39
  (200 shorter events, 23.9 us)
Async XLA Ops:
  7.2 11.6 %copy-start.4 = (bf16[8,256,128]{2,1,0:T(8,128)(2,1)S(1)}, bf16[8,256,128]{2,1,0:T(8,128)(2,1)}, u32[]{:S(2)}) copy-start(bf16[8,256,128]{2,1,0:T(8,128)(2,1)} %param.37) | copy-start | bytes 1572868
  7.2 11.6 %copy-start.3 = (bf16[8,256,128]{2,1,0:T(8,128)(2,1)S(1)}, bf16[8,256,128]{2,1,0:T(8,128)(2,1)}, u32[]{:S(2)}) copy-start(bf16[8,256,128]{2,1,0:T(8,128)(2,1)} %param.38) | copy-start | bytes 1572868
  9.1 10.4 %all-to-all-start = ((bf16[4,32,896]{2,1,0:T(8,128)(2,1)}), bf16[4,32,896]{2,1,0:T(8,128)(2,1)S(1)}, u32[]{:S(2)}, u32[]{:S(2)}) async-start(bf16[4,32,896]{2,1,0:T(8,128)(2,1)} %get-tuple-element.27), calls=%async_computation | async-start | bytes 458752 | tf_op jit(solution)/shard_map/all_to_all | solution.py:39
  14.1 93.1 %all-gather.2.cloned.1.call-start = ((), (), s32[]{:S(2)}) async-start(), calls=%async_computation.12 | async-start | bytes 2785280 | tf_op jit(solution)/shard_map/all_gather | solution.py:187
  18.8 29.4 %copy-start.7 = (f32[128]{0:T(128)S(1)}, f32[128]{0:T(128)}, u32[]{:S(2)}) copy-start(f32[128]{0:T(128)} %param.28) | copy-start | bytes 1540
  18.8 29.5 %copy-start.8 = (f32[128]{0:T(128)S(1)}, f32[128]{0:T(128)}, u32[]{:S(2)}) copy-start(f32[128]{0:T(128)} %param.27) | copy-start | bytes 1540
  18.9 44.1 %copy-start.9 = (s32[8]{0:T(128)S(1)}, s32[8]{0:T(128)}, u32[]{:S(2)}) copy-start(s32[8]{0:T(128)} %param.39) | copy-start | bytes 100
  20.8 26.9 %all-to-all-start.1 = ((bf16[16,30,128]{2,1,0:T(8,128)(2,1)}), bf16[16,30,128]{2,1,0:T(8,128)(2,1)S(1)}, u32[]{:S(2)}, u32[]{:S(2)}) async-start(bf16[16,30,128]{2,1,0:T(8,128)(2,1)} %copy.265), calls=%async_computation.1 | async-start | bytes 262144 | tf_op jit(solution)/shard_map/all_to_all | solution.py:39
  36.1 12.8 %collective-permute-start = (bf16[2,2,256,128]{3,2,1,0:T(8,128)(2,1)S(1)}, bf16[2,2,256,128]{3,2,1,0:T(8,128)(2,1)S(1)}, u32[]{:S(2)}, u32[]{:S(2)}) collective-permute-start(bf16[2,2,256,128]{3,2,1,0:T(8,128)(2,1)S(1)} %get-tuple-element.29), channel_id=1, source_target_pairs={{0,8},{8,0},{16,24},{24,16},{1,9},{9,1},{17,25},{25,17},{2,10},{10... | collective-permute-start | bytes 786440 | tf_op jit(solution)/shard_map/ppermute | solution.py:209
  38.9 9.9 %collective-permute-start.1 = (bf16[2,2,256,128]{3,2,1,0:T(8,128)(2,1)S(1)}, bf16[2,2,256,128]{3,2,1,0:T(8,128)(2,1)S(1)}, u32[]{:S(2)}, u32[]{:S(2)}) collective-permute-start(bf16[2,2,256,128]{3,2,1,0:T(8,128)(2,1)S(1)} %get-tuple-element.30), channel_id=1, source_target_pairs={{0,24},{8,16},{16,8},{24,0},{1,25},{9,17},{17,9},{25,1},{2,26},{10... | collective-permute-start | bytes 786440 | tf_op jit(solution)/shard_map/ppermute | solution.py:209
  49.5 22.0 %all-to-all-start.2 = ((bf16[16,32,128]{2,1,0:T(8,128)(2,1)}), bf16[16,32,128]{2,1,0:T(8,128)(2,1)S(1)}, u32[]{:S(2)}, u32[]{:S(2)}) async-start(bf16[16,32,128]{2,1,0:T(8,128)(2,1)} %broadcast_in_dim.69), calls=%async_computation.2 | async-start | bytes 262144 | tf_op jit(solution)/shard_map/all_to_all | solution.py:39
  59.4 8.7 %collective-permute-start.2 = (bf16[2,2,256,128]{3,2,1,0:T(8,128)(2,1)S(1)}, bf16[2,2,256,128]{3,2,1,0:T(8,128)(2,1)S(1)}, u32[]{:S(2)}, u32[]{:S(2)}) collective-permute-start(bf16[2,2,256,128]{3,2,1,0:T(8,128)(2,1)S(1)} %get-tuple-element.34), channel_id=1, source_target_pairs={{0,16},{8,24},{16,0},{24,8},{1,17},{9,25},{17,1},{25,9},{2,18},{10... | collective-permute-start | bytes 786440 | tf_op jit(solution)/shard_map/ppermute | solution.py:209
  63.1 20.2 %copy-start.6 = (s32[256]{0:T(256)}, s32[256]{0:T(256)S(1)}, u32[]{:S(2)}) copy-start(s32[256]{0:T(256)S(1)} %iota_add_fusion) | copy-start | bytes 3076
  74.9 21.0 %all-to-all-start.3 = ((bf16[16,30,128]{2,1,0:T(8,128)(2,1)}), bf16[16,30,128]{2,1,0:T(8,128)(2,1)S(1)}, u32[]{:S(2)}, u32[]{:S(2)}) async-start(bf16[16,30,128]{2,1,0:T(8,128)(2,1)} %copy.282), calls=%async_computation.3 | async-start | bytes 262144 | tf_op jit(solution)/shard_map/all_to_all | solution.py:39
  98.2 8.8 %all-to-all-start.4 = ((bf16[4,228,128]{2,1,0:T(8,128)(2,1)}), bf16[4,228,128]{2,1,0:T(8,128)(2,1)S(1)}, u32[]{:S(2)}, u32[]{:S(2)}) async-start(bf16[4,228,128]{2,1,0:T(8,128)(2,1)} %pad_maximum_fusion.1), calls=%async_computation.4 | async-start | bytes 475136 | tf_op jit(solution)/shard_map/all_to_all | solution.py:39
  109.1 18.8 %copy-start.1 = (bf16[512,2560]{1,0:T(8,128)(2,1)S(1)}, bf16[512,2560]{1,0:T(8,128)(2,1)}, u32[]{:S(2)}) copy-start(bf16[512,2560]{1,0:T(8,128)(2,1)} %all-gather.2.cloned.1.call-done) | copy-start | bytes 7864324
  109.8 17.7 %all-to-all-start.5 = ((bf16[8,24,512]{2,1,0:T(8,128)(2,1)}), bf16[8,24,512]{2,1,0:T(8,128)(2,1)S(1)}, u32[]{:S(2)}, u32[]{:S(2)}) async-start(bf16[8,24,512]{2,1,0:T(8,128)(2,1)} %bitcast.51), calls=%async_computation.5 | async-start | bytes 393216 | tf_op jit(solution)/shard_map/all_to_all | solution.py:39
  138.1 10.4 %all-to-all-start.7 = ((bf16[8,12,128]{2,1,0:T(8,128)(2,1)}), bf16[8,12,128]{2,1,0:T(8,128)(2,1)S(1)}, u32[]{:S(2)}, u32[]{:S(2)}) async-start(bf16[8,12,128]{2,1,0:T(8,128)(2,1)} %copy.300), calls=%async_computation.7 | async-start | bytes 65536 | tf_op jit(solution)/shard_map/all_to_all | solution.py:39
  179.0 5.3 %copy-start = (bf16[16,192,128]{2,1,0:T(8,128)(2,1)}, bf16[16,192,128]{2,1,0:T(8,128)(2,1)S(1)}, u32[]{:S(2)}) copy-start(bf16[16,192,128]{2,1,0:T(8,128)(2,1)S(1)} %all_to_all.62.refs_2_) | copy-start | bytes 2359300
  179.0 8.1 %collective-permute-start.3 = (bf16[16,192,128]{2,1,0:T(8,128)(2,1)S(1)}, bf16[16,192,128]{2,1,0:T(8,128)(2,1)S(1)}, u32[]{:S(2)}, u32[]{:S(2)}) collective-permute-start(bf16[16,192,128]{2,1,0:T(8,128)(2,1)S(1)} %all_to_all.62.refs_2_), channel_id=1, source_target_pairs={{0,1},{1,0},{2,3},{3,2},{4,5},{5,4},{6,7},{7,6},{8,9},{9,8},{10,11... | collective-permute-start | bytes 2359304 | tf_op jit(solution)/shard_map/ppermute | solution.py:335
  187.1 19.0 %copy-start.5 = (f32[192,256]{1,0:T(8,128)S(1)}, f32[192,256]{1,0:T(8,128)}, u32[]{:S(2)}) copy-start(f32[192,256]{1,0:T(8,128)} %get-tuple-element.44) | copy-start | bytes 589828
  187.1 0.9 copy-start.2
  190.8 10.9 %all-to-all-start.10 = ((f32[32,1,512]{2,1,0:T(1,128)}), f32[32,1,512]{2,1,0:T(1,128)S(1)}, u32[]{:S(2)}, u32[]{:S(2)}) async-start(f32[32,1,512]{2,1,0:T(1,128)} %get-tuple-element.47), calls=%async_computation.10 | async-start | bytes 131072 | tf_op jit(solution)/shard_map/all_to_all | solution.py:39
  202.6 15.0 %all-to-all-start.11 = ((f32[16,1,512]{2,1,0:T(1,128)}), f32[16,1,512]{2,1,0:T(1,128)S(1)}, u32[]{:S(2)}, u32[]{:S(2)}) async-start(f32[16,1,512]{2,1,0:T(1,128)} %broadcast_in_dim.83), calls=%async_computation.11 | async-start | bytes 65536 | tf_op jit(solution)/shard_map/all_to_all | solution.py:39
Sparse Core Ops, SparseCore 0:
  17.6 79.8 all-gather.1
